TPU v7x, 256 devices: a whole 4x4x8 slice. The times are simulated.
256 devices in a mesh: dp: 16 (over x_hi, y, core), seq: 16 (over z, x_lo).
Axes of the slice: x: 4 (x_hi: 2, x_lo: 2; x = x_hi * 2 + x_lo), y: 4, z: 8, core: 2. Of those that a mesh axis runs over, the one named last changes fastest.
Arguments:
- layer_input: bfloat16 [16, 2048, 5120], P('dp', 'seq'), may hold values from -6 to 6
- query_states: bfloat16 [16, 2048, 2560], P('dp', 'seq'), may hold values from -24 to 24
- key_states: bfloat16 [16, 2048, 512], P('dp', 'seq'), may hold values from -6 to 6
- out_grad: bfloat16 [16, 2048, 2560], P('dp', 'seq'), may hold values from -12 to 12
- value_weight: bfloat16 [5120, 512], P('dp'), may hold values from -0.078125 to 0.078125
- segment_ids: int32 [16, 2048], P('dp'), may hold values from 0 to 31, as said below
- pair_split: int32 [16, 32], P('dp'), may hold values from 1 to 2047, as said below
Outputs:
- query_grad: bfloat16 [16, 2048, 2560], P('dp', 'seq')
- key_grad: bfloat16 [16, 2048, 512], P('dp', 'seq')
- input_grad: bfloat16 [16, 2048, 5120], P('dp', 'seq')
- weight_grad: float32 [5120, 512], P('dp', 'seq')
Inputs may be any that keep to these rules, and one draw needn't show every extreme that they name: `segment_ids`: each packed row holds 32 sentence pairs numbered 0 to 31 in order along the row; each pair has 16 to 112 positions, every row has a pair of exactly 112, and the pair lengths of a row can be matched two by two into sums of 128. pair_split[r, s] lies after the first position of pair s and at or before its last position; in every row the first pair's second sentence begins at position 1 and the last pair's at position 2047.
All inputs are finite; a program needn't handle non-finite values.
Results may differ from a plain program's by a relative error of at most 0.0057.
Values may be sent and summed in bfloat16 or wider, within the bound.
A program may use at most 128 MiB of HBM per device.

v0:
```python
import jax
import jax.numpy as jnp
from jax import lax
from jax.sharding import PartitionSpec as P

HD = 128


def with_halo(cells, sides, width):
    for axis, dim in sides:
        count = lax.axis_size(axis)
        ends = count - 1
        head = lax.slice_in_dim(cells, 0, width, axis=dim)
        tail = lax.slice_in_dim(cells, cells.shape[dim] - width, cells.shape[dim], axis=dim)
        cells = jnp.concatenate(
            [
                lax.ppermute(tail, axis, [(i, (i + 1) % count) for i in range(ends)]),
                cells,
                lax.ppermute(head, axis, [((i + 1) % count, i) for i in range(ends)]),
            ],
            axis=dim,
        )
    return cells


def passed_along(array, axis, by):
    count = lax.axis_size(axis)
    pairs = [(i, i + by) for i in range(count) if 0 <= i + by < count]
    return lax.ppermute(array, axis, pairs)


def attend_block(query_rows, key_rows, value_rows, grad_rows, visible):
    rows_here = query_rows.shape[0]
    keys_here = key_rows.shape[0]
    head_count = key_rows.shape[1] // HD
    group_size = query_rows.shape[1] // key_rows.shape[1]
    score_scale = HD ** (-0.5)
    high = lax.Precision.HIGHEST
    query_split = query_rows.reshape(rows_here, head_count, group_size, HD)
    grad_split = grad_rows.reshape(rows_here, head_count, group_size, HD)
    key_split = key_rows.reshape(keys_here, head_count, HD)
    value_split = value_rows.reshape(keys_here, head_count, HD)
    query_parts = []
    key_parts = []
    value_parts = []
    for kv_group in range(head_count):
        query_head = query_split[:, kv_group]
        grad_head = grad_split[:, kv_group]
        key_head = key_split[:, kv_group]
        value_head = value_split[:, kv_group]
        scores = (
            jnp.einsum("qgd,kd->gqk", query_head, key_head, preferred_element_type=jnp.float32)
            * score_scale
        )
        masked = jnp.where(visible[None], scores, -1e30)
        highest = jnp.max(masked, axis=-1, keepdims=True)
        weights = jnp.where(visible[None], jnp.exp(masked - highest), 0.0)
        attention = weights / jnp.sum(weights, axis=-1, keepdims=True)
        attention_low = attention.astype(jnp.bfloat16)
        prob_grad = jnp.einsum(
            "qgd,kd->gqk", grad_head, value_head, preferred_element_type=jnp.float32
        )
        row_delta = jnp.sum(attention * prob_grad, axis=-1, keepdims=True)
        score_grad = attention * (prob_grad - row_delta)
        key_wide = key_head.astype(jnp.float32)
        query_wide = query_head.astype(jnp.float32)
        query_parts.append(
            jnp.einsum("gqk,kd->qgd", score_grad, key_wide, precision=high) * score_scale
        )
        key_parts.append(
            jnp.einsum("gqk,qgd->kd", score_grad, query_wide, precision=high) * score_scale
        )
        value_parts.append(
            jnp.einsum("gqk,qgd->kd", attention_low, grad_head, preferred_element_type=jnp.float32)
        )
    query_grad = jnp.stack(query_parts, axis=1).reshape(rows_here, -1)
    kv_grad = jnp.concatenate(key_parts + value_parts, axis=1)
    return (query_grad, kv_grad)


def local(layer_input, query_states, key_states, out_grad, value_weight, segment_ids, pair_split):
    layer_rows = layer_input[0]
    tok_count = layer_rows.shape[0]
    kv_width = key_states.shape[2]
    row_base = lax.axis_index("seq") * tok_count
    columns = layer_rows
    value_rows = jnp.dot(
        columns,
        lax.all_gather(value_weight, "dp", axis=0, tiled=True),
        preferred_element_type=jnp.float32,
    )
    value_low = value_rows.astype(jnp.bfloat16)
    both_states = jnp.concatenate([key_states[0], value_low], axis=1)
    extended = with_halo(both_states, (("seq", 0),), tok_count)
    key_block = extended[:, :kv_width]
    value_block = extended[:, kv_width:]
    seg_row = segment_ids[0]
    fill_ids = jnp.full((tok_count,), -1, jnp.int32)
    padded_ids = jnp.concatenate([fill_ids, seg_row, fill_ids])
    seg_key = lax.dynamic_slice_in_dim(padded_ids, row_base, tok_count + 2 * tok_count, 0)
    seg_query = lax.dynamic_slice_in_dim(seg_row, row_base, tok_count, 0)
    pair_numbers = jnp.arange(pair_split.shape[1], dtype=jnp.int32)
    split_query = jnp.sum(
        jnp.where(seg_query[:, None] == pair_numbers[None, :], pair_split[0][None, :], 0), axis=1
    )
    pos_query = row_base + jnp.arange(tok_count, dtype=jnp.int32)
    pos_key = row_base - tok_count + jnp.arange(tok_count + 2 * tok_count, dtype=jnp.int32)
    visible = (seg_key[None, :] == seg_query[:, None]) & (
        (pos_key[None, :] <= pos_query[:, None]) | (pos_key[None, :] < split_query[:, None])
    )
    query_grad, kv_grad = attend_block(
        query_states[0], key_block, value_block, out_grad[0], visible
    )
    lower_rim = kv_grad[:tok_count]
    upper_rim = kv_grad[tok_count + tok_count :]
    center = kv_grad[tok_count : tok_count + tok_count]
    from_upper = passed_along(lower_rim, "seq", -1)
    from_lower = passed_along(upper_rim, "seq", 1)
    center = center + from_upper + from_lower
    key_grad = center[:, :kv_width].astype(jnp.bfloat16)
    value_grad = center[:, kv_width:].astype(jnp.bfloat16)
    input_grad = lax.dot_general(
        value_grad,
        lax.all_gather(value_weight, "dp", axis=0, tiled=True),
        (((1,), (1,)), ((), ())),
        preferred_element_type=jnp.float32,
    )
    columns = layer_rows
    own_rows = lax.psum_scatter(
        lax.dot_general(
            columns, value_grad, (((0,), (0,)), ((), ())), preferred_element_type=jnp.float32
        ),
        "dp",
        scatter_dimension=0,
        tiled=True,
    )
    summed = lax.psum_scatter(own_rows, "seq", scatter_dimension=1, tiled=True)
    devices_all = lax.axis_size("dp") * lax.axis_size("seq")
    weight_grad = summed / devices_all
    return (
        query_grad.astype(jnp.bfloat16)[None],
        key_grad[None],
        input_grad.astype(jnp.bfloat16)[None],
        weight_grad,
    )


def solution(mesh):
    return jax.shard_map(
        local,
        mesh=mesh,
        in_specs=(
            P("dp", "seq", None),
            P("dp", "seq", None),
            P("dp", "seq", None),
            P("dp", "seq", None),
            P("dp", None),
            P("dp", None),
            P("dp", None),
        ),
        out_specs=(
            P("dp", "seq", None),
            P("dp", "seq", None),
            P("dp", "seq", None),
            P("dp", "seq"),
        ),
        check_vma=False,
    )
```

profile of v0, /device:TPU:26, one launch (start us, length us, event | category | flops | bytes accessed | tf_op | source)
XLA Modules:
  0.0 365.0 jit_solution(11370934144328889524)
XLA Ops:
  10.2 65.3 %all-gather.2.cloned.1.call-done = bf16[5120,512]{1,0:T(8,128)(2,1)} async-done(((bf16[320,512]{1,0:T(8,128)(2,1)}), bf16[5120,512]{1,0:T(8,128)(2,1)}) %all-gather.2.cloned.1.call-update) | async-done | bytes 5242896 | tf_op jit(solution)/shard_map/all_gather | solution.py:89
  75.5 3.3 fusion.36
  79.6 3.4 collective-permute-start.1
  82.9 3.4 collective-permute-start
  89.1 2.2 collective-permute-done.1
  91.3 5.5 %collective-permute-done = bf16[128,1024]{1,0:T(8,128)(2,1)} collective-permute-done((bf16[128,1024]{1,0:T(8,128)(2,1)}, bf16[128,1024]{1,0:T(8,128)(2,1)}, u32[]{:S(2)}, u32[]{:S(2)}) %collective-permute-start) | collective-permute-done | bytes 262176 | tf_op jit(solution)/shard_map/ppermute | solution.py:17
  101.5 1.4 fusion.79
  105.8 1.6 multiply_reduce_fusion.3
  115.2 1.8 fusion.35
  117.0 1.8 fusion.34
  118.8 1.8 fusion.33
  120.7 1.8 fusion.32
  122.5 1.9 collective-permute-start.2
  124.5 5.0 %collective-permute-start.3 = (f32[128,1024]{0,1:T(8,128)S(1)}, f32[128,1024]{0,1:T(8,128)S(1)}, u32[]{:S(2)}, u32[]{:S(2)}) collective-permute-start(f32[128,1024]{0,1:T(8,128)S(1)} %get-tuple-element.21), channel_id=1, source_target_pairs={{0,1},{1,2},{2,3},{3,4},{4,5},{5,6},{6,7},{7,8},{8,9},{9,10},{10,1... | collective-permute-start | bytes 1572872 | tf_op jit(solution)/shard_map/ppermute | solution.py:29
  129.5 9.8 %collective-permute-done.2 = f32[128,1024]{0,1:T(8,128)S(1)} collective-permute-done((f32[128,1024]{0,1:T(8,128)S(1)}, f32[128,1024]{0,1:T(8,128)S(1)}, u32[]{:S(2)}, u32[]{:S(2)}) %collective-permute-start.2) | collective-permute-done | bytes 524320 | tf_op jit(solution)/shard_map/ppermute | solution.py:29
  139.3 11.1 %collective-permute-done.3 = f32[128,1024]{0,1:T(8,128)S(1)} collective-permute-done((f32[128,1024]{0,1:T(8,128)S(1)}, f32[128,1024]{0,1:T(8,128)S(1)}, u32[]{:S(2)}, u32[]{:S(2)}) %collective-permute-start.3) | collective-permute-done | bytes 524320 | tf_op jit(solution)/shard_map/ppermute | solution.py:29
  150.5 5.3 %convolution_bitcast_fusion = f32[5120,512]{0,1:T(8,128)} fusion(bf16[1,128,5120]{2,1,0:T(8,128)(2,1)S(1)} %copy-done, bf16[128,1024]{0,1:T(8,128)(2,1)S(1)} %fusion.52), kind=kOutput, calls=%fused_computation.4 | convolution fusion | flops 671088640 | bytes 11927552 | tf_op jit(solution)/shard_map/dot_general | solution.py:130
  155.8 11.4 %copy.205 = f32[5120,512]{1,0:T(8,128)} copy(f32[5120,512]{0,1:T(8,128)} %convolution_bitcast_fusion) | data formatting | bytes 20971520
  168.1 2.2 fusion.50
  170.3 116.1 %reduce-scatter.7.cloned.1.call-done = f32[320,512]{1,0:T(8,128)} async-done(((f32[5120,512]{1,0:T(8,128)}), f32[320,512]{1,0:T(8,128)}) %reduce-scatter.7.cloned.1.call-update) | async-done | bytes 655376
  286.4 2.2 copy.206
  288.7 2.3 fusion.49
  295.4 5.4 %fusion.4 = bf16[1,128,5120]{2,1,0:T(8,128)(2,1)} fusion(bf16[5120,512]{1,0:T(8,128)(2,1)} %all-gather.2.cloned.1.call-done, bf16[128,1024]{0,1:T(8,128)(2,1)S(1)} %fusion.52), kind=kOutput, calls=%fused_computation.6 | convolution fusion | flops 671744000 | bytes 6684672 | tf_op jit(solution)/shard_map/dot_general | solution.py:122
  300.7 56.3 %reduce-scatter.5.cloned.1.call-done = f32[320,32]{0,1:T(8,128)} async-done(((f32[320,512]{0,1:T(8,128)}), f32[320,32]{0,1:T(8,128)}) %reduce-scatter.5.cloned.1.call-update) | async-done | bytes 40976 | tf_op jit(solution)/shard_map/reduce_scatter | solution.py:137
  (114 shorter events, 28.3 us)
Async XLA Ops:
  7.2 68.3 %copy-start = (bf16[1,128,5120]{2,1,0:T(8,128)(2,1)S(1)}, bf16[1,128,5120]{2,1,0:T(8,128)(2,1)}, u32[]{:S(2)}) copy-start(bf16[1,128,5120]{2,1,0:T(8,128)(2,1)} %param.7) | copy-start | bytes 3932164
  7.2 68.3 %all-gather.2.cloned.1.call-start = ((), (), s32[]{:S(2)}) async-start(), calls=%async_computation.2 | async-start | bytes 5570560 | tf_op jit(solution)/shard_map/all_gather | solution.py:89
  7.9 278.5 %reduce-scatter.7.cloned.1.call-start = ((), (), s32[]{:S(2)}) async-start(), calls=%async_computation.4 | async-start | bytes 11141120
  10.2 68.7 %copy-start.4 = (bf16[1,128,512]{2,1,0:T(8,128)(2,1)S(1)}, bf16[1,128,512]{2,1,0:T(8,128)(2,1)}, u32[]{:S(2)}) copy-start(bf16[1,128,512]{2,1,0:T(8,128)(2,1)} %param.9) | copy-start | bytes 393220
  10.2 76.7 %copy-start.1 = (bf16[1,128,2560]{2,1,0:T(8,128)(2,1)S(1)}, bf16[1,128,2560]{2,1,0:T(8,128)(2,1)}, u32[]{:S(2)}) copy-start(bf16[1,128,2560]{2,1,0:T(8,128)(2,1)} %param.8) | copy-start | bytes 1966084
  78.8 8.3 %copy-start.2 = (bf16[1,128,2560]{2,1,0:T(8,128)(2,1)S(1)}, bf16[1,128,2560]{2,1,0:T(8,128)(2,1)}, u32[]{:S(2)}) copy-start(bf16[1,128,2560]{2,1,0:T(8,128)(2,1)} %param.10) | copy-start | bytes 1966084
  79.6 11.7 %collective-permute-start.1 = (bf16[128,1024]{1,0:T(8,128)(2,1)}, bf16[128,1024]{1,0:T(8,128)(2,1)}, u32[]{:S(2)}, u32[]{:S(2)}) collective-permute-start(bf16[128,1024]{1,0:T(8,128)(2,1)} %pad_maximum_fusion.2), channel_id=1, source_target_pairs={{1,0},{2,1},{3,2},{4,3},{5,4},{6,5},{7,6},{8,7},{9,8},{10,9},{11,1... | collective-permute-start | bytes 786440 | tf_op jit(solution)/shard_map/ppermute | solution.py:19
  82.9 13.8 %collective-permute-start = (bf16[128,1024]{1,0:T(8,128)(2,1)}, bf16[128,1024]{1,0:T(8,128)(2,1)}, u32[]{:S(2)}, u32[]{:S(2)}) collective-permute-start(bf16[128,1024]{1,0:T(8,128)(2,1)} %pad_maximum_fusion.2), channel_id=1, source_target_pairs={{0,1},{1,2},{2,3},{3,4},{4,5},{5,6},{6,7},{7,8},{8,9},{9,10},{10,1... | collective-permute-start | bytes 786440 | tf_op jit(solution)/shard_map/ppermute | solution.py:17
  89.1 15.3 %copy-start.16 = (pred[128,384]{0,1:T(8,128)(4,1)}, pred[128,384]{0,1:T(8,128)(4,1)S(1)}, u32[]{:S(2)}) copy-start(pred[128,384]{0,1:T(8,128)(4,1)S(1)} %or_and_fusion) | copy-start | bytes 147460
  100.1 2.9 copy-start.9
  100.1 2.9 copy-start.11
  100.1 2.9 copy-start.7
  100.1 4.3 %copy-start.5 = (bf16[384,1,128]{2,1,0:T(2,128)(2,1)}, bf16[384,1,128]{2,1,0:T(2,128)(2,1)S(1)}, u32[]{:S(2)}) copy-start(bf16[384,1,128]{2,1,0:T(2,128)(2,1)S(1)} %get-tuple-element.27) | copy-start | bytes 294916
  105.8 1.7 copy-start.22
  107.5 1.8 copy-start.21
  122.5 16.7 %collective-permute-start.2 = (f32[128,1024]{0,1:T(8,128)S(1)}, f32[128,1024]{0,1:T(8,128)S(1)}, u32[]{:S(2)}, u32[]{:S(2)}) collective-permute-start(f32[128,1024]{0,1:T(8,128)S(1)} %get-tuple-element.20), channel_id=1, source_target_pairs={{1,0},{2,1},{3,2},{4,3},{5,4},{6,5},{7,6},{8,7},{9,8},{10,9},{11,1... | collective-permute-start | bytes 1572872 | tf_op jit(solution)/shard_map/ppermute | solution.py:29
  124.5 25.9 %collective-permute-start.3 = (f32[128,1024]{0,1:T(8,128)S(1)}, f32[128,1024]{0,1:T(8,128)S(1)}, u32[]{:S(2)}, u32[]{:S(2)}) collective-permute-start(f32[128,1024]{0,1:T(8,128)S(1)} %get-tuple-element.21), channel_id=1, source_target_pairs={{0,1},{1,2},{2,3},{3,4},{4,5},{5,6},{6,7},{7,8},{8,9},{9,10},{10,1... | collective-permute-start | bytes 1572872 | tf_op jit(solution)/shard_map/ppermute | solution.py:29
  167.2 189.8 %reduce-scatter.5.cloned.1.call-start = ((), (), s32[]{:S(2)}) async-start(), calls=%async_computation.3 | async-start | bytes 835584 | tf_op jit(solution)/shard_map/reduce_scatter | solution.py:137
  170.3 118.3 %copy-start.10 = (bf16[384,1,128]{2,1,0:T(2,128)(2,1)S(1)}, bf16[384,1,128]{2,1,0:T(2,128)(2,1)}, u32[]{:S(2)}) copy-start(bf16[384,1,128]{2,1,0:T(2,128)(2,1)} %copy-done.9) | copy-start | bytes 294916
  170.3 118.3 %copy-start.30 = (f32[5,128]{1,0:T(8,128)S(1)}, f32[5,128]{1,0:T(8,128)}, u32[]{:S(2)}) copy-start(f32[5,128]{1,0:T(8,128)} %copy-done.29) | copy-start | bytes 7684
  288.7 2.4 copy-start.8
  288.7 2.4 copy-start.20
  288.7 2.4 copy-start.25
  288.7 2.4 copy-start.32
  (20 other events, 23.5 us)
Sparse Core Ops, SparseCore 0:
  10.8 64.6 all-gather.1
  167.4 118.9 reduce-scatter.6
  288.9 68.0 reduce-scatter.4
where the time goes:
time: 369 us; the launch traced here: 365 us
  waiting for transfers between devices  267 us (72%)
  matrix products  38.3 us (10%)
  local copies, waits for them, and re-layouts  25.4 us (7%)
  between operations  14.3 us (4%)
  starting transfers between devices  13.8 us (4%)
  other arithmetic  6.27 us (2%)
    unnamed x4, waiting for transfers between devices  117 us
    all_gather x1, waiting for transfers between devices, local(): lax.all_gather(value_weight, 'dp', axis=0, tiled=True)  65.3 us
    reduce_scatter x1, waiting for transfers between devices, local(): summed = lax.psum_scatter(own_rows, 'seq', scatter_dimension=1, tiled=True)  56.3 us
    unnamed x80, local copies, waits for them, and re-layouts  22.4 us
    ppermute x2, waiting for transfers between devices, passed_along(): return lax.ppermute(array, axis, pairs)  20.9 us
  transfers between devices with their start and end apart: 7, of which 7 were waited for; matrix products, arithmetic and copies ran while one was open for 5% of the time, Pallas kernels for 0%

commit v1 on v0

--- a/solution.py
+++ b/solution.py
@@ -125,14 +125,18 @@
         (((1,), (1,)), ((), ())),
         preferred_element_type=jnp.float32,
     )
-    columns = layer_rows
-    own_rows = lax.psum_scatter(
-        lax.dot_general(
-            columns, value_grad, (((0,), (0,)), ((), ())), preferred_element_type=jnp.float32
-        ),
+    dp_count = lax.axis_size("dp")
+    model_width = layer_rows.shape[1]
+    input_blocks = lax.all_to_all(
+        layer_rows.reshape(tok_count, dp_count, model_width // dp_count).transpose(1, 0, 2),
         "dp",
-        scatter_dimension=0,
+        0,
+        0,
         tiled=True,
+    )
+    grad_rows = lax.all_gather(value_grad, "dp", axis=0, tiled=False)
+    own_rows = jnp.einsum(
+        "rtk,rtc->kc", input_blocks, grad_rows, preferred_element_type=jnp.float32
     )
     summed = lax.psum_scatter(own_rows, "seq", scatter_dimension=1, tiled=True)
     devices_all = lax.axis_size("dp") * lax.axis_size("seq")

time: 369 us -> 294 us (0.80)
  waiting for transfers between devices: 267 us -> 200 us
  starting transfers between devices: 13.8 us -> 20.6 us
  local copies, waits for them, and re-layouts: 25.4 us -> 19 us
  matrix products: 38.3 us -> 33.3 us
    unnamed x4, waiting for transfers between devices: 117 us -> 56.5 us
    reduce_scatter x1 -> x0, waiting for transfers between devices: 56.3 us -> none  [local(): summed = lax.psum_scatter(own_rows, 'seq', scatter_dimension=1, tiled=True)]
    all_gather x0 -> x1, waiting for transfers between devices: none -> 47.6 us  [local(): grad_rows = lax.all_gather(value_grad, 'dp', axis=0, tiled=False)]
    unnamed x80 -> x86, local copies, waits for them, and re-layouts: 22.4 us -> 12.5 us
    all_to_all x0 -> x1, starting transfers between devices: none -> 6.74 us  [local(): lax.all_to_all(layer_rows.reshape(tok_count, dp_count, model_width // dp_...]
  transfers between devices with their start and end apart: 7 -> 8, of which waited for: 7 -> 7; matrix products, arithmetic and copies ran while one was open for 5% -> 6% of each run, Pallas kernels for 0% -> 0%
where the time goes in v1:
time: 294 us; the launch traced here: 290 us
  waiting for transfers between devices  200 us (68%)
  matrix products  33.3 us (11%)
  starting transfers between devices  20.6 us (7%)
  local copies, waits for them, and re-layouts  19 us (6%)
  between operations  14.3 us (5%)
    all_gather x1, waiting for transfers between devices, local(): lax.all_gather(value_weight, 'dp', axis=0, tiled=True)  65.3 us
    unnamed x4, waiting for transfers between devices  56.5 us
    all_gather x1, waiting for transfers between devices, local(): grad_rows = lax.all_gather(value_grad, 'dp', axis=0, tiled=False)  47.6 us
    ppermute x2, waiting for transfers between devices, passed_along(): return lax.ppermute(array, axis, pairs)  21.1 us
    unnamed x86, local copies, waits for them, and re-layouts  12.5 us
    ppermute x2, starting transfers between devices, passed_along(): return lax.ppermute(array, axis, pairs)  6.87 us
    all_to_all x1, starting transfers between devices, local(): lax.all_to_all(layer_rows.reshape(tok_count, dp_count, model_width // dp_...  6.74 us
    dot_general x4, matrix products, attend_block(): jnp.einsum('gqk,qgd->kd', attention_low, grad_head, preferred_element_typ...  6.62 us
  transfers between devices with their start and end apart: 8, of which 7 were waited for; matrix products, arithmetic and copies ran while one was open for 6% of the time, Pallas kernels for 0%

profile of v1, /device:TPU:26, one launch (start us, length us, event | category | flops | bytes accessed | tf_op | source)
XLA Modules:
  0.0 290.0 jit_solution(11749638976114022956)
XLA Ops:
  10.1 65.3 %all-gather.4.cloned.1.call-done = bf16[5120,512]{1,0:T(8,128)(2,1)} async-done(((bf16[320,512]{1,0:T(8,128)(2,1)}), bf16[5120,512]{1,0:T(8,128)(2,1)}) %all-gather.4.cloned.1.call-update) | async-done | bytes 5242896 | tf_op jit(solution)/shard_map/all_gather | solution.py:89
  75.5 3.8 %fusion.35 = bf16[128,512]{1,0:T(8,128)(2,1)S(1)} fusion(bf16[5120,512]{1,0:T(8,128)(2,1)} %all-gather.4.cloned.1.call-done, bf16[1,128,5120]{2,1,0:T(8,128)(2,1)} %param.7), kind=kOutput, calls=%fused_computation.53 | convolution fusion | flops 671154176 | bytes 6684672 | tf_op jit(solution)/shard_map/dot_general | solution.py:87
  79.3 3.5 %collective-permute-start.1 = (bf16[128,1024]{1,0:T(8,128)(2,1)S(1)}, bf16[128,1024]{1,0:T(8,128)(2,1)S(1)}, u32[]{:S(2)}, u32[]{:S(2)}) collective-permute-start(bf16[128,1024]{1,0:T(8,128)(2,1)S(1)} %pad_maximum_fusion.2), channel_id=1, source_target_pairs={{1,0},{2,1},{3,2},{4,3},{5,4},{6,5},{7,6},{8,7},{9,8},{10,9},{11,1... | collective-permute-start | bytes 786440 | tf_op jit(solution)/shard_map/ppermute | solution.py:19
  82.8 3.4 %collective-permute-start = (bf16[128,1024]{1,0:T(8,128)(2,1)S(1)}, bf16[128,1024]{1,0:T(8,128)(2,1)}, u32[]{:S(2)}, u32[]{:S(2)}) collective-permute-start(bf16[128,1024]{1,0:T(8,128)(2,1)S(1)} %pad_maximum_fusion.2), channel_id=1, source_target_pairs={{0,1},{1,2},{2,3},{3,4},{4,5},{5,6},{6,7},{7,8},{8,9},{9,10},{10,1... | collective-permute-start | bytes 786440 | tf_op jit(solution)/shard_map/ppermute | solution.py:17
  87.1 3.7 %collective-permute-done.1 = bf16[128,1024]{1,0:T(8,128)(2,1)S(1)} collective-permute-done((bf16[128,1024]{1,0:T(8,128)(2,1)S(1)}, bf16[128,1024]{1,0:T(8,128)(2,1)S(1)}, u32[]{:S(2)}, u32[]{:S(2)}) %collective-permute-start.1) | collective-permute-done | bytes 262176 | tf_op jit(solution)/shard_map/ppermute | solution.py:19
  90.8 5.6 %collective-permute-done = bf16[128,1024]{1,0:T(8,128)(2,1)} collective-permute-done((bf16[128,1024]{1,0:T(8,128)(2,1)S(1)}, bf16[128,1024]{1,0:T(8,128)(2,1)}, u32[]{:S(2)}, u32[]{:S(2)}) %collective-permute-start) | collective-permute-done | bytes 262176 | tf_op jit(solution)/shard_map/ppermute | solution.py:17
  99.7 1.5 fusion.79
  104.0 1.5 fusion.76
  105.6 1.6 multiply_reduce_fusion.3
  115.0 1.7 fusion.34
  116.7 1.7 fusion.33
  118.4 1.6 fusion.32
  120.0 1.6 fusion.31
  121.7 2.1 collective-permute-start.2
  123.8 4.8 %collective-permute-start.3 = (f32[128,1024]{0,1:T(8,128)S(1)}, f32[128,1024]{0,1:T(8,128)S(1)}, u32[]{:S(2)}, u32[]{:S(2)}) collective-permute-start(f32[128,1024]{0,1:T(8,128)S(1)} %get-tuple-element.21), channel_id=1, source_target_pairs={{0,1},{1,2},{2,3},{3,4},{4,5},{5,6},{6,7},{7,8},{8,9},{9,10},{10,1... | collective-permute-start | bytes 1572872 | tf_op jit(solution)/shard_map/ppermute | solution.py:29
  128.6 10.0 %collective-permute-done.2 = f32[128,1024]{0,1:T(8,128)S(1)} collective-permute-done((f32[128,1024]{0,1:T(8,128)S(1)}, f32[128,1024]{0,1:T(8,128)S(1)}, u32[]{:S(2)}, u32[]{:S(2)}) %collective-permute-start.2) | collective-permute-done | bytes 524320 | tf_op jit(solution)/shard_map/ppermute | solution.py:29
  138.6 11.1 %collective-permute-done.3 = f32[128,1024]{0,1:T(8,128)S(1)} collective-permute-done((f32[128,1024]{0,1:T(8,128)S(1)}, f32[128,1024]{0,1:T(8,128)S(1)}, u32[]{:S(2)}, u32[]{:S(2)}) %collective-permute-start.3) | collective-permute-done | bytes 524320 | tf_op jit(solution)/shard_map/ppermute | solution.py:29
  152.0 6.7 %all-to-all-start = ((bf16[16,128,320]{1,2,0:T(8,128)(2,1)}), bf16[16,128,320]{1,2,0:T(8,128)(2,1)}, u32[]{:S(2)}, u32[]{:S(2)}) async-start(bf16[16,128,320]{1,2,0:T(8,128)(2,1)} %bitcast.64), calls=%async_computation | async-start | bytes 2621440 | tf_op jit(solution)/shard_map/all_to_all | solution.py:130
  158.8 47.6 %all-gather.6.cloned.1.call-done = bf16[2048,512]{0,1:T(8,128)(2,1)} async-done(((bf16[128,512]{0,1:T(8,128)(2,1)}), bf16[2048,512]{0,1:T(8,128)(2,1)}) %all-gather.6.cloned.1.call-update) | async-done | bytes 2097168 | tf_op jit(solution)/shard_map/all_gather | solution.py:137
  206.4 2.9 copy.217
  209.3 2.1 convolution_bitcast_fusion.4
  212.9 2.0 fusion.49
  220.7 5.4 %fusion.4 = bf16[1,128,5120]{2,1,0:T(8,128)(2,1)} fusion(bf16[5120,512]{1,0:T(8,128)(2,1)} %all-gather.4.cloned.1.call-done, bf16[128,1024]{0,1:T(8,128)(2,1)S(1)} %fusion.51), kind=kOutput, calls=%fused_computation.5 | convolution fusion | flops 671744000 | bytes 6684672 | tf_op jit(solution)/shard_map/dot_general | solution.py:122
  226.0 55.7 %reduce-scatter.4.cloned.1.call-done = f32[32,320]{1,0:T(8,128)} async-done(((f32[512,320]{1,0:T(8,128)}), f32[32,320]{1,0:T(8,128)}) %reduce-scatter.4.cloned.1.call-update) | async-done | bytes 40976
  (123 shorter events, 28.6 us)
Async XLA Ops:
  7.2 68.3 %all-gather.4.cloned.1.call-start = ((), (), s32[]{:S(2)}) async-start(), calls=%async_computation.2 | async-start | bytes 5570560 | tf_op jit(solution)/shard_map/all_gather | solution.py:89
  7.9 198.5 %all-gather.6.cloned.1.call-start = ((), (), s32[]{:S(2)}) async-start(), calls=%async_computation.3 | async-start | bytes 2228224 | tf_op jit(solution)/shard_map/all_gather | solution.py:137
  10.1 69.1 %copy-start.7 = (bf16[1,128,512]{2,1,0:T(8,128)(2,1)S(1)}, bf16[1,128,512]{2,1,0:T(8,128)(2,1)}, u32[]{:S(2)}) copy-start(bf16[1,128,512]{2,1,0:T(8,128)(2,1)} %param.9) | copy-start | bytes 393220
  10.1 76.0 %copy-start.1 = (bf16[1,128,2560]{2,1,0:T(8,128)(2,1)S(1)}, bf16[1,128,2560]{2,1,0:T(8,128)(2,1)}, u32[]{:S(2)}) copy-start(bf16[1,128,2560]{2,1,0:T(8,128)(2,1)} %param.8) | copy-start | bytes 1966084
  79.2 7.3 %copy-start.2 = (bf16[1,128,2560]{2,1,0:T(8,128)(2,1)S(1)}, bf16[1,128,2560]{2,1,0:T(8,128)(2,1)}, u32[]{:S(2)}) copy-start(bf16[1,128,2560]{2,1,0:T(8,128)(2,1)} %param.10) | copy-start | bytes 1966084
  79.3 11.5 %collective-permute-start.1 = (bf16[128,1024]{1,0:T(8,128)(2,1)S(1)}, bf16[128,1024]{1,0:T(8,128)(2,1)S(1)}, u32[]{:S(2)}, u32[]{:S(2)}) collective-permute-start(bf16[128,1024]{1,0:T(8,128)(2,1)S(1)} %pad_maximum_fusion.2), channel_id=1, source_target_pairs={{1,0},{2,1},{3,2},{4,3},{5,4},{6,5},{7,6},{8,7},{9,8},{10,9},{11,1... | collective-permute-start | bytes 786440 | tf_op jit(solution)/shard_map/ppermute | solution.py:19
  82.8 13.6 %collective-permute-start = (bf16[128,1024]{1,0:T(8,128)(2,1)S(1)}, bf16[128,1024]{1,0:T(8,128)(2,1)}, u32[]{:S(2)}, u32[]{:S(2)}) collective-permute-start(bf16[128,1024]{1,0:T(8,128)(2,1)S(1)} %pad_maximum_fusion.2), channel_id=1, source_target_pairs={{0,1},{1,2},{2,3},{3,4},{4,5},{5,6},{6,7},{7,8},{8,9},{9,10},{10,1... | collective-permute-start | bytes 786440 | tf_op jit(solution)/shard_map/ppermute | solution.py:17
  86.5 17.5 %copy-start.3 = (bf16[1,128,2560]{1,2,0:T(8,128)(2,1)}, bf16[1,128,2560]{1,2,0:T(8,128)(2,1)S(1)}, u32[]{:S(2)}) copy-start(bf16[1,128,2560]{1,2,0:T(8,128)(2,1)S(1)} %copy.143) | copy-start | bytes 1966084
  86.9 18.7 %copy-start.5 = (bf16[1,128,2560]{1,2,0:T(8,128)(2,1)}, bf16[1,128,2560]{1,2,0:T(8,128)(2,1)S(1)}, u32[]{:S(2)}) copy-start(bf16[1,128,2560]{1,2,0:T(8,128)(2,1)S(1)} %copy.146) | copy-start | bytes 1966084
  87.1 17.0 %copy-start.15 = (pred[128,384]{0,1:T(8,128)(4,1)}, pred[128,384]{0,1:T(8,128)(4,1)S(1)}, u32[]{:S(2)}) copy-start(pred[128,384]{0,1:T(8,128)(4,1)S(1)} %or_and_fusion) | copy-start | bytes 147460
  99.6 2.9 %copy-start.8 = (bf16[384,1,128]{2,1,0:T(2,128)(2,1)}, bf16[384,1,128]{2,1,0:T(2,128)(2,1)S(1)}, u32[]{:S(2)}) copy-start(bf16[384,1,128]{2,1,0:T(2,128)(2,1)S(1)} %get-tuple-element.26) | copy-start | bytes 294916
  99.7 2.9 %copy-start.10 = (bf16[384,1,128]{2,1,0:T(2,128)(2,1)}, bf16[384,1,128]{2,1,0:T(2,128)(2,1)S(1)}, u32[]{:S(2)}) copy-start(bf16[384,1,128]{2,1,0:T(2,128)(2,1)S(1)} %get-tuple-element.24) | copy-start | bytes 294916
  105.5 1.7 copy-start.22
  107.2 1.8 copy-start.20
  113.2 1.8 copy-start.37
  121.7 28.8 %copy-start = (bf16[1,128,5120]{2,1,0:T(8,128)(2,1)S(1)}, bf16[1,128,5120]{2,1,0:T(8,128)(2,1)}, u32[]{:S(2)}) copy-start(bf16[1,128,5120]{2,1,0:T(8,128)(2,1)} %param.7) | copy-start | bytes 3932164
  121.7 16.9 %collective-permute-start.2 = (f32[128,1024]{0,1:T(8,128)S(1)}, f32[128,1024]{0,1:T(8,128)S(1)}, u32[]{:S(2)}, u32[]{:S(2)}) collective-permute-start(f32[128,1024]{0,1:T(8,128)S(1)} %get-tuple-element.20), channel_id=1, source_target_pairs={{1,0},{2,1},{3,2},{4,3},{5,4},{6,5},{7,6},{8,7},{9,8},{10,9},{11,1... | collective-permute-start | bytes 1572872 | tf_op jit(solution)/shard_map/ppermute | solution.py:29
  123.8 25.9 %collective-permute-start.3 = (f32[128,1024]{0,1:T(8,128)S(1)}, f32[128,1024]{0,1:T(8,128)S(1)}, u32[]{:S(2)}, u32[]{:S(2)}) collective-permute-start(f32[128,1024]{0,1:T(8,128)S(1)} %get-tuple-element.21), channel_id=1, source_target_pairs={{0,1},{1,2},{2,3},{3,4},{4,5},{5,6},{6,7},{7,8},{8,9},{9,10},{10,1... | collective-permute-start | bytes 1572872 | tf_op jit(solution)/shard_map/ppermute | solution.py:29
  152.0 57.3 %all-to-all-start = ((bf16[16,128,320]{1,2,0:T(8,128)(2,1)}), bf16[16,128,320]{1,2,0:T(8,128)(2,1)}, u32[]{:S(2)}, u32[]{:S(2)}) async-start(bf16[16,128,320]{1,2,0:T(8,128)(2,1)} %bitcast.64), calls=%async_computation | async-start | bytes 2621440 | tf_op jit(solution)/shard_map/all_to_all | solution.py:130
  158.7 123.1 %reduce-scatter.4.cloned.1.call-start = ((), (), s32[]{:S(2)}) async-start(), calls=%async_computation.4 | async-start | bytes 835584
  212.9 2.1 copy-start.9
  212.9 2.1 copy-start.21
  212.9 2.1 copy-start.26
  212.9 2.1 copy-start.34
  (23 other events, 29.5 us)
Sparse Core Ops, SparseCore 0:
  10.8 64.6 all-gather.3
  150.6 55.6 all-gather.5
  212.8 68.9 reduce-scatter.3

commit v2 on v1

--- a/solution.py
+++ b/solution.py
@@ -21,6 +21,19 @@
             axis=dim,
         )
     return cells
+
+
+def gathered(array, axis):
+    count = lax.axis_size(axis)
+    copies = jnp.broadcast_to(array[None], (count,) + array.shape)
+    return lax.all_to_all(copies, axis, 0, 0, tiled=True)
+
+
+def scattered_sum(array, axis):
+    count = lax.axis_size(axis)
+    rows, cols = array.shape
+    pieces = array.reshape(rows, count, cols // count).transpose(1, 0, 2)
+    return jnp.sum(lax.all_to_all(pieces, axis, 0, 0, tiled=True), axis=0)
 
 
 def passed_along(array, axis, by):
@@ -84,11 +97,8 @@
     kv_width = key_states.shape[2]
     row_base = lax.axis_index("seq") * tok_count
     columns = layer_rows
-    value_rows = jnp.dot(
-        columns,
-        lax.all_gather(value_weight, "dp", axis=0, tiled=True),
-        preferred_element_type=jnp.float32,
-    )
+    weight_full = gathered(value_weight, "dp").reshape(-1, value_weight.shape[1])
+    value_rows = jnp.dot(columns, weight_full, preferred_element_type=jnp.float32)
     value_low = value_rows.astype(jnp.bfloat16)
     both_states = jnp.concatenate([key_states[0], value_low], axis=1)
     extended = with_halo(both_states, (("seq", 0),), tok_count)
@@ -121,7 +131,7 @@
     value_grad = center[:, kv_width:].astype(jnp.bfloat16)
     input_grad = lax.dot_general(
         value_grad,
-        lax.all_gather(value_weight, "dp", axis=0, tiled=True),
+        weight_full,
         (((1,), (1,)), ((), ())),
         preferred_element_type=jnp.float32,
     )
@@ -134,11 +144,11 @@
         0,
         tiled=True,
     )
-    grad_rows = lax.all_gather(value_grad, "dp", axis=0, tiled=False)
+    grad_rows = gathered(value_grad, "dp")
     own_rows = jnp.einsum(
         "rtk,rtc->kc", input_blocks, grad_rows, preferred_element_type=jnp.float32
     )
-    summed = lax.psum_scatter(own_rows, "seq", scatter_dimension=1, tiled=True)
+    summed = scattered_sum(own_rows, "seq")
     devices_all = lax.axis_size("dp") * lax.axis_size("seq")
     weight_grad = summed / devices_all
     return (

time: 294 us -> 251 us (0.85)
  waiting for transfers between devices: 200 us -> 154 us
  starting transfers between devices: 20.6 us -> 42 us
  between operations: 14.3 us -> 1.13 us
    all_to_all x0 -> x3, waiting for transfers between devices: none -> 116 us  [the longest x2 106 us: gathered(): return lax.all_to_all(copies, axis, 0, 0, tiled=True)]
    all_gather x2 -> x0, waiting for transfers between devices: 113 us -> none  [the longest x1 65.3 us: local(): lax.all_gather(value_weight, 'dp', axis=0, tiled=True)]
    unnamed x4 -> x0, waiting for transfers between devices: 56.5 us -> none
    all_to_all x0 -> x3, starting transfers between devices: none -> 23.2 us  [the longest x2 13.1 us: gathered(): return lax.all_to_all(copies, axis, 0, 0, tiled=True)]
    broadcast_in_dim x0 -> x2, local copies, waits for them, and re-layouts: none -> 5.39 us  [gathered(): copies = jnp.broadcast_to(array[None], (count,) + array.shape)]
    ppermute x1, waiting for transfers between devices: 3.7 us -> 8.6 us  [with_halo(): lax.ppermute(head, axis, [((i + 1) % count, i) for i in range(ends)])]
    unnamed x86 -> x61, local copies, waits for them, and re-layouts: 12.5 us -> 9 us
  transfers between devices with their start and end apart: 8 -> 8, of which waited for: 7 -> 7; matrix products, arithmetic and copies ran while one was open for 6% -> 15% of each run, Pallas kernels for 0% -> 0%
where the time goes in v2:
time: 251 us; the launch traced here: 250 us
  waiting for transfers between devices  154 us (61%)
  starting transfers between devices  42 us (17%)
  matrix products  32.6 us (13%)
  local copies, waits for them, and re-layouts  17.9 us (7%)
    all_to_all x2, waiting for transfers between devices, gathered(): return lax.all_to_all(copies, axis, 0, 0, tiled=True)  106 us
    ppermute x2, waiting for transfers between devices, passed_along(): return lax.ppermute(array, axis, pairs)  20.7 us
    all_to_all x2, starting transfers between devices, gathered(): return lax.all_to_all(copies, axis, 0, 0, tiled=True)  13.1 us
    all_to_all x1, waiting for transfers between devices, scattered_sum(): return jnp.sum(lax.all_to_all(pieces, axis, 0, 0, tiled=True), axis=0)  10.2 us
    all_to_all x1, starting transfers between devices, scattered_sum(): return jnp.sum(lax.all_to_all(pieces, axis, 0, 0, tiled=True), axis=0)  10.1 us
    unnamed x61, local copies, waits for them, and re-layouts  9 us
    ppermute x1, waiting for transfers between devices, with_halo(): lax.ppermute(head, axis, [((i + 1) % count, i) for i in range(ends)])  8.6 us
    ppermute x1, waiting for transfers between devices, with_halo(): lax.ppermute(tail, axis, [(i, (i + 1) % count) for i in range(ends)])  8.34 us
  transfers between devices with their start and end apart: 8, of which 7 were waited for; matrix products, arithmetic and copies ran while one was open for 15% of the time, Pallas kernels for 0%

profile of v2, /device:TPU:26, one launch (start us, length us, event | category | flops | bytes accessed | tf_op | source)
XLA Modules:
  0.0 249.6 jit_solution(2922815647009103756)
XLA Ops:
  0.6 3.8 %broadcast_in_dim.106 = bf16[16,320,512]{2,1,0:T(8,128)(2,1)} broadcast(bf16[320,512]{1,0:T(8,128)(2,1)} %param.11), dimensions={1,2} | broadcast | bytes 5570560 | tf_op jit(solution)/shard_map/broadcast_in_dim | solution.py:28
  4.5 6.4 %all-to-all-start = ((bf16[16,320,512]{2,1,0:T(8,128)(2,1)}), bf16[16,320,512]{2,1,0:T(8,128)(2,1)}, u32[]{:S(2)}, u32[]{:S(2)}) async-start(bf16[16,320,512]{2,1,0:T(8,128)(2,1)} %broadcast_in_dim.106), calls=%async_computation | async-start | bytes 10485760 | tf_op jit(solution)/shard_map/all_to_all | solution.py:29
  12.5 77.6 %all-to-all-done = bf16[16,320,512]{2,1,0:T(8,128)(2,1)} async-done(((bf16[16,320,512]{2,1,0:T(8,128)(2,1)}), bf16[16,320,512]{2,1,0:T(8,128)(2,1)}, u32[]{:S(2)}, u32[]{:S(2)}) %all-to-all-start) | async-done | bytes 5242912 | tf_op jit(solution)/shard_map/all_to_all | solution.py:29
  90.1 4.5 %all-to-all-start.2 = ((bf16[16,128,320]{1,2,0:T(8,128)(2,1)}), bf16[16,128,320]{1,2,0:T(8,128)(2,1)}, u32[]{:S(2)}, u32[]{:S(2)}) async-start(bf16[16,128,320]{1,2,0:T(8,128)(2,1)} %bitcast.64), calls=%async_computation.2 | async-start | bytes 2621440 | tf_op jit(solution)/shard_map/all_to_all | solution.py:140
  94.7 3.4 %fusion.35 = bf16[128,512]{1,0:T(8,128)(2,1)S(1)} fusion(bf16[5120,512]{1,0:T(8,128)(2,1)} %bitcast.2, bf16[1,128,5120]{2,1,0:T(8,128)(2,1)S(1)} %copy-done), kind=kOutput, calls=%fused_computation.53 | convolution fusion | flops 671154176 | bytes 6684672 | tf_op jit(solution)/shard_map/dot_general | solution.py:101
  98.1 4.2 %collective-permute-start.1 = (bf16[128,1024]{1,0:T(8,128)(2,1)S(1)}, bf16[128,1024]{1,0:T(8,128)(2,1)S(1)}, u32[]{:S(2)}, u32[]{:S(2)}) collective-permute-start(bf16[128,1024]{1,0:T(8,128)(2,1)S(1)} %pad_maximum_fusion.2), channel_id=1, source_target_pairs={{1,0},{2,1},{3,2},{4,3},{5,4},{6,5},{7,6},{8,7},{9,8},{10,9},{11,1... | collective-permute-start | bytes 786440 | tf_op jit(solution)/shard_map/ppermute | solution.py:19
  102.4 3.3 %collective-permute-start = (bf16[128,1024]{1,0:T(8,128)(2,1)S(1)}, bf16[128,1024]{1,0:T(8,128)(2,1)}, u32[]{:S(2)}, u32[]{:S(2)}) collective-permute-start(bf16[128,1024]{1,0:T(8,128)(2,1)S(1)} %pad_maximum_fusion.2), channel_id=1, source_target_pairs={{0,1},{1,2},{2,3},{3,4},{4,5},{5,6},{6,7},{7,8},{8,9},{9,10},{10,1... | collective-permute-start | bytes 786440 | tf_op jit(solution)/shard_map/ppermute | solution.py:17
  106.5 8.6 %collective-permute-done.1 = bf16[128,1024]{1,0:T(8,128)(2,1)S(1)} collective-permute-done((bf16[128,1024]{1,0:T(8,128)(2,1)S(1)}, bf16[128,1024]{1,0:T(8,128)(2,1)S(1)}, u32[]{:S(2)}, u32[]{:S(2)}) %collective-permute-start.1) | collective-permute-done | bytes 262176 | tf_op jit(solution)/shard_map/ppermute | solution.py:19
  115.1 8.3 %collective-permute-done = bf16[128,1024]{1,0:T(8,128)(2,1)} collective-permute-done((bf16[128,1024]{1,0:T(8,128)(2,1)S(1)}, bf16[128,1024]{1,0:T(8,128)(2,1)}, u32[]{:S(2)}, u32[]{:S(2)}) %collective-permute-start) | collective-permute-done | bytes 262176 | tf_op jit(solution)/shard_map/ppermute | solution.py:17
  132.5 1.6 multiply_reduce_fusion.3
  141.9 1.7 fusion.34
  146.0 1.9 collective-permute-start.2
  147.9 4.8 %collective-permute-start.3 = (f32[128,1024]{0,1:T(8,128)S(1)}, f32[128,1024]{0,1:T(8,128)S(1)}, u32[]{:S(2)}, u32[]{:S(2)}) collective-permute-start(f32[128,1024]{0,1:T(8,128)S(1)} %get-tuple-element.17), channel_id=1, source_target_pairs={{0,1},{1,2},{2,3},{3,4},{4,5},{5,6},{6,7},{7,8},{8,9},{9,10},{10,1... | collective-permute-start | bytes 1572872 | tf_op jit(solution)/shard_map/ppermute | solution.py:42
  152.7 9.6 %collective-permute-done.2 = f32[128,1024]{0,1:T(8,128)S(1)} collective-permute-done((f32[128,1024]{0,1:T(8,128)S(1)}, f32[128,1024]{0,1:T(8,128)S(1)}, u32[]{:S(2)}, u32[]{:S(2)}) %collective-permute-start.2) | collective-permute-done | bytes 524320 | tf_op jit(solution)/shard_map/ppermute | solution.py:42
  162.3 11.1 %collective-permute-done.3 = f32[128,1024]{0,1:T(8,128)S(1)} collective-permute-done((f32[128,1024]{0,1:T(8,128)S(1)}, f32[128,1024]{0,1:T(8,128)S(1)}, u32[]{:S(2)}, u32[]{:S(2)}) %collective-permute-start.3) | collective-permute-done | bytes 524320 | tf_op jit(solution)/shard_map/ppermute | solution.py:42
  173.7 1.6 broadcast_in_dim.116
  175.3 6.7 %all-to-all-start.1 = ((bf16[16,128,512]{2,1,0:T(8,128)(2,1)}), bf16[16,128,512]{2,1,0:T(8,128)(2,1)S(1)}, u32[]{:S(2)}, u32[]{:S(2)}) async-start(bf16[16,128,512]{2,1,0:T(8,128)(2,1)} %broadcast_in_dim.116), calls=%async_computation.1 | async-start | bytes 4194304 | tf_op jit(solution)/shard_map/all_to_all | solution.py:29
  182.0 2.8 %fusion.49 = bf16[128,1,5,128]{0,3,2,1:T(8,128)(2,1)} fusion(f32[5,128,384]{1,2,0:T(8,128)} %copy-done.27, f32[5,128]{1,0:T(8,128)S(1)} %get-tuple-element.44, bf16[384,1,128]{2,1,0:T(2,128)(2,1)S(1)} %copy-done.9, f32[5,128,384]{1,2,0:T(8,128)} %get-tuple-element.43, f32[5,128]{1,0:T(8,128)S(1)} %get-tuple-element.42), kind=kOutput, calls=%fused_computation.69 | convolution fusion | flops 378388480 | bytes 2233344 | tf_op jit(solution)/shard_map/gqk,kd->qgd/dot_general | solution.py:81
  184.8 28.2 %all-to-all-done.1 = bf16[16,128,512]{2,1,0:T(8,128)(2,1)S(1)} async-done(((bf16[16,128,512]{2,1,0:T(8,128)(2,1)}), bf16[16,128,512]{2,1,0:T(8,128)(2,1)S(1)}, u32[]{:S(2)}, u32[]{:S(2)}) %all-to-all-start.1) | async-done | bytes 2097184 | tf_op jit(solution)/shard_map/all_to_all | solution.py:29
  213.0 2.1 convolution_bitcast_fusion.4
  216.4 10.1 %all-to-all-start.3 = ((f32[16,320,32]{1,2,0:T(8,128)}), f32[16,320,32]{1,2,0:T(8,128)S(1)}, u32[]{:S(2)}, u32[]{:S(2)}) async-start(f32[16,320,32]{1,2,0:T(8,128)} %bitcast.68), calls=%async_computation.3 | async-start | bytes 1572864 | tf_op jit(solution)/shard_map/all_to_all | solution.py:36
  226.5 2.3 fusion.47
  233.4 5.4 %fusion.4 = bf16[1,128,5120]{2,1,0:T(8,128)(2,1)} fusion(bf16[5120,512]{1,0:T(8,128)(2,1)} %bitcast.2, bf16[128,1024]{0,1:T(8,128)(2,1)S(1)} %fusion.51), kind=kOutput, calls=%fused_computation.5 | convolution fusion | flops 671744000 | bytes 6684672 | tf_op jit(solution)/shard_map/dot_general | solution.py:132
  238.7 10.2 %all-to-all-done.3 = f32[16,320,32]{1,2,0:T(8,128)S(1)} async-done(((f32[16,320,32]{1,2,0:T(8,128)}), f32[16,320,32]{1,2,0:T(8,128)S(1)}, u32[]{:S(2)}, u32[]{:S(2)}) %all-to-all-start.3) | async-done | bytes 655392 | tf_op jit(solution)/shard_map/all_to_all | solution.py:36
  (99 shorter events, 28.0 us)
Async XLA Ops:
  4.5 6.4 %copy-start = (bf16[1,128,5120]{2,1,0:T(8,128)(2,1)S(1)}, bf16[1,128,5120]{2,1,0:T(8,128)(2,1)}, u32[]{:S(2)}) copy-start(bf16[1,128,5120]{2,1,0:T(8,128)(2,1)} %param.7) | copy-start | bytes 3932164
  4.5 85.7 %all-to-all-start = ((bf16[16,320,512]{2,1,0:T(8,128)(2,1)}), bf16[16,320,512]{2,1,0:T(8,128)(2,1)}, u32[]{:S(2)}, u32[]{:S(2)}) async-start(bf16[16,320,512]{2,1,0:T(8,128)(2,1)} %broadcast_in_dim.106), calls=%async_computation | async-start | bytes 10485760 | tf_op jit(solution)/shard_map/all_to_all | solution.py:29
  10.9 1.6 copy-start.15
  90.1 83.6 %all-to-all-start.2 = ((bf16[16,128,320]{1,2,0:T(8,128)(2,1)}), bf16[16,128,320]{1,2,0:T(8,128)(2,1)}, u32[]{:S(2)}, u32[]{:S(2)}) async-start(bf16[16,128,320]{1,2,0:T(8,128)(2,1)} %bitcast.64), calls=%async_computation.2 | async-start | bytes 2621440 | tf_op jit(solution)/shard_map/all_to_all | solution.py:140
  94.7 3.4 %copy-start.3 = (bf16[1,128,512]{2,1,0:T(8,128)(2,1)S(1)}, bf16[1,128,512]{2,1,0:T(8,128)(2,1)}, u32[]{:S(2)}) copy-start(bf16[1,128,512]{2,1,0:T(8,128)(2,1)} %param.9) | copy-start | bytes 393220
  94.7 11.0 %copy-start.1 = (bf16[1,128,2560]{2,1,0:T(8,128)(2,1)S(1)}, bf16[1,128,2560]{2,1,0:T(8,128)(2,1)}, u32[]{:S(2)}) copy-start(bf16[1,128,2560]{2,1,0:T(8,128)(2,1)} %param.8) | copy-start | bytes 1966084
  98.1 7.9 %copy-start.2 = (bf16[1,128,2560]{2,1,0:T(8,128)(2,1)S(1)}, bf16[1,128,2560]{2,1,0:T(8,128)(2,1)}, u32[]{:S(2)}) copy-start(bf16[1,128,2560]{2,1,0:T(8,128)(2,1)} %param.10) | copy-start | bytes 1966084
  98.1 17.0 %collective-permute-start.1 = (bf16[128,1024]{1,0:T(8,128)(2,1)S(1)}, bf16[128,1024]{1,0:T(8,128)(2,1)S(1)}, u32[]{:S(2)}, u32[]{:S(2)}) collective-permute-start(bf16[128,1024]{1,0:T(8,128)(2,1)S(1)} %pad_maximum_fusion.2), channel_id=1, source_target_pairs={{1,0},{2,1},{3,2},{4,3},{5,4},{6,5},{7,6},{8,7},{9,8},{10,9},{11,1... | collective-permute-start | bytes 786440 | tf_op jit(solution)/shard_map/ppermute | solution.py:19
  102.4 21.1 %collective-permute-start = (bf16[128,1024]{1,0:T(8,128)(2,1)S(1)}, bf16[128,1024]{1,0:T(8,128)(2,1)}, u32[]{:S(2)}, u32[]{:S(2)}) collective-permute-start(bf16[128,1024]{1,0:T(8,128)(2,1)S(1)} %pad_maximum_fusion.2), channel_id=1, source_target_pairs={{0,1},{1,2},{2,3},{3,4},{4,5},{5,6},{6,7},{7,8},{8,9},{9,10},{10,1... | collective-permute-start | bytes 786440 | tf_op jit(solution)/shard_map/ppermute | solution.py:17
  126.7 5.9 %copy-start.8 = (bf16[384,1,128]{2,1,0:T(2,128)(2,1)}, bf16[384,1,128]{2,1,0:T(2,128)(2,1)S(1)}, u32[]{:S(2)}) copy-start(bf16[384,1,128]{2,1,0:T(2,128)(2,1)S(1)} %get-tuple-element.20) | copy-start | bytes 294916
  126.7 16.9 %copy-start.6 = (bf16[384,1,128]{2,1,0:T(2,128)(2,1)}, bf16[384,1,128]{2,1,0:T(2,128)(2,1)S(1)}, u32[]{:S(2)}) copy-start(bf16[384,1,128]{2,1,0:T(2,128)(2,1)S(1)} %get-tuple-element.22) | copy-start | bytes 294916
  126.7 18.4 %copy-start.4 = (bf16[384,1,128]{2,1,0:T(2,128)(2,1)}, bf16[384,1,128]{2,1,0:T(2,128)(2,1)S(1)}, u32[]{:S(2)}) copy-start(bf16[384,1,128]{2,1,0:T(2,128)(2,1)S(1)} %get-tuple-element.23) | copy-start | bytes 294916
  132.5 1.6 copy-start.21
  134.1 1.6 copy-start.20
  136.1 2.5 %copy-start.24 = (f32[5,128,384]{1,2,0:T(8,128)}, f32[5,128,384]{1,2,0:T(8,128)S(1)}, u32[]{:S(2)}) copy-start(f32[5,128,384]{1,2,0:T(8,128)S(1)} %get-tuple-element.37) | copy-start | bytes 2949124
  146.0 16.4 %collective-permute-start.2 = (f32[128,1024]{0,1:T(8,128)S(1)}, f32[128,1024]{0,1:T(8,128)S(1)}, u32[]{:S(2)}, u32[]{:S(2)}) collective-permute-start(f32[128,1024]{0,1:T(8,128)S(1)} %get-tuple-element.16), channel_id=1, source_target_pairs={{1,0},{2,1},{3,2},{4,3},{5,4},{6,5},{7,6},{8,7},{9,8},{10,9},{11,1... | collective-permute-start | bytes 1572872 | tf_op jit(solution)/shard_map/ppermute | solution.py:42
  147.9 25.6 %collective-permute-start.3 = (f32[128,1024]{0,1:T(8,128)S(1)}, f32[128,1024]{0,1:T(8,128)S(1)}, u32[]{:S(2)}, u32[]{:S(2)}) collective-permute-start(f32[128,1024]{0,1:T(8,128)S(1)} %get-tuple-element.17), channel_id=1, source_target_pairs={{0,1},{1,2},{2,3},{3,4},{4,5},{5,6},{6,7},{7,8},{8,9},{9,10},{10,1... | collective-permute-start | bytes 1572872 | tf_op jit(solution)/shard_map/ppermute | solution.py:42
  175.3 6.7 %copy-start.9 = (bf16[384,1,128]{2,1,0:T(2,128)(2,1)S(1)}, bf16[384,1,128]{2,1,0:T(2,128)(2,1)}, u32[]{:S(2)}) copy-start(bf16[384,1,128]{2,1,0:T(2,128)(2,1)} %copy-done.8) | copy-start | bytes 294916
  175.3 37.8 %all-to-all-start.1 = ((bf16[16,128,512]{2,1,0:T(8,128)(2,1)}), bf16[16,128,512]{2,1,0:T(8,128)(2,1)S(1)}, u32[]{:S(2)}, u32[]{:S(2)}) async-start(bf16[16,128,512]{2,1,0:T(8,128)(2,1)} %broadcast_in_dim.116), calls=%async_computation.1 | async-start | bytes 4194304 | tf_op jit(solution)/shard_map/all_to_all | solution.py:29
  216.4 32.6 %all-to-all-start.3 = ((f32[16,320,32]{1,2,0:T(8,128)}), f32[16,320,32]{1,2,0:T(8,128)S(1)}, u32[]{:S(2)}, u32[]{:S(2)}) async-start(f32[16,320,32]{1,2,0:T(8,128)} %bitcast.68), calls=%async_computation.3 | async-start | bytes 1572864 | tf_op jit(solution)/shard_map/all_to_all | solution.py:36
  226.5 2.4 copy-start.7
  226.5 2.4 copy-start.19
  226.5 2.4 copy-start.23
  228.9 1.6 copy-start.26
  (12 other events, 13.4 us)

commit v3 on v2

--- a/solution.py
+++ b/solution.py
@@ -42,11 +42,44 @@
     return lax.ppermute(array, axis, pairs)
 
 
-def attend_block(query_rows, key_rows, value_rows, grad_rows, visible):
+def split_heads(query_rows, key_rows):
     rows_here = query_rows.shape[0]
     keys_here = key_rows.shape[0]
     head_count = key_rows.shape[1] // HD
     group_size = query_rows.shape[1] // key_rows.shape[1]
+    return rows_here, keys_here, head_count, group_size
+
+
+def attend_first(query_rows, key_rows, grad_rows, visible):
+    rows_here, keys_here, head_count, group_size = split_heads(query_rows, key_rows)
+    score_scale = HD ** (-0.5)
+    query_split = query_rows.reshape(rows_here, head_count, group_size, HD)
+    grad_split = grad_rows.reshape(rows_here, head_count, group_size, HD)
+    key_split = key_rows.reshape(keys_here, head_count, HD)
+    attentions = []
+    value_parts = []
+    for kv_group in range(head_count):
+        query_head = query_split[:, kv_group]
+        grad_head = grad_split[:, kv_group]
+        key_head = key_split[:, kv_group]
+        scores = (
+            jnp.einsum("qgd,kd->gqk", query_head, key_head, preferred_element_type=jnp.float32)
+            * score_scale
+        )
+        masked = jnp.where(visible[None], scores, -1e30)
+        highest = jnp.max(masked, axis=-1, keepdims=True)
+        weights = jnp.where(visible[None], jnp.exp(masked - highest), 0.0)
+        attention = weights / jnp.sum(weights, axis=-1, keepdims=True)
+        attention_low = attention.astype(jnp.bfloat16)
+        attentions.append(attention)
+        value_parts.append(
+            jnp.einsum("gqk,qgd->kd", attention_low, grad_head, preferred_element_type=jnp.float32)
+        )
+    return attentions, jnp.concatenate(value_parts, axis=1)
+
+
+def attend_second(query_rows, key_rows, value_rows, grad_rows, attentions):
+    rows_here, keys_here, head_count, group_size = split_heads(query_rows, key_rows)
     score_scale = HD ** (-0.5)
     high = lax.Precision.HIGHEST
     query_split = query_rows.reshape(rows_here, head_count, group_size, HD)
@@ -55,21 +88,12 @@
     value_split = value_rows.reshape(keys_here, head_count, HD)
     query_parts = []
     key_parts = []
-    value_parts = []
     for kv_group in range(head_count):
         query_head = query_split[:, kv_group]
         grad_head = grad_split[:, kv_group]
         key_head = key_split[:, kv_group]
         value_head = value_split[:, kv_group]
-        scores = (
-            jnp.einsum("qgd,kd->gqk", query_head, key_head, preferred_element_type=jnp.float32)
-            * score_scale
-        )
-        masked = jnp.where(visible[None], scores, -1e30)
-        highest = jnp.max(masked, axis=-1, keepdims=True)
-        weights = jnp.where(visible[None], jnp.exp(masked - highest), 0.0)
-        attention = weights / jnp.sum(weights, axis=-1, keepdims=True)
-        attention_low = attention.astype(jnp.bfloat16)
+        attention = attentions[kv_group]
         prob_grad = jnp.einsum(
             "qgd,kd->gqk", grad_head, value_head, preferred_element_type=jnp.float32
         )
@@ -83,27 +107,38 @@
         key_parts.append(
             jnp.einsum("gqk,qgd->kd", score_grad, query_wide, precision=high) * score_scale
         )
-        value_parts.append(
-            jnp.einsum("gqk,qgd->kd", attention_low, grad_head, preferred_element_type=jnp.float32)
-        )
     query_grad = jnp.stack(query_parts, axis=1).reshape(rows_here, -1)
-    kv_grad = jnp.concatenate(key_parts + value_parts, axis=1)
-    return (query_grad, kv_grad)
+    return query_grad, jnp.concatenate(key_parts, axis=1)
+
+
+def rim_sum(grad_block, tok_count):
+    lower_rim = grad_block[:tok_count]
+    upper_rim = grad_block[tok_count + tok_count :]
+    center = grad_block[tok_count : tok_count + tok_count]
+    from_upper = passed_along(lower_rim, "seq", -1)
+    from_lower = passed_along(upper_rim, "seq", 1)
+    return center + from_upper + from_lower
 
 
 def local(layer_input, query_states, key_states, out_grad, value_weight, segment_ids, pair_split):
     layer_rows = layer_input[0]
     tok_count = layer_rows.shape[0]
-    kv_width = key_states.shape[2]
     row_base = lax.axis_index("seq") * tok_count
-    columns = layer_rows
-    weight_full = gathered(value_weight, "dp").reshape(-1, value_weight.shape[1])
-    value_rows = jnp.dot(columns, weight_full, preferred_element_type=jnp.float32)
-    value_low = value_rows.astype(jnp.bfloat16)
-    both_states = jnp.concatenate([key_states[0], value_low], axis=1)
-    extended = with_halo(both_states, (("seq", 0),), tok_count)
-    key_block = extended[:, :kv_width]
-    value_block = extended[:, kv_width:]
+    dp_count = lax.axis_size("dp")
+    model_width = layer_rows.shape[1]
+    weight_rows, kv_width = value_weight.shape
+    weight_copies = jnp.broadcast_to(value_weight[None], (dp_count, weight_rows, kv_width))
+    input_pieces = (
+        layer_rows.reshape(tok_count, dp_count, model_width // dp_count)
+        .transpose(1, 0, 2)
+        .reshape(dp_count, -1, kv_width)
+    )
+    arrived = lax.all_to_all(
+        jnp.concatenate([weight_copies, input_pieces], axis=1), "dp", 0, 0, tiled=True
+    )
+    weight_full = arrived[:, :weight_rows].reshape(-1, kv_width)
+    input_blocks = arrived[:, weight_rows:].reshape(dp_count, tok_count, -1)
+    key_block = with_halo(key_states[0], (("seq", 0),), tok_count)
     seg_row = segment_ids[0]
     fill_ids = jnp.full((tok_count,), -1, jnp.int32)
     padded_ids = jnp.concatenate([fill_ids, seg_row, fill_ids])
@@ -118,39 +153,27 @@
     visible = (seg_key[None, :] == seg_query[:, None]) & (
         (pos_key[None, :] <= pos_query[:, None]) | (pos_key[None, :] < split_query[:, None])
     )
-    query_grad, kv_grad = attend_block(
-        query_states[0], key_block, value_block, out_grad[0], visible
-    )
-    lower_rim = kv_grad[:tok_count]
-    upper_rim = kv_grad[tok_count + tok_count :]
-    center = kv_grad[tok_count : tok_count + tok_count]
-    from_upper = passed_along(lower_rim, "seq", -1)
-    from_lower = passed_along(upper_rim, "seq", 1)
-    center = center + from_upper + from_lower
-    key_grad = center[:, :kv_width].astype(jnp.bfloat16)
-    value_grad = center[:, kv_width:].astype(jnp.bfloat16)
+    attentions, value_part = attend_first(query_states[0], key_block, out_grad[0], visible)
+    value_grad = rim_sum(value_part, tok_count).astype(jnp.bfloat16)
+    grad_rows = gathered(value_grad, "dp")
+    own_rows = jnp.einsum(
+        "rtk,rtc->kc", input_blocks, grad_rows, preferred_element_type=jnp.float32
+    )
+    summed = scattered_sum(own_rows, "seq")
+    devices_all = lax.axis_size("dp") * lax.axis_size("seq")
+    weight_grad = summed / devices_all
+    value_rows = jnp.dot(layer_rows, weight_full, preferred_element_type=jnp.float32)
+    value_block = with_halo(value_rows.astype(jnp.bfloat16), (("seq", 0),), tok_count)
+    query_grad, key_part = attend_second(
+        query_states[0], key_block, value_block, out_grad[0], attentions
+    )
+    key_grad = rim_sum(key_part, tok_count).astype(jnp.bfloat16)
     input_grad = lax.dot_general(
         value_grad,
         weight_full,
         (((1,), (1,)), ((), ())),
         preferred_element_type=jnp.float32,
     )
-    dp_count = lax.axis_size("dp")
-    model_width = layer_rows.shape[1]
-    input_blocks = lax.all_to_all(
-        layer_rows.reshape(tok_count, dp_count, model_width // dp_count).transpose(1, 0, 2),
-        "dp",
-        0,
-        0,
-        tiled=True,
-    )
-    grad_rows = gathered(value_grad, "dp")
-    own_rows = jnp.einsum(
-        "rtk,rtc->kc", input_blocks, grad_rows, preferred_element_type=jnp.float32
-    )
-    summed = scattered_sum(own_rows, "seq")
-    devices_all = lax.axis_size("dp") * lax.axis_size("seq")
-    weight_grad = summed / devices_all
     return (
         query_grad.astype(jnp.bfloat16)[None],
         key_grad[None],

time: 251 us -> 238 us (0.948)
  waiting for transfers between devices: 154 us -> 107 us
  starting transfers between devices: 42 us -> 73.1 us
  local copies, waits for them, and re-layouts: 17.9 us -> 22.8 us
  matrix products: 32.6 us -> 28.1 us
    all_to_all x2 -> x1, waiting for transfers between devices: 106 us -> 13.8 us  [gathered(): return lax.all_to_all(copies, axis, 0, 0, tiled=True)]
    ppermute x1 -> x2, waiting for transfers between devices: 8.6 us -> 66.2 us  [with_halo(): lax.ppermute(head, axis, [((i + 1) % count, i) for i in range(ends)])]
    all_to_all x2 -> x1, starting transfers between devices: 13.1 us -> 27.2 us  [gathered(): return lax.all_to_all(copies, axis, 0, 0, tiled=True)]
    all_to_all x1, waiting for transfers between devices: 10.2 us -> 0.01 us  [scattered_sum(): return jnp.sum(lax.all_to_all(pieces, axis, 0, 0, tiled=True), axis=0)]
    ppermute x2 -> x4, starting transfers between devices: 6.74 us -> 13.5 us  [passed_along(): return lax.ppermute(array, axis, pairs)]
    ppermute x1 -> x2, starting transfers between devices: 3.28 us -> 8.22 us  [with_halo(): lax.ppermute(tail, axis, [(i, (i + 1) % count) for i in range(ends)])]
    reshape x2 -> x3, local copies, waits for them, and re-layouts: 0.19 us -> 5 us  [the longest x1 2.81 us: local(): input_blocks = arrived[:, weight_rows:].reshape(dp_count, tok_count, -1)]
    dot_general x17, matrix products: 19.3 us -> 15 us  [the longest x4 6 us: attend_first(): jnp.einsum('gqk,qgd->kd', attention_low, grad_head, preferred_element_typ...]
  transfers between devices with their start and end apart: 8 -> 11, of which waited for: 7 -> 7; matrix products, arithmetic and copies ran while one was open for 15% -> 17% of each run, Pallas kernels for 0% -> 0%
where the time goes in v3:
time: 238 us; the launch traced here: 237 us
  waiting for transfers between devices  107 us (45%)
  starting transfers between devices  73.1 us (31%)
  matrix products  28.1 us (12%)
  local copies, waits for them, and re-layouts  22.8 us (10%)
  other arithmetic  4.68 us (2%)
    ppermute x2, waiting for transfers between devices, with_halo(): lax.ppermute(head, axis, [((i + 1) % count, i) for i in range(ends)])  66.2 us
    all_to_all x1, starting transfers between devices, gathered(): return lax.all_to_all(copies, axis, 0, 0, tiled=True)  27.2 us
    ppermute x4, waiting for transfers between devices, passed_along(): return lax.ppermute(array, axis, pairs)  21.8 us
    all_to_all x1, waiting for transfers between devices, gathered(): return lax.all_to_all(copies, axis, 0, 0, tiled=True)  13.8 us
    ppermute x4, starting transfers between devices, passed_along(): return lax.ppermute(array, axis, pairs)  13.5 us
    all_to_all x1, starting transfers between devices, scattered_sum(): return jnp.sum(lax.all_to_all(pieces, axis, 0, 0, tiled=True), axis=0)  12.4 us
    unnamed x40, local copies, waits for them, and re-layouts  8.22 us
    ppermute x2, starting transfers between devices, with_halo(): lax.ppermute(tail, axis, [(i, (i + 1) % count) for i in range(ends)])  8.22 us
  transfers between devices with their start and end apart: 11, of which 7 were waited for; matrix products, arithmetic and copies ran while one was open for 17% of the time, Pallas kernels for 0%

profile of v3, /device:TPU:26, one launch (start us, length us, event | category | flops | bytes accessed | tf_op | source)
XLA Modules:
  0.0 236.8 jit_solution(3252245367066943068)
XLA Ops:
  3.3 2.1 reshape.148
  6.8 3.3 %pad_maximum_fusion = bf16[16,400,512]{2,1,0:T(8,128)(2,1)} fusion(bf16[16,80,512]{2,1,0:T(8,128)(2,1)S(1)} %reshape.148, bf16[16,320,512]{2,1,0:T(8,128)(2,1)S(1)} %broadcast_in_dim.113), kind=kLoop, calls=%fused_computation.4 | loop fusion | flops 13107200 | bytes 13107200 | tf_op jit(solution)/shard_map/concatenate | solution.py:137
  10.2 6.4 %all-to-all-start = ((bf16[16,400,512]{2,1,0:T(8,128)(2,1)}), bf16[16,400,512]{2,1,0:T(8,128)(2,1)}, u32[]{:S(2)}, u32[]{:S(2)}) async-start(bf16[16,400,512]{2,1,0:T(8,128)(2,1)} %pad_maximum_fusion), calls=%async_computation | async-start | bytes 13107200 | tf_op jit(solution)/shard_map/all_to_all | solution.py:136
  16.7 3.5 %collective-permute-start.1 = (bf16[128,512]{0,1:T(8,128)(2,1)S(1)}, bf16[128,512]{0,1:T(8,128)(2,1)S(1)}, u32[]{:S(2)}, u32[]{:S(2)}) collective-permute-start(bf16[128,512]{0,1:T(8,128)(2,1)S(1)} %bitcast.316), channel_id=1, source_target_pairs={{1,0},{2,1},{3,2},{4,3},{5,4},{6,5},{7,6},{8,7},{9,8},{10,9},{11,1... | collective-permute-start | bytes 393224 | tf_op jit(solution)/shard_map/ppermute | solution.py:19
  20.2 3.4 %collective-permute-start = (bf16[128,512]{0,1:T(8,128)(2,1)S(1)}, bf16[128,512]{0,1:T(8,128)(2,1)S(1)}, u32[]{:S(2)}, u32[]{:S(2)}) collective-permute-start(bf16[128,512]{0,1:T(8,128)(2,1)S(1)} %bitcast.317), channel_id=1, source_target_pairs={{0,1},{1,2},{2,3},{3,4},{4,5},{5,6},{6,7},{7,8},{8,9},{9,10},{10,1... | collective-permute-start | bytes 393224 | tf_op jit(solution)/shard_map/ppermute | solution.py:17
  24.9 66.2 %collective-permute-done.1 = bf16[128,512]{0,1:T(8,128)(2,1)S(1)} collective-permute-done((bf16[128,512]{0,1:T(8,128)(2,1)S(1)}, bf16[128,512]{0,1:T(8,128)(2,1)S(1)}, u32[]{:S(2)}, u32[]{:S(2)}) %collective-permute-start.1) | collective-permute-done | bytes 131104 | tf_op jit(solution)/shard_map/ppermute | solution.py:19
  91.2 5.0 %collective-permute-done = bf16[128,512]{0,1:T(8,128)(2,1)S(1)} collective-permute-done((bf16[128,512]{0,1:T(8,128)(2,1)S(1)}, bf16[128,512]{0,1:T(8,128)(2,1)S(1)}, u32[]{:S(2)}, u32[]{:S(2)}) %collective-permute-start) | collective-permute-done | bytes 131104 | tf_op jit(solution)/shard_map/ppermute | solution.py:17
  108.3 1.9 collective-permute-start.6
  110.3 4.8 %collective-permute-start.7 = (f32[128,512]{0,1:T(8,128)S(1)}, f32[128,512]{0,1:T(8,128)S(1)}, u32[]{:S(2)}, u32[]{:S(2)}) collective-permute-start(f32[128,512]{0,1:T(8,128)S(1)} %get-tuple-element.21), channel_id=1, source_target_pairs={{0,1},{1,2},{2,3},{3,4},{4,5},{5,6},{6,7},{7,8},{8,9},{9,10},{10,1... | collective-permute-start | bytes 786440 | tf_op jit(solution)/shard_map/ppermute | solution.py:42
  115.1 4.0 %collective-permute-done.6 = f32[128,512]{0,1:T(8,128)S(1)} collective-permute-done((f32[128,512]{0,1:T(8,128)S(1)}, f32[128,512]{0,1:T(8,128)S(1)}, u32[]{:S(2)}, u32[]{:S(2)}) %collective-permute-start.6) | collective-permute-done | bytes 262176 | tf_op jit(solution)/shard_map/ppermute | solution.py:42
  119.1 5.5 %collective-permute-done.7 = f32[128,512]{0,1:T(8,128)S(1)} collective-permute-done((f32[128,512]{0,1:T(8,128)S(1)}, f32[128,512]{0,1:T(8,128)S(1)}, u32[]{:S(2)}, u32[]{:S(2)}) %collective-permute-start.7) | collective-permute-done | bytes 262176 | tf_op jit(solution)/shard_map/ppermute | solution.py:42
  126.3 27.2 %all-to-all-start.1 = ((bf16[16,128,512]{1,2,0:T(8,128)(2,1)}), bf16[16,128,512]{1,2,0:T(8,128)(2,1)}, u32[]{:S(2)}, u32[]{:S(2)}) async-start(bf16[16,128,512]{1,2,0:T(8,128)(2,1)} %broadcast_in_dim.116), calls=%async_computation.1 | async-start | bytes 4194304 | tf_op jit(solution)/shard_map/all_to_all | solution.py:29
  153.6 3.1 %slice.110 = bf16[16,320,512]{2,1,0:T(8,128)(2,1)S(1)} slice(bf16[16,400,512]{2,1,0:T(8,128)(2,1)} %all-to-all-done), slice={[0:16], [0:320], [0:512]} | slice | bytes 10485760 | tf_op jit(solution)/shard_map/slice | solution.py:139
  156.7 2.4 copy-done
  161.9 4.8 %collective-permute-start.2 = (bf16[128,512]{1,0:T(8,128)(2,1)S(1)}, bf16[128,512]{1,0:T(8,128)(2,1)S(1)}, u32[]{:S(2)}, u32[]{:S(2)}) collective-permute-start(bf16[128,512]{1,0:T(8,128)(2,1)S(1)} %fusion.47), channel_id=1, source_target_pairs={{0,1},{1,2},{2,3},{3,4},{4,5},{5,6},{6,7},{7,8},{8,9},{9,10},{10,1... | collective-permute-start | bytes 393224 | tf_op jit(solution)/shard_map/ppermute | solution.py:17
  168.1 2.8 %reshape.151 = bf16[16,128,320]{2,1,0:T(8,128)(2,1)} reshape(bf16[16,80,512]{2,1,0:T(8,128)(2,1)S(1)} %slice.131) | data formatting | bytes 2621440 | tf_op jit(solution)/shard_map/reshape | solution.py:140
  170.9 13.8 %all-to-all-done.1 = bf16[16,128,512]{1,2,0:T(8,128)(2,1)} async-done(((bf16[16,128,512]{1,2,0:T(8,128)(2,1)}), bf16[16,128,512]{1,2,0:T(8,128)(2,1)}, u32[]{:S(2)}, u32[]{:S(2)}) %all-to-all-start.1) | async-done | bytes 2097184 | tf_op jit(solution)/shard_map/all_to_all | solution.py:29
  184.7 4.3 %fusion.29 = f32[16,320,32]{1,2,0:T(8,128)} fusion(bf16[16,32,16,128]{3,1,0,2:T(8,128)(2,1)} %bitcast.35, bf16[16,128,320]{2,1,0:T(8,128)(2,1)} %reshape.151), kind=kOutput, calls=%fused_computation.39 | convolution fusion | flops 671088640 | bytes 4063232 | tf_op jit(solution)/shard_map/rtk,rtc->kc/dot_general | solution.py:159
  189.1 2.9 %fusion.4 = bf16[1,128,5120]{2,1,0:T(8,128)(2,1)} fusion(bf16[128,512]{0,1:T(8,128)(2,1)S(1)} %fusion.55, bf16[5120,512]{1,0:T(8,128)(2,1)S(1)} %bitcast.297), kind=kOutput, calls=%fused_computation.6 | convolution fusion | flops 671744000 | bytes 6684672 | tf_op jit(solution)/shard_map/dot_general | solution.py:171
  192.0 12.4 %all-to-all-start.2 = ((f32[16,320,32]{1,2,0:T(8,128)}), f32[16,320,32]{1,2,0:T(8,128)S(1)}, u32[]{:S(2)}, u32[]{:S(2)}) async-start(f32[16,320,32]{1,2,0:T(8,128)} %fusion.29), calls=%async_computation.2 | async-start | bytes 1572864 | tf_op jit(solution)/shard_map/all_to_all | solution.py:36
  212.9 2.0 collective-permute-start.4
  214.9 4.7 %collective-permute-start.5 = (f32[128,512]{0,1:T(8,128)S(1)}, f32[128,512]{0,1:T(8,128)S(1)}, u32[]{:S(2)}, u32[]{:S(2)}) collective-permute-start(f32[128,512]{0,1:T(8,128)S(1)} %get-tuple-element.23), channel_id=1, source_target_pairs={{0,1},{1,2},{2,3},{3,4},{4,5},{5,6},{6,7},{7,8},{8,9},{9,10},{10,1... | collective-permute-start | bytes 786440 | tf_op jit(solution)/shard_map/ppermute | solution.py:42
  222.9 8.0 %collective-permute-done.4 = f32[128,512]{0,1:T(8,128)S(1)} collective-permute-done((f32[128,512]{0,1:T(8,128)S(1)}, f32[128,512]{0,1:T(8,128)S(1)}, u32[]{:S(2)}, u32[]{:S(2)}) %collective-permute-start.4) | collective-permute-done | bytes 262176 | tf_op jit(solution)/shard_map/ppermute | solution.py:42
  230.9 4.4 %collective-permute-done.5 = f32[128,512]{0,1:T(8,128)S(1)} collective-permute-done((f32[128,512]{0,1:T(8,128)S(1)}, f32[128,512]{0,1:T(8,128)S(1)}, u32[]{:S(2)}, u32[]{:S(2)}) %collective-permute-start.5) | collective-permute-done | bytes 262176 | tf_op jit(solution)/shard_map/ppermute | solution.py:42
  (92 shorter events, 36.6 us)
Async XLA Ops:
  10.1 6.4 %copy-start.8 = (bf16[1,128,512]{2,1,0:T(8,128)(2,1)S(1)}, bf16[1,128,512]{2,1,0:T(8,128)(2,1)}, u32[]{:S(2)}) copy-start(bf16[1,128,512]{2,1,0:T(8,128)(2,1)} %param.9) | copy-start | bytes 393220
  10.2 13.6 %copy-start.2 = (bf16[1,128,2560]{2,1,0:T(8,128)(2,1)S(1)}, bf16[1,128,2560]{2,1,0:T(8,128)(2,1)}, u32[]{:S(2)}) copy-start(bf16[1,128,2560]{2,1,0:T(8,128)(2,1)} %param.8) | copy-start | bytes 1966084
  10.2 114.5 %all-to-all-start = ((bf16[16,400,512]{2,1,0:T(8,128)(2,1)}), bf16[16,400,512]{2,1,0:T(8,128)(2,1)}, u32[]{:S(2)}, u32[]{:S(2)}) async-start(bf16[16,400,512]{2,1,0:T(8,128)(2,1)} %pad_maximum_fusion), calls=%async_computation | async-start | bytes 13107200 | tf_op jit(solution)/shard_map/all_to_all | solution.py:136
  16.6 7.5 %copy-start.3 = (bf16[1,128,2560]{2,1,0:T(8,128)(2,1)S(1)}, bf16[1,128,2560]{2,1,0:T(8,128)(2,1)}, u32[]{:S(2)}) copy-start(bf16[1,128,2560]{2,1,0:T(8,128)(2,1)} %param.10) | copy-start | bytes 1966084
  16.6 7.9 %copy-start.9 = (s32[1,2048]{1,0:T(1,128)S(1)}, s32[1,2048]{1,0:T(1,128)}, u32[]{:S(2)}) copy-start(s32[1,2048]{1,0:T(1,128)} %param.12) | copy-start | bytes 24580
  16.6 8.0 %copy-start.10 = (s32[1,32]{1,0:T(1,128)S(1)}, s32[1,32]{1,0:T(1,128)}, u32[]{:S(2)}) copy-start(s32[1,32]{1,0:T(1,128)} %param.13) | copy-start | bytes 388
  16.7 74.4 %collective-permute-start.1 = (bf16[128,512]{0,1:T(8,128)(2,1)S(1)}, bf16[128,512]{0,1:T(8,128)(2,1)S(1)}, u32[]{:S(2)}, u32[]{:S(2)}) collective-permute-start(bf16[128,512]{0,1:T(8,128)(2,1)S(1)} %bitcast.316), channel_id=1, source_target_pairs={{1,0},{2,1},{3,2},{4,3},{5,4},{6,5},{7,6},{8,7},{9,8},{10,9},{11,1... | collective-permute-start | bytes 393224 | tf_op jit(solution)/shard_map/ppermute | solution.py:19
  20.2 76.0 %collective-permute-start = (bf16[128,512]{0,1:T(8,128)(2,1)S(1)}, bf16[128,512]{0,1:T(8,128)(2,1)S(1)}, u32[]{:S(2)}, u32[]{:S(2)}) collective-permute-start(bf16[128,512]{0,1:T(8,128)(2,1)S(1)} %bitcast.317), channel_id=1, source_target_pairs={{0,1},{1,2},{2,3},{3,4},{4,5},{5,6},{6,7},{7,8},{8,9},{9,10},{10,1... | collective-permute-start | bytes 393224 | tf_op jit(solution)/shard_map/ppermute | solution.py:17
  24.4 82.3 %copy-start.4 = (bf16[1,128,2560]{1,2,0:T(8,128)(2,1)}, bf16[1,128,2560]{1,2,0:T(8,128)(2,1)S(1)}, u32[]{:S(2)}) copy-start(bf16[1,128,2560]{1,2,0:T(8,128)(2,1)S(1)} %copy.151) | copy-start | bytes 1966084
  96.3 8.9 %copy-start.6 = (bf16[384,4,128]{2,0,1:T(8,128)(2,1)}, bf16[384,4,128]{2,0,1:T(8,128)(2,1)S(1)}, u32[]{:S(2)}) copy-start(bf16[384,4,128]{2,0,1:T(8,128)(2,1)S(1)} %pad_maximum_fusion.4) | copy-start | bytes 1179652
  108.3 10.7 %collective-permute-start.6 = (f32[128,512]{0,1:T(8,128)S(1)}, f32[128,512]{0,1:T(8,128)S(1)}, u32[]{:S(2)}, u32[]{:S(2)}) collective-permute-start(f32[128,512]{0,1:T(8,128)S(1)} %get-tuple-element.20), channel_id=1, source_target_pairs={{1,0},{2,1},{3,2},{4,3},{5,4},{6,5},{7,6},{8,7},{9,8},{10,9},{11,1... | collective-permute-start | bytes 786440 | tf_op jit(solution)/shard_map/ppermute | solution.py:42
  110.3 14.3 %collective-permute-start.7 = (f32[128,512]{0,1:T(8,128)S(1)}, f32[128,512]{0,1:T(8,128)S(1)}, u32[]{:S(2)}, u32[]{:S(2)}) collective-permute-start(f32[128,512]{0,1:T(8,128)S(1)} %get-tuple-element.21), channel_id=1, source_target_pairs={{0,1},{1,2},{2,3},{3,4},{4,5},{5,6},{6,7},{7,8},{8,9},{9,10},{10,1... | collective-permute-start | bytes 786440 | tf_op jit(solution)/shard_map/ppermute | solution.py:42
  126.3 58.4 %all-to-all-start.1 = ((bf16[16,128,512]{1,2,0:T(8,128)(2,1)}), bf16[16,128,512]{1,2,0:T(8,128)(2,1)}, u32[]{:S(2)}, u32[]{:S(2)}) async-start(bf16[16,128,512]{1,2,0:T(8,128)(2,1)} %broadcast_in_dim.116), calls=%async_computation.1 | async-start | bytes 4194304 | tf_op jit(solution)/shard_map/all_to_all | solution.py:29
  153.5 5.5 %copy-start.1 = (bf16[1,128,5120]{2,1,0:T(8,128)(2,1)S(1)}, bf16[1,128,5120]{2,1,0:T(8,128)(2,1)}, u32[]{:S(2)}) copy-start(bf16[1,128,5120]{2,1,0:T(8,128)(2,1)} %param.7) | copy-start | bytes 3932164
  156.7 2.4 %copy-start = (bf16[16,320,512]{2,1,0:T(8,128)(2,1)}, bf16[16,320,512]{2,1,0:T(8,128)(2,1)S(1)}, u32[]{:S(2)}) copy-start(bf16[16,320,512]{2,1,0:T(8,128)(2,1)S(1)} %slice.110) | copy-start | bytes 15728644
  159.9 44.5 %collective-permute-start.3 = (bf16[128,512]{1,0:T(8,128)(2,1)S(1)}, bf16[128,512]{1,0:T(8,128)(2,1)S(1)}, u32[]{:S(2)}, u32[]{:S(2)}) collective-permute-start(bf16[128,512]{1,0:T(8,128)(2,1)S(1)} %fusion.47), channel_id=1, source_target_pairs={{1,0},{2,1},{3,2},{4,3},{5,4},{6,5},{7,6},{8,7},{9,8},{10,9},{11,1... | collective-permute-start | bytes 393224 | tf_op jit(solution)/shard_map/ppermute | solution.py:19
  161.9 42.6 %collective-permute-start.2 = (bf16[128,512]{1,0:T(8,128)(2,1)S(1)}, bf16[128,512]{1,0:T(8,128)(2,1)S(1)}, u32[]{:S(2)}, u32[]{:S(2)}) collective-permute-start(bf16[128,512]{1,0:T(8,128)(2,1)S(1)} %fusion.47), channel_id=1, source_target_pairs={{0,1},{1,2},{2,3},{3,4},{4,5},{5,6},{6,7},{7,8},{8,9},{9,10},{10,1... | collective-permute-start | bytes 393224 | tf_op jit(solution)/shard_map/ppermute | solution.py:17
  168.1 21.0 %slice-start = ((s8[5242880]{0:T(1024)(128)(4,1)}), s8[1048576]{0:T(1024)(128)(4,1)S(1)}, s32[]{:S(2)}) async-start(s8[5242880]{0:T(1024)(128)(4,1)} %bitcast.295), calls=%async_computation.3 | async-start | bytes 2097152
  184.7 4.4 %slice-start.1 = ((s8[5242880]{0:T(1024)(128)(4,1)}), s8[4194304]{0:T(1024)(128)(4,1)S(1)}, s32[]{:S(2)}) async-start(s8[5242880]{0:T(1024)(128)(4,1)} %bitcast.295), calls=%async_computation.4 | async-start | bytes 8388608
  191.9 13.2 %copy-start.5 = (bf16[1,128,2560]{1,2,0:T(8,128)(2,1)S(1)}, bf16[1,128,2560]{1,2,0:T(8,128)(2,1)}, u32[]{:S(2)}) copy-start(bf16[1,128,2560]{1,2,0:T(8,128)(2,1)} %copy-done.4) | copy-start | bytes 1966084
  192.0 44.1 %all-to-all-start.2 = ((f32[16,320,32]{1,2,0:T(8,128)}), f32[16,320,32]{1,2,0:T(8,128)S(1)}, u32[]{:S(2)}, u32[]{:S(2)}) async-start(f32[16,320,32]{1,2,0:T(8,128)} %fusion.29), calls=%async_computation.2 | async-start | bytes 1572864 | tf_op jit(solution)/shard_map/all_to_all | solution.py:36
  205.1 1.6 copy-start.7
  212.9 18.0 %collective-permute-start.4 = (f32[128,512]{0,1:T(8,128)S(1)}, f32[128,512]{0,1:T(8,128)S(1)}, u32[]{:S(2)}, u32[]{:S(2)}) collective-permute-start(f32[128,512]{0,1:T(8,128)S(1)} %get-tuple-element.22), channel_id=1, source_target_pairs={{1,0},{2,1},{3,2},{4,3},{5,4},{6,5},{7,6},{8,7},{9,8},{10,9},{11,1... | collective-permute-start | bytes 786440 | tf_op jit(solution)/shard_map/ppermute | solution.py:42
  214.9 20.3 %collective-permute-start.5 = (f32[128,512]{0,1:T(8,128)S(1)}, f32[128,512]{0,1:T(8,128)S(1)}, u32[]{:S(2)}, u32[]{:S(2)}) collective-permute-start(f32[128,512]{0,1:T(8,128)S(1)} %get-tuple-element.23), channel_id=1, source_target_pairs={{0,1},{1,2},{2,3},{3,4},{4,5},{5,6},{6,7},{7,8},{8,9},{9,10},{10,1... | collective-permute-start | bytes 786440 | tf_op jit(solution)/shard_map/ppermute | solution.py:42
  (4 other events, 5.4 us)

commit v4 on v3

--- a/solution.py
+++ b/solution.py
@@ -26,6 +26,10 @@
 def gathered(array, axis):
     count = lax.axis_size(axis)
     copies = jnp.broadcast_to(array[None], (count,) + array.shape)
+    return lax.all_to_all(copies, axis, 0, 0, tiled=True)
+
+
+def gathered_copies(copies, axis):
     return lax.all_to_all(copies, axis, 0, 0, tiled=True)
 
 
@@ -127,18 +131,15 @@
     dp_count = lax.axis_size("dp")
     model_width = layer_rows.shape[1]
     weight_rows, kv_width = value_weight.shape
+    key_block = with_halo(key_states[0], (("seq", 0),), tok_count)
     weight_copies = jnp.broadcast_to(value_weight[None], (dp_count, weight_rows, kv_width))
+    key_block, weight_copies = lax.optimization_barrier((key_block, weight_copies))
+    weight_full = gathered_copies(weight_copies, "dp").reshape(-1, kv_width)
     input_pieces = (
         layer_rows.reshape(tok_count, dp_count, model_width // dp_count)
         .transpose(1, 0, 2)
         .reshape(dp_count, -1, kv_width)
     )
-    arrived = lax.all_to_all(
-        jnp.concatenate([weight_copies, input_pieces], axis=1), "dp", 0, 0, tiled=True
-    )
-    weight_full = arrived[:, :weight_rows].reshape(-1, kv_width)
-    input_blocks = arrived[:, weight_rows:].reshape(dp_count, tok_count, -1)
-    key_block = with_halo(key_states[0], (("seq", 0),), tok_count)
     seg_row = segment_ids[0]
     fill_ids = jnp.full((tok_count,), -1, jnp.int32)
     padded_ids = jnp.concatenate([fill_ids, seg_row, fill_ids])
@@ -155,7 +156,11 @@
     )
     attentions, value_part = attend_first(query_states[0], key_block, out_grad[0], visible)
     value_grad = rim_sum(value_part, tok_count).astype(jnp.bfloat16)
-    grad_rows = gathered(value_grad, "dp")
+    value_grad, weight_full = lax.optimization_barrier((value_grad, weight_full))
+    grad_copies = jnp.broadcast_to(value_grad[None], (dp_count,) + value_grad.shape)
+    arrived = gathered_copies(jnp.concatenate([grad_copies, input_pieces], axis=1), "dp")
+    grad_rows = arrived[:, :tok_count]
+    input_blocks = arrived[:, tok_count:].reshape(dp_count, tok_count, -1)
     own_rows = jnp.einsum(
         "rtk,rtc->kc", input_blocks, grad_rows, preferred_element_type=jnp.float32
     )

time: 238 us -> 230 us (0.966)
  starting transfers between devices: 73.1 us -> 54.3 us
  local copies, waits for them, and re-layouts: 22.8 us -> 35.5 us
  waiting for transfers between devices: 107 us -> 96.9 us
  matrix products: 28.1 us -> 34.1 us
  other arithmetic: 4.68 us -> 7.15 us
    ppermute x2, waiting for transfers between devices: 66.2 us -> 1.38 us  [with_halo(): lax.ppermute(head, axis, [((i + 1) % count, i) for i in range(ends)])]
    ppermute x4, waiting for transfers between devices: 21.8 us -> 57.1 us  [passed_along(): return lax.ppermute(array, axis, pairs)]
    all_to_all x2, waiting for transfers between devices: 13.8 us -> 35.7 us  [gathered_copies(): return lax.all_to_all(copies, axis, 0, 0, tiled=True)]
    all_to_all x2, starting transfers between devices: 33.6 us -> 15.1 us  [gathered_copies(): return lax.all_to_all(copies, axis, 0, 0, tiled=True)]
    unnamed x40 -> x63, local copies, waits for them, and re-layouts: 8.22 us -> 14.1 us
    dot_general x1, matrix products: 0.85 us -> 4 us  [local(): jnp.dot(layer_rows, weight_full, preferred_element_type=jnp.float32)]
    dot_general x4, matrix products: 2.74 us -> 5.78 us  [attend_second(): jnp.einsum('gqk,kd->qgd', score_grad, key_wide, precision=high)]
    broadcast_in_dim x1, local copies, waits for them, and re-layouts: 1.47 us -> 3.99 us  [local(): jnp.broadcast_to(value_weight[None], (dp_count, weight_rows, kv_width))]
  transfers between devices with their start and end apart: 11 -> 11, of which waited for: 7 -> 7; matrix products, arithmetic and copies ran while one was open for 17% -> 21% of each run, Pallas kernels for 0% -> 0%
where the time goes in v4:
time: 230 us; the launch traced here: 229 us
  waiting for transfers between devices  96.9 us (42%)
  starting transfers between devices  54.3 us (24%)
  local copies, waits for them, and re-layouts  35.5 us (15%)
  matrix products  34.1 us (15%)
  other arithmetic  7.15 us (3%)
    ppermute x4, waiting for transfers between devices, passed_along(): return lax.ppermute(array, axis, pairs)  57.1 us
    all_to_all x2, waiting for transfers between devices, gathered_copies(): return lax.all_to_all(copies, axis, 0, 0, tiled=True)  35.7 us
    all_to_all x2, starting transfers between devices, gathered_copies(): return lax.all_to_all(copies, axis, 0, 0, tiled=True)  15.1 us
    unnamed x63, local copies, waits for them, and re-layouts  14.1 us
    ppermute x4, starting transfers between devices, passed_along(): return lax.ppermute(array, axis, pairs)  13.8 us
    all_to_all x1, starting transfers between devices, scattered_sum(): return jnp.sum(lax.all_to_all(pieces, axis, 0, 0, tiled=True), axis=0)  11.7 us
    ppermute x2, starting transfers between devices, with_halo(): lax.ppermute(tail, axis, [(i, (i + 1) % count) for i in range(ends)])  9.12 us
    dot_general x4, matrix products, attend_second(): jnp.einsum('gqk,kd->qgd', score_grad, key_wide, precision=high)  5.78 us
  transfers between devices with their start and end apart: 11, of which 7 were waited for; matrix products, arithmetic and copies ran while one was open for 21% of the time, Pallas kernels for 0%

profile of v4, /device:TPU:26, one launch (start us, length us, event | category | flops | bytes accessed | tf_op | source)
XLA Modules:
  0.0 229.1 jit_solution(17899302066024139506)
XLA Ops:
  1.7 2.4 %collective-permute-start.1 = (bf16[128,512]{0,1:T(8,128)(2,1)S(1)}, bf16[128,512]{0,1:T(8,128)(2,1)S(1)}, u32[]{:S(2)}, u32[]{:S(2)}) collective-permute-start(bf16[128,512]{0,1:T(8,128)(2,1)S(1)} %bitcast.306), channel_id=1, source_target_pairs={{1,0},{2,1},{3,2},{4,3},{5,4},{6,5},{7,6},{8,7},{9,8},{10,9},{11,1... | collective-permute-start | bytes 393224 | tf_op jit(solution)/shard_map/ppermute | solution.py:19
  4.1 4.3 %collective-permute-start = (bf16[128,512]{0,1:T(8,128)(2,1)S(1)}, bf16[128,512]{0,1:T(8,128)(2,1)S(1)}, u32[]{:S(2)}, u32[]{:S(2)}) collective-permute-start(bf16[128,512]{0,1:T(8,128)(2,1)S(1)} %bitcast.307), channel_id=1, source_target_pairs={{0,1},{1,2},{2,3},{3,4},{4,5},{5,6},{6,7},{7,8},{8,9},{9,10},{10,1... | collective-permute-start | bytes 393224 | tf_op jit(solution)/shard_map/ppermute | solution.py:17
  9.8 2.7 %collective-permute-done = bf16[128,512]{0,1:T(8,128)(2,1)S(1)} collective-permute-done((bf16[128,512]{0,1:T(8,128)(2,1)S(1)}, bf16[128,512]{0,1:T(8,128)(2,1)S(1)}, u32[]{:S(2)}, u32[]{:S(2)}) %collective-permute-start) | collective-permute-done | bytes 131104 | tf_op jit(solution)/shard_map/ppermute | solution.py:17
  12.6 4.0 %broadcast_in_dim.106 = bf16[16,320,512]{2,1,0:T(8,128)(2,1)} broadcast(bf16[320,512]{1,0:T(8,128)(2,1)} %param.11), dimensions={1,2} | broadcast | bytes 5570560 | tf_op jit(solution)/shard_map/broadcast_in_dim | solution.py:135
  16.6 6.4 %all-to-all-start = ((bf16[16,320,512]{2,1,0:T(8,128)(2,1)}), bf16[16,320,512]{2,1,0:T(8,128)(2,1)}, u32[]{:S(2)}, u32[]{:S(2)}) async-start(bf16[16,320,512]{2,1,0:T(8,128)(2,1)} %broadcast_in_dim.106), calls=%async_computation | async-start | bytes 10485760 | tf_op jit(solution)/shard_map/all_to_all | solution.py:33
  37.8 4.7 %collective-permute-start.3 = (f32[128,512]{0,1:T(8,128)}, f32[128,512]{0,1:T(8,128)S(1)}, u32[]{:S(2)}, u32[]{:S(2)}) collective-permute-start(f32[128,512]{0,1:T(8,128)} %get-tuple-element.31), channel_id=1, source_target_pairs={{0,1},{1,2},{2,3},{3,4},{4,5},{5,6},{6,7},{7,8},{8,9},{9,10},{10,1... | collective-permute-start | bytes 786440 | tf_op jit(solution)/shard_map/ppermute | solution.py:46
  45.8 2.9 %reshape.149 = bf16[16,80,512]{2,1,0:T(8,128)(2,1)} reshape(bf16[16,128,320]{2,1,0:T(8,128)(2,1)S(1)} %copy.178) | data formatting | bytes 2621440 | tf_op jit(solution)/shard_map/reshape | solution.py:141
  48.8 37.6 %collective-permute-done.2 = f32[128,512]{0,1:T(8,128)S(1)} collective-permute-done((f32[128,512]{0,1:T(8,128)}, f32[128,512]{0,1:T(8,128)S(1)}, u32[]{:S(2)}, u32[]{:S(2)}) %collective-permute-start.2) | collective-permute-done | bytes 262176 | tf_op jit(solution)/shard_map/ppermute | solution.py:46
  86.3 6.5 %collective-permute-done.3 = f32[128,512]{0,1:T(8,128)S(1)} collective-permute-done((f32[128,512]{0,1:T(8,128)}, f32[128,512]{0,1:T(8,128)S(1)}, u32[]{:S(2)}, u32[]{:S(2)}) %collective-permute-start.3) | collective-permute-done | bytes 262176 | tf_op jit(solution)/shard_map/ppermute | solution.py:46
  93.8 8.4 %all-to-all-done = bf16[16,320,512]{2,1,0:T(8,128)(2,1)} async-done(((bf16[16,320,512]{2,1,0:T(8,128)(2,1)}), bf16[16,320,512]{2,1,0:T(8,128)(2,1)}, u32[]{:S(2)}, u32[]{:S(2)}) %all-to-all-start) | async-done | bytes 5242912 | tf_op jit(solution)/shard_map/all_to_all | solution.py:33
  102.2 4.0 %fusion.50 = bf16[128,512]{1,0:T(8,128)(2,1)} fusion(bf16[5120,512]{1,0:T(8,128)(2,1)} %bitcast.31, bf16[1,128,5120]{2,1,0:T(8,128)(2,1)S(1)} %copy-done), kind=kOutput, calls=%fused_computation.66 | convolution fusion | flops 671154176 | bytes 6684672 | tf_op jit(solution)/shard_map/dot_general | solution.py:170
  108.3 4.8 %collective-permute-start.4 = (bf16[128,512]{1,0:T(8,128)(2,1)}, bf16[128,512]{1,0:T(8,128)(2,1)}, u32[]{:S(2)}, u32[]{:S(2)}) collective-permute-start(bf16[128,512]{1,0:T(8,128)(2,1)} %fusion.50), channel_id=1, source_target_pairs={{0,1},{1,2},{2,3},{3,4},{4,5},{5,6},{6,7},{7,8},{8,9},{9,10},{10,1... | collective-permute-start | bytes 393224 | tf_op jit(solution)/shard_map/ppermute | solution.py:17
  115.6 8.7 %all-to-all-start.1 = ((bf16[16,208,512]{2,1,0:T(8,128)(2,1)}), bf16[16,208,512]{2,1,0:T(8,128)(2,1)S(1)}, u32[]{:S(2)}, u32[]{:S(2)}) async-start(bf16[16,208,512]{2,1,0:T(8,128)(2,1)} %pad_maximum_fusion), calls=%async_computation.1 | async-start | bytes 6815744 | tf_op jit(solution)/shard_map/all_to_all | solution.py:33
  124.3 5.4 %fusion.4 = bf16[1,128,5120]{2,1,0:T(8,128)(2,1)} fusion(bf16[128,512]{0,1:T(8,128)(2,1)S(1)} %fusion.60, bf16[5120,512]{1,0:T(8,128)(2,1)} %bitcast.31), kind=kOutput, calls=%fused_computation.5 | convolution fusion | flops 671744000 | bytes 6684672 | tf_op jit(solution)/shard_map/dot_general | solution.py:176
  133.4 2.5 %fusion.78 = (bf16[384,1,128]{2,1,0:T(2,128)(2,1)S(1)}, bf16[384,1,128]{2,1,0:T(2,128)(2,1)S(1)}, bf16[384,1,128]{2,1,0:T(2,128)(2,1)S(1)}, bf16[384,1,128]{2,1,0:T(2,128)(2,1)S(1)}) fusion(bf16[384,4,128]{2,1,0:T(4,128)(2,1)} %reshape.148), kind=kLoop, calls=%fused_computation.137 | loop fusion | bytes 786432 | tf_op jit(solution)/shard_map/slice | solution.py:99
  145.0 2.2 fusion.49
  147.3 27.3 %all-to-all-done.1 = bf16[16,208,512]{2,1,0:T(8,128)(2,1)S(1)} async-done(((bf16[16,208,512]{2,1,0:T(8,128)(2,1)}), bf16[16,208,512]{2,1,0:T(8,128)(2,1)S(1)}, u32[]{:S(2)}, u32[]{:S(2)}) %all-to-all-start.1) | async-done | bytes 3407904 | tf_op jit(solution)/shard_map/all_to_all | solution.py:33
  176.1 4.6 %copy.227 = bf16[16,128,512]{1,0,2:T(8,128)(2,1)} copy(bf16[16,128,512]{2,1,0:T(8,128)(2,1)} %slice.131) | data formatting | bytes 4194304
  181.8 4.4 %reshape.150 = bf16[16,128,320]{2,1,0:T(8,128)(2,1)} reshape(bf16[16,80,512]{2,1,0:T(8,128)(2,1)} %slice.130) | data formatting | bytes 2621440 | tf_op jit(solution)/shard_map/reshape | solution.py:163
  186.2 3.6 %fusion.30 = f32[16,320,32]{1,2,0:T(8,128)} fusion(bf16[16,32,16,128]{3,2,1,0:T(8,128)(2,1)S(1)} %bitcast.289, bf16[16,128,320]{2,1,0:T(8,128)(2,1)} %reshape.150), kind=kOutput, calls=%fused_computation.40 | convolution fusion | flops 671088640 | bytes 4063232 | tf_op jit(solution)/shard_map/rtk,rtc->kc/dot_general | solution.py:164
  189.8 11.7 %all-to-all-start.2 = ((f32[16,320,32]{1,2,0:T(8,128)}), f32[16,320,32]{1,2,0:T(8,128)S(1)}, u32[]{:S(2)}, u32[]{:S(2)}) async-start(f32[16,320,32]{1,2,0:T(8,128)} %fusion.30), calls=%async_computation.2 | async-start | bytes 1572864 | tf_op jit(solution)/shard_map/all_to_all | solution.py:40
  203.8 4.9 %collective-permute-start.7 = (f32[128,512]{0,1:T(8,128)S(1)}, f32[128,512]{0,1:T(8,128)S(1)}, u32[]{:S(2)}, u32[]{:S(2)}) collective-permute-start(f32[128,512]{0,1:T(8,128)S(1)} %get-tuple-element.29), channel_id=1, source_target_pairs={{0,1},{1,2},{2,3},{3,4},{4,5},{5,6},{6,7},{7,8},{8,9},{9,10},{10,1... | collective-permute-start | bytes 786440 | tf_op jit(solution)/shard_map/ppermute | solution.py:46
  208.8 2.2 fusion.47
  214.6 13.1 %collective-permute-done.6 = f32[128,512]{0,1:T(8,128)S(1)} collective-permute-done((f32[128,512]{0,1:T(8,128)S(1)}, f32[128,512]{0,1:T(8,128)S(1)}, u32[]{:S(2)}, u32[]{:S(2)}) %collective-permute-start.6) | collective-permute-done | bytes 262176 | tf_op jit(solution)/shard_map/ppermute | solution.py:46
  (112 shorter events, 48.6 us)
Async XLA Ops:
  1.7 8.1 %collective-permute-start.1 = (bf16[128,512]{0,1:T(8,128)(2,1)S(1)}, bf16[128,512]{0,1:T(8,128)(2,1)S(1)}, u32[]{:S(2)}, u32[]{:S(2)}) collective-permute-start(bf16[128,512]{0,1:T(8,128)(2,1)S(1)} %bitcast.306), channel_id=1, source_target_pairs={{1,0},{2,1},{3,2},{4,3},{5,4},{6,5},{7,6},{8,7},{9,8},{10,9},{11,1... | collective-permute-start | bytes 393224 | tf_op jit(solution)/shard_map/ppermute | solution.py:19
  4.1 8.4 %collective-permute-start = (bf16[128,512]{0,1:T(8,128)(2,1)S(1)}, bf16[128,512]{0,1:T(8,128)(2,1)S(1)}, u32[]{:S(2)}, u32[]{:S(2)}) collective-permute-start(bf16[128,512]{0,1:T(8,128)(2,1)S(1)} %bitcast.307), channel_id=1, source_target_pairs={{0,1},{1,2},{2,3},{3,4},{4,5},{5,6},{6,7},{7,8},{8,9},{9,10},{10,1... | collective-permute-start | bytes 393224 | tf_op jit(solution)/shard_map/ppermute | solution.py:17
  12.6 18.4 %copy-start.11 = (bf16[384,512]{0,1:T(8,128)(2,1)}, bf16[384,512]{0,1:T(8,128)(2,1)S(1)}, u32[]{:S(2)}) copy-start(bf16[384,512]{0,1:T(8,128)(2,1)S(1)} %pad_maximum_fusion.4) | copy-start | bytes 1179652
  16.6 6.4 %copy-start.5 = (bf16[1,128,2560]{2,1,0:T(8,128)(2,1)S(1)}, bf16[1,128,2560]{2,1,0:T(8,128)(2,1)}, u32[]{:S(2)}) copy-start(bf16[1,128,2560]{2,1,0:T(8,128)(2,1)} %param.8) | copy-start | bytes 1966084
  16.6 6.8 %copy-start.6 = (bf16[1,128,2560]{2,1,0:T(8,128)(2,1)S(1)}, bf16[1,128,2560]{2,1,0:T(8,128)(2,1)}, u32[]{:S(2)}) copy-start(bf16[1,128,2560]{2,1,0:T(8,128)(2,1)} %param.10) | copy-start | bytes 1966084
  16.6 85.7 %all-to-all-start = ((bf16[16,320,512]{2,1,0:T(8,128)(2,1)}), bf16[16,320,512]{2,1,0:T(8,128)(2,1)}, u32[]{:S(2)}, u32[]{:S(2)}) async-start(bf16[16,320,512]{2,1,0:T(8,128)(2,1)} %broadcast_in_dim.106), calls=%async_computation | async-start | bytes 10485760 | tf_op jit(solution)/shard_map/all_to_all | solution.py:33
  23.3 7.6 %copy-start.7 = (bf16[1,128,2560]{1,2,0:T(8,128)(2,1)}, bf16[1,128,2560]{1,2,0:T(8,128)(2,1)S(1)}, u32[]{:S(2)}) copy-start(bf16[1,128,2560]{1,2,0:T(8,128)(2,1)S(1)} %copy.139) | copy-start | bytes 1966084
  23.7 8.8 %copy-start.9 = (bf16[1,128,2560]{1,2,0:T(8,128)(2,1)}, bf16[1,128,2560]{1,2,0:T(8,128)(2,1)S(1)}, u32[]{:S(2)}) copy-start(bf16[1,128,2560]{1,2,0:T(8,128)(2,1)S(1)} %copy.141) | copy-start | bytes 1966084
  33.9 8.6 %copy-start = (bf16[1,128,5120]{2,1,0:T(8,128)(2,1)S(1)}, bf16[1,128,5120]{2,1,0:T(8,128)(2,1)}, u32[]{:S(2)}) copy-start(bf16[1,128,5120]{2,1,0:T(8,128)(2,1)} %param.7) | copy-start | bytes 3932164
  35.8 50.6 %collective-permute-start.2 = (f32[128,512]{0,1:T(8,128)}, f32[128,512]{0,1:T(8,128)S(1)}, u32[]{:S(2)}, u32[]{:S(2)}) collective-permute-start(f32[128,512]{0,1:T(8,128)} %get-tuple-element.30), channel_id=1, source_target_pairs={{1,0},{2,1},{3,2},{4,3},{5,4},{6,5},{7,6},{8,7},{9,8},{10,9},{11,1... | collective-permute-start | bytes 786440 | tf_op jit(solution)/shard_map/ppermute | solution.py:46
  37.8 55.0 %collective-permute-start.3 = (f32[128,512]{0,1:T(8,128)}, f32[128,512]{0,1:T(8,128)S(1)}, u32[]{:S(2)}, u32[]{:S(2)}) collective-permute-start(f32[128,512]{0,1:T(8,128)} %get-tuple-element.31), channel_id=1, source_target_pairs={{0,1},{1,2},{2,3},{3,4},{4,5},{5,6},{6,7},{7,8},{8,9},{9,10},{10,1... | collective-permute-start | bytes 786440 | tf_op jit(solution)/shard_map/ppermute | solution.py:46
  106.2 7.2 %copy-start.1 = (bf16[16,80,512]{2,1,0:T(8,128)(2,1)S(1)}, bf16[16,80,512]{2,1,0:T(8,128)(2,1)}, u32[]{:S(2)}) copy-start(bf16[16,80,512]{2,1,0:T(8,128)(2,1)} %reshape.149) | copy-start | bytes 3932164
  106.2 23.5 %collective-permute-start.5 = (bf16[128,512]{1,0:T(8,128)(2,1)}, bf16[128,512]{1,0:T(8,128)(2,1)}, u32[]{:S(2)}, u32[]{:S(2)}) collective-permute-start(bf16[128,512]{1,0:T(8,128)(2,1)} %fusion.50), channel_id=1, source_target_pairs={{1,0},{2,1},{3,2},{4,3},{5,4},{6,5},{7,6},{8,7},{9,8},{10,9},{11,1... | collective-permute-start | bytes 393224 | tf_op jit(solution)/shard_map/ppermute | solution.py:19
  108.3 21.4 %collective-permute-start.4 = (bf16[128,512]{1,0:T(8,128)(2,1)}, bf16[128,512]{1,0:T(8,128)(2,1)}, u32[]{:S(2)}, u32[]{:S(2)}) collective-permute-start(bf16[128,512]{1,0:T(8,128)(2,1)} %fusion.50), channel_id=1, source_target_pairs={{0,1},{1,2},{2,3},{3,4},{4,5},{5,6},{6,7},{7,8},{8,9},{9,10},{10,1... | collective-permute-start | bytes 393224 | tf_op jit(solution)/shard_map/ppermute | solution.py:17
  115.6 59.0 %all-to-all-start.1 = ((bf16[16,208,512]{2,1,0:T(8,128)(2,1)}), bf16[16,208,512]{2,1,0:T(8,128)(2,1)S(1)}, u32[]{:S(2)}, u32[]{:S(2)}) async-start(bf16[16,208,512]{2,1,0:T(8,128)(2,1)} %pad_maximum_fusion), calls=%async_computation.1 | async-start | bytes 6815744 | tf_op jit(solution)/shard_map/all_to_all | solution.py:33
  139.1 4.3 %copy-start.23 = (f32[5,128,384]{1,2,0:T(8,128)}, f32[5,128,384]{1,2,0:T(8,128)S(1)}, u32[]{:S(2)}) copy-start(f32[5,128,384]{1,2,0:T(8,128)S(1)} %get-tuple-element.49) | copy-start | bytes 2949124
  181.8 4.4 %copy-start.4 = (bf16[16,128,512]{1,0,2:T(8,128)(2,1)S(1)}, bf16[16,128,512]{1,0,2:T(8,128)(2,1)}, u32[]{:S(2)}) copy-start(bf16[16,128,512]{1,0,2:T(8,128)(2,1)} %copy.227) | copy-start | bytes 6291460
  186.2 15.4 %copy-start.2 = (f32[384,512]{0,1:T(8,128)S(1)}, f32[384,512]{0,1:T(8,128)}, u32[]{:S(2)}) copy-start(f32[384,512]{0,1:T(8,128)} %pad_maximum_fusion.2) | copy-start | bytes 2359300
  189.8 18.9 %copy-start.12 = (bf16[384,512]{0,1:T(8,128)(2,1)S(1)}, bf16[384,512]{0,1:T(8,128)(2,1)}, u32[]{:S(2)}) copy-start(bf16[384,512]{0,1:T(8,128)(2,1)} %copy-done.11) | copy-start | bytes 1179652
  189.8 38.6 %all-to-all-start.2 = ((f32[16,320,32]{1,2,0:T(8,128)}), f32[16,320,32]{1,2,0:T(8,128)S(1)}, u32[]{:S(2)}, u32[]{:S(2)}) async-start(f32[16,320,32]{1,2,0:T(8,128)} %fusion.30), calls=%async_computation.2 | async-start | bytes 1572864 | tf_op jit(solution)/shard_map/all_to_all | solution.py:40
  201.6 9.3 %copy-start.20 = (f32[5,128,384]{1,2,0:T(8,128)S(1)}, f32[5,128,384]{1,2,0:T(8,128)}, u32[]{:S(2)}) copy-start(f32[5,128,384]{1,2,0:T(8,128)} %get-tuple-element.37) | copy-start | bytes 2949124
  201.6 9.3 %copy-start.27 = (f32[5,128,384]{1,2,0:T(8,128)S(1)}, f32[5,128,384]{1,2,0:T(8,128)}, u32[]{:S(2)}) copy-start(f32[5,128,384]{1,2,0:T(8,128)} %copy-done.26) | copy-start | bytes 2949124
  201.6 26.0 %collective-permute-start.6 = (f32[128,512]{0,1:T(8,128)S(1)}, f32[128,512]{0,1:T(8,128)S(1)}, u32[]{:S(2)}, u32[]{:S(2)}) collective-permute-start(f32[128,512]{0,1:T(8,128)S(1)} %get-tuple-element.28), channel_id=1, source_target_pairs={{1,0},{2,1},{3,2},{4,3},{5,4},{6,5},{7,6},{8,7},{9,8},{10,9},{11,1... | collective-permute-start | bytes 786440 | tf_op jit(solution)/shard_map/ppermute | solution.py:46
  203.8 23.8 %collective-permute-start.7 = (f32[128,512]{0,1:T(8,128)S(1)}, f32[128,512]{0,1:T(8,128)S(1)}, u32[]{:S(2)}, u32[]{:S(2)}) collective-permute-start(f32[128,512]{0,1:T(8,128)S(1)} %get-tuple-element.29), channel_id=1, source_target_pairs={{0,1},{1,2},{2,3},{3,4},{4,5},{5,6},{6,7},{7,8},{8,9},{9,10},{10,1... | collective-permute-start | bytes 786440 | tf_op jit(solution)/shard_map/ppermute | solution.py:46
  (15 other events, 24.4 us)

commit v5 on v4

--- a/solution.py
+++ b/solution.py
@@ -135,11 +135,7 @@
     weight_copies = jnp.broadcast_to(value_weight[None], (dp_count, weight_rows, kv_width))
     key_block, weight_copies = lax.optimization_barrier((key_block, weight_copies))
     weight_full = gathered_copies(weight_copies, "dp").reshape(-1, kv_width)
-    input_pieces = (
-        layer_rows.reshape(tok_count, dp_count, model_width // dp_count)
-        .transpose(1, 0, 2)
-        .reshape(dp_count, -1, kv_width)
-    )
+    input_pieces = layer_rows.reshape(tok_count, dp_count, model_width // dp_count).transpose(1, 0, 2)
     seg_row = segment_ids[0]
     fill_ids = jnp.full((tok_count,), -1, jnp.int32)
     padded_ids = jnp.concatenate([fill_ids, seg_row, fill_ids])
@@ -158,13 +154,14 @@
     value_grad = rim_sum(value_part, tok_count).astype(jnp.bfloat16)
     value_grad, weight_full = lax.optimization_barrier((value_grad, weight_full))
     grad_copies = jnp.broadcast_to(value_grad[None], (dp_count,) + value_grad.shape)
-    arrived = gathered_copies(jnp.concatenate([grad_copies, input_pieces], axis=1), "dp")
-    grad_rows = arrived[:, :tok_count]
-    input_blocks = arrived[:, tok_count:].reshape(dp_count, tok_count, -1)
-    own_rows = jnp.einsum(
-        "rtk,rtc->kc", input_blocks, grad_rows, preferred_element_type=jnp.float32
-    )
-    summed = scattered_sum(own_rows, "seq")
+    arrived = gathered_copies(jnp.concatenate([grad_copies, input_pieces], axis=2), "dp")
+    seq_count = lax.axis_size("seq")
+    grad_rows = arrived[:, :, :kv_width].reshape(dp_count, tok_count, seq_count, -1)
+    input_blocks = arrived[:, :, kv_width:]
+    own_pieces = jnp.einsum(
+        "rtk,rtjc->jkc", input_blocks, grad_rows, preferred_element_type=jnp.float32
+    )
+    summed = jnp.sum(gathered_copies(own_pieces, "seq"), axis=0)
     devices_all = lax.axis_size("dp") * lax.axis_size("seq")
     weight_grad = summed / devices_all
     value_rows = jnp.dot(layer_rows, weight_full, preferred_element_type=jnp.float32)

time: 230 us -> 219 us (0.952)
  local copies, waits for them, and re-layouts: 35.5 us -> 18.7 us
  waiting for transfers between devices: 96.9 us -> 104 us
  matrix products: 34.1 us -> 30.6 us
    all_to_all x2 -> x3, starting transfers between devices: 15.1 us -> 27.6 us  [gathered_copies(): return lax.all_to_all(copies, axis, 0, 0, tiled=True)]
    all_to_all x1 -> x0, starting transfers between devices: 11.7 us -> none  [scattered_sum(): return jnp.sum(lax.all_to_all(pieces, axis, 0, 0, tiled=True), axis=0)]
    reshape x2 -> x0, local copies, waits for them, and re-layouts: 7.3 us -> none  [the longest x1 4.37 us: local(): input_blocks = arrived[:, tok_count:].reshape(dp_count, tok_count, -1)]
    ppermute x4, waiting for transfers between devices: 57.1 us -> 63.8 us  [passed_along(): return lax.ppermute(array, axis, pairs)]
    unnamed x63 -> x64, local copies, waits for them, and re-layouts: 14.1 us -> 7.95 us
    slice x2 -> x1, local copies, waits for them, and re-layouts: 2.7 us -> 0.14 us  [local(): arrived[:, :, :kv_width].reshape(dp_count, tok_count, seq_count, -1)]
    all_to_all x2 -> x3, waiting for transfers between devices: 35.7 us -> 36.6 us  [gathered_copies(): return lax.all_to_all(copies, axis, 0, 0, tiled=True)]
  transfers between devices with their start and end apart: 11 -> 11, of which waited for: 7 -> 7; matrix products, arithmetic and copies ran while one was open for 21% -> 19% of each run, Pallas kernels for 0% -> 0%
where the time goes in v5:
time: 219 us; the launch traced here: 218 us
  waiting for transfers between devices  104 us (47%)
  starting transfers between devices  54.6 us (25%)
  matrix products  30.6 us (14%)
  local copies, waits for them, and re-layouts  18.7 us (9%)
  other arithmetic  8.1 us (4%)
    ppermute x4, waiting for transfers between devices, passed_along(): return lax.ppermute(array, axis, pairs)  63.8 us
    all_to_all x3, waiting for transfers between devices, gathered_copies(): return lax.all_to_all(copies, axis, 0, 0, tiled=True)  36.6 us
    all_to_all x3, starting transfers between devices, gathered_copies(): return lax.all_to_all(copies, axis, 0, 0, tiled=True)  27.6 us
    ppermute x4, starting transfers between devices, passed_along(): return lax.ppermute(array, axis, pairs)  13.6 us
    ppermute x2, starting transfers between devices, with_halo(): lax.ppermute(tail, axis, [(i, (i + 1) % count) for i in range(ends)])  9.12 us
    unnamed x64, local copies, waits for them, and re-layouts  7.95 us
    dot_general x4, matrix products, attend_second(): jnp.einsum('gqk,kd->qgd', score_grad, key_wide, precision=high)  5.82 us
    dot_general x1, matrix products, local(): lax.dot_general(value_grad, weight_full, (((1,), (1,)), ((), ())), prefer...  5.37 us
  transfers between devices with their start and end apart: 11, of which 7 were waited for; matrix products, arithmetic and copies ran while one was open for 19% of the time, Pallas kernels for 0%

profile of v5, /device:TPU:26, one launch (start us, length us, event | category | flops | bytes accessed | tf_op | source)
XLA Modules:
  0.0 217.6 jit_solution(8553633887420971314)
XLA Ops:
  1.7 2.4 %collective-permute-start.1 = (bf16[128,512]{0,1:T(8,128)(2,1)S(1)}, bf16[128,512]{0,1:T(8,128)(2,1)S(1)}, u32[]{:S(2)}, u32[]{:S(2)}) collective-permute-start(bf16[128,512]{0,1:T(8,128)(2,1)S(1)} %bitcast.305), channel_id=1, source_target_pairs={{1,0},{2,1},{3,2},{4,3},{5,4},{6,5},{7,6},{8,7},{9,8},{10,9},{11,1... | collective-permute-start | bytes 393224 | tf_op jit(solution)/shard_map/ppermute | solution.py:19
  4.1 4.3 %collective-permute-start = (bf16[128,512]{0,1:T(8,128)(2,1)S(1)}, bf16[128,512]{0,1:T(8,128)(2,1)S(1)}, u32[]{:S(2)}, u32[]{:S(2)}) collective-permute-start(bf16[128,512]{0,1:T(8,128)(2,1)S(1)} %bitcast.306), channel_id=1, source_target_pairs={{0,1},{1,2},{2,3},{3,4},{4,5},{5,6},{6,7},{7,8},{8,9},{9,10},{10,1... | collective-permute-start | bytes 393224 | tf_op jit(solution)/shard_map/ppermute | solution.py:17
  9.8 2.7 %collective-permute-done = bf16[128,512]{0,1:T(8,128)(2,1)S(1)} collective-permute-done((bf16[128,512]{0,1:T(8,128)(2,1)S(1)}, bf16[128,512]{0,1:T(8,128)(2,1)S(1)}, u32[]{:S(2)}, u32[]{:S(2)}) %collective-permute-start) | collective-permute-done | bytes 131104 | tf_op jit(solution)/shard_map/ppermute | solution.py:17
  12.6 4.0 %broadcast_in_dim.106 = bf16[16,320,512]{2,1,0:T(8,128)(2,1)} broadcast(bf16[320,512]{1,0:T(8,128)(2,1)} %param.11), dimensions={1,2} | broadcast | bytes 5570560 | tf_op jit(solution)/shard_map/broadcast_in_dim | solution.py:135
  16.5 6.4 %all-to-all-start = ((bf16[16,320,512]{2,1,0:T(8,128)(2,1)}), bf16[16,320,512]{2,1,0:T(8,128)(2,1)}, u32[]{:S(2)}, u32[]{:S(2)}) async-start(bf16[16,320,512]{2,1,0:T(8,128)(2,1)} %broadcast_in_dim.106), calls=%async_computation | async-start | bytes 10485760 | tf_op jit(solution)/shard_map/all_to_all | solution.py:33
  34.7 2.0 collective-permute-start.2
  36.8 4.7 %collective-permute-start.3 = (f32[128,512]{0,1:T(8,128)}, f32[128,512]{0,1:T(8,128)}, u32[]{:S(2)}, u32[]{:S(2)}) collective-permute-start(f32[128,512]{0,1:T(8,128)} %get-tuple-element.27), channel_id=1, source_target_pairs={{0,1},{1,2},{2,3},{3,4},{4,5},{5,6},{6,7},{7,8},{8,9},{9,10},{10,1... | collective-permute-start | bytes 786440 | tf_op jit(solution)/shard_map/ppermute | solution.py:46
  42.3 44.1 %collective-permute-done.2 = f32[128,512]{0,1:T(8,128)} collective-permute-done((f32[128,512]{0,1:T(8,128)}, f32[128,512]{0,1:T(8,128)}, u32[]{:S(2)}, u32[]{:S(2)}) %collective-permute-start.2) | collective-permute-done | bytes 262176 | tf_op jit(solution)/shard_map/ppermute | solution.py:46
  86.3 6.6 %collective-permute-done.3 = f32[128,512]{0,1:T(8,128)} collective-permute-done((f32[128,512]{0,1:T(8,128)}, f32[128,512]{0,1:T(8,128)}, u32[]{:S(2)}, u32[]{:S(2)}) %collective-permute-start.3) | collective-permute-done | bytes 262176 | tf_op jit(solution)/shard_map/ppermute | solution.py:46
  94.0 8.2 %all-to-all-done = bf16[16,320,512]{2,1,0:T(8,128)(2,1)} async-done(((bf16[16,320,512]{2,1,0:T(8,128)(2,1)}), bf16[16,320,512]{2,1,0:T(8,128)(2,1)}, u32[]{:S(2)}, u32[]{:S(2)}) %all-to-all-start) | async-done | bytes 5242912 | tf_op jit(solution)/shard_map/all_to_all | solution.py:33
  102.2 4.0 %fusion.44 = bf16[128,512]{1,0:T(8,128)(2,1)} fusion(bf16[5120,512]{1,0:T(8,128)(2,1)} %bitcast.32, bf16[1,128,5120]{2,1,0:T(8,128)(2,1)S(1)} %copy-done), kind=kOutput, calls=%fused_computation.65 | convolution fusion | flops 671154176 | bytes 6684672 | tf_op jit(solution)/shard_map/dot_general | solution.py:167
  108.1 4.8 %collective-permute-start.4 = (bf16[128,512]{1,0:T(8,128)(2,1)}, bf16[128,512]{1,0:T(8,128)(2,1)}, u32[]{:S(2)}, u32[]{:S(2)}) collective-permute-start(bf16[128,512]{1,0:T(8,128)(2,1)} %fusion.44), channel_id=1, source_target_pairs={{0,1},{1,2},{2,3},{3,4},{4,5},{5,6},{6,7},{7,8},{8,9},{9,10},{10,1... | collective-permute-start | bytes 393224 | tf_op jit(solution)/shard_map/ppermute | solution.py:17
  113.4 2.0 pad_maximum_fusion
  115.4 8.9 %all-to-all-start.1 = ((bf16[16,128,832]{1,2,0:T(8,128)(2,1)}), bf16[16,128,832]{1,2,0:T(8,128)(2,1)S(1)}, u32[]{:S(2)}, u32[]{:S(2)}) async-start(bf16[16,128,832]{1,2,0:T(8,128)(2,1)} %pad_maximum_fusion), calls=%async_computation.1 | async-start | bytes 6815744 | tf_op jit(solution)/shard_map/all_to_all | solution.py:33
  124.3 5.4 %fusion.4 = bf16[1,128,5120]{2,1,0:T(8,128)(2,1)} fusion(bf16[128,512]{0,1:T(8,128)(2,1)S(1)} %fusion.54, bf16[5120,512]{1,0:T(8,128)(2,1)} %bitcast.32), kind=kOutput, calls=%fused_computation.5 | convolution fusion | flops 671744000 | bytes 6684672 | tf_op jit(solution)/shard_map/dot_general | solution.py:173
  133.4 2.4 %fusion.72 = (bf16[384,1,128]{2,1,0:T(2,128)(2,1)S(1)}, bf16[384,1,128]{2,1,0:T(2,128)(2,1)S(1)}, bf16[384,1,128]{2,1,0:T(2,128)(2,1)S(1)}, bf16[384,1,128]{2,1,0:T(2,128)(2,1)S(1)}) fusion(bf16[384,4,128]{2,1,0:T(4,128)(2,1)} %reshape.143), kind=kLoop, calls=%fused_computation.136 | loop fusion | bytes 786432 | tf_op jit(solution)/shard_map/slice | solution.py:99
  144.0 2.2 %fusion.43 = bf16[128,1,5,128]{0,3,2,1:T(8,128)(2,1)} fusion(f32[5,128,384]{1,2,0:T(8,128)S(1)} %get-tuple-element.47, f32[5,128]{1,0:T(8,128)S(1)} %get-tuple-element.46, bf16[384,4,128]{0,2,1:T(8,128)(2,1)} %bitcast.312, f32[5,128,384]{1,2,0:T(8,128)S(1)} %copy-done.23, f32[5,128]{1,0:T(8,128)S(1)} %get-tuple-element.38), kind=kOutput, calls=%fused_computation.64 | convolution fusion | flops 378388480 | bytes 2233344 | tf_op jit(solution)/shard_map/gqk,kd->qgd/dot_general | solution.py:109
  146.2 28.3 %all-to-all-done.1 = bf16[16,128,832]{1,2,0:T(8,128)(2,1)S(1)} async-done(((bf16[16,128,832]{1,2,0:T(8,128)(2,1)}), bf16[16,128,832]{1,2,0:T(8,128)(2,1)S(1)}, u32[]{:S(2)}, u32[]{:S(2)}) %all-to-all-start.1) | async-done | bytes 3407904 | tf_op jit(solution)/shard_map/all_to_all | solution.py:33
  174.7 2.2 fusion.28
  176.9 12.3 %all-to-all-start.2 = ((f32[16,320,32]{1,2,0:T(8,128)}), f32[16,320,32]{1,2,0:T(8,128)S(1)}, u32[]{:S(2)}, u32[]{:S(2)}) async-start(f32[16,320,32]{1,2,0:T(8,128)} %fusion.28), calls=%async_computation.2 | async-start | bytes 1572864 | tf_op jit(solution)/shard_map/all_to_all | solution.py:33
  190.3 2.0 collective-permute-start.6
  192.3 4.9 %collective-permute-start.7 = (f32[128,512]{0,1:T(8,128)S(1)}, f32[128,512]{0,1:T(8,128)S(1)}, u32[]{:S(2)}, u32[]{:S(2)}) collective-permute-start(f32[128,512]{0,1:T(8,128)S(1)} %get-tuple-element.25), channel_id=1, source_target_pairs={{0,1},{1,2},{2,3},{3,4},{4,5},{5,6},{6,7},{7,8},{8,9},{9,10},{10,1... | collective-permute-start | bytes 786440 | tf_op jit(solution)/shard_map/ppermute | solution.py:46
  197.2 2.2 %fusion.41 = bf16[128,1,5,128]{0,3,2,1:T(8,128)(2,1)S(1)} fusion(f32[5,128,384]{1,2,0:T(8,128)} %copy-done.26, f32[5,128]{1,0:T(8,128)S(1)} %get-tuple-element.42, bf16[384,4,128]{0,2,1:T(8,128)(2,1)} %bitcast.313, f32[5,128,384]{1,2,0:T(8,128)} %copy-done.18, f32[5,128]{1,0:T(8,128)S(1)} %get-tuple-element.34), kind=kOutput, calls=%fused_computation.62 | convolution fusion | flops 378388480 | bytes 2233344 | tf_op jit(solution)/shard_map/gqk,kd->qgd/dot_general | solution.py:109
  202.0 13.1 %collective-permute-done.6 = f32[128,512]{0,1:T(8,128)S(1)} collective-permute-done((f32[128,512]{0,1:T(8,128)S(1)}, f32[128,512]{0,1:T(8,128)S(1)}, u32[]{:S(2)}, u32[]{:S(2)}) %collective-permute-start.6) | collective-permute-done | bytes 262176 | tf_op jit(solution)/shard_map/ppermute | solution.py:46
  (108 shorter events, 36.3 us)
Async XLA Ops:
  1.7 8.1 %collective-permute-start.1 = (bf16[128,512]{0,1:T(8,128)(2,1)S(1)}, bf16[128,512]{0,1:T(8,128)(2,1)S(1)}, u32[]{:S(2)}, u32[]{:S(2)}) collective-permute-start(bf16[128,512]{0,1:T(8,128)(2,1)S(1)} %bitcast.305), channel_id=1, source_target_pairs={{1,0},{2,1},{3,2},{4,3},{5,4},{6,5},{7,6},{8,7},{9,8},{10,9},{11,1... | collective-permute-start | bytes 393224 | tf_op jit(solution)/shard_map/ppermute | solution.py:19
  4.1 8.4 %collective-permute-start = (bf16[128,512]{0,1:T(8,128)(2,1)S(1)}, bf16[128,512]{0,1:T(8,128)(2,1)S(1)}, u32[]{:S(2)}, u32[]{:S(2)}) collective-permute-start(bf16[128,512]{0,1:T(8,128)(2,1)S(1)} %bitcast.306), channel_id=1, source_target_pairs={{0,1},{1,2},{2,3},{3,4},{4,5},{5,6},{6,7},{7,8},{8,9},{9,10},{10,1... | collective-permute-start | bytes 393224 | tf_op jit(solution)/shard_map/ppermute | solution.py:17
  12.6 18.1 %copy-start.7 = (bf16[384,512]{0,1:T(8,128)(2,1)}, bf16[384,512]{0,1:T(8,128)(2,1)S(1)}, u32[]{:S(2)}) copy-start(bf16[384,512]{0,1:T(8,128)(2,1)S(1)} %pad_maximum_fusion.4) | copy-start | bytes 1179652
  16.5 6.4 %copy-start.1 = (bf16[1,128,2560]{2,1,0:T(8,128)(2,1)S(1)}, bf16[1,128,2560]{2,1,0:T(8,128)(2,1)}, u32[]{:S(2)}) copy-start(bf16[1,128,2560]{2,1,0:T(8,128)(2,1)} %param.8) | copy-start | bytes 1966084
  16.5 6.8 %copy-start.2 = (bf16[1,128,2560]{2,1,0:T(8,128)(2,1)S(1)}, bf16[1,128,2560]{2,1,0:T(8,128)(2,1)}, u32[]{:S(2)}) copy-start(bf16[1,128,2560]{2,1,0:T(8,128)(2,1)} %param.10) | copy-start | bytes 1966084
  16.5 7.1 %copy-start.13 = (s32[1,2048]{1,0:T(1,128)S(1)}, s32[1,2048]{1,0:T(1,128)}, u32[]{:S(2)}) copy-start(s32[1,2048]{1,0:T(1,128)} %param.12) | copy-start | bytes 24580
  16.5 7.3 %copy-start.14 = (s32[1,32]{1,0:T(1,128)S(1)}, s32[1,32]{1,0:T(1,128)}, u32[]{:S(2)}) copy-start(s32[1,32]{1,0:T(1,128)} %param.13) | copy-start | bytes 388
  16.5 85.7 %all-to-all-start = ((bf16[16,320,512]{2,1,0:T(8,128)(2,1)}), bf16[16,320,512]{2,1,0:T(8,128)(2,1)}, u32[]{:S(2)}, u32[]{:S(2)}) async-start(bf16[16,320,512]{2,1,0:T(8,128)(2,1)} %broadcast_in_dim.106), calls=%async_computation | async-start | bytes 10485760 | tf_op jit(solution)/shard_map/all_to_all | solution.py:33
  23.3 7.4 %copy-start.3 = (bf16[1,128,2560]{1,2,0:T(8,128)(2,1)}, bf16[1,128,2560]{1,2,0:T(8,128)(2,1)S(1)}, u32[]{:S(2)}) copy-start(bf16[1,128,2560]{1,2,0:T(8,128)(2,1)S(1)} %copy.89) | copy-start | bytes 1966084
  23.6 8.5 %copy-start.5 = (bf16[1,128,2560]{1,2,0:T(8,128)(2,1)}, bf16[1,128,2560]{1,2,0:T(8,128)(2,1)S(1)}, u32[]{:S(2)}) copy-start(bf16[1,128,2560]{1,2,0:T(8,128)(2,1)S(1)} %copy.91) | copy-start | bytes 1966084
  32.2 9.3 %copy-start = (bf16[1,128,5120]{2,1,0:T(8,128)(2,1)S(1)}, bf16[1,128,5120]{2,1,0:T(8,128)(2,1)}, u32[]{:S(2)}) copy-start(bf16[1,128,5120]{2,1,0:T(8,128)(2,1)} %param.7) | copy-start | bytes 3932164
  34.7 51.6 %collective-permute-start.2 = (f32[128,512]{0,1:T(8,128)}, f32[128,512]{0,1:T(8,128)}, u32[]{:S(2)}, u32[]{:S(2)}) collective-permute-start(f32[128,512]{0,1:T(8,128)} %get-tuple-element.26), channel_id=1, source_target_pairs={{1,0},{2,1},{3,2},{4,3},{5,4},{6,5},{7,6},{8,7},{9,8},{10,9},{11,1... | collective-permute-start | bytes 786440 | tf_op jit(solution)/shard_map/ppermute | solution.py:46
  36.8 56.1 %collective-permute-start.3 = (f32[128,512]{0,1:T(8,128)}, f32[128,512]{0,1:T(8,128)}, u32[]{:S(2)}, u32[]{:S(2)}) collective-permute-start(f32[128,512]{0,1:T(8,128)} %get-tuple-element.27), channel_id=1, source_target_pairs={{0,1},{1,2},{2,3},{3,4},{4,5},{5,6},{6,7},{7,8},{8,9},{9,10},{10,1... | collective-permute-start | bytes 786440 | tf_op jit(solution)/shard_map/ppermute | solution.py:46
  106.2 23.5 %collective-permute-start.5 = (bf16[128,512]{1,0:T(8,128)(2,1)}, bf16[128,512]{1,0:T(8,128)(2,1)}, u32[]{:S(2)}, u32[]{:S(2)}) collective-permute-start(bf16[128,512]{1,0:T(8,128)(2,1)} %fusion.44), channel_id=1, source_target_pairs={{1,0},{2,1},{3,2},{4,3},{5,4},{6,5},{7,6},{8,7},{9,8},{10,9},{11,1... | collective-permute-start | bytes 393224 | tf_op jit(solution)/shard_map/ppermute | solution.py:19
  108.1 21.5 %collective-permute-start.4 = (bf16[128,512]{1,0:T(8,128)(2,1)}, bf16[128,512]{1,0:T(8,128)(2,1)}, u32[]{:S(2)}, u32[]{:S(2)}) collective-permute-start(bf16[128,512]{1,0:T(8,128)(2,1)} %fusion.44), channel_id=1, source_target_pairs={{0,1},{1,2},{2,3},{3,4},{4,5},{5,6},{6,7},{7,8},{8,9},{9,10},{10,1... | collective-permute-start | bytes 393224 | tf_op jit(solution)/shard_map/ppermute | solution.py:17
  115.4 59.2 %all-to-all-start.1 = ((bf16[16,128,832]{1,2,0:T(8,128)(2,1)}), bf16[16,128,832]{1,2,0:T(8,128)(2,1)S(1)}, u32[]{:S(2)}, u32[]{:S(2)}) async-start(bf16[16,128,832]{1,2,0:T(8,128)(2,1)} %pad_maximum_fusion), calls=%async_computation.1 | async-start | bytes 6815744 | tf_op jit(solution)/shard_map/all_to_all | solution.py:33
  176.9 22.6 %copy-start.8 = (bf16[384,512]{0,1:T(8,128)(2,1)S(1)}, bf16[384,512]{0,1:T(8,128)(2,1)}, u32[]{:S(2)}) copy-start(bf16[384,512]{0,1:T(8,128)(2,1)} %copy-done.7) | copy-start | bytes 1179652
  176.9 22.6 %copy-start.21 = (f32[5,128,384]{1,2,0:T(8,128)S(1)}, f32[5,128,384]{1,2,0:T(8,128)}, u32[]{:S(2)}) copy-start(f32[5,128,384]{1,2,0:T(8,128)} %get-tuple-element.33) | copy-start | bytes 2949124
  176.9 40.1 %all-to-all-start.2 = ((f32[16,320,32]{1,2,0:T(8,128)}), f32[16,320,32]{1,2,0:T(8,128)S(1)}, u32[]{:S(2)}, u32[]{:S(2)}) async-start(f32[16,320,32]{1,2,0:T(8,128)} %fusion.28), calls=%async_computation.2 | async-start | bytes 1572864 | tf_op jit(solution)/shard_map/all_to_all | solution.py:33
  189.1 10.3 %copy-start.28 = (f32[5,128,384]{1,2,0:T(8,128)S(1)}, f32[5,128,384]{1,2,0:T(8,128)}, u32[]{:S(2)}) copy-start(f32[5,128,384]{1,2,0:T(8,128)} %copy-done.27) | copy-start | bytes 2949124
  190.3 24.9 %collective-permute-start.6 = (f32[128,512]{0,1:T(8,128)S(1)}, f32[128,512]{0,1:T(8,128)S(1)}, u32[]{:S(2)}, u32[]{:S(2)}) collective-permute-start(f32[128,512]{0,1:T(8,128)S(1)} %get-tuple-element.24), channel_id=1, source_target_pairs={{1,0},{2,1},{3,2},{4,3},{5,4},{6,5},{7,6},{8,7},{9,8},{10,9},{11,1... | collective-permute-start | bytes 786440 | tf_op jit(solution)/shard_map/ppermute | solution.py:46
  192.3 7.8 %copy-start.17 = (f32[5,128,384]{1,2,0:T(8,128)S(1)}, f32[5,128,384]{1,2,0:T(8,128)}, u32[]{:S(2)}) copy-start(f32[5,128,384]{1,2,0:T(8,128)} %copy-done.15) | copy-start | bytes 2949124
  192.3 7.8 %copy-start.25 = (f32[5,128,384]{1,2,0:T(8,128)S(1)}, f32[5,128,384]{1,2,0:T(8,128)}, u32[]{:S(2)}) copy-start(f32[5,128,384]{1,2,0:T(8,128)} %copy-done.24) | copy-start | bytes 2949124
  192.3 22.8 %collective-permute-start.7 = (f32[128,512]{0,1:T(8,128)S(1)}, f32[128,512]{0,1:T(8,128)S(1)}, u32[]{:S(2)}, u32[]{:S(2)}) collective-permute-start(f32[128,512]{0,1:T(8,128)S(1)} %get-tuple-element.25), channel_id=1, source_target_pairs={{0,1},{1,2},{2,3},{3,4},{4,5},{5,6},{6,7},{7,8},{8,9},{9,10},{10,1... | collective-permute-start | bytes 786440 | tf_op jit(solution)/shard_map/ppermute | solution.py:46
  (16 other events, 34.3 us)

commit v6 on v5

--- a/solution.py
+++ b/solution.py
@@ -27,6 +27,43 @@
     count = lax.axis_size(axis)
     copies = jnp.broadcast_to(array[None], (count,) + array.shape)
     return lax.all_to_all(copies, axis, 0, 0, tiled=True)
+
+
+def spread_weight(weight, ready):
+    dp_count = lax.axis_size("dp")
+    seq_count = lax.axis_size("seq")
+    half = dp_count // 2
+    cores = 2
+    y_count = half // cores
+    rows, width = weight.shape
+    partner_pairs = [
+        (d * seq_count + s, (d ^ half) * seq_count + (s ^ 1))
+        for d in range(dp_count)
+        for s in range(seq_count)
+    ]
+    held = jnp.stack([weight, lax.ppermute(weight, ("dp", "seq"), partner_pairs)])
+    ring = [held]
+    for shift in range(1, y_count):
+        pairs = []
+        for d in range(dp_count):
+            upper, y_here, core = d // half, (d // cores) % y_count, d % cores
+            pairs.append((d, upper * half + ((y_here + shift) % y_count) * cores + core))
+        ring.append(lax.ppermute(held, "dp", pairs))
+    mine, ready = lax.optimization_barrier((jnp.stack(ring), ready))
+    sibling = lax.ppermute(mine, "dp", [(d, d ^ 1) for d in range(dp_count)])
+    stacked = jnp.stack([mine, sibling]).reshape(dp_count, rows, width)
+    me = lax.axis_index("dp")
+    upper, y_here, core = me // half, (me // cores) % y_count, me % cores
+    core_of = jnp.arange(2)[:, None, None]
+    shift_of = jnp.arange(y_count)[None, :, None]
+    upper_of = jnp.arange(2)[None, None, :]
+    owner = (
+        ((upper + upper_of) % 2) * half
+        + ((y_here - shift_of) % y_count) * cores
+        + (core + core_of) % 2
+    )
+    order = jnp.argsort(owner.reshape(-1))
+    return jnp.take(stacked, order, axis=0).reshape(-1, width), ready
 
 
 def gathered_copies(copies, axis):
@@ -132,9 +169,7 @@
     model_width = layer_rows.shape[1]
     weight_rows, kv_width = value_weight.shape
     key_block = with_halo(key_states[0], (("seq", 0),), tok_count)
-    weight_copies = jnp.broadcast_to(value_weight[None], (dp_count, weight_rows, kv_width))
-    key_block, weight_copies = lax.optimization_barrier((key_block, weight_copies))
-    weight_full = gathered_copies(weight_copies, "dp").reshape(-1, kv_width)
+    weight_full, key_block = spread_weight(value_weight, key_block)
     input_pieces = layer_rows.reshape(tok_count, dp_count, model_width // dp_count).transpose(1, 0, 2)
     seg_row = segment_ids[0]
     fill_ids = jnp.full((tok_count,), -1, jnp.int32)
@@ -151,8 +186,8 @@
         (pos_key[None, :] <= pos_query[:, None]) | (pos_key[None, :] < split_query[:, None])
     )
     attentions, value_part = attend_first(query_states[0], key_block, out_grad[0], visible)
+    value_part, weight_full = lax.optimization_barrier((value_part, weight_full))
     value_grad = rim_sum(value_part, tok_count).astype(jnp.bfloat16)
-    value_grad, weight_full = lax.optimization_barrier((value_grad, weight_full))
     grad_copies = jnp.broadcast_to(value_grad[None], (dp_count,) + value_grad.shape)
     arrived = gathered_copies(jnp.concatenate([grad_copies, input_pieces], axis=2), "dp")
     seq_count = lax.axis_size("seq")

time: 219 us -> 217 us (level)
  waiting for transfers between devices: 104 us -> 77.3 us
  other arithmetic: 8.1 us -> 26 us
  matrix products: 30.6 us -> 40.3 us
  starting transfers between devices: 54.6 us -> 49.1 us
    ppermute x4, waiting for transfers between devices: 63.8 us -> 12.4 us  [passed_along(): return lax.ppermute(array, axis, pairs)]
    ppermute x0 -> x5, waiting for transfers between devices: none -> 26.2 us  [the longest x3 19.7 us: spread_weight(): ring.append(lax.ppermute(held, 'dp', pairs))]
    all_to_all x3 -> x2, starting transfers between devices: 27.6 us -> 17.5 us  [gathered_copies(): return lax.all_to_all(copies, axis, 0, 0, tiled=True)]
    another operation x0 -> x3, other arithmetic: none -> 8.22 us  [the longest x1 4.52 us: spread_weight(): stacked = jnp.stack([mine, sibling]).reshape(dp_count, rows, width)]
    sub x4, matrix products: 3.13 us -> 9.61 us  [attend_first(): weights = jnp.where(visible[None], jnp.exp(masked - highest), 0.0)]
    dot_general x4, matrix products: 3 us -> 8.87 us  [attend_second(): jnp.einsum('gqk,qgd->kd', score_grad, query_wide, precision=high)]
    gather x0 -> x1, local copies, waits for them, and re-layouts: none -> 5.85 us  [spread_weight(): return (jnp.take(stacked, order, axis=0).reshape(-1, width), ready)]
    select_n x0 -> x3, other arithmetic: none -> 5.35 us  [the longest x2 5.34 us: spread_weight(): return (jnp.take(stacked, order, axis=0).reshape(-1, width), ready)]
  transfers between devices with their start and end apart: 11 -> 15, of which waited for: 7 -> 8; matrix products, arithmetic and copies ran while one was open for 19% -> 28% of each run, Pallas kernels for 0% -> 0%
where the time goes in v6:
time: 217 us; the launch traced here: 214 us
  waiting for transfers between devices  77.3 us (36%)
  starting transfers between devices  49.1 us (23%)
  matrix products  40.3 us (19%)
  other arithmetic  26 us (12%)
  local copies, waits for them, and re-layouts  20.6 us (9%)
    all_to_all x2, waiting for transfers between devices, gathered_copies(): return lax.all_to_all(copies, axis, 0, 0, tiled=True)  32 us
    ppermute x3, waiting for transfers between devices, spread_weight(): ring.append(lax.ppermute(held, 'dp', pairs))  19.7 us
    all_to_all x2, starting transfers between devices, gathered_copies(): return lax.all_to_all(copies, axis, 0, 0, tiled=True)  17.5 us
    ppermute x4, starting transfers between devices, passed_along(): return lax.ppermute(array, axis, pairs)  12.9 us
    ppermute x4, waiting for transfers between devices, passed_along(): return lax.ppermute(array, axis, pairs)  12.4 us
    unnamed x84, local copies, waits for them, and re-layouts  9.77 us
    sub x4, matrix products, attend_first(): weights = jnp.where(visible[None], jnp.exp(masked - highest), 0.0)  9.61 us
    ppermute x2, starting transfers between devices, with_halo(): lax.ppermute(tail, axis, [(i, (i + 1) % count) for i in range(ends)])  9.12 us
  transfers between devices with their start and end apart: 15, of which 8 were waited for; matrix products, arithmetic and copies ran while one was open for 28% of the time, Pallas kernels for 0%

profile of v6, /device:TPU:26, one launch (start us, length us, event | category | flops | bytes accessed | tf_op | source)
XLA Modules:
  0.0 214.4 jit_solution(1303231373436031490)
XLA Ops:
  1.7 2.4 %collective-permute-start.5 = (bf16[128,512]{0,1:T(8,128)(2,1)S(1)}, bf16[128,512]{0,1:T(8,128)(2,1)S(1)}, u32[]{:S(2)}, u32[]{:S(2)}) collective-permute-start(bf16[128,512]{0,1:T(8,128)(2,1)S(1)} %bitcast.321), channel_id=1, source_target_pairs={{1,0},{2,1},{3,2},{4,3},{5,4},{6,5},{7,6},{8,7},{9,8},{10,9},{11,1... | collective-permute-start | bytes 393224 | tf_op jit(solution)/shard_map/ppermute | solution.py:19
  4.2 4.3 %collective-permute-start.4 = (bf16[128,512]{0,1:T(8,128)(2,1)S(1)}, bf16[128,512]{0,1:T(8,128)(2,1)}, u32[]{:S(2)}, u32[]{:S(2)}) collective-permute-start(bf16[128,512]{0,1:T(8,128)(2,1)S(1)} %bitcast.322), channel_id=1, source_target_pairs={{0,1},{1,2},{2,3},{3,4},{4,5},{5,6},{6,7},{7,8},{8,9},{9,10},{10,1... | collective-permute-start | bytes 393224 | tf_op jit(solution)/shard_map/ppermute | solution.py:17
  11.2 6.4 %collective-permute-done = bf16[320,512]{1,0:T(8,128)(2,1)S(1)} collective-permute-done((bf16[320,512]{1,0:T(8,128)(2,1)}, bf16[320,512]{1,0:T(8,128)(2,1)S(1)}, u32[]{:S(2)}, u32[]{:S(2)}) %collective-permute-start) | collective-permute-done | bytes 327712 | tf_op jit(solution)/shard_map/ppermute | solution.py:44
  30.9 19.1 %collective-permute-done.3 = bf16[2,320,512]{2,1,0:T(8,128)(2,1)S(1)} collective-permute-done((bf16[2,320,512]{2,1,0:T(8,128)(2,1)}, bf16[2,320,512]{2,1,0:T(8,128)(2,1)S(1)}, u32[]{:S(2)}, u32[]{:S(2)}) %collective-permute-start.3) | collective-permute-done | bytes 655392 | tf_op jit(solution)/shard_map/ppermute | solution.py:51
  55.1 2.4 %fusion.77 = (f32[5,128]{1,0:T(8,128)S(1)}, f32[5,128,384]{1,2,0:T(8,128)}) fusion(pred[128,384]{0,1:T(8,128)(4,1)S(1)} %or_and_fusion, bf16[128,4,5,128]{0,3,2,1:T(8,128)(2,1)} %bitcast.305, bf16[384,4,128]{0,2,1:T(8,128)(2,1)} %bitcast.324), kind=kOutput, calls=%fused_computation.160 | convolution fusion | flops 64143744 | bytes 1346048 | tf_op jit(solution)/shard_map/sub | solution.py:112
  59.7 2.4 %fusion.78 = (f32[5,128]{1,0:T(8,128)S(1)}, f32[5,128,384]{1,2,0:T(8,128)}) fusion(pred[128,384]{0,1:T(8,128)(4,1)S(1)} %or_and_fusion, bf16[128,4,5,128]{0,3,2,1:T(8,128)(2,1)S(1)} %bitcast.308, bf16[384,4,128]{0,2,1:T(8,128)(2,1)} %bitcast.325), kind=kOutput, calls=%fused_computation.161 | convolution fusion | flops 64143744 | bytes 1346048 | tf_op jit(solution)/shard_map/sub | solution.py:112
  64.3 2.4 %fusion.79 = (f32[5,128]{1,0:T(8,128)S(1)}, f32[5,128,384]{1,2,0:T(8,128)}) fusion(pred[128,384]{0,1:T(8,128)(4,1)S(1)} %or_and_fusion, bf16[128,4,5,128]{0,3,2,1:T(8,128)(2,1)S(1)} %bitcast.309, bf16[384,4,128]{0,2,1:T(8,128)(2,1)} %bitcast.326), kind=kOutput, calls=%fused_computation.162 | convolution fusion | flops 64143744 | bytes 1346048 | tf_op jit(solution)/shard_map/sub | solution.py:112
  73.0 4.5 %pad_maximum_fusion = bf16[2,4,2,320,512]{4,3,2,1,0:T(8,128)(2,1)} fusion(bf16[1,4,2,320,512]{4,3,2,1,0:T(8,128)(2,1)} %bitcast.39, bf16[1,4,2,320,512]{4,3,2,1,0:T(8,128)(2,1)S(1)} %bitcast.298), kind=kLoop, calls=%fused_computation.7 | loop fusion | flops 2621440 | bytes 10485760 | tf_op jit(solution)/shard_map/stack | solution.py:54
  77.5 5.8 %gather_fusion = bf16[16,320,512]{2,1,0:T(8,128)(2,1)} fusion(bf16[16,320,512]{2,1,0:T(8,128)(2,1)} %bitcast.297, s32[1024]{0:T(1024)} %pad_clamp_fusion), kind=kCustom, calls=%fused_computation | custom fusion | bytes 10485824 | tf_op jit(solution)/shard_map/jit(_take)/gather | solution.py:66
  83.4 4.8 %bitcast_select_fusion = bf16[5120,512]{1,0:T(8,128)(2,1)S(1)} fusion(bf16[16,320,512]{2,1,0:T(8,128)(2,1)} %gather_fusion, pred[5120]{0:T(1024)(128)(4,1)S(1)} %broadcast_in_dim.127), kind=kLoop, calls=%fused_computation.8 | loop fusion | flops 2621440 | bytes 10490880 | tf_op jit(solution)/shard_map/jit(_take)/select_n | solution.py:66
  89.1 5.1 %collective-permute-start.12 = (f32[128,512]{0,1:T(8,128)}, f32[128,512]{0,1:T(8,128)}, u32[]{:S(2)}, u32[]{:S(2)}) collective-permute-start(f32[128,512]{0,1:T(8,128)} %get-tuple-element.27), channel_id=1, source_target_pairs={{0,1},{1,2},{2,3},{3,4},{4,5},{5,6},{6,7},{7,8},{8,9},{9,10},{10,1... | collective-permute-start | bytes 786440 | tf_op jit(solution)/shard_map/ppermute | solution.py:83
  98.9 4.8 %collective-permute-start.7 = (bf16[128,512]{1,0:T(8,128)(2,1)S(1)}, bf16[128,512]{1,0:T(8,128)(2,1)}, u32[]{:S(2)}, u32[]{:S(2)}) collective-permute-start(bf16[128,512]{1,0:T(8,128)(2,1)S(1)} %fusion.44), channel_id=1, source_target_pairs={{0,1},{1,2},{2,3},{3,4},{4,5},{5,6},{6,7},{7,8},{8,9},{9,10},{10,1... | collective-permute-start | bytes 393224 | tf_op jit(solution)/shard_map/ppermute | solution.py:17
  104.5 4.0 %collective-permute-done.8 = bf16[128,512]{1,0:T(8,128)(2,1)} collective-permute-done((bf16[128,512]{1,0:T(8,128)(2,1)S(1)}, bf16[128,512]{1,0:T(8,128)(2,1)}, u32[]{:S(2)}, u32[]{:S(2)}) %collective-permute-start.8) | collective-permute-done | bytes 131104 | tf_op jit(solution)/shard_map/ppermute | solution.py:19
  108.6 2.7 %collective-permute-done.7 = bf16[128,512]{1,0:T(8,128)(2,1)} collective-permute-done((bf16[128,512]{1,0:T(8,128)(2,1)S(1)}, bf16[128,512]{1,0:T(8,128)(2,1)}, u32[]{:S(2)}, u32[]{:S(2)}) %collective-permute-start.7) | collective-permute-done | bytes 131104 | tf_op jit(solution)/shard_map/ppermute | solution.py:17
  116.6 7.2 %all-to-all-start = ((bf16[16,128,832]{1,2,0:T(8,128)(2,1)}), bf16[16,128,832]{1,2,0:T(8,128)(2,1)S(1)}, u32[]{:S(2)}, u32[]{:S(2)}) async-start(bf16[16,128,832]{1,2,0:T(8,128)(2,1)} %pad_maximum_fusion.1), calls=%async_computation | async-start | bytes 6815744 | tf_op jit(solution)/shard_map/all_to_all | solution.py:70
  123.8 2.4 %fusion.76 = (bf16[384,1,128]{2,1,0:T(2,128)(2,1)S(1)}, bf16[384,1,128]{2,1,0:T(2,128)(2,1)S(1)}, bf16[384,1,128]{2,1,0:T(2,128)(2,1)S(1)}, bf16[384,1,128]{2,1,0:T(2,128)(2,1)S(1)}) fusion(bf16[384,4,128]{2,1,0:T(4,128)(2,1)} %reshape.256), kind=kLoop, calls=%fused_computation.159 | loop fusion | bytes 786432 | tf_op jit(solution)/shard_map/slice | solution.py:136
  135.6 3.1 %fusion.36 = f32[384,128]{0,1:T(8,128)} fusion(f32[5,128,384]{1,2,0:T(8,128)} %copy-done.24, f32[5,128]{1,0:T(8,128)} %copy-done.35, bf16[128,4,5,128]{0,3,2,1:T(8,128)(2,1)} %bitcast.306, f32[5,128,384]{1,2,0:T(8,128)} %get-tuple-element.37, f32[5,128]{1,0:T(8,128)S(1)} %get-tuple-element.36), kind=kOutput, calls=%fused_computation.58 | convolution fusion | flops 378273792 | bytes 2333184 | tf_op jit(solution)/shard_map/gqk,qgd->kd/dot_general | solution.py:149
  142.3 32.0 %all-to-all-done = bf16[16,128,832]{1,2,0:T(8,128)(2,1)S(1)} async-done(((bf16[16,128,832]{1,2,0:T(8,128)(2,1)}), bf16[16,128,832]{1,2,0:T(8,128)(2,1)S(1)}, u32[]{:S(2)}, u32[]{:S(2)}) %all-to-all-start) | async-done | bytes 3407904 | tf_op jit(solution)/shard_map/all_to_all | solution.py:70
  176.6 10.3 %all-to-all-start.1 = ((f32[16,320,32]{1,2,0:T(8,128)}), f32[16,320,32]{1,2,0:T(8,128)S(1)}, u32[]{:S(2)}, u32[]{:S(2)}) async-start(f32[16,320,32]{1,2,0:T(8,128)} %fusion.28), calls=%async_computation.1 | async-start | bytes 1572864 | tf_op jit(solution)/shard_map/all_to_all | solution.py:70
  189.3 3.4 %collective-permute-start.10 = (f32[128,512]{0,1:T(8,128)S(1)}, f32[128,512]{0,1:T(8,128)S(1)}, u32[]{:S(2)}, u32[]{:S(2)}) collective-permute-start(f32[128,512]{0,1:T(8,128)S(1)} %get-tuple-element.29), channel_id=1, source_target_pairs={{0,1},{1,2},{2,3},{3,4},{4,5},{5,6},{6,7},{7,8},{8,9},{9,10},{10,1... | collective-permute-start | bytes 786440 | tf_op jit(solution)/shard_map/ppermute | solution.py:83
  192.7 2.5 %collective-permute-start.9 = (f32[128,512]{0,1:T(8,128)S(1)}, f32[128,512]{0,1:T(8,128)S(1)}, u32[]{:S(2)}, u32[]{:S(2)}) collective-permute-start(f32[128,512]{0,1:T(8,128)S(1)} %get-tuple-element.28), channel_id=1, source_target_pairs={{1,0},{2,1},{3,2},{4,3},{5,4},{6,5},{7,6},{8,7},{9,8},{10,9},{11,1... | collective-permute-start | bytes 786440 | tf_op jit(solution)/shard_map/ppermute | solution.py:83
  195.2 5.4 %fusion.4 = bf16[1,128,5120]{2,1,0:T(8,128)(2,1)} fusion(bf16[128,512]{0,1:T(8,128)(2,1)S(1)} %add_convert_fusion, bf16[5120,512]{1,0:T(8,128)(2,1)} %copy-done), kind=kOutput, calls=%fused_computation.6 | convolution fusion | flops 671744000 | bytes 6684672 | tf_op jit(solution)/shard_map/dot_general | solution.py:208
  200.5 9.8 %collective-permute-done.10 = f32[128,512]{0,1:T(8,128)S(1)} collective-permute-done((f32[128,512]{0,1:T(8,128)S(1)}, f32[128,512]{0,1:T(8,128)S(1)}, u32[]{:S(2)}, u32[]{:S(2)}) %collective-permute-start.10) | collective-permute-done | bytes 262176 | tf_op jit(solution)/shard_map/ppermute | solution.py:83
  210.3 2.6 %collective-permute-done.9 = f32[128,512]{0,1:T(8,128)S(1)} collective-permute-done((f32[128,512]{0,1:T(8,128)S(1)}, f32[128,512]{0,1:T(8,128)S(1)}, u32[]{:S(2)}, u32[]{:S(2)}) %collective-permute-start.9) | collective-permute-done | bytes 262176 | tf_op jit(solution)/shard_map/ppermute | solution.py:83
  (153 shorter events, 63.3 us)
Async XLA Ops:
  0.6 26.1 %copy-start.5 = (bf16[1,128,2560]{2,1,0:T(8,128)(2,1)S(1)}, bf16[1,128,2560]{2,1,0:T(8,128)(2,1)}, u32[]{:S(2)}) copy-start(bf16[1,128,2560]{2,1,0:T(8,128)(2,1)} %param.10) | copy-start | bytes 1966084
  1.7 27.5 %collective-permute-start.5 = (bf16[128,512]{0,1:T(8,128)(2,1)S(1)}, bf16[128,512]{0,1:T(8,128)(2,1)S(1)}, u32[]{:S(2)}, u32[]{:S(2)}) collective-permute-start(bf16[128,512]{0,1:T(8,128)(2,1)S(1)} %bitcast.321), channel_id=1, source_target_pairs={{1,0},{2,1},{3,2},{4,3},{5,4},{6,5},{7,6},{8,7},{9,8},{10,9},{11,1... | collective-permute-start | bytes 393224 | tf_op jit(solution)/shard_map/ppermute | solution.py:19
  4.2 25.0 %collective-permute-start.4 = (bf16[128,512]{0,1:T(8,128)(2,1)S(1)}, bf16[128,512]{0,1:T(8,128)(2,1)}, u32[]{:S(2)}, u32[]{:S(2)}) collective-permute-start(bf16[128,512]{0,1:T(8,128)(2,1)S(1)} %bitcast.322), channel_id=1, source_target_pairs={{0,1},{1,2},{2,3},{3,4},{4,5},{5,6},{6,7},{7,8},{8,9},{9,10},{10,1... | collective-permute-start | bytes 393224 | tf_op jit(solution)/shard_map/ppermute | solution.py:17
  8.5 9.2 %collective-permute-start = (bf16[320,512]{1,0:T(8,128)(2,1)}, bf16[320,512]{1,0:T(8,128)(2,1)S(1)}, u32[]{:S(2)}, u32[]{:S(2)}) collective-permute-start(bf16[320,512]{1,0:T(8,128)(2,1)} %param.11), channel_id=1, source_target_pairs={{0,129},{1,128},{2,131},{3,130},{4,133},{5,132},{6,135},{7,134},{8... | collective-permute-start | bytes 983048 | tf_op jit(solution)/shard_map/ppermute | solution.py:44
  19.6 30.5 %collective-permute-start.3 = (bf16[2,320,512]{2,1,0:T(8,128)(2,1)}, bf16[2,320,512]{2,1,0:T(8,128)(2,1)S(1)}, u32[]{:S(2)}, u32[]{:S(2)}) collective-permute-start(bf16[2,320,512]{2,1,0:T(8,128)(2,1)} %get-tuple-element.31), channel_id=1, source_target_pairs={{0,96},{16,112},{32,0},{48,16},{64,32},{80,48},{96,64},{112,80},{1... | collective-permute-start | bytes 1966088 | tf_op jit(solution)/shard_map/ppermute | solution.py:51
  20.3 29.7 %collective-permute-start.2 = (bf16[2,320,512]{2,1,0:T(8,128)(2,1)}, bf16[2,320,512]{2,1,0:T(8,128)(2,1)S(1)}, u32[]{:S(2)}, u32[]{:S(2)}) collective-permute-start(bf16[2,320,512]{2,1,0:T(8,128)(2,1)} %get-tuple-element.31), channel_id=1, source_target_pairs={{0,64},{16,80},{32,96},{48,112},{64,0},{80,16},{96,32},{112,48},{1... | collective-permute-start | bytes 1966088 | tf_op jit(solution)/shard_map/ppermute | solution.py:51
  21.3 29.4 %collective-permute-start.1 = (bf16[2,320,512]{2,1,0:T(8,128)(2,1)}, bf16[2,320,512]{2,1,0:T(8,128)(2,1)S(1)}, u32[]{:S(2)}, u32[]{:S(2)}) collective-permute-start(bf16[2,320,512]{2,1,0:T(8,128)(2,1)} %get-tuple-element.31), channel_id=1, source_target_pairs={{0,32},{16,48},{32,64},{48,80},{64,96},{80,112},{96,0},{112,16},{1... | collective-permute-start | bytes 1966088 | tf_op jit(solution)/shard_map/ppermute | solution.py:51
  26.7 26.7 %copy-start.16 = (s32[1,2048]{1,0:T(1,128)S(1)}, s32[1,2048]{1,0:T(1,128)}, u32[]{:S(2)}) copy-start(s32[1,2048]{1,0:T(1,128)} %param.12) | copy-start | bytes 24580
  53.3 6.4 %copy-start.6 = (bf16[1,128,2560]{1,2,0:T(8,128)(2,1)S(1)}, bf16[1,128,2560]{1,2,0:T(8,128)(2,1)}, u32[]{:S(2)}) copy-start(bf16[1,128,2560]{1,2,0:T(8,128)(2,1)} %copy.89) | copy-start | bytes 1966084
  53.3 19.7 %collective-permute-start.6 = (bf16[4,2,320,512]{3,2,1,0:T(8,128)(2,1)S(1)}, bf16[4,2,320,512]{3,2,1,0:T(8,128)(2,1)}, u32[]{:S(2)}, u32[]{:S(2)}) collective-permute-start(bf16[4,2,320,512]{3,2,1,0:T(8,128)(2,1)S(1)} %pad_maximum_fusion.2), channel_id=1, source_target_pairs={{0,16},{16,0},{32,48},{48,32},{64,80},{80,64},{96,112},{112,96},{1... | collective-permute-start | bytes 7864328 | tf_op jit(solution)/shard_map/ppermute | solution.py:53
  83.4 12.7 %copy-start.1 = (bf16[1,128,5120]{2,1,0:T(8,128)(2,1)S(1)}, bf16[1,128,5120]{2,1,0:T(8,128)(2,1)}, u32[]{:S(2)}) copy-start(bf16[1,128,5120]{2,1,0:T(8,128)(2,1)} %param.7) | copy-start | bytes 3932164
  88.2 8.8 %copy-start = (bf16[5120,512]{1,0:T(8,128)(2,1)}, bf16[5120,512]{1,0:T(8,128)(2,1)S(1)}, u32[]{:S(2)}) copy-start(bf16[5120,512]{1,0:T(8,128)(2,1)S(1)} %bitcast_select_fusion) | copy-start | bytes 15728644
  89.1 24.1 %collective-permute-start.12 = (f32[128,512]{0,1:T(8,128)}, f32[128,512]{0,1:T(8,128)}, u32[]{:S(2)}, u32[]{:S(2)}) collective-permute-start(f32[128,512]{0,1:T(8,128)} %get-tuple-element.27), channel_id=1, source_target_pairs={{0,1},{1,2},{2,3},{3,4},{4,5},{5,6},{6,7},{7,8},{8,9},{9,10},{10,1... | collective-permute-start | bytes 786440 | tf_op jit(solution)/shard_map/ppermute | solution.py:83
  94.2 18.9 %collective-permute-start.11 = (f32[128,512]{0,1:T(8,128)}, f32[128,512]{0,1:T(8,128)}, u32[]{:S(2)}, u32[]{:S(2)}) collective-permute-start(f32[128,512]{0,1:T(8,128)} %get-tuple-element.26), channel_id=1, source_target_pairs={{1,0},{2,1},{3,2},{4,3},{5,4},{6,5},{7,6},{8,7},{9,8},{10,9},{11,1... | collective-permute-start | bytes 786440 | tf_op jit(solution)/shard_map/ppermute | solution.py:83
  97.0 11.6 %collective-permute-start.8 = (bf16[128,512]{1,0:T(8,128)(2,1)S(1)}, bf16[128,512]{1,0:T(8,128)(2,1)}, u32[]{:S(2)}, u32[]{:S(2)}) collective-permute-start(bf16[128,512]{1,0:T(8,128)(2,1)S(1)} %fusion.44), channel_id=1, source_target_pairs={{1,0},{2,1},{3,2},{4,3},{5,4},{6,5},{7,6},{8,7},{9,8},{10,9},{11,1... | collective-permute-start | bytes 393224 | tf_op jit(solution)/shard_map/ppermute | solution.py:19
  98.9 12.4 %collective-permute-start.7 = (bf16[128,512]{1,0:T(8,128)(2,1)S(1)}, bf16[128,512]{1,0:T(8,128)(2,1)}, u32[]{:S(2)}, u32[]{:S(2)}) collective-permute-start(bf16[128,512]{1,0:T(8,128)(2,1)S(1)} %fusion.44), channel_id=1, source_target_pairs={{0,1},{1,2},{2,3},{3,4},{4,5},{5,6},{6,7},{7,8},{8,9},{9,10},{10,1... | collective-permute-start | bytes 393224 | tf_op jit(solution)/shard_map/ppermute | solution.py:17
  116.6 57.6 %all-to-all-start = ((bf16[16,128,832]{1,2,0:T(8,128)(2,1)}), bf16[16,128,832]{1,2,0:T(8,128)(2,1)S(1)}, u32[]{:S(2)}, u32[]{:S(2)}) async-start(bf16[16,128,832]{1,2,0:T(8,128)(2,1)} %pad_maximum_fusion.1), calls=%async_computation | async-start | bytes 6815744 | tf_op jit(solution)/shard_map/all_to_all | solution.py:70
  174.4 12.5 %copy-start.34 = (f32[5,128]{1,0:T(8,128)S(1)}, f32[5,128]{1,0:T(8,128)}, u32[]{:S(2)}) copy-start(f32[5,128]{1,0:T(8,128)} %copy-done.33) | copy-start | bytes 7684
  176.6 12.6 %copy-start.10 = (f32[384,128]{0,1:T(8,128)S(1)}, f32[384,128]{0,1:T(8,128)}, u32[]{:S(2)}) copy-start(f32[384,128]{0,1:T(8,128)} %fusion.36) | copy-start | bytes 589828
  176.6 12.6 %copy-start.11 = (f32[384,128]{0,1:T(8,128)S(1)}, f32[384,128]{0,1:T(8,128)}, u32[]{:S(2)}) copy-start(f32[384,128]{0,1:T(8,128)} %fusion.37) | copy-start | bytes 589828
  176.6 12.6 %copy-start.12 = (f32[384,128]{0,1:T(8,128)S(1)}, f32[384,128]{0,1:T(8,128)}, u32[]{:S(2)}) copy-start(f32[384,128]{0,1:T(8,128)} %fusion.38) | copy-start | bytes 589828
  176.6 37.2 %all-to-all-start.1 = ((f32[16,320,32]{1,2,0:T(8,128)}), f32[16,320,32]{1,2,0:T(8,128)S(1)}, u32[]{:S(2)}, u32[]{:S(2)}) async-start(f32[16,320,32]{1,2,0:T(8,128)} %fusion.28), calls=%async_computation.1 | async-start | bytes 1572864 | tf_op jit(solution)/shard_map/all_to_all | solution.py:70
  189.3 21.0 %collective-permute-start.10 = (f32[128,512]{0,1:T(8,128)S(1)}, f32[128,512]{0,1:T(8,128)S(1)}, u32[]{:S(2)}, u32[]{:S(2)}) collective-permute-start(f32[128,512]{0,1:T(8,128)S(1)} %get-tuple-element.29), channel_id=1, source_target_pairs={{0,1},{1,2},{2,3},{3,4},{4,5},{5,6},{6,7},{7,8},{8,9},{9,10},{10,1... | collective-permute-start | bytes 786440 | tf_op jit(solution)/shard_map/ppermute | solution.py:83
  192.7 20.3 %collective-permute-start.9 = (f32[128,512]{0,1:T(8,128)S(1)}, f32[128,512]{0,1:T(8,128)S(1)}, u32[]{:S(2)}, u32[]{:S(2)}) collective-permute-start(f32[128,512]{0,1:T(8,128)S(1)} %get-tuple-element.28), channel_id=1, source_target_pairs={{1,0},{2,1},{3,2},{4,3},{5,4},{6,5},{7,6},{8,7},{9,8},{10,9},{11,1... | collective-permute-start | bytes 786440 | tf_op jit(solution)/shard_map/ppermute | solution.py:83
  (30 other events, 71.3 us)

commit v7 on v6

--- a/solution.py
+++ b/solution.py
@@ -62,8 +62,7 @@
         + ((y_here - shift_of) % y_count) * cores
         + (core + core_of) % 2
     )
-    order = jnp.argsort(owner.reshape(-1))
-    return jnp.take(stacked, order, axis=0).reshape(-1, width), ready
+    return stacked, owner.reshape(-1), ready
 
 
 def gathered_copies(copies, axis):
@@ -169,7 +168,7 @@
     model_width = layer_rows.shape[1]
     weight_rows, kv_width = value_weight.shape
     key_block = with_halo(key_states[0], (("seq", 0),), tok_count)
-    weight_full, key_block = spread_weight(value_weight, key_block)
+    weight_slots, slot_owner, key_block = spread_weight(value_weight, key_block)
     input_pieces = layer_rows.reshape(tok_count, dp_count, model_width // dp_count).transpose(1, 0, 2)
     seg_row = segment_ids[0]
     fill_ids = jnp.full((tok_count,), -1, jnp.int32)
@@ -186,8 +185,9 @@
         (pos_key[None, :] <= pos_query[:, None]) | (pos_key[None, :] < split_query[:, None])
     )
     attentions, value_part = attend_first(query_states[0], key_block, out_grad[0], visible)
-    value_part, weight_full = lax.optimization_barrier((value_part, weight_full))
     value_grad = rim_sum(value_part, tok_count).astype(jnp.bfloat16)
+    value_grad, weight_slots = lax.optimization_barrier((value_grad, weight_slots))
+    weight_full = weight_slots.reshape(-1, kv_width)
     grad_copies = jnp.broadcast_to(value_grad[None], (dp_count,) + value_grad.shape)
     arrived = gathered_copies(jnp.concatenate([grad_copies, input_pieces], axis=2), "dp")
     seq_count = lax.axis_size("seq")
@@ -199,22 +199,28 @@
     summed = jnp.sum(gathered_copies(own_pieces, "seq"), axis=0)
     devices_all = lax.axis_size("dp") * lax.axis_size("seq")
     weight_grad = summed / devices_all
-    value_rows = jnp.dot(layer_rows, weight_full, preferred_element_type=jnp.float32)
+    input_slots = jnp.take(
+        layer_rows.reshape(tok_count, dp_count, -1), slot_owner, axis=1, mode="clip"
+    ).reshape(tok_count, -1)
+    value_rows = jnp.dot(input_slots, weight_full, preferred_element_type=jnp.float32)
     value_block = with_halo(value_rows.astype(jnp.bfloat16), (("seq", 0),), tok_count)
     query_grad, key_part = attend_second(
         query_states[0], key_block, value_block, out_grad[0], attentions
     )
     key_grad = rim_sum(key_part, tok_count).astype(jnp.bfloat16)
-    input_grad = lax.dot_general(
+    grad_slots = lax.dot_general(
         value_grad,
         weight_full,
         (((1,), (1,)), ((), ())),
         preferred_element_type=jnp.float32,
-    )
+    ).astype(jnp.bfloat16)
+    input_grad = jnp.take(
+        grad_slots.reshape(tok_count, dp_count, -1), jnp.argsort(slot_owner), axis=1, mode="clip"
+    ).reshape(tok_count, -1)
     return (
         query_grad.astype(jnp.bfloat16)[None],
         key_grad[None],
-        input_grad.astype(jnp.bfloat16)[None],
+        input_grad[None],
         weight_grad,
     )
 

time: 217 us -> 199 us (0.917)
  waiting for transfers between devices: 77.3 us -> 66.9 us
  matrix products: 40.3 us -> 31.6 us
  local copies, waits for them, and re-layouts: 20.6 us -> 28.7 us
  other arithmetic: 26 us -> 19.9 us
    all_to_all x2, waiting for transfers between devices: 32 us -> 19.8 us  [gathered_copies(): return lax.all_to_all(copies, axis, 0, 0, tiled=True)]
    ppermute x4, waiting for transfers between devices: 12.4 us -> 20 us  [passed_along(): return lax.ppermute(array, axis, pairs)]
    dot_general x4, matrix products: 8.87 us -> 3.01 us  [attend_second(): jnp.einsum('gqk,qgd->kd', score_grad, query_wide, precision=high)]
    select_n x2 -> x0, other arithmetic: 5.34 us -> none  [spread_weight(): return (jnp.take(stacked, order, axis=0).reshape(-1, width), ready)]
    unnamed x84 -> x69, local copies, waits for them, and re-layouts: 9.77 us -> 15 us
    sub x4, matrix products: 9.61 us -> 5.08 us  [attend_first(): weights = jnp.where(visible[None], jnp.exp(masked - highest), 0.0)]
    ppermute x2, waiting for transfers between devices: 4.05 us -> 0.01 us  [with_halo(): lax.ppermute(head, axis, [((i + 1) % count, i) for i in range(ends)])]
    dot_general x4, matrix products: 2.73 us -> 5.49 us  [attend_second(): jnp.einsum('gqk,kd->qgd', score_grad, key_wide, precision=high)]
  transfers between devices with their start and end apart: 15 -> 15, of which waited for: 8 -> 8; matrix products, arithmetic and copies ran while one was open for 28% -> 32% of each run, Pallas kernels for 0% -> 0%
where the time goes in v7:
time: 199 us; the launch traced here: 197 us
  waiting for transfers between devices  66.9 us (34%)
  starting transfers between devices  49.1 us (25%)
  matrix products  31.6 us (16%)
  local copies, waits for them, and re-layouts  28.7 us (14%)
  other arithmetic  19.9 us (10%)
    ppermute x3, waiting for transfers between devices, spread_weight(): ring.append(lax.ppermute(held, 'dp', pairs))  21.3 us
    ppermute x4, waiting for transfers between devices, passed_along(): return lax.ppermute(array, axis, pairs)  20 us
    all_to_all x2, waiting for transfers between devices, gathered_copies(): return lax.all_to_all(copies, axis, 0, 0, tiled=True)  19.8 us
    all_to_all x2, starting transfers between devices, gathered_copies(): return lax.all_to_all(copies, axis, 0, 0, tiled=True)  16.6 us
    unnamed x69, local copies, waits for them, and re-layouts  15 us
    ppermute x4, starting transfers between devices, passed_along(): return lax.ppermute(array, axis, pairs)  12.9 us
    ppermute x2, starting transfers between devices, with_halo(): lax.ppermute(tail, axis, [(i, (i + 1) % count) for i in range(ends)])  10.2 us
    dot_general x4, matrix products, attend_first(): jnp.einsum('gqk,qgd->kd', attention_low, grad_head, preferred_element_typ...  6.08 us
  transfers between devices with their start and end apart: 15, of which 8 were waited for; matrix products, arithmetic and copies ran while one was open for 32% of the time, Pallas kernels for 0%

profile of v7, /device:TPU:26, one launch (start us, length us, event | category | flops | bytes accessed | tf_op | source)
XLA Modules:
  0.0 197.3 jit_solution(14060273707479965334)
XLA Ops:
  1.7 2.4 %collective-permute-start.5 = (bf16[128,512]{0,1:T(8,128)(2,1)S(1)}, bf16[128,512]{0,1:T(8,128)(2,1)S(1)}, u32[]{:S(2)}, u32[]{:S(2)}) collective-permute-start(bf16[128,512]{0,1:T(8,128)(2,1)S(1)} %bitcast.327), channel_id=1, source_target_pairs={{1,0},{2,1},{3,2},{4,3},{5,4},{6,5},{7,6},{8,7},{9,8},{10,9},{11,1... | collective-permute-start | bytes 393224 | tf_op jit(solution)/shard_map/ppermute | solution.py:19
  4.2 4.3 %collective-permute-start.4 = (bf16[128,512]{0,1:T(8,128)(2,1)S(1)}, bf16[128,512]{0,1:T(8,128)(2,1)}, u32[]{:S(2)}, u32[]{:S(2)}) collective-permute-start(bf16[128,512]{0,1:T(8,128)(2,1)S(1)} %bitcast.328), channel_id=1, source_target_pairs={{0,1},{1,2},{2,3},{3,4},{4,5},{5,6},{6,7},{7,8},{8,9},{9,10},{10,1... | collective-permute-start | bytes 393224 | tf_op jit(solution)/shard_map/ppermute | solution.py:17
  11.9 5.7 %collective-permute-done = bf16[320,512]{1,0:T(8,128)(2,1)S(1)} collective-permute-done((bf16[320,512]{1,0:T(8,128)(2,1)}, bf16[320,512]{1,0:T(8,128)(2,1)S(1)}, u32[]{:S(2)}, u32[]{:S(2)}) %collective-permute-start) | collective-permute-done | bytes 327712 | tf_op jit(solution)/shard_map/ppermute | solution.py:44
  21.3 2.2 %collective-permute-start.1 = (bf16[2,320,512]{2,1,0:T(8,128)(2,1)}, bf16[2,320,512]{2,1,0:T(8,128)(2,1)S(1)}, u32[]{:S(2)}, u32[]{:S(2)}) collective-permute-start(bf16[2,320,512]{2,1,0:T(8,128)(2,1)} %get-tuple-element.31), channel_id=1, source_target_pairs={{0,32},{16,48},{32,64},{48,80},{64,96},{80,112},{96,0},{112,16},{1... | collective-permute-start | bytes 1966088 | tf_op jit(solution)/shard_map/ppermute | solution.py:51
  25.4 2.2 %copy.94 = bf16[1,128,2560]{1,2,0:T(8,128)(2,1)} copy(bf16[1,128,2560]{2,1,0:T(8,128)(2,1)} %param.10) | data formatting | bytes 1310720 | tf_op args[3]
  29.3 20.7 %collective-permute-done.3 = bf16[2,320,512]{2,1,0:T(8,128)(2,1)S(1)} collective-permute-done((bf16[2,320,512]{2,1,0:T(8,128)(2,1)}, bf16[2,320,512]{2,1,0:T(8,128)(2,1)S(1)}, u32[]{:S(2)}, u32[]{:S(2)}) %collective-permute-start.3) | collective-permute-done | bytes 655392 | tf_op jit(solution)/shard_map/ppermute | solution.py:51
  60.0 2.2 %convolution_bitcast_fusion.6 = f32[384,128]{0,1:T(8,128)} fusion(bf16[128,4,5,128]{0,3,2,1:T(8,128)(2,1)S(1)} %bitcast.322, f32[5,128,384]{1,2,0:T(8,128)} %get-tuple-element.41, f32[5,128]{1,0:T(8,128)S(1)} %get-tuple-element.40), kind=kOutput, calls=%fused_computation.54 | convolution fusion | flops 63406080 | bytes 1347584 | tf_op jit(solution)/shard_map/gqk,qgd->kd/dot_general | solution.py:116
  66.2 5.1 %collective-permute-start.7 = (f32[128,512]{0,1:T(8,128)}, f32[128,512]{0,1:T(8,128)}, u32[]{:S(2)}, u32[]{:S(2)}) collective-permute-start(f32[128,512]{0,1:T(8,128)} %get-tuple-element.29), channel_id=1, source_target_pairs={{0,1},{1,2},{2,3},{3,4},{4,5},{5,6},{6,7},{7,8},{8,9},{9,10},{10,1... | collective-permute-start | bytes 786440 | tf_op jit(solution)/shard_map/ppermute | solution.py:82
  77.9 5.0 %collective-permute-done.6 = f32[128,512]{0,1:T(8,128)} collective-permute-done((f32[128,512]{0,1:T(8,128)}, f32[128,512]{0,1:T(8,128)}, u32[]{:S(2)}, u32[]{:S(2)}) %collective-permute-start.6) | collective-permute-done | bytes 262176 | tf_op jit(solution)/shard_map/ppermute | solution.py:82
  84.0 3.0 %pad_maximum_fusion = bf16[2,4,2,320,512]{4,3,2,1,0:T(8,128)(2,1)S(1)} fusion(bf16[1,4,2,320,512]{4,3,2,1,0:T(8,128)(2,1)} %bitcast.41, bf16[1,4,2,320,512]{4,3,2,1,0:T(8,128)(2,1)} %bitcast.40), kind=kLoop, calls=%fused_computation.7 | loop fusion | flops 2621440 | bytes 10485760 | tf_op jit(solution)/shard_map/stack | solution.py:54
  91.2 5.9 %collective-permute-start.9 = (bf16[128,512]{1,0:T(8,128)(2,1)}, bf16[128,512]{1,0:T(8,128)(2,1)}, u32[]{:S(2)}, u32[]{:S(2)}) collective-permute-start(bf16[128,512]{1,0:T(8,128)(2,1)} %fusion.35), channel_id=1, source_target_pairs={{0,1},{1,2},{2,3},{3,4},{4,5},{5,6},{6,7},{7,8},{8,9},{9,10},{10,1... | collective-permute-start | bytes 393224 | tf_op jit(solution)/shard_map/ppermute | solution.py:17
  99.6 6.2 %all-to-all-start = ((bf16[16,128,832]{1,2,0:T(8,128)(2,1)}), bf16[16,128,832]{1,2,0:T(8,128)(2,1)S(1)}, u32[]{:S(2)}, u32[]{:S(2)}) async-start(bf16[16,128,832]{1,2,0:T(8,128)(2,1)} %pad_maximum_fusion.1), calls=%async_computation | async-start | bytes 6815744 | tf_op jit(solution)/shard_map/all_to_all | solution.py:69
  105.8 5.4 %convolution_convert_fusion = bf16[128,5120]{1,0:T(8,128)(2,1)} fusion(bf16[128,512]{0,1:T(8,128)(2,1)S(1)} %fusion.53, bf16[5120,512]{1,0:T(8,128)(2,1)} %bitcast.301), kind=kOutput, calls=%fused_computation.6 | convolution fusion | flops 671744000 | bytes 6684672 | tf_op jit(solution)/shard_map/dot_general | solution.py:211
  111.2 2.4 %copy.129 = bf16[128,5120]{0,1:T(8,128)(2,1)} copy(bf16[128,5120]{1,0:T(8,128)(2,1)} %convolution_convert_fusion) | data formatting | bytes 2621440 | tf_op jit(solution)/shard_map/convert_element_type | solution.py:216
  113.6 3.1 %gather_fusion.1 = bf16[16,128,320]{1,2,0:T(8,128)(2,1)} fusion(bf16[128,16,320]{0,2,1:T(8,128)(2,1)} %bitcast.304, s32[1024]{0:T(1024)S(1)} %pad_clamp_fusion), kind=kCustom, calls=%fused_computation.1 | custom fusion | bytes 2621504 | tf_op jit(solution)/shard_map/jit(_take)/gather | solution.py:217
  116.7 2.4 %copy.132 = bf16[1,128,5120]{2,1,0:T(8,128)(2,1)} copy(bf16[1,128,5120]{1,2,0:T(8,128)(2,1)} %bitcast.305) | data formatting | bytes 2621440
  122.7 2.3 %fusion.77 = (bf16[384,1,128]{2,1,0:T(2,128)(2,1)S(1)}, bf16[384,1,128]{2,1,0:T(2,128)(2,1)S(1)}, bf16[384,1,128]{2,1,0:T(2,128)(2,1)S(1)}, bf16[384,1,128]{2,1,0:T(2,128)(2,1)S(1)}) fusion(bf16[384,4,128]{2,1,0:T(4,128)(2,1)} %reshape.278), kind=kLoop, calls=%fused_computation.159 | loop fusion | bytes 786432 | tf_op jit(solution)/shard_map/slice | solution.py:135
  134.1 2.2 %fusion.42 = bf16[128,1,5,128]{0,3,2,1:T(8,128)(2,1)} fusion(f32[5,128,384]{1,2,0:T(8,128)S(1)} %get-tuple-element.45, f32[5,128]{1,0:T(8,128)S(1)} %get-tuple-element.44, bf16[384,4,128]{0,2,1:T(8,128)(2,1)} %bitcast.331, f32[5,128,384]{1,2,0:T(8,128)S(1)} %copy-done.21, f32[5,128]{1,0:T(8,128)S(1)} %copy-done.30), kind=kOutput, calls=%fused_computation.65 | convolution fusion | flops 378388480 | bytes 2233344 | tf_op jit(solution)/shard_map/gqk,kd->qgd/dot_general | solution.py:145
  136.4 19.8 %all-to-all-done = bf16[16,128,832]{1,2,0:T(8,128)(2,1)S(1)} async-done(((bf16[16,128,832]{1,2,0:T(8,128)(2,1)}), bf16[16,128,832]{1,2,0:T(8,128)(2,1)S(1)}, u32[]{:S(2)}, u32[]{:S(2)}) %all-to-all-start) | async-done | bytes 3407904 | tf_op jit(solution)/shard_map/all_to_all | solution.py:69
  158.5 10.4 %all-to-all-start.1 = ((f32[16,320,32]{1,2,0:T(8,128)}), f32[16,320,32]{1,2,0:T(8,128)S(1)}, u32[]{:S(2)}, u32[]{:S(2)}) async-start(f32[16,320,32]{1,2,0:T(8,128)} %fusion.27), calls=%async_computation.1 | async-start | bytes 1572864 | tf_op jit(solution)/shard_map/all_to_all | solution.py:69
  170.1 3.4 %collective-permute-start.12 = (f32[128,512]{0,1:T(8,128)S(1)}, f32[128,512]{0,1:T(8,128)S(1)}, u32[]{:S(2)}, u32[]{:S(2)}) collective-permute-start(f32[128,512]{0,1:T(8,128)S(1)} %get-tuple-element.27), channel_id=1, source_target_pairs={{0,1},{1,2},{2,3},{3,4},{4,5},{5,6},{6,7},{7,8},{8,9},{9,10},{10,1... | collective-permute-start | bytes 786440 | tf_op jit(solution)/shard_map/ppermute | solution.py:82
  173.5 2.5 %collective-permute-start.11 = (f32[128,512]{0,1:T(8,128)S(1)}, f32[128,512]{0,1:T(8,128)S(1)}, u32[]{:S(2)}, u32[]{:S(2)}) collective-permute-start(f32[128,512]{0,1:T(8,128)S(1)} %get-tuple-element.26), channel_id=1, source_target_pairs={{1,0},{2,1},{3,2},{4,3},{5,4},{6,5},{7,6},{8,7},{9,8},{10,9},{11,1... | collective-permute-start | bytes 786440 | tf_op jit(solution)/shard_map/ppermute | solution.py:82
  181.5 10.8 %collective-permute-done.12 = f32[128,512]{0,1:T(8,128)S(1)} collective-permute-done((f32[128,512]{0,1:T(8,128)S(1)}, f32[128,512]{0,1:T(8,128)S(1)}, u32[]{:S(2)}, u32[]{:S(2)}) %collective-permute-start.12) | collective-permute-done | bytes 262176 | tf_op jit(solution)/shard_map/ppermute | solution.py:82
  192.3 2.6 %collective-permute-done.11 = f32[128,512]{0,1:T(8,128)S(1)} collective-permute-done((f32[128,512]{0,1:T(8,128)S(1)}, f32[128,512]{0,1:T(8,128)S(1)}, u32[]{:S(2)}, u32[]{:S(2)}) %collective-permute-start.11) | collective-permute-done | bytes 262176 | tf_op jit(solution)/shard_map/ppermute | solution.py:82
  (136 shorter events, 64.0 us)
Async XLA Ops:
  0.6 23.7 %copy-start.2 = (bf16[1,128,2560]{2,1,0:T(8,128)(2,1)S(1)}, bf16[1,128,2560]{2,1,0:T(8,128)(2,1)}, u32[]{:S(2)}) copy-start(bf16[1,128,2560]{2,1,0:T(8,128)(2,1)} %param.8) | copy-start | bytes 1966084
  1.7 25.9 %collective-permute-start.5 = (bf16[128,512]{0,1:T(8,128)(2,1)S(1)}, bf16[128,512]{0,1:T(8,128)(2,1)S(1)}, u32[]{:S(2)}, u32[]{:S(2)}) collective-permute-start(bf16[128,512]{0,1:T(8,128)(2,1)S(1)} %bitcast.327), channel_id=1, source_target_pairs={{1,0},{2,1},{3,2},{4,3},{5,4},{6,5},{7,6},{8,7},{9,8},{10,9},{11,1... | collective-permute-start | bytes 393224 | tf_op jit(solution)/shard_map/ppermute | solution.py:19
  4.2 23.4 %collective-permute-start.4 = (bf16[128,512]{0,1:T(8,128)(2,1)S(1)}, bf16[128,512]{0,1:T(8,128)(2,1)}, u32[]{:S(2)}, u32[]{:S(2)}) collective-permute-start(bf16[128,512]{0,1:T(8,128)(2,1)S(1)} %bitcast.328), channel_id=1, source_target_pairs={{0,1},{1,2},{2,3},{3,4},{4,5},{5,6},{6,7},{7,8},{8,9},{9,10},{10,1... | collective-permute-start | bytes 393224 | tf_op jit(solution)/shard_map/ppermute | solution.py:17
  8.5 9.2 %collective-permute-start = (bf16[320,512]{1,0:T(8,128)(2,1)}, bf16[320,512]{1,0:T(8,128)(2,1)S(1)}, u32[]{:S(2)}, u32[]{:S(2)}) collective-permute-start(bf16[320,512]{1,0:T(8,128)(2,1)} %param.11), channel_id=1, source_target_pairs={{0,129},{1,128},{2,131},{3,130},{4,133},{5,132},{6,135},{7,134},{8... | collective-permute-start | bytes 983048 | tf_op jit(solution)/shard_map/ppermute | solution.py:44
  19.6 30.5 %collective-permute-start.3 = (bf16[2,320,512]{2,1,0:T(8,128)(2,1)}, bf16[2,320,512]{2,1,0:T(8,128)(2,1)S(1)}, u32[]{:S(2)}, u32[]{:S(2)}) collective-permute-start(bf16[2,320,512]{2,1,0:T(8,128)(2,1)} %get-tuple-element.31), channel_id=1, source_target_pairs={{0,96},{16,112},{32,0},{48,16},{64,32},{80,48},{96,64},{112,80},{1... | collective-permute-start | bytes 1966088 | tf_op jit(solution)/shard_map/ppermute | solution.py:51
  20.3 29.7 %collective-permute-start.2 = (bf16[2,320,512]{2,1,0:T(8,128)(2,1)}, bf16[2,320,512]{2,1,0:T(8,128)(2,1)S(1)}, u32[]{:S(2)}, u32[]{:S(2)}) collective-permute-start(bf16[2,320,512]{2,1,0:T(8,128)(2,1)} %get-tuple-element.31), channel_id=1, source_target_pairs={{0,64},{16,80},{32,96},{48,112},{64,0},{80,16},{96,32},{112,48},{1... | collective-permute-start | bytes 1966088 | tf_op jit(solution)/shard_map/ppermute | solution.py:51
  21.3 29.4 %collective-permute-start.1 = (bf16[2,320,512]{2,1,0:T(8,128)(2,1)}, bf16[2,320,512]{2,1,0:T(8,128)(2,1)S(1)}, u32[]{:S(2)}, u32[]{:S(2)}) collective-permute-start(bf16[2,320,512]{2,1,0:T(8,128)(2,1)} %get-tuple-element.31), channel_id=1, source_target_pairs={{0,32},{16,48},{32,64},{48,80},{64,96},{80,112},{96,0},{112,16},{1... | collective-permute-start | bytes 1966088 | tf_op jit(solution)/shard_map/ppermute | solution.py:51
  52.5 31.5 %collective-permute-start.8 = (bf16[4,2,320,512]{3,2,1,0:T(8,128)(2,1)}, bf16[4,2,320,512]{3,2,1,0:T(8,128)(2,1)}, u32[]{:S(2)}, u32[]{:S(2)}) collective-permute-start(bf16[4,2,320,512]{3,2,1,0:T(8,128)(2,1)} %pad_maximum_fusion.2), channel_id=1, source_target_pairs={{0,16},{16,0},{32,48},{48,32},{64,80},{80,64},{96,112},{112,96},{1... | collective-permute-start | bytes 7864328 | tf_op jit(solution)/shard_map/ppermute | solution.py:53
  63.7 9.7 %copy-start.1 = (bf16[1,128,5120]{2,1,0:T(8,128)(2,1)S(1)}, bf16[1,128,5120]{2,1,0:T(8,128)(2,1)}, u32[]{:S(2)}) copy-start(bf16[1,128,5120]{2,1,0:T(8,128)(2,1)} %param.7) | copy-start | bytes 3932164
  66.2 11.7 %collective-permute-start.7 = (f32[128,512]{0,1:T(8,128)}, f32[128,512]{0,1:T(8,128)}, u32[]{:S(2)}, u32[]{:S(2)}) collective-permute-start(f32[128,512]{0,1:T(8,128)} %get-tuple-element.29), channel_id=1, source_target_pairs={{0,1},{1,2},{2,3},{3,4},{4,5},{5,6},{6,7},{7,8},{8,9},{9,10},{10,1... | collective-permute-start | bytes 786440 | tf_op jit(solution)/shard_map/ppermute | solution.py:82
  71.4 11.5 %collective-permute-start.6 = (f32[128,512]{0,1:T(8,128)}, f32[128,512]{0,1:T(8,128)}, u32[]{:S(2)}, u32[]{:S(2)}) collective-permute-start(f32[128,512]{0,1:T(8,128)} %get-tuple-element.28), channel_id=1, source_target_pairs={{1,0},{2,1},{3,2},{4,3},{5,4},{6,5},{7,6},{8,7},{9,8},{10,9},{11,1... | collective-permute-start | bytes 786440 | tf_op jit(solution)/shard_map/ppermute | solution.py:82
  89.3 29.8 %collective-permute-start.10 = (bf16[128,512]{1,0:T(8,128)(2,1)}, bf16[128,512]{1,0:T(8,128)(2,1)}, u32[]{:S(2)}, u32[]{:S(2)}) collective-permute-start(bf16[128,512]{1,0:T(8,128)(2,1)} %fusion.35), channel_id=1, source_target_pairs={{1,0},{2,1},{3,2},{4,3},{5,4},{6,5},{7,6},{8,7},{9,8},{10,9},{11,1... | collective-permute-start | bytes 393224 | tf_op jit(solution)/shard_map/ppermute | solution.py:19
  91.2 27.9 %collective-permute-start.9 = (bf16[128,512]{1,0:T(8,128)(2,1)}, bf16[128,512]{1,0:T(8,128)(2,1)}, u32[]{:S(2)}, u32[]{:S(2)}) collective-permute-start(bf16[128,512]{1,0:T(8,128)(2,1)} %fusion.35), channel_id=1, source_target_pairs={{0,1},{1,2},{2,3},{3,4},{4,5},{5,6},{6,7},{7,8},{8,9},{9,10},{10,1... | collective-permute-start | bytes 393224 | tf_op jit(solution)/shard_map/ppermute | solution.py:17
  99.6 56.6 %all-to-all-start = ((bf16[16,128,832]{1,2,0:T(8,128)(2,1)}), bf16[16,128,832]{1,2,0:T(8,128)(2,1)S(1)}, u32[]{:S(2)}, u32[]{:S(2)}) async-start(bf16[16,128,832]{1,2,0:T(8,128)(2,1)} %pad_maximum_fusion.1), calls=%async_computation | async-start | bytes 6815744 | tf_op jit(solution)/shard_map/all_to_all | solution.py:69
  116.7 8.4 %copy-start.30 = (f32[5,128]{1,0:T(8,128)S(1)}, f32[5,128]{1,0:T(8,128)}, u32[]{:S(2)}) copy-start(f32[5,128]{1,0:T(8,128)} %copy-done.29) | copy-start | bytes 7684
  122.7 3.9 %copy-start.16 = (f32[5,128,384]{1,2,0:T(8,128)S(1)}, f32[5,128,384]{1,2,0:T(8,128)}, u32[]{:S(2)}) copy-start(f32[5,128,384]{1,2,0:T(8,128)} %copy-done.15) | copy-start | bytes 2949124
  126.9 3.9 %copy-start.26 = (f32[5,128,384]{1,2,0:T(8,128)}, f32[5,128,384]{1,2,0:T(8,128)S(1)}, u32[]{:S(2)}) copy-start(f32[5,128,384]{1,2,0:T(8,128)S(1)} %get-tuple-element.47) | copy-start | bytes 2949124
  158.5 17.5 %copy-start.8 = (bf16[384,512]{0,1:T(8,128)(2,1)S(1)}, bf16[384,512]{0,1:T(8,128)(2,1)}, u32[]{:S(2)}) copy-start(bf16[384,512]{0,1:T(8,128)(2,1)} %pad_maximum_fusion.7) | copy-start | bytes 1179652
  158.5 17.5 %copy-start.17 = (f32[5,128,384]{1,2,0:T(8,128)S(1)}, f32[5,128,384]{1,2,0:T(8,128)}, u32[]{:S(2)}) copy-start(f32[5,128,384]{1,2,0:T(8,128)} %copy-done.15) | copy-start | bytes 2949124
  158.5 38.2 %all-to-all-start.1 = ((f32[16,320,32]{1,2,0:T(8,128)}), f32[16,320,32]{1,2,0:T(8,128)S(1)}, u32[]{:S(2)}, u32[]{:S(2)}) async-start(f32[16,320,32]{1,2,0:T(8,128)} %fusion.27), calls=%async_computation.1 | async-start | bytes 1572864 | tf_op jit(solution)/shard_map/all_to_all | solution.py:69
  168.8 9.0 %copy-start.19 = (f32[5,128,384]{1,2,0:T(8,128)S(1)}, f32[5,128,384]{1,2,0:T(8,128)}, u32[]{:S(2)}) copy-start(f32[5,128,384]{1,2,0:T(8,128)} %get-tuple-element.41) | copy-start | bytes 2949124
  168.9 9.0 %copy-start.25 = (f32[5,128,384]{1,2,0:T(8,128)S(1)}, f32[5,128,384]{1,2,0:T(8,128)}, u32[]{:S(2)}) copy-start(f32[5,128,384]{1,2,0:T(8,128)} %copy-done.24) | copy-start | bytes 2949124
  170.1 22.2 %collective-permute-start.12 = (f32[128,512]{0,1:T(8,128)S(1)}, f32[128,512]{0,1:T(8,128)S(1)}, u32[]{:S(2)}, u32[]{:S(2)}) collective-permute-start(f32[128,512]{0,1:T(8,128)S(1)} %get-tuple-element.27), channel_id=1, source_target_pairs={{0,1},{1,2},{2,3},{3,4},{4,5},{5,6},{6,7},{7,8},{8,9},{9,10},{10,1... | collective-permute-start | bytes 786440 | tf_op jit(solution)/shard_map/ppermute | solution.py:82
  173.5 21.4 %collective-permute-start.11 = (f32[128,512]{0,1:T(8,128)S(1)}, f32[128,512]{0,1:T(8,128)S(1)}, u32[]{:S(2)}, u32[]{:S(2)}) collective-permute-start(f32[128,512]{0,1:T(8,128)S(1)} %get-tuple-element.26), channel_id=1, source_target_pairs={{1,0},{2,1},{3,2},{4,3},{5,4},{6,5},{7,6},{8,7},{9,8},{10,9},{11,1... | collective-permute-start | bytes 786440 | tf_op jit(solution)/shard_map/ppermute | solution.py:82
  (22 other events, 44.1 us)

commit v8 on v7

--- a/solution.py
+++ b/solution.py
@@ -186,7 +186,6 @@
     )
     attentions, value_part = attend_first(query_states[0], key_block, out_grad[0], visible)
     value_grad = rim_sum(value_part, tok_count).astype(jnp.bfloat16)
-    value_grad, weight_slots = lax.optimization_barrier((value_grad, weight_slots))
     weight_full = weight_slots.reshape(-1, kv_width)
     grad_copies = jnp.broadcast_to(value_grad[None], (dp_count,) + value_grad.shape)
     arrived = gathered_copies(jnp.concatenate([grad_copies, input_pieces], axis=2), "dp")

time: 199 us -> 209 us (1.050)
  the two profiles are of different devices: /device:TPU:26 before, /device:TPU:40 now
where the time goes in v8:
time: 209 us; the launch traced here: 207 us
  waiting for transfers between devices  74.9 us (36%)
  starting transfers between devices  52.3 us (25%)
  matrix products  30.9 us (15%)
  local copies, waits for them, and re-layouts  28.1 us (13%)
  other arithmetic  19.9 us (10%)
    ppermute x2, waiting for transfers between devices, with_halo(): lax.ppermute(head, axis, [((i + 1) % count, i) for i in range(ends)])  28.1 us
    ppermute x3, waiting for transfers between devices, spread_weight(): ring.append(lax.ppermute(held, 'dp', pairs))  20.5 us
    ppermute x4, waiting for transfers between devices, passed_along(): return lax.ppermute(array, axis, pairs)  18.9 us
    all_to_all x2, starting transfers between devices, gathered_copies(): return lax.all_to_all(copies, axis, 0, 0, tiled=True)  18.2 us
    ppermute x4, starting transfers between devices, passed_along(): return lax.ppermute(array, axis, pairs)  13.5 us
    unnamed x67, local copies, waits for them, and re-layouts  13.1 us
    ppermute x2, starting transfers between devices, with_halo(): lax.ppermute(tail, axis, [(i, (i + 1) % count) for i in range(ends)])  7 us
    sub x4, matrix products, attend_first(): weights = jnp.where(visible[None], jnp.exp(masked - highest), 0.0)  6.87 us
  transfers between devices with their start and end apart: 15, of which 10 were waited for; matrix products, arithmetic and copies ran while one was open for 32% of the time, Pallas kernels for 0%

profile of v8, /device:TPU:40, one launch (start us, length us, event | category | flops | bytes accessed | tf_op | source)
XLA Modules:
  0.0 207.3 jit_solution(3594112589541971095)
XLA Ops:
  1.7 2.9 %collective-permute-start.5 = (bf16[128,512]{0,1:T(8,128)(2,1)S(1)}, bf16[128,512]{0,1:T(8,128)(2,1)S(1)}, u32[]{:S(2)}, u32[]{:S(2)}) collective-permute-start(bf16[128,512]{0,1:T(8,128)(2,1)S(1)} %bitcast.328), channel_id=1, source_target_pairs={{1,0},{2,1},{3,2},{4,3},{5,4},{6,5},{7,6},{8,7},{9,8},{10,9},{11,1... | collective-permute-start | bytes 393224 | tf_op jit(solution)/shard_map/ppermute | solution.py:19
  4.7 2.9 %collective-permute-start.4 = (bf16[128,512]{0,1:T(8,128)(2,1)S(1)}, bf16[128,512]{0,1:T(8,128)(2,1)}, u32[]{:S(2)}, u32[]{:S(2)}) collective-permute-start(bf16[128,512]{0,1:T(8,128)(2,1)S(1)} %bitcast.329), channel_id=1, source_target_pairs={{0,1},{1,2},{2,3},{3,4},{4,5},{5,6},{6,7},{7,8},{8,9},{9,10},{10,1... | collective-permute-start | bytes 393224 | tf_op jit(solution)/shard_map/ppermute | solution.py:17
  7.6 3.7 %collective-permute-start = (bf16[320,512]{1,0:T(8,128)(2,1)}, bf16[320,512]{1,0:T(8,128)(2,1)S(1)}, u32[]{:S(2)}, u32[]{:S(2)}) collective-permute-start(bf16[320,512]{1,0:T(8,128)(2,1)} %param.11), channel_id=1, source_target_pairs={{0,129},{1,128},{2,131},{3,130},{4,133},{5,132},{6,135},{7,134},{8... | collective-permute-start | bytes 983048 | tf_op jit(solution)/shard_map/ppermute | solution.py:44
  13.6 5.1 %collective-permute-done = bf16[320,512]{1,0:T(8,128)(2,1)S(1)} collective-permute-done((bf16[320,512]{1,0:T(8,128)(2,1)}, bf16[320,512]{1,0:T(8,128)(2,1)S(1)}, u32[]{:S(2)}, u32[]{:S(2)}) %collective-permute-start) | collective-permute-done | bytes 327712 | tf_op jit(solution)/shard_map/ppermute | solution.py:44
  21.0 2.6 %collective-permute-start.2 = (bf16[2,320,512]{2,1,0:T(8,128)(2,1)}, bf16[2,320,512]{2,1,0:T(8,128)(2,1)S(1)}, u32[]{:S(2)}, u32[]{:S(2)}) collective-permute-start(bf16[2,320,512]{2,1,0:T(8,128)(2,1)} %get-tuple-element.27), channel_id=1, source_target_pairs={{0,64},{16,80},{32,96},{48,112},{64,0},{80,16},{96,32},{112,48},{1... | collective-permute-start | bytes 1966088 | tf_op jit(solution)/shard_map/ppermute | solution.py:51
  31.4 6.0 %collective-permute-done.3 = bf16[2,320,512]{2,1,0:T(8,128)(2,1)S(1)} collective-permute-done((bf16[2,320,512]{2,1,0:T(8,128)(2,1)}, bf16[2,320,512]{2,1,0:T(8,128)(2,1)S(1)}, u32[]{:S(2)}, u32[]{:S(2)}) %collective-permute-start.3) | collective-permute-done | bytes 655392 | tf_op jit(solution)/shard_map/ppermute | solution.py:51
  37.5 13.7 %collective-permute-done.2 = bf16[2,320,512]{2,1,0:T(8,128)(2,1)S(1)} collective-permute-done((bf16[2,320,512]{2,1,0:T(8,128)(2,1)}, bf16[2,320,512]{2,1,0:T(8,128)(2,1)S(1)}, u32[]{:S(2)}, u32[]{:S(2)}) %collective-permute-start.2) | collective-permute-done | bytes 655392 | tf_op jit(solution)/shard_map/ppermute | solution.py:51
  53.8 2.5 %fusion.70 = (f32[5,128]{1,0:T(8,128)S(1)}, f32[5,128,384]{1,2,0:T(8,128)}) fusion(pred[128,384]{0,1:T(8,128)(4,1)S(1)} %copy-done.12, bf16[128,4,5,128]{0,3,2,1:T(8,128)(2,1)S(1)} %bitcast.312, bf16[384,4,128]{0,2,1:T(8,128)(2,1)} %bitcast.331), kind=kOutput, calls=%fused_computation.157 | convolution fusion | flops 64143744 | bytes 1346048 | tf_op jit(solution)/shard_map/sub | solution.py:111
  70.4 4.7 %collective-permute-start.11 = (f32[128,512]{0,1:T(8,128)}, f32[128,512]{0,1:T(8,128)}, u32[]{:S(2)}, u32[]{:S(2)}) collective-permute-start(f32[128,512]{0,1:T(8,128)} %get-tuple-element.22), channel_id=1, source_target_pairs={{1,0},{2,1},{3,2},{4,3},{5,4},{6,5},{7,6},{8,7},{9,8},{10,9},{11,1... | collective-permute-start | bytes 786440 | tf_op jit(solution)/shard_map/ppermute | solution.py:82
  80.0 5.5 %collective-permute-done.11 = f32[128,512]{0,1:T(8,128)} collective-permute-done((f32[128,512]{0,1:T(8,128)}, f32[128,512]{0,1:T(8,128)}, u32[]{:S(2)}, u32[]{:S(2)}) %collective-permute-start.11) | collective-permute-done | bytes 262176 | tf_op jit(solution)/shard_map/ppermute | solution.py:82
  88.9 6.4 %all-to-all-start = ((bf16[16,128,832]{1,2,0:T(8,128)(2,1)}), bf16[16,128,832]{1,2,0:T(8,128)(2,1)S(1)}, u32[]{:S(2)}, u32[]{:S(2)}) async-start(bf16[16,128,832]{1,2,0:T(8,128)(2,1)} %pad_maximum_fusion.1), calls=%async_computation | async-start | bytes 6815744 | tf_op jit(solution)/shard_map/all_to_all | solution.py:69
  95.3 3.1 %pad_maximum_fusion = bf16[2,4,2,320,512]{4,3,2,1,0:T(8,128)(2,1)S(1)} fusion(bf16[1,4,2,320,512]{4,3,2,1,0:T(8,128)(2,1)} %bitcast.21, bf16[1,4,2,320,512]{4,3,2,1,0:T(8,128)(2,1)} %bitcast.20), kind=kLoop, calls=%fused_computation.7 | loop fusion | flops 2621440 | bytes 10485760 | tf_op jit(solution)/shard_map/stack | solution.py:54
  101.9 4.1 %collective-permute-start.7 = (bf16[128,512]{1,0:T(8,128)(2,1)}, bf16[128,512]{1,0:T(8,128)(2,1)}, u32[]{:S(2)}, u32[]{:S(2)}) collective-permute-start(bf16[128,512]{1,0:T(8,128)(2,1)} %convolution_convert_fusion.1), channel_id=1, source_target_pairs={{0,1},{1,2},{2,3},{3,4},{4,5},{5,6},{6,7},{7,8},{8,9},{9,10},{10,1... | collective-permute-start | bytes 393224 | tf_op jit(solution)/shard_map/ppermute | solution.py:17
  106.0 2.9 %convolution_convert_fusion = bf16[128,5120]{1,0:T(8,128)(2,1)} fusion(bf16[128,512]{0,1:T(8,128)(2,1)S(1)} %fusion.43, bf16[5120,512]{1,0:T(8,128)(2,1)S(1)} %bitcast.301), kind=kOutput, calls=%fused_computation.6 | convolution fusion | flops 671744000 | bytes 6684672 | tf_op jit(solution)/shard_map/dot_general | solution.py:210
  108.9 2.4 %copy.136 = bf16[128,5120]{0,1:T(8,128)(2,1)} copy(bf16[128,5120]{1,0:T(8,128)(2,1)} %convolution_convert_fusion) | data formatting | bytes 2621440 | tf_op jit(solution)/shard_map/convert_element_type | solution.py:215
  111.3 3.1 %gather_fusion.1 = bf16[16,128,320]{1,2,0:T(8,128)(2,1)} fusion(bf16[128,16,320]{0,2,1:T(8,128)(2,1)} %bitcast.305, s32[1024]{0:T(1024)S(1)} %pad_clamp_fusion), kind=kCustom, calls=%fused_computation.1 | custom fusion | bytes 2621504 | tf_op jit(solution)/shard_map/jit(_take)/gather | solution.py:216
  114.5 2.4 %copy.139 = bf16[1,128,5120]{2,1,0:T(8,128)(2,1)} copy(bf16[1,128,5120]{1,2,0:T(8,128)(2,1)} %bitcast.306) | data formatting | bytes 2621440
  116.9 28.1 %collective-permute-done.8 = bf16[128,512]{1,0:T(8,128)(2,1)} collective-permute-done((bf16[128,512]{1,0:T(8,128)(2,1)}, bf16[128,512]{1,0:T(8,128)(2,1)}, u32[]{:S(2)}, u32[]{:S(2)}) %collective-permute-start.8) | collective-permute-done | bytes 131104 | tf_op jit(solution)/shard_map/ppermute | solution.py:19
  145.0 2.3 %collective-permute-done.7 = bf16[128,512]{1,0:T(8,128)(2,1)} collective-permute-done((bf16[128,512]{1,0:T(8,128)(2,1)}, bf16[128,512]{1,0:T(8,128)(2,1)}, u32[]{:S(2)}, u32[]{:S(2)}) %collective-permute-start.7) | collective-permute-done | bytes 131104 | tf_op jit(solution)/shard_map/ppermute | solution.py:17
  150.9 2.5 %fusion.69 = (bf16[384,1,128]{2,1,0:T(2,128)(2,1)S(1)}, bf16[384,1,128]{2,1,0:T(2,128)(2,1)S(1)}, bf16[384,1,128]{2,1,0:T(2,128)(2,1)S(1)}, bf16[384,1,128]{2,1,0:T(2,128)(2,1)S(1)}) fusion(bf16[384,4,128]{2,1,0:T(4,128)(2,1)} %reshape.274), kind=kLoop, calls=%fused_computation.156 | loop fusion | bytes 786432 | tf_op jit(solution)/shard_map/slice | solution.py:135
  167.0 11.8 %all-to-all-start.1 = ((f32[16,320,32]{1,2,0:T(8,128)}), f32[16,320,32]{1,2,0:T(8,128)S(1)}, u32[]{:S(2)}, u32[]{:S(2)}) async-start(f32[16,320,32]{1,2,0:T(8,128)} %fusion.25), calls=%async_computation.1 | async-start | bytes 1572864 | tf_op jit(solution)/shard_map/all_to_all | solution.py:69
  180.1 3.4 %collective-permute-start.10 = (f32[128,512]{0,1:T(8,128)S(1)}, f32[128,512]{0,1:T(8,128)S(1)}, u32[]{:S(2)}, u32[]{:S(2)}) collective-permute-start(f32[128,512]{0,1:T(8,128)S(1)} %get-tuple-element.25), channel_id=1, source_target_pairs={{0,1},{1,2},{2,3},{3,4},{4,5},{5,6},{6,7},{7,8},{8,9},{9,10},{10,1... | collective-permute-start | bytes 786440 | tf_op jit(solution)/shard_map/ppermute | solution.py:82
  183.5 3.4 %collective-permute-start.9 = (f32[128,512]{0,1:T(8,128)S(1)}, f32[128,512]{0,1:T(8,128)S(1)}, u32[]{:S(2)}, u32[]{:S(2)}) collective-permute-start(f32[128,512]{0,1:T(8,128)S(1)} %get-tuple-element.24), channel_id=1, source_target_pairs={{1,0},{2,1},{3,2},{4,3},{5,4},{6,5},{7,6},{8,7},{9,8},{10,9},{11,1... | collective-permute-start | bytes 786440 | tf_op jit(solution)/shard_map/ppermute | solution.py:82
  192.4 10.9 %collective-permute-done.10 = f32[128,512]{0,1:T(8,128)S(1)} collective-permute-done((f32[128,512]{0,1:T(8,128)S(1)}, f32[128,512]{0,1:T(8,128)S(1)}, u32[]{:S(2)}, u32[]{:S(2)}) %collective-permute-start.10) | collective-permute-done | bytes 262176 | tf_op jit(solution)/shard_map/ppermute | solution.py:82
  (134 shorter events, 69.7 us)
Async XLA Ops:
  0.6 25.8 %copy-start.2 = (bf16[1,128,2560]{2,1,0:T(8,128)(2,1)S(1)}, bf16[1,128,2560]{2,1,0:T(8,128)(2,1)}, u32[]{:S(2)}) copy-start(bf16[1,128,2560]{2,1,0:T(8,128)(2,1)} %param.8) | copy-start | bytes 1966084
  1.7 27.9 %collective-permute-start.5 = (bf16[128,512]{0,1:T(8,128)(2,1)S(1)}, bf16[128,512]{0,1:T(8,128)(2,1)S(1)}, u32[]{:S(2)}, u32[]{:S(2)}) collective-permute-start(bf16[128,512]{0,1:T(8,128)(2,1)S(1)} %bitcast.328), channel_id=1, source_target_pairs={{1,0},{2,1},{3,2},{4,3},{5,4},{6,5},{7,6},{8,7},{9,8},{10,9},{11,1... | collective-permute-start | bytes 393224 | tf_op jit(solution)/shard_map/ppermute | solution.py:19
  4.7 25.0 %collective-permute-start.4 = (bf16[128,512]{0,1:T(8,128)(2,1)S(1)}, bf16[128,512]{0,1:T(8,128)(2,1)}, u32[]{:S(2)}, u32[]{:S(2)}) collective-permute-start(bf16[128,512]{0,1:T(8,128)(2,1)S(1)} %bitcast.329), channel_id=1, source_target_pairs={{0,1},{1,2},{2,3},{3,4},{4,5},{5,6},{6,7},{7,8},{8,9},{9,10},{10,1... | collective-permute-start | bytes 393224 | tf_op jit(solution)/shard_map/ppermute | solution.py:17
  7.6 11.1 %collective-permute-start = (bf16[320,512]{1,0:T(8,128)(2,1)}, bf16[320,512]{1,0:T(8,128)(2,1)S(1)}, u32[]{:S(2)}, u32[]{:S(2)}) collective-permute-start(bf16[320,512]{1,0:T(8,128)(2,1)} %param.11), channel_id=1, source_target_pairs={{0,129},{1,128},{2,131},{3,130},{4,133},{5,132},{6,135},{7,134},{8... | collective-permute-start | bytes 983048 | tf_op jit(solution)/shard_map/ppermute | solution.py:44
  20.6 16.9 %collective-permute-start.3 = (bf16[2,320,512]{2,1,0:T(8,128)(2,1)}, bf16[2,320,512]{2,1,0:T(8,128)(2,1)S(1)}, u32[]{:S(2)}, u32[]{:S(2)}) collective-permute-start(bf16[2,320,512]{2,1,0:T(8,128)(2,1)} %get-tuple-element.27), channel_id=1, source_target_pairs={{0,96},{16,112},{32,0},{48,16},{64,32},{80,48},{96,64},{112,80},{1... | collective-permute-start | bytes 1966088 | tf_op jit(solution)/shard_map/ppermute | solution.py:51
  21.0 30.1 %collective-permute-start.2 = (bf16[2,320,512]{2,1,0:T(8,128)(2,1)}, bf16[2,320,512]{2,1,0:T(8,128)(2,1)S(1)}, u32[]{:S(2)}, u32[]{:S(2)}) collective-permute-start(bf16[2,320,512]{2,1,0:T(8,128)(2,1)} %get-tuple-element.27), channel_id=1, source_target_pairs={{0,64},{16,80},{32,96},{48,112},{64,0},{80,16},{96,32},{112,48},{1... | collective-permute-start | bytes 1966088 | tf_op jit(solution)/shard_map/ppermute | solution.py:51
  23.6 28.3 %collective-permute-start.1 = (bf16[2,320,512]{2,1,0:T(8,128)(2,1)}, bf16[2,320,512]{2,1,0:T(8,128)(2,1)S(1)}, u32[]{:S(2)}, u32[]{:S(2)}) collective-permute-start(bf16[2,320,512]{2,1,0:T(8,128)(2,1)} %get-tuple-element.27), channel_id=1, source_target_pairs={{0,32},{16,48},{32,64},{48,80},{64,96},{80,112},{96,0},{112,16},{1... | collective-permute-start | bytes 1966088 | tf_op jit(solution)/shard_map/ppermute | solution.py:51
  57.7 37.6 %collective-permute-start.6 = (bf16[4,2,320,512]{3,2,1,0:T(8,128)(2,1)}, bf16[4,2,320,512]{3,2,1,0:T(8,128)(2,1)}, u32[]{:S(2)}, u32[]{:S(2)}) collective-permute-start(bf16[4,2,320,512]{3,2,1,0:T(8,128)(2,1)} %pad_maximum_fusion.2), channel_id=1, source_target_pairs={{0,16},{16,0},{32,48},{48,32},{64,80},{80,64},{96,112},{112,96},{1... | collective-permute-start | bytes 7864328 | tf_op jit(solution)/shard_map/ppermute | solution.py:53
  65.8 9.4 %copy-start.1 = (bf16[1,128,5120]{2,1,0:T(8,128)(2,1)S(1)}, bf16[1,128,5120]{2,1,0:T(8,128)(2,1)}, u32[]{:S(2)}) copy-start(bf16[1,128,5120]{2,1,0:T(8,128)(2,1)} %param.7) | copy-start | bytes 3932164
  68.3 11.6 %collective-permute-start.12 = (f32[128,512]{0,1:T(8,128)}, f32[128,512]{0,1:T(8,128)}, u32[]{:S(2)}, u32[]{:S(2)}) collective-permute-start(f32[128,512]{0,1:T(8,128)} %get-tuple-element.23), channel_id=1, source_target_pairs={{0,1},{1,2},{2,3},{3,4},{4,5},{5,6},{6,7},{7,8},{8,9},{9,10},{10,1... | collective-permute-start | bytes 786440 | tf_op jit(solution)/shard_map/ppermute | solution.py:82
  70.4 15.1 %collective-permute-start.11 = (f32[128,512]{0,1:T(8,128)}, f32[128,512]{0,1:T(8,128)}, u32[]{:S(2)}, u32[]{:S(2)}) collective-permute-start(f32[128,512]{0,1:T(8,128)} %get-tuple-element.22), channel_id=1, source_target_pairs={{1,0},{2,1},{3,2},{4,3},{5,4},{6,5},{7,6},{8,7},{9,8},{10,9},{11,1... | collective-permute-start | bytes 786440 | tf_op jit(solution)/shard_map/ppermute | solution.py:82
  88.9 75.8 %all-to-all-start = ((bf16[16,128,832]{1,2,0:T(8,128)(2,1)}), bf16[16,128,832]{1,2,0:T(8,128)(2,1)S(1)}, u32[]{:S(2)}, u32[]{:S(2)}) async-start(bf16[16,128,832]{1,2,0:T(8,128)(2,1)} %pad_maximum_fusion.1), calls=%async_computation | async-start | bytes 6815744 | tf_op jit(solution)/shard_map/all_to_all | solution.py:69
  100.0 45.0 %collective-permute-start.8 = (bf16[128,512]{1,0:T(8,128)(2,1)}, bf16[128,512]{1,0:T(8,128)(2,1)}, u32[]{:S(2)}, u32[]{:S(2)}) collective-permute-start(bf16[128,512]{1,0:T(8,128)(2,1)} %convolution_convert_fusion.1), channel_id=1, source_target_pairs={{1,0},{2,1},{3,2},{4,3},{5,4},{6,5},{7,6},{8,7},{9,8},{10,9},{11,1... | collective-permute-start | bytes 393224 | tf_op jit(solution)/shard_map/ppermute | solution.py:19
  101.9 45.3 %collective-permute-start.7 = (bf16[128,512]{1,0:T(8,128)(2,1)}, bf16[128,512]{1,0:T(8,128)(2,1)}, u32[]{:S(2)}, u32[]{:S(2)}) collective-permute-start(bf16[128,512]{1,0:T(8,128)(2,1)} %convolution_convert_fusion.1), channel_id=1, source_target_pairs={{0,1},{1,2},{2,3},{3,4},{4,5},{5,6},{6,7},{7,8},{8,9},{9,10},{10,1... | collective-permute-start | bytes 393224 | tf_op jit(solution)/shard_map/ppermute | solution.py:17
  114.5 38.9 %copy-start.29 = (f32[5,128]{1,0:T(8,128)S(1)}, f32[5,128]{1,0:T(8,128)}, u32[]{:S(2)}) copy-start(f32[5,128]{1,0:T(8,128)} %copy-done.28) | copy-start | bytes 7684
  150.9 4.1 %copy-start.6 = (bf16[1,128,2560]{1,2,0:T(8,128)(2,1)S(1)}, bf16[1,128,2560]{1,2,0:T(8,128)(2,1)}, u32[]{:S(2)}) copy-start(bf16[1,128,2560]{1,2,0:T(8,128)(2,1)} %copy.98) | copy-start | bytes 1966084
  150.9 4.1 %copy-start.14 = (f32[5,128,384]{1,2,0:T(8,128)S(1)}, f32[5,128,384]{1,2,0:T(8,128)}, u32[]{:S(2)}) copy-start(f32[5,128,384]{1,2,0:T(8,128)} %copy-done.13) | copy-start | bytes 2949124
  167.0 19.8 %copy-start.8 = (bf16[384,512]{0,1:T(8,128)(2,1)S(1)}, bf16[384,512]{0,1:T(8,128)(2,1)}, u32[]{:S(2)}) copy-start(bf16[384,512]{0,1:T(8,128)(2,1)} %pad_maximum_fusion.7) | copy-start | bytes 1179652
  167.0 19.8 %copy-start.15 = (f32[5,128,384]{1,2,0:T(8,128)S(1)}, f32[5,128,384]{1,2,0:T(8,128)}, u32[]{:S(2)}) copy-start(f32[5,128,384]{1,2,0:T(8,128)} %copy-done.13) | copy-start | bytes 2949124
  167.0 39.6 %all-to-all-start.1 = ((f32[16,320,32]{1,2,0:T(8,128)}), f32[16,320,32]{1,2,0:T(8,128)S(1)}, u32[]{:S(2)}, u32[]{:S(2)}) async-start(f32[16,320,32]{1,2,0:T(8,128)} %fusion.25), calls=%async_computation.1 | async-start | bytes 1572864 | tf_op jit(solution)/shard_map/all_to_all | solution.py:69
  178.9 9.9 %copy-start.19 = (f32[5,128,384]{1,2,0:T(8,128)S(1)}, f32[5,128,384]{1,2,0:T(8,128)}, u32[]{:S(2)}) copy-start(f32[5,128,384]{1,2,0:T(8,128)} %get-tuple-element.41) | copy-start | bytes 2949124
  178.9 9.9 %copy-start.24 = (f32[5,128,384]{1,2,0:T(8,128)S(1)}, f32[5,128,384]{1,2,0:T(8,128)}, u32[]{:S(2)}) copy-start(f32[5,128,384]{1,2,0:T(8,128)} %copy-done.23) | copy-start | bytes 2949124
  180.1 23.2 %collective-permute-start.10 = (f32[128,512]{0,1:T(8,128)S(1)}, f32[128,512]{0,1:T(8,128)S(1)}, u32[]{:S(2)}, u32[]{:S(2)}) collective-permute-start(f32[128,512]{0,1:T(8,128)S(1)} %get-tuple-element.25), channel_id=1, source_target_pairs={{0,1},{1,2},{2,3},{3,4},{4,5},{5,6},{6,7},{7,8},{8,9},{9,10},{10,1... | collective-permute-start | bytes 786440 | tf_op jit(solution)/shard_map/ppermute | solution.py:82
  183.5 21.4 %collective-permute-start.9 = (f32[128,512]{0,1:T(8,128)S(1)}, f32[128,512]{0,1:T(8,128)S(1)}, u32[]{:S(2)}, u32[]{:S(2)}) collective-permute-start(f32[128,512]{0,1:T(8,128)S(1)} %get-tuple-element.24), channel_id=1, source_target_pairs={{1,0},{2,1},{3,2},{4,3},{5,4},{6,5},{7,6},{8,7},{9,8},{10,9},{11,1... | collective-permute-start | bytes 786440 | tf_op jit(solution)/shard_map/ppermute | solution.py:82
  (21 other events, 47.3 us)

commit v9 on v7

--- a/solution.py
+++ b/solution.py
@@ -29,7 +29,7 @@
     return lax.all_to_all(copies, axis, 0, 0, tiled=True)
 
 
-def spread_weight(weight, ready):
+def spread_weight(weight, ready, riders):
     dp_count = lax.axis_size("dp")
     seq_count = lax.axis_size("seq")
     half = dp_count // 2
@@ -49,7 +49,7 @@
             upper, y_here, core = d // half, (d // cores) % y_count, d % cores
             pairs.append((d, upper * half + ((y_here + shift) % y_count) * cores + core))
         ring.append(lax.ppermute(held, "dp", pairs))
-    mine, ready = lax.optimization_barrier((jnp.stack(ring), ready))
+    mine, ready, riders = lax.optimization_barrier((jnp.stack(ring), ready, riders))
     sibling = lax.ppermute(mine, "dp", [(d, d ^ 1) for d in range(dp_count)])
     stacked = jnp.stack([mine, sibling]).reshape(dp_count, rows, width)
     me = lax.axis_index("dp")
@@ -62,7 +62,7 @@
         + ((y_here - shift_of) % y_count) * cores
         + (core + core_of) % 2
     )
-    return stacked, owner.reshape(-1), ready
+    return stacked, owner.reshape(-1), ready, riders
 
 
 def gathered_copies(copies, axis):
@@ -168,8 +168,11 @@
     model_width = layer_rows.shape[1]
     weight_rows, kv_width = value_weight.shape
     key_block = with_halo(key_states[0], (("seq", 0),), tok_count)
-    weight_slots, slot_owner, key_block = spread_weight(value_weight, key_block)
     input_pieces = layer_rows.reshape(tok_count, dp_count, model_width // dp_count).transpose(1, 0, 2)
+    weight_slots, slot_owner, key_block, input_pieces = spread_weight(
+        value_weight, key_block, input_pieces
+    )
+    input_blocks = gathered_copies(input_pieces, "dp")
     seg_row = segment_ids[0]
     fill_ids = jnp.full((tok_count,), -1, jnp.int32)
     padded_ids = jnp.concatenate([fill_ids, seg_row, fill_ids])
@@ -185,14 +188,13 @@
         (pos_key[None, :] <= pos_query[:, None]) | (pos_key[None, :] < split_query[:, None])
     )
     attentions, value_part = attend_first(query_states[0], key_block, out_grad[0], visible)
+    value_part, input_blocks = lax.optimization_barrier((value_part, input_blocks))
     value_grad = rim_sum(value_part, tok_count).astype(jnp.bfloat16)
     value_grad, weight_slots = lax.optimization_barrier((value_grad, weight_slots))
     weight_full = weight_slots.reshape(-1, kv_width)
     grad_copies = jnp.broadcast_to(value_grad[None], (dp_count,) + value_grad.shape)
-    arrived = gathered_copies(jnp.concatenate([grad_copies, input_pieces], axis=2), "dp")
     seq_count = lax.axis_size("seq")
-    grad_rows = arrived[:, :, :kv_width].reshape(dp_count, tok_count, seq_count, -1)
-    input_blocks = arrived[:, :, kv_width:]
+    grad_rows = gathered_copies(grad_copies, "dp").reshape(dp_count, tok_count, seq_count, -1)
     own_pieces = jnp.einsum(
         "rtk,rtjc->jkc", input_blocks, grad_rows, preferred_element_type=jnp.float32
     )

time: 199 us -> 194 us (0.975)
  other arithmetic: 19.9 us -> 15.3 us
  starting transfers between devices: 49.1 us -> 53.6 us
  local copies, waits for them, and re-layouts: 28.7 us -> 24.5 us
    all_to_all x2 -> x3, starting transfers between devices: 16.6 us -> 24.3 us  [gathered_copies(): return lax.all_to_all(copies, axis, 0, 0, tiled=True)]
    gather x1, local copies, waits for them, and re-layouts: 3.08 us -> 0.8 us  [local(): jnp.take(grad_slots.reshape(tok_count, dp_count, -1), jnp.argsort(slot_ow...]
    concatenate x1 -> x0, other arithmetic: 2.03 us -> none  [local(): jnp.concatenate([grad_copies, input_pieces], axis=2)]
    unnamed x69 -> x77, local copies, waits for them, and re-layouts: 15 us -> 16.6 us
    all_to_all x2 -> x3, waiting for transfers between devices: 19.8 us -> 20 us  [gathered_copies(): return lax.all_to_all(copies, axis, 0, 0, tiled=True)]
  transfers between devices with their start and end apart: 15 -> 16, of which waited for: 8 -> 9; matrix products, arithmetic and copies ran while one was open for 32% -> 27% of each run, Pallas kernels for 0% -> 0%
where the time goes in v9:
time: 194 us; the launch traced here: 192 us
  waiting for transfers between devices  67 us (35%)
  starting transfers between devices  53.6 us (28%)
  matrix products  30.6 us (16%)
  local copies, waits for them, and re-layouts  24.5 us (13%)
  other arithmetic  15.3 us (8%)
    all_to_all x3, starting transfers between devices, gathered_copies(): return lax.all_to_all(copies, axis, 0, 0, tiled=True)  24.3 us
    ppermute x4, waiting for transfers between devices, passed_along(): return lax.ppermute(array, axis, pairs)  20.2 us
    all_to_all x3, waiting for transfers between devices, gathered_copies(): return lax.all_to_all(copies, axis, 0, 0, tiled=True)  20 us
    ppermute x3, waiting for transfers between devices, spread_weight(): ring.append(lax.ppermute(held, 'dp', pairs))  19.8 us
    unnamed x77, local copies, waits for them, and re-layouts  16.6 us
    ppermute x4, starting transfers between devices, passed_along(): return lax.ppermute(array, axis, pairs)  13.6 us
    ppermute x2, starting transfers between devices, with_halo(): lax.ppermute(tail, axis, [(i, (i + 1) % count) for i in range(ends)])  8.62 us
    ppermute x1, waiting for transfers between devices, spread_weight(): lax.ppermute(weight, ('dp', 'seq'), partner_pairs)  6.96 us
  transfers between devices with their start and end apart: 16, of which 9 were waited for; matrix products, arithmetic and copies ran while one was open for 27% of the time, Pallas kernels for 0%

profile of v9, /device:TPU:26, one launch (start us, length us, event | category | flops | bytes accessed | tf_op | source)
XLA Modules:
  0.0 192.2 jit_solution(301877427676227716)
XLA Ops:
  1.8 3.8 %collective-permute-start.4 = (bf16[128,512]{0,1:T(8,128)(2,1)S(1)}, bf16[128,512]{0,1:T(8,128)(2,1)S(1)}, u32[]{:S(2)}, u32[]{:S(2)}) collective-permute-start(bf16[128,512]{0,1:T(8,128)(2,1)S(1)} %bitcast.323), channel_id=1, source_target_pairs={{0,1},{1,2},{2,3},{3,4},{4,5},{5,6},{6,7},{7,8},{8,9},{9,10},{10,1... | collective-permute-start | bytes 393224 | tf_op jit(solution)/shard_map/ppermute | solution.py:17
  10.0 7.0 %collective-permute-done = bf16[320,512]{1,0:T(8,128)(2,1)S(1)} collective-permute-done((bf16[320,512]{1,0:T(8,128)(2,1)}, bf16[320,512]{1,0:T(8,128)(2,1)S(1)}, u32[]{:S(2)}, u32[]{:S(2)}) %collective-permute-start) | collective-permute-done | bytes 327712 | tf_op jit(solution)/shard_map/ppermute | solution.py:44
  19.1 2.6 %collective-permute-start.2 = (bf16[2,320,512]{2,1,0:T(8,128)(2,1)}, bf16[2,320,512]{2,1,0:T(8,128)(2,1)S(1)}, u32[]{:S(2)}, u32[]{:S(2)}) collective-permute-start(bf16[2,320,512]{2,1,0:T(8,128)(2,1)} %get-tuple-element.37), channel_id=1, source_target_pairs={{0,64},{16,80},{32,96},{48,112},{64,0},{80,16},{96,32},{112,48},{1... | collective-permute-start | bytes 1966088 | tf_op jit(solution)/shard_map/ppermute | solution.py:51
  24.0 2.2 %copy.92 = bf16[1,128,2560]{1,2,0:T(8,128)(2,1)} copy(bf16[1,128,2560]{2,1,0:T(8,128)(2,1)} %param.8) | data formatting | bytes 1310720 | tf_op args[1]
  26.1 2.2 %copy.94 = bf16[1,128,2560]{1,2,0:T(8,128)(2,1)} copy(bf16[1,128,2560]{2,1,0:T(8,128)(2,1)} %param.10) | data formatting | bytes 1310720 | tf_op args[3]
  30.1 6.7 %collective-permute-done.1 = bf16[2,320,512]{2,1,0:T(8,128)(2,1)S(1)} collective-permute-done((bf16[2,320,512]{2,1,0:T(8,128)(2,1)}, bf16[2,320,512]{2,1,0:T(8,128)(2,1)S(1)}, u32[]{:S(2)}, u32[]{:S(2)}) %collective-permute-start.1) | collective-permute-done | bytes 655392 | tf_op jit(solution)/shard_map/ppermute | solution.py:51
  38.5 11.4 %collective-permute-done.3 = bf16[2,320,512]{2,1,0:T(8,128)(2,1)} collective-permute-done((bf16[2,320,512]{2,1,0:T(8,128)(2,1)}, bf16[2,320,512]{2,1,0:T(8,128)(2,1)}, u32[]{:S(2)}, u32[]{:S(2)}) %collective-permute-start.3) | collective-permute-done | bytes 655392 | tf_op jit(solution)/shard_map/ppermute | solution.py:51
  49.9 2.9 %pad_maximum_fusion.1 = bf16[4,2,320,512]{3,2,1,0:T(8,128)(2,1)} fusion(bf16[1,2,320,512]{3,2,1,0:T(8,128)(2,1)} %bitcast.5, bf16[1,2,320,512]{3,2,1,0:T(8,128)(2,1)S(1)} %bitcast.306, bf16[1,2,320,512]{3,2,1,0:T(8,128)(2,1)S(1)} %bitcast.305, bf16[1,2,320,512]{3,2,1,0:T(8,128)(2,1)S(1)} %get-tuple-element.36), kind=kLoop, calls=%fused_computation.8 | loop fusion | flops 3932160 | bytes 5242880 | tf_op jit(solution)/shard_map/stack | solution.py:52
  52.8 8.4 %all-to-all-start = ((bf16[16,128,320]{1,2,0:T(8,128)(2,1)}), bf16[16,128,320]{1,2,0:T(8,128)(2,1)S(1)}, u32[]{:S(2)}, u32[]{:S(2)}) async-start(bf16[16,128,320]{1,2,0:T(8,128)(2,1)} %bitcast.8), calls=%async_computation | async-start | bytes 2621440 | tf_op jit(solution)/shard_map/all_to_all | solution.py:69
  69.4 2.2 %convolution_bitcast_fusion.5 = f32[384,128]{0,1:T(8,128)} fusion(bf16[128,4,5,128]{0,3,2,1:T(8,128)(2,1)S(1)} %bitcast.317, f32[5,128,384]{1,2,0:T(8,128)} %get-tuple-element.45, f32[5,128]{1,0:T(8,128)S(1)} %get-tuple-element.44), kind=kOutput, calls=%fused_computation.52 | convolution fusion | flops 63406080 | bytes 1347584 | tf_op jit(solution)/shard_map/gqk,qgd->kd/dot_general | solution.py:116
  74.7 6.0 %all-to-all-done = bf16[16,128,320]{1,2,0:T(8,128)(2,1)S(1)} async-done(((bf16[16,128,320]{1,2,0:T(8,128)(2,1)}), bf16[16,128,320]{1,2,0:T(8,128)(2,1)S(1)}, u32[]{:S(2)}, u32[]{:S(2)}) %all-to-all-start) | async-done | bytes 1310752 | tf_op jit(solution)/shard_map/all_to_all | solution.py:69
  83.6 4.8 %collective-permute-start.7 = (f32[128,512]{0,1:T(8,128)}, f32[128,512]{0,1:T(8,128)}, u32[]{:S(2)}, u32[]{:S(2)}) collective-permute-start(f32[128,512]{0,1:T(8,128)} %get-tuple-element.35), channel_id=1, source_target_pairs={{0,1},{1,2},{2,3},{3,4},{4,5},{5,6},{6,7},{7,8},{8,9},{9,10},{10,1... | collective-permute-start | bytes 786440 | tf_op jit(solution)/shard_map/ppermute | solution.py:82
  93.4 5.5 %collective-permute-done.7 = f32[128,512]{0,1:T(8,128)} collective-permute-done((f32[128,512]{0,1:T(8,128)}, f32[128,512]{0,1:T(8,128)}, u32[]{:S(2)}, u32[]{:S(2)}) %collective-permute-start.7) | collective-permute-done | bytes 262176 | tf_op jit(solution)/shard_map/ppermute | solution.py:82
  100.0 3.0 %pad_maximum_fusion = bf16[2,4,2,320,512]{4,3,2,1,0:T(8,128)(2,1)S(1)} fusion(bf16[1,4,2,320,512]{4,3,2,1,0:T(8,128)(2,1)} %bitcast.42, bf16[1,4,2,320,512]{4,3,2,1,0:T(8,128)(2,1)} %bitcast.41), kind=kLoop, calls=%fused_computation.7 | loop fusion | flops 2621440 | bytes 10485760 | tf_op jit(solution)/shard_map/stack | solution.py:54
  107.2 4.8 %collective-permute-start.9 = (bf16[128,512]{1,0:T(8,128)(2,1)S(1)}, bf16[128,512]{1,0:T(8,128)(2,1)S(1)}, u32[]{:S(2)}, u32[]{:S(2)}) collective-permute-start(bf16[128,512]{1,0:T(8,128)(2,1)S(1)} %fusion.38), channel_id=1, source_target_pairs={{0,1},{1,2},{2,3},{3,4},{4,5},{5,6},{6,7},{7,8},{8,9},{9,10},{10,1... | collective-permute-start | bytes 393224 | tf_op jit(solution)/shard_map/ppermute | solution.py:17
  113.8 4.9 %all-to-all-start.1 = ((bf16[16,128,512]{1,2,0:T(8,128)(2,1)}), bf16[16,128,512]{1,2,0:T(8,128)(2,1)}, u32[]{:S(2)}, u32[]{:S(2)}) async-start(bf16[16,128,512]{1,2,0:T(8,128)(2,1)} %broadcast_in_dim.114), calls=%async_computation.1 | async-start | bytes 4194304 | tf_op jit(solution)/shard_map/all_to_all | solution.py:69
  118.8 4.3 %convolution_convert_fusion = bf16[128,5120]{1,0:T(8,128)(2,1)S(1)} fusion(bf16[128,512]{0,1:T(8,128)(2,1)S(1)} %add_convert_fusion, bf16[5120,512]{1,0:T(8,128)(2,1)} %bitcast.301), kind=kOutput, calls=%fused_computation.6 | convolution fusion | flops 671744000 | bytes 6684672 | tf_op jit(solution)/shard_map/dot_general | solution.py:213
  136.0 14.0 %all-to-all-done.1 = bf16[16,128,512]{1,2,0:T(8,128)(2,1)} async-done(((bf16[16,128,512]{1,2,0:T(8,128)(2,1)}), bf16[16,128,512]{1,2,0:T(8,128)(2,1)}, u32[]{:S(2)}, u32[]{:S(2)}) %all-to-all-start.1) | async-done | bytes 2097184 | tf_op jit(solution)/shard_map/all_to_all | solution.py:69
  150.0 3.7 %fusion.28 = f32[16,320,32]{1,2,0:T(8,128)} fusion(bf16[16,128,16,32]{1,3,2,0:T(8,128)(2,1)} %bitcast.78, bf16[16,128,320]{1,2,0:T(8,128)(2,1)S(1)} %copy-done.3), kind=kOutput, calls=%fused_computation.41 | convolution fusion | flops 671088640 | bytes 4063232 | tf_op jit(solution)/shard_map/rtk,rtjc->jkc/dot_general | solution.py:198
  153.7 11.0 %all-to-all-start.2 = ((f32[16,320,32]{1,2,0:T(8,128)}), f32[16,320,32]{1,2,0:T(8,128)S(1)}, u32[]{:S(2)}, u32[]{:S(2)}) async-start(f32[16,320,32]{1,2,0:T(8,128)} %fusion.28), calls=%async_computation.2 | async-start | bytes 1572864 | tf_op jit(solution)/shard_map/all_to_all | solution.py:69
  164.7 2.1 %collective-permute-start.11 = (f32[128,512]{0,1:T(8,128)S(1)}, f32[128,512]{0,1:T(8,128)S(1)}, u32[]{:S(2)}, u32[]{:S(2)}) collective-permute-start(f32[128,512]{0,1:T(8,128)S(1)} %get-tuple-element.32), channel_id=1, source_target_pairs={{1,0},{2,1},{3,2},{4,3},{5,4},{6,5},{7,6},{8,7},{9,8},{10,9},{11,1... | collective-permute-start | bytes 786440 | tf_op jit(solution)/shard_map/ppermute | solution.py:82
  166.9 4.7 %collective-permute-start.12 = (f32[128,512]{0,1:T(8,128)S(1)}, f32[128,512]{0,1:T(8,128)S(1)}, u32[]{:S(2)}, u32[]{:S(2)}) collective-permute-start(f32[128,512]{0,1:T(8,128)S(1)} %get-tuple-element.33), channel_id=1, source_target_pairs={{0,1},{1,2},{2,3},{3,4},{4,5},{5,6},{6,7},{7,8},{8,9},{9,10},{10,1... | collective-permute-start | bytes 786440 | tf_op jit(solution)/shard_map/ppermute | solution.py:82
  171.6 2.2 %fusion.47 = bf16[128,1,5,128]{0,3,2,1:T(8,128)(2,1)S(1)} fusion(f32[5,128,384]{1,2,0:T(8,128)} %copy-done.24, f32[5,128]{1,0:T(8,128)S(1)} %copy-done.34, bf16[384,4,128]{0,2,1:T(8,128)(2,1)S(1)} %bitcast.331, f32[5,128,384]{1,2,0:T(8,128)} %get-tuple-element.47, f32[5,128]{1,0:T(8,128)S(1)} %get-tuple-element.46), kind=kOutput, calls=%fused_computation.66 | convolution fusion | flops 378388480 | bytes 2236416 | tf_op jit(solution)/shard_map/gqk,kd->qgd/dot_general | solution.py:145
  177.4 13.3 %collective-permute-done.11 = f32[128,512]{0,1:T(8,128)S(1)} collective-permute-done((f32[128,512]{0,1:T(8,128)S(1)}, f32[128,512]{0,1:T(8,128)S(1)}, u32[]{:S(2)}, u32[]{:S(2)}) %collective-permute-start.11) | collective-permute-done | bytes 262176 | tf_op jit(solution)/shard_map/ppermute | solution.py:82
  (144 shorter events, 57.3 us)
Async XLA Ops:
  0.6 21.9 %copy-start.1 = (bf16[1,128,5120]{2,1,0:T(8,128)(2,1)S(1)}, bf16[1,128,5120]{2,1,0:T(8,128)(2,1)}, u32[]{:S(2)}) copy-start(bf16[1,128,5120]{2,1,0:T(8,128)(2,1)} %param.7) | copy-start | bytes 3932164
  1.8 26.5 %collective-permute-start.4 = (bf16[128,512]{0,1:T(8,128)(2,1)S(1)}, bf16[128,512]{0,1:T(8,128)(2,1)S(1)}, u32[]{:S(2)}, u32[]{:S(2)}) collective-permute-start(bf16[128,512]{0,1:T(8,128)(2,1)S(1)} %bitcast.323), channel_id=1, source_target_pairs={{0,1},{1,2},{2,3},{3,4},{4,5},{5,6},{6,7},{7,8},{8,9},{9,10},{10,1... | collective-permute-start | bytes 393224 | tf_op jit(solution)/shard_map/ppermute | solution.py:17
  5.6 22.7 %collective-permute-start.5 = (bf16[128,512]{0,1:T(8,128)(2,1)S(1)}, bf16[128,512]{0,1:T(8,128)(2,1)}, u32[]{:S(2)}, u32[]{:S(2)}) collective-permute-start(bf16[128,512]{0,1:T(8,128)(2,1)S(1)} %bitcast.324), channel_id=1, source_target_pairs={{1,0},{2,1},{3,2},{4,3},{5,4},{6,5},{7,6},{8,7},{9,8},{10,9},{11,1... | collective-permute-start | bytes 393224 | tf_op jit(solution)/shard_map/ppermute | solution.py:19
  7.6 9.3 %collective-permute-start = (bf16[320,512]{1,0:T(8,128)(2,1)}, bf16[320,512]{1,0:T(8,128)(2,1)S(1)}, u32[]{:S(2)}, u32[]{:S(2)}) collective-permute-start(bf16[320,512]{1,0:T(8,128)(2,1)} %param.11), channel_id=1, source_target_pairs={{0,129},{1,128},{2,131},{3,130},{4,133},{5,132},{6,135},{7,134},{8... | collective-permute-start | bytes 983048 | tf_op jit(solution)/shard_map/ppermute | solution.py:44
  18.9 17.9 %collective-permute-start.1 = (bf16[2,320,512]{2,1,0:T(8,128)(2,1)}, bf16[2,320,512]{2,1,0:T(8,128)(2,1)S(1)}, u32[]{:S(2)}, u32[]{:S(2)}) collective-permute-start(bf16[2,320,512]{2,1,0:T(8,128)(2,1)} %get-tuple-element.37), channel_id=1, source_target_pairs={{0,32},{16,48},{32,64},{48,80},{64,96},{80,112},{96,0},{112,16},{1... | collective-permute-start | bytes 1966088 | tf_op jit(solution)/shard_map/ppermute | solution.py:51
  19.1 19.4 %collective-permute-start.2 = (bf16[2,320,512]{2,1,0:T(8,128)(2,1)}, bf16[2,320,512]{2,1,0:T(8,128)(2,1)S(1)}, u32[]{:S(2)}, u32[]{:S(2)}) collective-permute-start(bf16[2,320,512]{2,1,0:T(8,128)(2,1)} %get-tuple-element.37), channel_id=1, source_target_pairs={{0,64},{16,80},{32,96},{48,112},{64,0},{80,16},{96,32},{112,48},{1... | collective-permute-start | bytes 1966088 | tf_op jit(solution)/shard_map/ppermute | solution.py:51
  21.7 28.2 %collective-permute-start.3 = (bf16[2,320,512]{2,1,0:T(8,128)(2,1)}, bf16[2,320,512]{2,1,0:T(8,128)(2,1)}, u32[]{:S(2)}, u32[]{:S(2)}) collective-permute-start(bf16[2,320,512]{2,1,0:T(8,128)(2,1)} %get-tuple-element.37), channel_id=1, source_target_pairs={{0,96},{16,112},{32,0},{48,16},{64,32},{80,48},{96,64},{112,80},{1... | collective-permute-start | bytes 1966088 | tf_op jit(solution)/shard_map/ppermute | solution.py:51
  52.8 10.0 %copy-start.6 = (bf16[1,128,2560]{1,2,0:T(8,128)(2,1)S(1)}, bf16[1,128,2560]{1,2,0:T(8,128)(2,1)}, u32[]{:S(2)}) copy-start(bf16[1,128,2560]{1,2,0:T(8,128)(2,1)} %copy.94) | copy-start | bytes 1966084
  52.8 27.9 %all-to-all-start = ((bf16[16,128,320]{1,2,0:T(8,128)(2,1)}), bf16[16,128,320]{1,2,0:T(8,128)(2,1)S(1)}, u32[]{:S(2)}, u32[]{:S(2)}) async-start(bf16[16,128,320]{1,2,0:T(8,128)(2,1)} %bitcast.8), calls=%async_computation | async-start | bytes 2621440 | tf_op jit(solution)/shard_map/all_to_all | solution.py:69
  61.2 38.8 %collective-permute-start.8 = (bf16[4,2,320,512]{3,2,1,0:T(8,128)(2,1)}, bf16[4,2,320,512]{3,2,1,0:T(8,128)(2,1)}, u32[]{:S(2)}, u32[]{:S(2)}) collective-permute-start(bf16[4,2,320,512]{3,2,1,0:T(8,128)(2,1)} %pad_maximum_fusion.1), channel_id=1, source_target_pairs={{0,16},{16,0},{32,48},{48,32},{64,80},{80,64},{96,112},{112,96},{1... | collective-permute-start | bytes 7864328 | tf_op jit(solution)/shard_map/ppermute | solution.py:53
  80.7 9.1 %copy-start.2 = (bf16[16,128,320]{1,2,0:T(8,128)(2,1)}, bf16[16,128,320]{1,2,0:T(8,128)(2,1)S(1)}, u32[]{:S(2)}) copy-start(bf16[16,128,320]{1,2,0:T(8,128)(2,1)S(1)} %all-to-all-done) | copy-start | bytes 3932164
  81.7 11.7 %collective-permute-start.6 = (f32[128,512]{0,1:T(8,128)}, f32[128,512]{0,1:T(8,128)}, u32[]{:S(2)}, u32[]{:S(2)}) collective-permute-start(f32[128,512]{0,1:T(8,128)} %get-tuple-element.34), channel_id=1, source_target_pairs={{1,0},{2,1},{3,2},{4,3},{5,4},{6,5},{7,6},{8,7},{9,8},{10,9},{11,1... | collective-permute-start | bytes 786440 | tf_op jit(solution)/shard_map/ppermute | solution.py:82
  83.6 15.3 %collective-permute-start.7 = (f32[128,512]{0,1:T(8,128)}, f32[128,512]{0,1:T(8,128)}, u32[]{:S(2)}, u32[]{:S(2)}) collective-permute-start(f32[128,512]{0,1:T(8,128)} %get-tuple-element.35), channel_id=1, source_target_pairs={{0,1},{1,2},{2,3},{3,4},{4,5},{5,6},{6,7},{7,8},{8,9},{9,10},{10,1... | collective-permute-start | bytes 786440 | tf_op jit(solution)/shard_map/ppermute | solution.py:82
  105.3 20.9 %collective-permute-start.10 = (bf16[128,512]{1,0:T(8,128)(2,1)S(1)}, bf16[128,512]{1,0:T(8,128)(2,1)S(1)}, u32[]{:S(2)}, u32[]{:S(2)}) collective-permute-start(bf16[128,512]{1,0:T(8,128)(2,1)S(1)} %fusion.38), channel_id=1, source_target_pairs={{1,0},{2,1},{3,2},{4,3},{5,4},{6,5},{7,6},{8,7},{9,8},{10,9},{11,1... | collective-permute-start | bytes 393224 | tf_op jit(solution)/shard_map/ppermute | solution.py:19
  107.2 19.0 %collective-permute-start.9 = (bf16[128,512]{1,0:T(8,128)(2,1)S(1)}, bf16[128,512]{1,0:T(8,128)(2,1)S(1)}, u32[]{:S(2)}, u32[]{:S(2)}) collective-permute-start(bf16[128,512]{1,0:T(8,128)(2,1)S(1)} %fusion.38), channel_id=1, source_target_pairs={{0,1},{1,2},{2,3},{3,4},{4,5},{5,6},{6,7},{7,8},{8,9},{9,10},{10,1... | collective-permute-start | bytes 393224 | tf_op jit(solution)/shard_map/ppermute | solution.py:17
  113.8 36.1 %all-to-all-start.1 = ((bf16[16,128,512]{1,2,0:T(8,128)(2,1)}), bf16[16,128,512]{1,2,0:T(8,128)(2,1)}, u32[]{:S(2)}, u32[]{:S(2)}) async-start(bf16[16,128,512]{1,2,0:T(8,128)(2,1)} %broadcast_in_dim.114), calls=%async_computation.1 | async-start | bytes 4194304 | tf_op jit(solution)/shard_map/all_to_all | solution.py:69
  134.6 15.4 %copy-start.3 = (bf16[16,128,320]{1,2,0:T(8,128)(2,1)S(1)}, bf16[16,128,320]{1,2,0:T(8,128)(2,1)}, u32[]{:S(2)}) copy-start(bf16[16,128,320]{1,2,0:T(8,128)(2,1)} %copy-done.2) | copy-start | bytes 3932164
  153.7 17.9 %copy-start.34 = (f32[5,128]{1,0:T(8,128)S(1)}, f32[5,128]{1,0:T(8,128)}, u32[]{:S(2)}) copy-start(f32[5,128]{1,0:T(8,128)} %copy-done.33) | copy-start | bytes 7684
  153.7 37.8 %all-to-all-start.2 = ((f32[16,320,32]{1,2,0:T(8,128)}), f32[16,320,32]{1,2,0:T(8,128)S(1)}, u32[]{:S(2)}, u32[]{:S(2)}) async-start(f32[16,320,32]{1,2,0:T(8,128)} %fusion.28), calls=%async_computation.2 | async-start | bytes 1572864 | tf_op jit(solution)/shard_map/all_to_all | solution.py:69
  164.7 9.1 %copy-start.17 = (f32[5,128,384]{1,2,0:T(8,128)S(1)}, f32[5,128,384]{1,2,0:T(8,128)}, u32[]{:S(2)}) copy-start(f32[5,128,384]{1,2,0:T(8,128)} %get-tuple-element.45) | copy-start | bytes 2949124
  164.7 9.1 %copy-start.23 = (f32[5,128,384]{1,2,0:T(8,128)S(1)}, f32[5,128,384]{1,2,0:T(8,128)}, u32[]{:S(2)}) copy-start(f32[5,128,384]{1,2,0:T(8,128)} %copy-done.22) | copy-start | bytes 2949124
  164.7 9.1 %copy-start.32 = (f32[5,128]{1,0:T(8,128)S(1)}, f32[5,128]{1,0:T(8,128)}, u32[]{:S(2)}) copy-start(f32[5,128]{1,0:T(8,128)} %copy-done.31) | copy-start | bytes 7684
  164.7 26.0 %collective-permute-start.11 = (f32[128,512]{0,1:T(8,128)S(1)}, f32[128,512]{0,1:T(8,128)S(1)}, u32[]{:S(2)}, u32[]{:S(2)}) collective-permute-start(f32[128,512]{0,1:T(8,128)S(1)} %get-tuple-element.32), channel_id=1, source_target_pairs={{1,0},{2,1},{3,2},{4,3},{5,4},{6,5},{7,6},{8,7},{9,8},{10,9},{11,1... | collective-permute-start | bytes 786440 | tf_op jit(solution)/shard_map/ppermute | solution.py:82
  166.9 23.8 %collective-permute-start.12 = (f32[128,512]{0,1:T(8,128)S(1)}, f32[128,512]{0,1:T(8,128)S(1)}, u32[]{:S(2)}, u32[]{:S(2)}) collective-permute-start(f32[128,512]{0,1:T(8,128)S(1)} %get-tuple-element.33), channel_id=1, source_target_pairs={{0,1},{1,2},{2,3},{3,4},{4,5},{5,6},{6,7},{7,8},{8,9},{9,10},{10,1... | collective-permute-start | bytes 786440 | tf_op jit(solution)/shard_map/ppermute | solution.py:82
  (27 other events, 69.6 us)

commit v10 on v9

--- a/solution.py
+++ b/solution.py
@@ -198,9 +198,6 @@
     own_pieces = jnp.einsum(
         "rtk,rtjc->jkc", input_blocks, grad_rows, preferred_element_type=jnp.float32
     )
-    summed = jnp.sum(gathered_copies(own_pieces, "seq"), axis=0)
-    devices_all = lax.axis_size("dp") * lax.axis_size("seq")
-    weight_grad = summed / devices_all
     input_slots = jnp.take(
         layer_rows.reshape(tok_count, dp_count, -1), slot_owner, axis=1, mode="clip"
     ).reshape(tok_count, -1)
@@ -210,6 +207,10 @@
         query_states[0], key_block, value_block, out_grad[0], attentions
     )
     key_grad = rim_sum(key_part, tok_count).astype(jnp.bfloat16)
+    key_grad, own_pieces = lax.optimization_barrier((key_grad, own_pieces))
+    summed = jnp.sum(gathered_copies(own_pieces, "seq"), axis=0)
+    devices_all = lax.axis_size("dp") * lax.axis_size("seq")
+    weight_grad = summed / devices_all
     grad_slots = lax.dot_general(
         value_grad,
         weight_full,

time: 194 us -> 196 us (1.010)
  the two profiles are of different devices: /device:TPU:26 before, /device:TPU:8 now
where the time goes in v10:
time: 196 us; the launch traced here: 195 us
  waiting for transfers between devices  62.8 us (32%)
  starting transfers between devices  59.1 us (30%)
  matrix products  31.2 us (16%)
  local copies, waits for them, and re-layouts  24.3 us (12%)
  other arithmetic  16 us (8%)
    ppermute x4, waiting for transfers between devices, passed_along(): return lax.ppermute(array, axis, pairs)  29.4 us
    all_to_all x3, starting transfers between devices, gathered_copies(): return lax.all_to_all(copies, axis, 0, 0, tiled=True)  27.1 us
    ppermute x3, waiting for transfers between devices, spread_weight(): ring.append(lax.ppermute(held, 'dp', pairs))  18 us
    unnamed x91, local copies, waits for them, and re-layouts  15.8 us
    ppermute x4, starting transfers between devices, passed_along(): return lax.ppermute(array, axis, pairs)  11 us
    all_to_all x3, waiting for transfers between devices, gathered_copies(): return lax.all_to_all(copies, axis, 0, 0, tiled=True)  10.2 us
    ppermute x2, starting transfers between devices, with_halo(): lax.ppermute(tail, axis, [(i, (i + 1) % count) for i in range(ends)])  10.2 us
    dot_general x4, matrix products, attend_first(): jnp.einsum('gqk,qgd->kd', attention_low, grad_head, preferred_element_typ...  6.73 us
  transfers between devices with their start and end apart: 16, of which 8 were waited for; matrix products, arithmetic and copies ran while one was open for 28% of the time, Pallas kernels for 0%

profile of v10, /device:TPU:8, one launch (start us, length us, event | category | flops | bytes accessed | tf_op | source)
XLA Modules:
  0.0 194.8 jit_solution(2795402049610001287)
XLA Ops:
  3.1 5.2 %collective-permute-start.4 = (bf16[128,512]{0,1:T(8,128)(2,1)S(1)}, bf16[128,512]{0,1:T(8,128)(2,1)}, u32[]{:S(2)}, u32[]{:S(2)}) collective-permute-start(bf16[128,512]{0,1:T(8,128)(2,1)S(1)} %bitcast.325), channel_id=1, source_target_pairs={{0,1},{1,2},{2,3},{3,4},{4,5},{5,6},{6,7},{7,8},{8,9},{9,10},{10,1... | collective-permute-start | bytes 393224 | tf_op jit(solution)/shard_map/ppermute | solution.py:17
  8.3 3.1 %collective-permute-start = (bf16[320,512]{1,0:T(8,128)(2,1)}, bf16[320,512]{1,0:T(8,128)(2,1)S(1)}, u32[]{:S(2)}, u32[]{:S(2)}) collective-permute-start(bf16[320,512]{1,0:T(8,128)(2,1)} %param.11), channel_id=1, source_target_pairs={{0,129},{1,128},{2,131},{3,130},{4,133},{5,132},{6,135},{7,134},{8... | collective-permute-start | bytes 983048 | tf_op jit(solution)/shard_map/ppermute | solution.py:44
  13.6 5.1 %collective-permute-done = bf16[320,512]{1,0:T(8,128)(2,1)S(1)} collective-permute-done((bf16[320,512]{1,0:T(8,128)(2,1)}, bf16[320,512]{1,0:T(8,128)(2,1)S(1)}, u32[]{:S(2)}, u32[]{:S(2)}) %collective-permute-start) | collective-permute-done | bytes 327712 | tf_op jit(solution)/shard_map/ppermute | solution.py:44
  21.1 2.6 %collective-permute-start.2 = (bf16[2,320,512]{2,1,0:T(8,128)(2,1)}, bf16[2,320,512]{2,1,0:T(8,128)(2,1)S(1)}, u32[]{:S(2)}, u32[]{:S(2)}) collective-permute-start(bf16[2,320,512]{2,1,0:T(8,128)(2,1)} %get-tuple-element.41), channel_id=1, source_target_pairs={{0,64},{16,80},{32,96},{48,112},{64,0},{80,16},{96,32},{112,48},{1... | collective-permute-start | bytes 1966088 | tf_op jit(solution)/shard_map/ppermute | solution.py:51
  26.4 2.2 %copy.92 = bf16[1,128,2560]{1,2,0:T(8,128)(2,1)} copy(bf16[1,128,2560]{2,1,0:T(8,128)(2,1)} %param.8) | data formatting | bytes 1310720 | tf_op args[1]
  30.0 2.2 %copy.94 = bf16[1,128,2560]{1,2,0:T(8,128)(2,1)} copy(bf16[1,128,2560]{2,1,0:T(8,128)(2,1)} %param.10) | data formatting | bytes 1310720 | tf_op args[3]
  34.0 3.5 %collective-permute-done.3 = bf16[2,320,512]{2,1,0:T(8,128)(2,1)S(1)} collective-permute-done((bf16[2,320,512]{2,1,0:T(8,128)(2,1)}, bf16[2,320,512]{2,1,0:T(8,128)(2,1)S(1)}, u32[]{:S(2)}, u32[]{:S(2)}) %collective-permute-start.3) | collective-permute-done | bytes 655392 | tf_op jit(solution)/shard_map/ppermute | solution.py:51
  37.5 13.5 %collective-permute-done.2 = bf16[2,320,512]{2,1,0:T(8,128)(2,1)S(1)} collective-permute-done((bf16[2,320,512]{2,1,0:T(8,128)(2,1)}, bf16[2,320,512]{2,1,0:T(8,128)(2,1)S(1)}, u32[]{:S(2)}, u32[]{:S(2)}) %collective-permute-start.2) | collective-permute-done | bytes 655392 | tf_op jit(solution)/shard_map/ppermute | solution.py:51
  52.0 2.9 %pad_maximum_fusion.1 = bf16[4,2,320,512]{3,2,1,0:T(8,128)(2,1)} fusion(bf16[1,2,320,512]{3,2,1,0:T(8,128)(2,1)S(1)} %bitcast.305, bf16[1,2,320,512]{3,2,1,0:T(8,128)(2,1)S(1)} %bitcast.306, bf16[1,2,320,512]{3,2,1,0:T(8,128)(2,1)} %bitcast.3, bf16[1,2,320,512]{3,2,1,0:T(8,128)(2,1)S(1)} %get-tuple-element.40), kind=kLoop, calls=%fused_computation.8 | loop fusion | flops 3932160 | bytes 5242880 | tf_op jit(solution)/shard_map/stack | solution.py:52
  54.9 6.5 %all-to-all-start = ((bf16[16,128,320]{1,2,0:T(8,128)(2,1)}), bf16[16,128,320]{1,2,0:T(8,128)(2,1)S(1)}, u32[]{:S(2)}, u32[]{:S(2)}) async-start(bf16[16,128,320]{1,2,0:T(8,128)(2,1)} %bitcast.8), calls=%async_computation | async-start | bytes 2621440 | tf_op jit(solution)/shard_map/all_to_all | solution.py:69
  69.1 2.2 %convolution_bitcast_fusion.6 = f32[384,128]{0,1:T(8,128)} fusion(bf16[128,4,5,128]{0,3,2,1:T(8,128)(2,1)S(1)} %bitcast.318, f32[5,128,384]{1,2,0:T(8,128)} %get-tuple-element.51, f32[5,128]{1,0:T(8,128)S(1)} %get-tuple-element.50), kind=kOutput, calls=%fused_computation.53 | convolution fusion | flops 63406080 | bytes 1347584 | tf_op jit(solution)/shard_map/gqk,qgd->kd/dot_general | solution.py:116
  74.4 3.0 %all-to-all-done = bf16[16,128,320]{1,2,0:T(8,128)(2,1)S(1)} async-done(((bf16[16,128,320]{1,2,0:T(8,128)(2,1)}), bf16[16,128,320]{1,2,0:T(8,128)(2,1)S(1)}, u32[]{:S(2)}, u32[]{:S(2)}) %all-to-all-start) | async-done | bytes 1310752 | tf_op jit(solution)/shard_map/all_to_all | solution.py:69
  78.3 4.0 %collective-permute-start.7 = (f32[128,512]{0,1:T(8,128)}, f32[128,512]{0,1:T(8,128)}, u32[]{:S(2)}, u32[]{:S(2)}) collective-permute-start(f32[128,512]{0,1:T(8,128)} %get-tuple-element.39), channel_id=1, source_target_pairs={{0,1},{1,2},{2,3},{3,4},{4,5},{5,6},{6,7},{7,8},{8,9},{9,10},{10,1... | collective-permute-start | bytes 786440 | tf_op jit(solution)/shard_map/ppermute | solution.py:82
  85.9 8.0 %collective-permute-done.7 = f32[128,512]{0,1:T(8,128)} collective-permute-done((f32[128,512]{0,1:T(8,128)}, f32[128,512]{0,1:T(8,128)}, u32[]{:S(2)}, u32[]{:S(2)}) %collective-permute-start.7) | collective-permute-done | bytes 262176 | tf_op jit(solution)/shard_map/ppermute | solution.py:82
  95.0 3.0 %pad_maximum_fusion = bf16[2,4,2,320,512]{4,3,2,1,0:T(8,128)(2,1)S(1)} fusion(bf16[1,4,2,320,512]{4,3,2,1,0:T(8,128)(2,1)} %bitcast.42, bf16[1,4,2,320,512]{4,3,2,1,0:T(8,128)(2,1)} %bitcast.41), kind=kLoop, calls=%fused_computation.7 | loop fusion | flops 2621440 | bytes 10485760 | tf_op jit(solution)/shard_map/stack | solution.py:54
  101.6 5.0 %collective-permute-start.9 = (bf16[128,512]{1,0:T(8,128)(2,1)S(1)}, bf16[128,512]{1,0:T(8,128)(2,1)S(1)}, u32[]{:S(2)}, u32[]{:S(2)}) collective-permute-start(bf16[128,512]{1,0:T(8,128)(2,1)S(1)} %fusion.38), channel_id=1, source_target_pairs={{0,1},{1,2},{2,3},{3,4},{4,5},{5,6},{6,7},{7,8},{8,9},{9,10},{10,1... | collective-permute-start | bytes 393224 | tf_op jit(solution)/shard_map/ppermute | solution.py:17
  108.4 8.3 %all-to-all-start.1 = ((bf16[16,128,512]{1,2,0:T(8,128)(2,1)}), bf16[16,128,512]{1,2,0:T(8,128)(2,1)S(1)}, u32[]{:S(2)}, u32[]{:S(2)}) async-start(bf16[16,128,512]{1,2,0:T(8,128)(2,1)} %broadcast_in_dim.112), calls=%async_computation.1 | async-start | bytes 4194304 | tf_op jit(solution)/shard_map/all_to_all | solution.py:69
  126.5 4.4 %collective-permute-start.12 = (f32[128,512]{0,1:T(8,128)}, f32[128,512]{0,1:T(8,128)S(1)}, u32[]{:S(2)}, u32[]{:S(2)}) collective-permute-start(f32[128,512]{0,1:T(8,128)} %get-tuple-element.37), channel_id=1, source_target_pairs={{0,1},{1,2},{2,3},{3,4},{4,5},{5,6},{6,7},{7,8},{8,9},{9,10},{10,1... | collective-permute-start | bytes 786440 | tf_op jit(solution)/shard_map/ppermute | solution.py:82
  133.5 21.4 %collective-permute-done.12 = f32[128,512]{0,1:T(8,128)S(1)} collective-permute-done((f32[128,512]{0,1:T(8,128)}, f32[128,512]{0,1:T(8,128)S(1)}, u32[]{:S(2)}, u32[]{:S(2)}) %collective-permute-start.12) | collective-permute-done | bytes 262176 | tf_op jit(solution)/shard_map/ppermute | solution.py:82
  155.6 3.5 %fusion.28 = f32[16,320,32]{1,2,0:T(8,128)} fusion(bf16[16,128,16,32]{1,3,2,0:T(8,128)(2,1)S(1)} %bitcast.304, bf16[16,128,320]{1,2,0:T(8,128)(2,1)} %copy-done.2), kind=kOutput, calls=%fused_computation.41 | convolution fusion | flops 671088640 | bytes 4063232 | tf_op jit(solution)/shard_map/rtk,rtjc->jkc/dot_general | solution.py:198
  159.1 12.3 %all-to-all-start.2 = ((f32[16,320,32]{1,2,0:T(8,128)}), f32[16,320,32]{1,2,0:T(8,128)S(1)}, u32[]{:S(2)}, u32[]{:S(2)}) async-start(f32[16,320,32]{1,2,0:T(8,128)} %fusion.28), calls=%async_computation.2 | async-start | bytes 1572864 | tf_op jit(solution)/shard_map/all_to_all | solution.py:69
  171.4 4.3 %convolution_convert_fusion = bf16[128,5120]{1,0:T(8,128)(2,1)S(1)} fusion(bf16[128,512]{0,1:T(8,128)(2,1)S(1)} %add_convert_fusion, bf16[5120,512]{1,0:T(8,128)(2,1)} %bitcast.300), kind=kOutput, calls=%fused_computation.6 | convolution fusion | flops 671744000 | bytes 6684672 | tf_op jit(solution)/shard_map/dot_general | solution.py:214
  178.9 2.3 %fusion.45 = bf16[128,1,5,128]{0,3,2,1:T(8,128)(2,1)S(1)} fusion(f32[5,128,384]{1,2,0:T(8,128)} %copy-done.25, f32[5,128]{1,0:T(8,128)S(1)} %copy-done.41, bf16[384,4,128]{0,2,1:T(8,128)(2,1)S(1)} %bitcast.331, f32[5,128,384]{1,2,0:T(8,128)} %get-tuple-element.47, f32[5,128]{1,0:T(8,128)S(1)} %copy-done.27), kind=kOutput, calls=%fused_computation.64 | convolution fusion | flops 378388480 | bytes 2236416 | tf_op jit(solution)/shard_map/gqk,kd->qgd/dot_general | solution.py:145
  186.9 7.2 %all-to-all-done.2 = f32[16,320,32]{1,2,0:T(8,128)S(1)} async-done(((f32[16,320,32]{1,2,0:T(8,128)}), f32[16,320,32]{1,2,0:T(8,128)S(1)}, u32[]{:S(2)}, u32[]{:S(2)}) %all-to-all-start.2) | async-done | bytes 655392 | tf_op jit(solution)/shard_map/all_to_all | solution.py:69
  (158 shorter events, 57.5 us)
Async XLA Ops:
  0.6 28.0 %copy-start.1 = (bf16[1,128,5120]{2,1,0:T(8,128)(2,1)S(1)}, bf16[1,128,5120]{2,1,0:T(8,128)(2,1)}, u32[]{:S(2)}) copy-start(bf16[1,128,5120]{2,1,0:T(8,128)(2,1)} %param.7) | copy-start | bytes 3932164
  1.8 30.5 %collective-permute-start.5 = (bf16[128,512]{0,1:T(8,128)(2,1)S(1)}, bf16[128,512]{0,1:T(8,128)(2,1)S(1)}, u32[]{:S(2)}, u32[]{:S(2)}) collective-permute-start(bf16[128,512]{0,1:T(8,128)(2,1)S(1)} %bitcast.324), channel_id=1, source_target_pairs={{1,0},{2,1},{3,2},{4,3},{5,4},{6,5},{7,6},{8,7},{9,8},{10,9},{11,1... | collective-permute-start | bytes 393224 | tf_op jit(solution)/shard_map/ppermute | solution.py:19
  3.1 29.2 %collective-permute-start.4 = (bf16[128,512]{0,1:T(8,128)(2,1)S(1)}, bf16[128,512]{0,1:T(8,128)(2,1)}, u32[]{:S(2)}, u32[]{:S(2)}) collective-permute-start(bf16[128,512]{0,1:T(8,128)(2,1)S(1)} %bitcast.325), channel_id=1, source_target_pairs={{0,1},{1,2},{2,3},{3,4},{4,5},{5,6},{6,7},{7,8},{8,9},{9,10},{10,1... | collective-permute-start | bytes 393224 | tf_op jit(solution)/shard_map/ppermute | solution.py:17
  8.3 10.5 %collective-permute-start = (bf16[320,512]{1,0:T(8,128)(2,1)}, bf16[320,512]{1,0:T(8,128)(2,1)S(1)}, u32[]{:S(2)}, u32[]{:S(2)}) collective-permute-start(bf16[320,512]{1,0:T(8,128)(2,1)} %param.11), channel_id=1, source_target_pairs={{0,129},{1,128},{2,131},{3,130},{4,133},{5,132},{6,135},{7,134},{8... | collective-permute-start | bytes 983048 | tf_op jit(solution)/shard_map/ppermute | solution.py:44
  20.7 16.9 %collective-permute-start.3 = (bf16[2,320,512]{2,1,0:T(8,128)(2,1)}, bf16[2,320,512]{2,1,0:T(8,128)(2,1)S(1)}, u32[]{:S(2)}, u32[]{:S(2)}) collective-permute-start(bf16[2,320,512]{2,1,0:T(8,128)(2,1)} %get-tuple-element.41), channel_id=1, source_target_pairs={{0,96},{16,112},{32,0},{48,16},{64,32},{80,48},{96,64},{112,80},{1... | collective-permute-start | bytes 1966088 | tf_op jit(solution)/shard_map/ppermute | solution.py:51
  21.1 30.0 %collective-permute-start.2 = (bf16[2,320,512]{2,1,0:T(8,128)(2,1)}, bf16[2,320,512]{2,1,0:T(8,128)(2,1)S(1)}, u32[]{:S(2)}, u32[]{:S(2)}) collective-permute-start(bf16[2,320,512]{2,1,0:T(8,128)(2,1)} %get-tuple-element.41), channel_id=1, source_target_pairs={{0,64},{16,80},{32,96},{48,112},{64,0},{80,16},{96,32},{112,48},{1... | collective-permute-start | bytes 1966088 | tf_op jit(solution)/shard_map/ppermute | solution.py:51
  23.7 28.3 %collective-permute-start.1 = (bf16[2,320,512]{2,1,0:T(8,128)(2,1)}, bf16[2,320,512]{2,1,0:T(8,128)(2,1)}, u32[]{:S(2)}, u32[]{:S(2)}) collective-permute-start(bf16[2,320,512]{2,1,0:T(8,128)(2,1)} %get-tuple-element.41), channel_id=1, source_target_pairs={{0,32},{16,48},{32,64},{48,80},{64,96},{80,112},{96,0},{112,16},{1... | collective-permute-start | bytes 1966088 | tf_op jit(solution)/shard_map/ppermute | solution.py:51
  54.9 6.7 %copy-start.3 = (bf16[1,128,2560]{1,2,0:T(8,128)(2,1)S(1)}, bf16[1,128,2560]{1,2,0:T(8,128)(2,1)}, u32[]{:S(2)}) copy-start(bf16[1,128,2560]{1,2,0:T(8,128)(2,1)} %copy.92) | copy-start | bytes 1966084
  54.9 6.7 %copy-start.8 = (bf16[384,512]{0,1:T(8,128)(2,1)S(1)}, bf16[384,512]{0,1:T(8,128)(2,1)}, u32[]{:S(2)}) copy-start(bf16[384,512]{0,1:T(8,128)(2,1)} %pad_maximum_fusion.6) | copy-start | bytes 1179652
  54.9 6.7 %copy-start.11 = (pred[128,384]{0,1:T(8,128)(4,1)S(1)}, pred[128,384]{0,1:T(8,128)(4,1)}, u32[]{:S(2)}) copy-start(pred[128,384]{0,1:T(8,128)(4,1)} %or_and_fusion) | copy-start | bytes 147460
  54.9 8.1 %copy-start.5 = (bf16[1,128,2560]{1,2,0:T(8,128)(2,1)S(1)}, bf16[1,128,2560]{1,2,0:T(8,128)(2,1)}, u32[]{:S(2)}) copy-start(bf16[1,128,2560]{1,2,0:T(8,128)(2,1)} %copy.94) | copy-start | bytes 1966084
  54.9 22.5 %all-to-all-start = ((bf16[16,128,320]{1,2,0:T(8,128)(2,1)}), bf16[16,128,320]{1,2,0:T(8,128)(2,1)S(1)}, u32[]{:S(2)}, u32[]{:S(2)}) async-start(bf16[16,128,320]{1,2,0:T(8,128)(2,1)} %bitcast.8), calls=%async_computation | async-start | bytes 2621440 | tf_op jit(solution)/shard_map/all_to_all | solution.py:69
  61.4 33.6 %collective-permute-start.8 = (bf16[4,2,320,512]{3,2,1,0:T(8,128)(2,1)}, bf16[4,2,320,512]{3,2,1,0:T(8,128)(2,1)}, u32[]{:S(2)}, u32[]{:S(2)}) collective-permute-start(bf16[4,2,320,512]{3,2,1,0:T(8,128)(2,1)} %pad_maximum_fusion.1), channel_id=1, source_target_pairs={{0,16},{16,0},{32,48},{48,32},{64,80},{80,64},{96,112},{112,96},{1... | collective-permute-start | bytes 7864328 | tf_op jit(solution)/shard_map/ppermute | solution.py:53
  63.0 58.3 %copy-start.26 = (f32[5,128]{1,0:T(8,128)}, f32[5,128]{1,0:T(8,128)S(1)}, u32[]{:S(2)}) copy-start(f32[5,128]{1,0:T(8,128)S(1)} %get-tuple-element.46) | copy-start | bytes 7684
  77.4 6.4 %copy-start.2 = (bf16[16,128,320]{1,2,0:T(8,128)(2,1)}, bf16[16,128,320]{1,2,0:T(8,128)(2,1)S(1)}, u32[]{:S(2)}) copy-start(bf16[16,128,320]{1,2,0:T(8,128)(2,1)S(1)} %all-to-all-done) | copy-start | bytes 3932164
  78.3 15.6 %collective-permute-start.7 = (f32[128,512]{0,1:T(8,128)}, f32[128,512]{0,1:T(8,128)}, u32[]{:S(2)}, u32[]{:S(2)}) collective-permute-start(f32[128,512]{0,1:T(8,128)} %get-tuple-element.39), channel_id=1, source_target_pairs={{0,1},{1,2},{2,3},{3,4},{4,5},{5,6},{6,7},{7,8},{8,9},{9,10},{10,1... | collective-permute-start | bytes 786440 | tf_op jit(solution)/shard_map/ppermute | solution.py:82
  82.3 11.6 %collective-permute-start.6 = (f32[128,512]{0,1:T(8,128)}, f32[128,512]{0,1:T(8,128)}, u32[]{:S(2)}, u32[]{:S(2)}) collective-permute-start(f32[128,512]{0,1:T(8,128)} %get-tuple-element.38), channel_id=1, source_target_pairs={{1,0},{2,1},{3,2},{4,3},{5,4},{6,5},{7,6},{8,7},{9,8},{10,9},{11,1... | collective-permute-start | bytes 786440 | tf_op jit(solution)/shard_map/ppermute | solution.py:82
  100.4 16.3 %collective-permute-start.10 = (bf16[128,512]{1,0:T(8,128)(2,1)S(1)}, bf16[128,512]{1,0:T(8,128)(2,1)S(1)}, u32[]{:S(2)}, u32[]{:S(2)}) collective-permute-start(bf16[128,512]{1,0:T(8,128)(2,1)S(1)} %fusion.38), channel_id=1, source_target_pairs={{1,0},{2,1},{3,2},{4,3},{5,4},{6,5},{7,6},{8,7},{9,8},{10,9},{11,1... | collective-permute-start | bytes 393224 | tf_op jit(solution)/shard_map/ppermute | solution.py:19
  101.6 15.1 %collective-permute-start.9 = (bf16[128,512]{1,0:T(8,128)(2,1)S(1)}, bf16[128,512]{1,0:T(8,128)(2,1)S(1)}, u32[]{:S(2)}, u32[]{:S(2)}) collective-permute-start(bf16[128,512]{1,0:T(8,128)(2,1)S(1)} %fusion.38), channel_id=1, source_target_pairs={{0,1},{1,2},{2,3},{3,4},{4,5},{5,6},{6,7},{7,8},{8,9},{9,10},{10,1... | collective-permute-start | bytes 393224 | tf_op jit(solution)/shard_map/ppermute | solution.py:17
  108.4 47.2 %all-to-all-start.1 = ((bf16[16,128,512]{1,2,0:T(8,128)(2,1)}), bf16[16,128,512]{1,2,0:T(8,128)(2,1)S(1)}, u32[]{:S(2)}, u32[]{:S(2)}) async-start(bf16[16,128,512]{1,2,0:T(8,128)(2,1)} %broadcast_in_dim.112), calls=%async_computation.1 | async-start | bytes 4194304 | tf_op jit(solution)/shard_map/all_to_all | solution.py:69
  119.5 3.8 %copy-start.21 = (f32[5,128,384]{1,2,0:T(8,128)}, f32[5,128,384]{1,2,0:T(8,128)S(1)}, u32[]{:S(2)}) copy-start(f32[5,128,384]{1,2,0:T(8,128)S(1)} %get-tuple-element.57) | copy-start | bytes 2949124
  126.5 28.4 %collective-permute-start.12 = (f32[128,512]{0,1:T(8,128)}, f32[128,512]{0,1:T(8,128)S(1)}, u32[]{:S(2)}, u32[]{:S(2)}) collective-permute-start(f32[128,512]{0,1:T(8,128)} %get-tuple-element.37), channel_id=1, source_target_pairs={{0,1},{1,2},{2,3},{3,4},{4,5},{5,6},{6,7},{7,8},{8,9},{9,10},{10,1... | collective-permute-start | bytes 786440 | tf_op jit(solution)/shard_map/ppermute | solution.py:82
  130.9 24.0 %collective-permute-start.11 = (f32[128,512]{0,1:T(8,128)}, f32[128,512]{0,1:T(8,128)S(1)}, u32[]{:S(2)}, u32[]{:S(2)}) collective-permute-start(f32[128,512]{0,1:T(8,128)} %get-tuple-element.36), channel_id=1, source_target_pairs={{1,0},{2,1},{3,2},{4,3},{5,4},{6,5},{7,6},{8,7},{9,8},{10,9},{11,1... | collective-permute-start | bytes 786440 | tf_op jit(solution)/shard_map/ppermute | solution.py:82
  159.1 35.0 %all-to-all-start.2 = ((f32[16,320,32]{1,2,0:T(8,128)}), f32[16,320,32]{1,2,0:T(8,128)S(1)}, u32[]{:S(2)}, u32[]{:S(2)}) async-start(f32[16,320,32]{1,2,0:T(8,128)} %fusion.28), calls=%async_computation.2 | async-start | bytes 1572864 | tf_op jit(solution)/shard_map/all_to_all | solution.py:69
  (34 other events, 67.1 us)

commit v11 on v9

--- a/solution.py
+++ b/solution.py
@@ -1,6 +1,8 @@
 import jax
 import jax.numpy as jnp
 from jax import lax
+from jax.experimental import pallas as pl
+from jax.experimental.pallas import tpu as pltpu
 from jax.sharding import PartitionSpec as P
 
 HD = 128
@@ -65,6 +67,51 @@
     return stacked, owner.reshape(-1), ready, riders
 
 
+def summed_pieces_kernel(count, pieces_ref, out_ref, landed, send_sems, recv_sems):
+    me = lax.axis_index("seq")
+    row = lax.axis_index("dp")
+    mesh_kind = pl.DeviceIdType.MESH
+    barrier = pltpu.get_barrier_semaphore()
+    for offset in range(1, count):
+        peer = lax.rem(me + offset, count)
+        pl.semaphore_signal(barrier, 1, device_id=(row, peer), device_id_type=mesh_kind)
+    pl.semaphore_wait(barrier, count - 1)
+    copies = []
+    for offset in range(1, count):
+        peer = lax.rem(me + offset, count)
+        copy = pltpu.make_async_remote_copy(
+            src_ref=pieces_ref.at[peer],
+            dst_ref=landed.at[offset],
+            send_sem=send_sems.at[offset],
+            recv_sem=recv_sems.at[offset],
+            device_id=(row, peer),
+            device_id_type=mesh_kind,
+        )
+        copy.start()
+        copies.append(copy)
+    total = pieces_ref[me]
+    for offset, copy in zip(range(1, count), copies):
+        copy.wait()
+        total = total + landed[offset]
+    out_ref[...] = total
+
+
+def summed_pieces(pieces):
+    count = pieces.shape[0]
+    return pl.pallas_call(
+        lambda *refs: summed_pieces_kernel(count, *refs),
+        out_shape=jax.ShapeDtypeStruct(pieces.shape[1:], pieces.dtype),
+        in_specs=[pl.BlockSpec(memory_space=pltpu.VMEM)],
+        out_specs=pl.BlockSpec(memory_space=pltpu.VMEM),
+        scratch_shapes=[
+            pltpu.VMEM(pieces.shape, pieces.dtype),
+            pltpu.SemaphoreType.DMA((count,)),
+            pltpu.SemaphoreType.DMA((count,)),
+        ],
+        compiler_params=pltpu.CompilerParams(collective_id=0, has_side_effects=True),
+    )(pieces)
+
+
 def gathered_copies(copies, axis):
     return lax.all_to_all(copies, axis, 0, 0, tiled=True)
 
@@ -196,9 +243,9 @@
     seq_count = lax.axis_size("seq")
     grad_rows = gathered_copies(grad_copies, "dp").reshape(dp_count, tok_count, seq_count, -1)
     own_pieces = jnp.einsum(
-        "rtk,rtjc->jkc", input_blocks, grad_rows, preferred_element_type=jnp.float32
-    )
-    summed = jnp.sum(gathered_copies(own_pieces, "seq"), axis=0)
+        "rtk,rtjc->jck", input_blocks, grad_rows, preferred_element_type=jnp.float32
+    )
+    summed = summed_pieces(own_pieces).T
     devices_all = lax.axis_size("dp") * lax.axis_size("seq")
     weight_grad = summed / devices_all
     input_slots = jnp.take(

time: 194 us -> 196 us (1.010)
  the two profiles are of different devices: /device:TPU:26 before, /device:TPU:76 now
where the time goes in v11:
time: 196 us; the launch traced here: 195 us
  waiting for transfers between devices  49.5 us (25%)
  starting transfers between devices  46.8 us (24%)
  Pallas kernels  30.1 us (15%)
  matrix products  28.5 us (15%)
  local copies, waits for them, and re-layouts  22.9 us (12%)
  other arithmetic  16.1 us (8%)
    pallas_call x1, Pallas kernels, summed_pieces(): pl.pallas_call(lambda *refs: summed_pieces_kernel(count, *refs), out_shap...  30.1 us
    ppermute x4, waiting for transfers between devices, passed_along(): return lax.ppermute(array, axis, pairs)  21.1 us
    ppermute x3, waiting for transfers between devices, spread_weight(): ring.append(lax.ppermute(held, 'dp', pairs))  18.1 us
    all_to_all x2, starting transfers between devices, gathered_copies(): return lax.all_to_all(copies, axis, 0, 0, tiled=True)  14.8 us
    unnamed x49, local copies, waits for them, and re-layouts  14.4 us
    ppermute x4, starting transfers between devices, passed_along(): return lax.ppermute(array, axis, pairs)  13.7 us
    ppermute x2, starting transfers between devices, with_halo(): lax.ppermute(head, axis, [((i + 1) % count, i) for i in range(ends)])  7.56 us
    ppermute x1, waiting for transfers between devices, spread_weight(): lax.ppermute(weight, ('dp', 'seq'), partner_pairs)  6.8 us
  transfers between devices with their start and end apart: 15, of which 8 were waited for; matrix products, arithmetic and copies ran while one was open for 26% of the time, Pallas kernels for 0%

profile of v11, /device:TPU:76, one launch (start us, length us, event | category | flops | bytes accessed | tf_op | source)
XLA Modules:
  0.0 195.1 jit_solution(14855197151747318653)
XLA Ops:
  1.8 3.1 %collective-permute-start.4 = (bf16[128,512]{0,1:T(8,128)(2,1)S(1)}, bf16[128,512]{0,1:T(8,128)(2,1)S(1)}, u32[]{:S(2)}, u32[]{:S(2)}) collective-permute-start(bf16[128,512]{0,1:T(8,128)(2,1)S(1)} %bitcast.323), channel_id=1, source_target_pairs={{0,1},{1,2},{2,3},{3,4},{4,5},{5,6},{6,7},{7,8},{8,9},{9,10},{10,1... | collective-permute-start | bytes 393224 | tf_op jit(solution)/shard_map/ppermute | solution.py:19
  4.9 3.6 %collective-permute-start.5 = (bf16[128,512]{0,1:T(8,128)(2,1)S(1)}, bf16[128,512]{0,1:T(8,128)(2,1)}, u32[]{:S(2)}, u32[]{:S(2)}) collective-permute-start(bf16[128,512]{0,1:T(8,128)(2,1)S(1)} %bitcast.324), channel_id=1, source_target_pairs={{1,0},{2,1},{3,2},{4,3},{5,4},{6,5},{7,6},{8,7},{9,8},{10,9},{11,1... | collective-permute-start | bytes 393224 | tf_op jit(solution)/shard_map/ppermute | solution.py:21
  10.9 6.8 %collective-permute-done = bf16[320,512]{1,0:T(8,128)(2,1)S(1)} collective-permute-done((bf16[320,512]{1,0:T(8,128)(2,1)}, bf16[320,512]{1,0:T(8,128)(2,1)S(1)}, u32[]{:S(2)}, u32[]{:S(2)}) %collective-permute-start) | collective-permute-done | bytes 327712 | tf_op jit(solution)/shard_map/ppermute | solution.py:46
  22.1 2.4 %collective-permute-start.3 = (bf16[2,320,512]{2,1,0:T(8,128)(2,1)}, bf16[2,320,512]{2,1,0:T(8,128)(2,1)}, u32[]{:S(2)}, u32[]{:S(2)}) collective-permute-start(bf16[2,320,512]{2,1,0:T(8,128)(2,1)} %get-tuple-element.37), channel_id=1, source_target_pairs={{0,96},{16,112},{32,0},{48,16},{64,32},{80,48},{96,64},{112,80},{1... | collective-permute-start | bytes 1966088 | tf_op jit(solution)/shard_map/ppermute | solution.py:53
  32.9 4.6 %collective-permute-done.1 = bf16[2,320,512]{2,1,0:T(8,128)(2,1)S(1)} collective-permute-done((bf16[2,320,512]{2,1,0:T(8,128)(2,1)}, bf16[2,320,512]{2,1,0:T(8,128)(2,1)S(1)}, u32[]{:S(2)}, u32[]{:S(2)}) %collective-permute-start.1) | collective-permute-done | bytes 655392 | tf_op jit(solution)/shard_map/ppermute | solution.py:53
  37.5 3.1 %collective-permute-done.2 = bf16[2,320,512]{2,1,0:T(8,128)(2,1)S(1)} collective-permute-done((bf16[2,320,512]{2,1,0:T(8,128)(2,1)}, bf16[2,320,512]{2,1,0:T(8,128)(2,1)S(1)}, u32[]{:S(2)}, u32[]{:S(2)}) %collective-permute-start.2) | collective-permute-done | bytes 655392 | tf_op jit(solution)/shard_map/ppermute | solution.py:53
  40.6 10.4 %collective-permute-done.3 = bf16[2,320,512]{2,1,0:T(8,128)(2,1)} collective-permute-done((bf16[2,320,512]{2,1,0:T(8,128)(2,1)}, bf16[2,320,512]{2,1,0:T(8,128)(2,1)}, u32[]{:S(2)}, u32[]{:S(2)}) %collective-permute-start.3) | collective-permute-done | bytes 655392 | tf_op jit(solution)/shard_map/ppermute | solution.py:53
  51.0 2.9 %pad_maximum_fusion.1 = bf16[4,2,320,512]{3,2,1,0:T(8,128)(2,1)} fusion(bf16[1,2,320,512]{3,2,1,0:T(8,128)(2,1)} %bitcast.5, bf16[1,2,320,512]{3,2,1,0:T(8,128)(2,1)S(1)} %bitcast.306, bf16[1,2,320,512]{3,2,1,0:T(8,128)(2,1)S(1)} %bitcast.305, bf16[1,2,320,512]{3,2,1,0:T(8,128)(2,1)S(1)} %get-tuple-element.36), kind=kLoop, calls=%fused_computation.8 | loop fusion | flops 3932160 | bytes 5242880 | tf_op jit(solution)/shard_map/stack | solution.py:54
  53.9 7.3 %all-to-all-start = ((bf16[16,128,320]{1,2,0:T(8,128)(2,1)}), bf16[16,128,320]{1,2,0:T(8,128)(2,1)S(1)}, u32[]{:S(2)}, u32[]{:S(2)}) async-start(bf16[16,128,320]{1,2,0:T(8,128)(2,1)} %bitcast.8), calls=%async_computation | async-start | bytes 2621440 | tf_op jit(solution)/shard_map/all_to_all | solution.py:116
  68.9 2.2 %convolution_bitcast_fusion.5 = f32[384,128]{0,1:T(8,128)} fusion(bf16[128,4,5,128]{0,3,2,1:T(8,128)(2,1)S(1)} %bitcast.317, f32[5,128,384]{1,2,0:T(8,128)} %get-tuple-element.45, f32[5,128]{1,0:T(8,128)S(1)} %get-tuple-element.44), kind=kOutput, calls=%fused_computation.52 | convolution fusion | flops 63406080 | bytes 1347584 | tf_op jit(solution)/shard_map/gqk,qgd->kd/dot_general | solution.py:163
  74.2 3.5 %all-to-all-done = bf16[16,128,320]{1,2,0:T(8,128)(2,1)S(1)} async-done(((bf16[16,128,320]{1,2,0:T(8,128)(2,1)}), bf16[16,128,320]{1,2,0:T(8,128)(2,1)S(1)}, u32[]{:S(2)}, u32[]{:S(2)}) %all-to-all-start) | async-done | bytes 1310752 | tf_op jit(solution)/shard_map/all_to_all | solution.py:116
  78.5 3.8 %collective-permute-start.6 = (f32[128,512]{0,1:T(8,128)}, f32[128,512]{0,1:T(8,128)}, u32[]{:S(2)}, u32[]{:S(2)}) collective-permute-start(f32[128,512]{0,1:T(8,128)} %get-tuple-element.34), channel_id=1, source_target_pairs={{1,0},{2,1},{3,2},{4,3},{5,4},{6,5},{7,6},{8,7},{9,8},{10,9},{11,1... | collective-permute-start | bytes 786440 | tf_op jit(solution)/shard_map/ppermute | solution.py:129
  82.3 2.4 %collective-permute-start.7 = (f32[128,512]{0,1:T(8,128)}, f32[128,512]{0,1:T(8,128)}, u32[]{:S(2)}, u32[]{:S(2)}) collective-permute-start(f32[128,512]{0,1:T(8,128)} %get-tuple-element.35), channel_id=1, source_target_pairs={{0,1},{1,2},{2,3},{3,4},{4,5},{5,6},{6,7},{7,8},{8,9},{9,10},{10,1... | collective-permute-start | bytes 786440 | tf_op jit(solution)/shard_map/ppermute | solution.py:129
  88.4 6.9 %collective-permute-done.6 = f32[128,512]{0,1:T(8,128)} collective-permute-done((f32[128,512]{0,1:T(8,128)}, f32[128,512]{0,1:T(8,128)}, u32[]{:S(2)}, u32[]{:S(2)}) %collective-permute-start.6) | collective-permute-done | bytes 262176 | tf_op jit(solution)/shard_map/ppermute | solution.py:129
  96.5 3.0 %pad_maximum_fusion = bf16[2,4,2,320,512]{4,3,2,1,0:T(8,128)(2,1)S(1)} fusion(bf16[1,4,2,320,512]{4,3,2,1,0:T(8,128)(2,1)} %bitcast.42, bf16[1,4,2,320,512]{4,3,2,1,0:T(8,128)(2,1)} %bitcast.41), kind=kLoop, calls=%fused_computation.7 | loop fusion | flops 2621440 | bytes 10485760 | tf_op jit(solution)/shard_map/stack | solution.py:56
  101.8 3.9 %collective-permute-start.10 = (bf16[128,512]{1,0:T(8,128)(2,1)S(1)}, bf16[128,512]{1,0:T(8,128)(2,1)S(1)}, u32[]{:S(2)}, u32[]{:S(2)}) collective-permute-start(bf16[128,512]{1,0:T(8,128)(2,1)S(1)} %fusion.38), channel_id=1, source_target_pairs={{1,0},{2,1},{3,2},{4,3},{5,4},{6,5},{7,6},{8,7},{9,8},{10,9},{11,1... | collective-permute-start | bytes 393224 | tf_op jit(solution)/shard_map/ppermute | solution.py:21
  105.8 2.4 %collective-permute-start.9 = (bf16[128,512]{1,0:T(8,128)(2,1)S(1)}, bf16[128,512]{1,0:T(8,128)(2,1)S(1)}, u32[]{:S(2)}, u32[]{:S(2)}) collective-permute-start(bf16[128,512]{1,0:T(8,128)(2,1)S(1)} %fusion.38), channel_id=1, source_target_pairs={{0,1},{1,2},{2,3},{3,4},{4,5},{5,6},{6,7},{7,8},{8,9},{9,10},{10,1... | collective-permute-start | bytes 393224 | tf_op jit(solution)/shard_map/ppermute | solution.py:19
  109.9 7.5 %all-to-all-start.1 = ((bf16[16,128,512]{1,2,0:T(8,128)(2,1)}), bf16[16,128,512]{1,2,0:T(8,128)(2,1)}, u32[]{:S(2)}, u32[]{:S(2)}) async-start(bf16[16,128,512]{1,2,0:T(8,128)(2,1)} %broadcast_in_dim.114), calls=%async_computation.1 | async-start | bytes 4194304 | tf_op jit(solution)/shard_map/all_to_all | solution.py:116
  117.5 4.3 %convolution_convert_fusion = bf16[128,5120]{1,0:T(8,128)(2,1)S(1)} fusion(bf16[128,512]{0,1:T(8,128)(2,1)S(1)} %add_convert_fusion, bf16[5120,512]{1,0:T(8,128)(2,1)} %bitcast.301), kind=kOutput, calls=%fused_computation.6 | convolution fusion | flops 671744000 | bytes 6684672 | tf_op jit(solution)/shard_map/dot_general | solution.py:260
  133.4 4.9 %collective-permute-start.11 = (f32[128,512]{0,1:T(8,128)}, f32[128,512]{0,1:T(8,128)S(1)}, u32[]{:S(2)}, u32[]{:S(2)}) collective-permute-start(f32[128,512]{0,1:T(8,128)} %get-tuple-element.32), channel_id=1, source_target_pairs={{1,0},{2,1},{3,2},{4,3},{5,4},{6,5},{7,6},{8,7},{9,8},{10,9},{11,1... | collective-permute-start | bytes 786440 | tf_op jit(solution)/shard_map/ppermute | solution.py:129
  138.4 2.6 %collective-permute-start.12 = (f32[128,512]{0,1:T(8,128)S(1)}, f32[128,512]{0,1:T(8,128)S(1)}, u32[]{:S(2)}, u32[]{:S(2)}) collective-permute-start(f32[128,512]{0,1:T(8,128)S(1)} %get-tuple-element.33), channel_id=1, source_target_pairs={{0,1},{1,2},{2,3},{3,4},{4,5},{5,6},{6,7},{7,8},{8,9},{9,10},{10,1... | collective-permute-start | bytes 786440 | tf_op jit(solution)/shard_map/ppermute | solution.py:129
  144.9 14.1 %collective-permute-done.11 = f32[128,512]{0,1:T(8,128)S(1)} collective-permute-done((f32[128,512]{0,1:T(8,128)}, f32[128,512]{0,1:T(8,128)S(1)}, u32[]{:S(2)}, u32[]{:S(2)}) %collective-permute-start.11) | collective-permute-done | bytes 262176 | tf_op jit(solution)/shard_map/ppermute | solution.py:129
  159.8 3.7 %fusion.28.refs_0_ = f32[16,32,320]{2,1,0:T(8,128)} fusion(bf16[16,128,16,32]{1,3,2,0:T(8,128)(2,1)} %bitcast.78, bf16[16,128,320]{1,2,0:T(8,128)(2,1)S(1)} %copy-done.3), kind=kOutput, calls=%fused_computation.41 | convolution fusion | flops 671088640 | bytes 4063232 | tf_op jit(solution)/shard_map/rtk,rtjc->jck/dot_general | solution.py:245
  163.5 30.1 %shard_map.102 = f32[32,320]{1,0:T(8,128)} custom-call(f32[16,32,320]{2,1,0:T(8,128)} %fusion.28.refs_0_), custom_call_target="tpu_custom_call" | custom-call | tf_op jit(solution)/shard_map/pallas_call | solution.py:101
  (114 shorter events, 54.3 us)
Async XLA Ops:
  0.6 24.8 %copy-start.1 = (bf16[1,128,5120]{2,1,0:T(8,128)(2,1)S(1)}, bf16[1,128,5120]{2,1,0:T(8,128)(2,1)}, u32[]{:S(2)}) copy-start(bf16[1,128,5120]{2,1,0:T(8,128)(2,1)} %param.7) | copy-start | bytes 3932164
  1.8 29.4 %collective-permute-start.4 = (bf16[128,512]{0,1:T(8,128)(2,1)S(1)}, bf16[128,512]{0,1:T(8,128)(2,1)S(1)}, u32[]{:S(2)}, u32[]{:S(2)}) collective-permute-start(bf16[128,512]{0,1:T(8,128)(2,1)S(1)} %bitcast.323), channel_id=1, source_target_pairs={{0,1},{1,2},{2,3},{3,4},{4,5},{5,6},{6,7},{7,8},{8,9},{9,10},{10,1... | collective-permute-start | bytes 393224 | tf_op jit(solution)/shard_map/ppermute | solution.py:19
  4.9 26.3 %collective-permute-start.5 = (bf16[128,512]{0,1:T(8,128)(2,1)S(1)}, bf16[128,512]{0,1:T(8,128)(2,1)}, u32[]{:S(2)}, u32[]{:S(2)}) collective-permute-start(bf16[128,512]{0,1:T(8,128)(2,1)S(1)} %bitcast.324), channel_id=1, source_target_pairs={{1,0},{2,1},{3,2},{4,3},{5,4},{6,5},{7,6},{8,7},{9,8},{10,9},{11,1... | collective-permute-start | bytes 393224 | tf_op jit(solution)/shard_map/ppermute | solution.py:21
  8.5 9.2 %collective-permute-start = (bf16[320,512]{1,0:T(8,128)(2,1)}, bf16[320,512]{1,0:T(8,128)(2,1)S(1)}, u32[]{:S(2)}, u32[]{:S(2)}) collective-permute-start(bf16[320,512]{1,0:T(8,128)(2,1)} %param.11), channel_id=1, source_target_pairs={{0,129},{1,128},{2,131},{3,130},{4,133},{5,132},{6,135},{7,134},{8... | collective-permute-start | bytes 983048 | tf_op jit(solution)/shard_map/ppermute | solution.py:46
  19.6 17.9 %collective-permute-start.1 = (bf16[2,320,512]{2,1,0:T(8,128)(2,1)}, bf16[2,320,512]{2,1,0:T(8,128)(2,1)S(1)}, u32[]{:S(2)}, u32[]{:S(2)}) collective-permute-start(bf16[2,320,512]{2,1,0:T(8,128)(2,1)} %get-tuple-element.37), channel_id=1, source_target_pairs={{0,32},{16,48},{32,64},{48,80},{64,96},{80,112},{96,0},{112,16},{1... | collective-permute-start | bytes 1966088 | tf_op jit(solution)/shard_map/ppermute | solution.py:53
  21.2 19.4 %collective-permute-start.2 = (bf16[2,320,512]{2,1,0:T(8,128)(2,1)}, bf16[2,320,512]{2,1,0:T(8,128)(2,1)S(1)}, u32[]{:S(2)}, u32[]{:S(2)}) collective-permute-start(bf16[2,320,512]{2,1,0:T(8,128)(2,1)} %get-tuple-element.37), channel_id=1, source_target_pairs={{0,64},{16,80},{32,96},{48,112},{64,0},{80,16},{96,32},{112,48},{1... | collective-permute-start | bytes 1966088 | tf_op jit(solution)/shard_map/ppermute | solution.py:53
  22.1 28.8 %collective-permute-start.3 = (bf16[2,320,512]{2,1,0:T(8,128)(2,1)}, bf16[2,320,512]{2,1,0:T(8,128)(2,1)}, u32[]{:S(2)}, u32[]{:S(2)}) collective-permute-start(bf16[2,320,512]{2,1,0:T(8,128)(2,1)} %get-tuple-element.37), channel_id=1, source_target_pairs={{0,96},{16,112},{32,0},{48,16},{64,32},{80,48},{96,64},{112,80},{1... | collective-permute-start | bytes 1966088 | tf_op jit(solution)/shard_map/ppermute | solution.py:53
  53.9 7.5 %copy-start.4 = (bf16[1,128,2560]{1,2,0:T(8,128)(2,1)S(1)}, bf16[1,128,2560]{1,2,0:T(8,128)(2,1)}, u32[]{:S(2)}) copy-start(bf16[1,128,2560]{1,2,0:T(8,128)(2,1)} %copy.92) | copy-start | bytes 1966084
  53.9 7.5 %copy-start.8 = (bf16[384,512]{0,1:T(8,128)(2,1)S(1)}, bf16[384,512]{0,1:T(8,128)(2,1)}, u32[]{:S(2)}) copy-start(bf16[384,512]{0,1:T(8,128)(2,1)} %pad_maximum_fusion.6) | copy-start | bytes 1179652
  53.9 7.5 %copy-start.11 = (pred[128,384]{0,1:T(8,128)(4,1)S(1)}, pred[128,384]{0,1:T(8,128)(4,1)}, u32[]{:S(2)}) copy-start(pred[128,384]{0,1:T(8,128)(4,1)} %or_and_fusion) | copy-start | bytes 147460
  53.9 8.9 %copy-start.6 = (bf16[1,128,2560]{1,2,0:T(8,128)(2,1)S(1)}, bf16[1,128,2560]{1,2,0:T(8,128)(2,1)}, u32[]{:S(2)}) copy-start(bf16[1,128,2560]{1,2,0:T(8,128)(2,1)} %copy.94) | copy-start | bytes 1966084
  53.9 23.7 %all-to-all-start = ((bf16[16,128,320]{1,2,0:T(8,128)(2,1)}), bf16[16,128,320]{1,2,0:T(8,128)(2,1)S(1)}, u32[]{:S(2)}, u32[]{:S(2)}) async-start(bf16[16,128,320]{1,2,0:T(8,128)(2,1)} %bitcast.8), calls=%async_computation | async-start | bytes 2621440 | tf_op jit(solution)/shard_map/all_to_all | solution.py:116
  61.2 35.3 %collective-permute-start.8 = (bf16[4,2,320,512]{3,2,1,0:T(8,128)(2,1)}, bf16[4,2,320,512]{3,2,1,0:T(8,128)(2,1)}, u32[]{:S(2)}, u32[]{:S(2)}) collective-permute-start(bf16[4,2,320,512]{3,2,1,0:T(8,128)(2,1)} %pad_maximum_fusion.1), channel_id=1, source_target_pairs={{0,16},{16,0},{32,48},{48,32},{64,80},{80,64},{96,112},{112,96},{1... | collective-permute-start | bytes 7864328 | tf_op jit(solution)/shard_map/ppermute | solution.py:55
  68.9 3.7 %copy-start.19 = (f32[5,128]{1,0:T(8,128)}, f32[5,128]{1,0:T(8,128)S(1)}, u32[]{:S(2)}) copy-start(f32[5,128]{1,0:T(8,128)S(1)} %get-tuple-element.44) | copy-start | bytes 7684
  77.6 8.6 %copy-start.2 = (bf16[16,128,320]{1,2,0:T(8,128)(2,1)}, bf16[16,128,320]{1,2,0:T(8,128)(2,1)S(1)}, u32[]{:S(2)}) copy-start(bf16[16,128,320]{1,2,0:T(8,128)(2,1)S(1)} %all-to-all-done) | copy-start | bytes 3932164
  78.5 16.8 %collective-permute-start.6 = (f32[128,512]{0,1:T(8,128)}, f32[128,512]{0,1:T(8,128)}, u32[]{:S(2)}, u32[]{:S(2)}) collective-permute-start(f32[128,512]{0,1:T(8,128)} %get-tuple-element.34), channel_id=1, source_target_pairs={{1,0},{2,1},{3,2},{4,3},{5,4},{6,5},{7,6},{8,7},{9,8},{10,9},{11,1... | collective-permute-start | bytes 786440 | tf_op jit(solution)/shard_map/ppermute | solution.py:129
  82.3 13.1 %collective-permute-start.7 = (f32[128,512]{0,1:T(8,128)}, f32[128,512]{0,1:T(8,128)}, u32[]{:S(2)}, u32[]{:S(2)}) collective-permute-start(f32[128,512]{0,1:T(8,128)} %get-tuple-element.35), channel_id=1, source_target_pairs={{0,1},{1,2},{2,3},{3,4},{4,5},{5,6},{6,7},{7,8},{8,9},{9,10},{10,1... | collective-permute-start | bytes 786440 | tf_op jit(solution)/shard_map/ppermute | solution.py:129
  101.8 23.0 %collective-permute-start.10 = (bf16[128,512]{1,0:T(8,128)(2,1)S(1)}, bf16[128,512]{1,0:T(8,128)(2,1)S(1)}, u32[]{:S(2)}, u32[]{:S(2)}) collective-permute-start(bf16[128,512]{1,0:T(8,128)(2,1)S(1)} %fusion.38), channel_id=1, source_target_pairs={{1,0},{2,1},{3,2},{4,3},{5,4},{6,5},{7,6},{8,7},{9,8},{10,9},{11,1... | collective-permute-start | bytes 393224 | tf_op jit(solution)/shard_map/ppermute | solution.py:21
  105.8 19.1 %collective-permute-start.9 = (bf16[128,512]{1,0:T(8,128)(2,1)S(1)}, bf16[128,512]{1,0:T(8,128)(2,1)S(1)}, u32[]{:S(2)}, u32[]{:S(2)}) collective-permute-start(bf16[128,512]{1,0:T(8,128)(2,1)S(1)} %fusion.38), channel_id=1, source_target_pairs={{0,1},{1,2},{2,3},{3,4},{4,5},{5,6},{6,7},{7,8},{8,9},{9,10},{10,1... | collective-permute-start | bytes 393224 | tf_op jit(solution)/shard_map/ppermute | solution.py:19
  109.9 49.8 %all-to-all-start.1 = ((bf16[16,128,512]{1,2,0:T(8,128)(2,1)}), bf16[16,128,512]{1,2,0:T(8,128)(2,1)}, u32[]{:S(2)}, u32[]{:S(2)}) async-start(bf16[16,128,512]{1,2,0:T(8,128)(2,1)} %broadcast_in_dim.114), calls=%async_computation.1 | async-start | bytes 4194304 | tf_op jit(solution)/shard_map/all_to_all | solution.py:116
  132.6 8.4 %copy-start.9 = (bf16[384,512]{0,1:T(8,128)(2,1)S(1)}, bf16[384,512]{0,1:T(8,128)(2,1)}, u32[]{:S(2)}) copy-start(bf16[384,512]{0,1:T(8,128)(2,1)} %pad_maximum_fusion.6) | copy-start | bytes 1179652
  133.4 25.6 %collective-permute-start.11 = (f32[128,512]{0,1:T(8,128)}, f32[128,512]{0,1:T(8,128)S(1)}, u32[]{:S(2)}, u32[]{:S(2)}) collective-permute-start(f32[128,512]{0,1:T(8,128)} %get-tuple-element.32), channel_id=1, source_target_pairs={{1,0},{2,1},{3,2},{4,3},{5,4},{6,5},{7,6},{8,7},{9,8},{10,9},{11,1... | collective-permute-start | bytes 786440 | tf_op jit(solution)/shard_map/ppermute | solution.py:129
  138.4 20.6 %collective-permute-start.12 = (f32[128,512]{0,1:T(8,128)S(1)}, f32[128,512]{0,1:T(8,128)S(1)}, u32[]{:S(2)}, u32[]{:S(2)}) collective-permute-start(f32[128,512]{0,1:T(8,128)S(1)} %get-tuple-element.33), channel_id=1, source_target_pairs={{0,1},{1,2},{2,3},{3,4},{4,5},{5,6},{6,7},{7,8},{8,9},{9,10},{10,1... | collective-permute-start | bytes 786440 | tf_op jit(solution)/shard_map/ppermute | solution.py:129
  143.7 16.1 %copy-start.3 = (bf16[16,128,320]{1,2,0:T(8,128)(2,1)S(1)}, bf16[16,128,320]{1,2,0:T(8,128)(2,1)}, u32[]{:S(2)}) copy-start(bf16[16,128,320]{1,2,0:T(8,128)(2,1)} %copy-done.2) | copy-start | bytes 3932164
  (12 other events, 18.4 us)

commit v12 on v9

--- a/solution.py
+++ b/solution.py
@@ -29,7 +29,7 @@
     return lax.all_to_all(copies, axis, 0, 0, tiled=True)
 
 
-def spread_weight(weight, ready, riders):
+def spread_weight(weight, ready):
     dp_count = lax.axis_size("dp")
     seq_count = lax.axis_size("seq")
     half = dp_count // 2
@@ -42,6 +42,7 @@
         for s in range(seq_count)
     ]
     held = jnp.stack([weight, lax.ppermute(weight, ("dp", "seq"), partner_pairs)])
+    held, ready = lax.optimization_barrier((held, ready))
     ring = [held]
     for shift in range(1, y_count):
         pairs = []
@@ -49,7 +50,15 @@
             upper, y_here, core = d // half, (d // cores) % y_count, d % cores
             pairs.append((d, upper * half + ((y_here + shift) % y_count) * cores + core))
         ring.append(lax.ppermute(held, "dp", pairs))
-    mine, ready, riders = lax.optimization_barrier((jnp.stack(ring), ready, riders))
+    return jnp.stack(ring), ready
+
+
+def finish_weight(mine):
+    dp_count = lax.axis_size("dp")
+    half = dp_count // 2
+    cores = 2
+    y_count = half // cores
+    rows, width = mine.shape[-2:]
     sibling = lax.ppermute(mine, "dp", [(d, d ^ 1) for d in range(dp_count)])
     stacked = jnp.stack([mine, sibling]).reshape(dp_count, rows, width)
     me = lax.axis_index("dp")
@@ -62,7 +71,7 @@
         + ((y_here - shift_of) % y_count) * cores
         + (core + core_of) % 2
     )
-    return stacked, owner.reshape(-1), ready, riders
+    return stacked, owner.reshape(-1)
 
 
 def gathered_copies(copies, axis):
@@ -90,7 +99,7 @@
     return rows_here, keys_here, head_count, group_size
 
 
-def attend_first(query_rows, key_rows, grad_rows, visible):
+def attend_first(query_rows, key_rows, grad_rows, visible, held):
     rows_here, keys_here, head_count, group_size = split_heads(query_rows, key_rows)
     score_scale = HD ** (-0.5)
     query_split = query_rows.reshape(rows_here, head_count, group_size, HD)
@@ -99,6 +108,10 @@
     attentions = []
     value_parts = []
     for kv_group in range(head_count):
+        if kv_group == head_count // 2:
+            held, attentions, value_parts = lax.optimization_barrier(
+                (held, attentions, value_parts)
+            )
         query_head = query_split[:, kv_group]
         grad_head = grad_split[:, kv_group]
         key_head = key_split[:, kv_group]
@@ -115,7 +128,7 @@
         value_parts.append(
             jnp.einsum("gqk,qgd->kd", attention_low, grad_head, preferred_element_type=jnp.float32)
         )
-    return attentions, jnp.concatenate(value_parts, axis=1)
+    return attentions, jnp.concatenate(value_parts, axis=1), held
 
 
 def attend_second(query_rows, key_rows, value_rows, grad_rows, attentions):
@@ -169,10 +182,7 @@
     weight_rows, kv_width = value_weight.shape
     key_block = with_halo(key_states[0], (("seq", 0),), tok_count)
     input_pieces = layer_rows.reshape(tok_count, dp_count, model_width // dp_count).transpose(1, 0, 2)
-    weight_slots, slot_owner, key_block, input_pieces = spread_weight(
-        value_weight, key_block, input_pieces
-    )
-    input_blocks = gathered_copies(input_pieces, "dp")
+    weight_ring, key_block = spread_weight(value_weight, key_block)
     seg_row = segment_ids[0]
     fill_ids = jnp.full((tok_count,), -1, jnp.int32)
     padded_ids = jnp.concatenate([fill_ids, seg_row, fill_ids])
@@ -187,7 +197,11 @@
     visible = (seg_key[None, :] == seg_query[:, None]) & (
         (pos_key[None, :] <= pos_query[:, None]) | (pos_key[None, :] < split_query[:, None])
     )
-    attentions, value_part = attend_first(query_states[0], key_block, out_grad[0], visible)
+    attentions, value_part, (weight_ring, input_pieces) = attend_first(
+        query_states[0], key_block, out_grad[0], visible, (weight_ring, input_pieces)
+    )
+    weight_slots, slot_owner = finish_weight(weight_ring)
+    input_blocks = gathered_copies(input_pieces, "dp")
     value_part, input_blocks = lax.optimization_barrier((value_part, input_blocks))
     value_grad = rim_sum(value_part, tok_count).astype(jnp.bfloat16)
     value_grad, weight_slots = lax.optimization_barrier((value_grad, weight_slots))

time: 194 us -> 198 us (1.021)
  waiting for transfers between devices: 67 us -> 57.6 us
  starting transfers between devices: 53.6 us -> 58.7 us
  local copies, waits for them, and re-layouts: 24.5 us -> 27.7 us
  matrix products: 30.6 us -> 33.2 us
    ppermute x4, waiting for transfers between devices: 20.2 us -> 6.21 us  [passed_along(): return lax.ppermute(array, axis, pairs)]
    all_to_all x3, waiting for transfers between devices: 20 us -> 28 us  [gathered_copies(): return lax.all_to_all(copies, axis, 0, 0, tiled=True)]
    all_to_all x3, starting transfers between devices: 24.3 us -> 29.6 us  [gathered_copies(): return lax.all_to_all(copies, axis, 0, 0, tiled=True)]
    ppermute x1, waiting for transfers between devices: 6.96 us -> 2.94 us  [spread_weight(): lax.ppermute(weight, ('dp', 'seq'), partner_pairs)]
    sub x4, matrix products: 5.94 us -> 8.59 us  [attend_first(): weights = jnp.where(visible[None], jnp.exp(masked - highest), 0.0)]
    div x0 -> x2, other arithmetic: none -> 2.54 us  [attend_first(): attention = weights / jnp.sum(weights, axis=-1, keepdims=True)]
    unnamed x77 -> x61, local copies, waits for them, and re-layouts: 16.6 us -> 17.7 us
  transfers between devices with their start and end apart: 16 -> 16, of which waited for: 9 -> 9; matrix products, arithmetic and copies ran while one was open for 27% -> 31% of each run, Pallas kernels for 0% -> 0%
where the time goes in v12:
time: 198 us; the launch traced here: 196 us
  starting transfers between devices  58.7 us (30%)
  waiting for transfers between devices  57.6 us (29%)
  matrix products  33.2 us (17%)
  local copies, waits for them, and re-layouts  27.7 us (14%)
  other arithmetic  17.2 us (9%)
    all_to_all x3, starting transfers between devices, gathered_copies(): return lax.all_to_all(copies, axis, 0, 0, tiled=True)  29.6 us
    all_to_all x3, waiting for transfers between devices, gathered_copies(): return lax.all_to_all(copies, axis, 0, 0, tiled=True)  28 us
    ppermute x3, waiting for transfers between devices, spread_weight(): ring.append(lax.ppermute(held, 'dp', pairs))  20.4 us
    unnamed x61, local copies, waits for them, and re-layouts  17.7 us
    ppermute x4, starting transfers between devices, passed_along(): return lax.ppermute(array, axis, pairs)  13.5 us
    ppermute x2, starting transfers between devices, with_halo(): lax.ppermute(tail, axis, [(i, (i + 1) % count) for i in range(ends)])  8.62 us
    sub x4, matrix products, attend_first(): weights = jnp.where(visible[None], jnp.exp(masked - highest), 0.0)  8.59 us
    ppermute x4, waiting for transfers between devices, passed_along(): return lax.ppermute(array, axis, pairs)  6.21 us
  transfers between devices with their start and end apart: 16, of which 9 were waited for; matrix products, arithmetic and copies ran while one was open for 31% of the time, Pallas kernels for 0%

profile of v12, /device:TPU:26, one launch (start us, length us, event | category | flops | bytes accessed | tf_op | source)
XLA Modules:
  0.0 195.5 jit_solution(10782990795132705479)
XLA Ops:
  1.7 3.8 %collective-permute-start.1 = (bf16[128,512]{0,1:T(8,128)(2,1)S(1)}, bf16[128,512]{0,1:T(8,128)(2,1)S(1)}, u32[]{:S(2)}, u32[]{:S(2)}) collective-permute-start(bf16[128,512]{0,1:T(8,128)(2,1)S(1)} %bitcast.333), channel_id=1, source_target_pairs={{0,1},{1,2},{2,3},{3,4},{4,5},{5,6},{6,7},{7,8},{8,9},{9,10},{10,1... | collective-permute-start | bytes 393224 | tf_op jit(solution)/shard_map/ppermute | solution.py:17
  10.8 2.7 %copy.88 = bf16[1,128,5120]{1,2,0:T(8,128)(2,1)} copy(bf16[1,128,5120]{2,1,0:T(8,128)(2,1)} %param.7) | data formatting | bytes 2621440 | tf_op args[0]
  13.9 2.9 %collective-permute-done = bf16[320,512]{1,0:T(8,128)(2,1)S(1)} collective-permute-done((bf16[320,512]{1,0:T(8,128)(2,1)}, bf16[320,512]{1,0:T(8,128)(2,1)S(1)}, u32[]{:S(2)}, u32[]{:S(2)}) %collective-permute-start) | collective-permute-done | bytes 327712 | tf_op jit(solution)/shard_map/ppermute | solution.py:44
  18.9 2.6 %collective-permute-start.4 = (bf16[2,320,512]{2,1,0:T(8,128)(2,1)S(1)}, bf16[2,320,512]{2,1,0:T(8,128)(2,1)}, u32[]{:S(2)}, u32[]{:S(2)}) collective-permute-start(bf16[2,320,512]{2,1,0:T(8,128)(2,1)S(1)} %pad_maximum_fusion.4), channel_id=1, source_target_pairs={{0,64},{16,80},{32,96},{48,112},{64,0},{80,16},{96,32},{112,48},{1... | collective-permute-start | bytes 1966088 | tf_op jit(solution)/shard_map/ppermute | solution.py:52
  24.6 2.4 %fusion.80 = (f32[5,128]{1,0:T(8,128)S(1)}, f32[5,128,384]{1,2,0:T(8,128)}) fusion(pred[128,384]{0,1:T(8,128)(4,1)S(1)} %or_and_fusion, bf16[128,4,5,128]{0,3,2,1:T(8,128)(2,1)S(1)} %bitcast.318, bf16[384,4,128]{0,2,1:T(8,128)(2,1)} %bitcast.326), kind=kOutput, calls=%fused_computation.158 | convolution fusion | flops 64143744 | bytes 1346048 | tf_op jit(solution)/shard_map/sub | solution.py:124
  29.1 7.3 %collective-permute-done.3 = bf16[2,320,512]{2,1,0:T(8,128)(2,1)} collective-permute-done((bf16[2,320,512]{2,1,0:T(8,128)(2,1)S(1)}, bf16[2,320,512]{2,1,0:T(8,128)(2,1)}, u32[]{:S(2)}, u32[]{:S(2)}) %collective-permute-start.3) | collective-permute-done | bytes 655392 | tf_op jit(solution)/shard_map/ppermute | solution.py:52
  38.2 11.4 %collective-permute-done.5 = bf16[2,320,512]{2,1,0:T(8,128)(2,1)} collective-permute-done((bf16[2,320,512]{2,1,0:T(8,128)(2,1)S(1)}, bf16[2,320,512]{2,1,0:T(8,128)(2,1)}, u32[]{:S(2)}, u32[]{:S(2)}) %collective-permute-start.5) | collective-permute-done | bytes 655392 | tf_op jit(solution)/shard_map/ppermute | solution.py:52
  49.6 3.3 %pad_maximum_fusion.1 = bf16[4,2,320,512]{3,2,1,0:T(8,128)(2,1)} fusion(bf16[1,2,320,512]{3,2,1,0:T(8,128)(2,1)} %bitcast.9, bf16[1,2,320,512]{3,2,1,0:T(8,128)(2,1)} %bitcast.8, bf16[1,2,320,512]{3,2,1,0:T(8,128)(2,1)} %bitcast.7, bf16[1,2,320,512]{3,2,1,0:T(8,128)(2,1)S(1)} %bitcast.315), kind=kLoop, calls=%fused_computation.8 | loop fusion | flops 3932160 | bytes 5242880 | tf_op jit(solution)/shard_map/stack | solution.py:53
  53.0 8.3 %all-to-all-start = ((bf16[16,128,320]{1,2,0:T(8,128)(2,1)}), bf16[16,128,320]{1,2,0:T(8,128)(2,1)}, u32[]{:S(2)}, u32[]{:S(2)}) async-start(bf16[16,128,320]{1,2,0:T(8,128)(2,1)} %bitcast.11), calls=%async_computation | async-start | bytes 2621440 | tf_op jit(solution)/shard_map/all_to_all | solution.py:78
  61.3 2.4 %fusion.79 = (f32[5,128]{1,0:T(8,128)S(1)}, f32[5,128,384]{1,2,0:T(8,128)}) fusion(pred[128,384]{0,1:T(8,128)(4,1)S(1)} %or_and_fusion, bf16[128,4,5,128]{0,3,2,1:T(8,128)(2,1)S(1)} %bitcast.319, bf16[384,4,128]{0,2,1:T(8,128)(2,1)} %bitcast.327), kind=kOutput, calls=%fused_computation.157 | convolution fusion | flops 64143744 | bytes 1346048 | tf_op jit(solution)/shard_map/sub | solution.py:124
  63.7 2.2 %convolution_bitcast_fusion.5 = f32[384,128]{1,0:T(8,128)} fusion(bf16[128,4,5,128]{0,3,2,1:T(8,128)(2,1)S(1)} %bitcast.309, f32[5,128,384]{1,2,0:T(8,128)} %get-tuple-element.53, f32[5,128]{1,0:T(8,128)S(1)} %get-tuple-element.52), kind=kOutput, calls=%fused_computation.52 | convolution fusion | flops 63406080 | bytes 1347584 | tf_op jit(solution)/shard_map/gqk,qgd->kd/dot_general | solution.py:129
  65.9 2.4 %fusion.78 = (f32[5,128]{1,0:T(8,128)S(1)}, f32[5,128,384]{1,2,0:T(8,128)}) fusion(pred[128,384]{0,1:T(8,128)(4,1)S(1)} %or_and_fusion, bf16[128,4,5,128]{0,3,2,1:T(8,128)(2,1)S(1)} %bitcast.320, bf16[384,4,128]{0,2,1:T(8,128)(2,1)} %bitcast.328), kind=kOutput, calls=%fused_computation.156 | convolution fusion | flops 64143744 | bytes 1346048 | tf_op jit(solution)/shard_map/sub | solution.py:124
  69.9 11.0 %all-to-all-done = bf16[16,128,320]{1,2,0:T(8,128)(2,1)} async-done(((bf16[16,128,320]{1,2,0:T(8,128)(2,1)}), bf16[16,128,320]{1,2,0:T(8,128)(2,1)}, u32[]{:S(2)}, u32[]{:S(2)}) %all-to-all-start) | async-done | bytes 1310752 | tf_op jit(solution)/shard_map/all_to_all | solution.py:78
  83.7 4.8 %collective-permute-start.7 = (f32[128,512]{1,0:T(8,128)}, f32[128,512]{1,0:T(8,128)}, u32[]{:S(2)}, u32[]{:S(2)}) collective-permute-start(f32[128,512]{1,0:T(8,128)} %get-tuple-element.45), channel_id=1, source_target_pairs={{0,1},{1,2},{2,3},{3,4},{4,5},{5,6},{6,7},{7,8},{8,9},{9,10},{10,1... | collective-permute-start | bytes 786440 | tf_op jit(solution)/shard_map/ppermute | solution.py:91
  94.1 4.9 %collective-permute-done.7 = f32[128,512]{1,0:T(8,128)} collective-permute-done((f32[128,512]{1,0:T(8,128)}, f32[128,512]{1,0:T(8,128)}, u32[]{:S(2)}, u32[]{:S(2)}) %collective-permute-start.7) | collective-permute-done | bytes 262176 | tf_op jit(solution)/shard_map/ppermute | solution.py:91
  100.2 3.0 %pad_maximum_fusion = bf16[2,4,2,320,512]{4,3,2,1,0:T(8,128)(2,1)S(1)} fusion(bf16[1,4,2,320,512]{4,3,2,1,0:T(8,128)(2,1)} %bitcast.42, bf16[1,4,2,320,512]{4,3,2,1,0:T(8,128)(2,1)} %bitcast.41), kind=kLoop, calls=%fused_computation.7 | loop fusion | flops 2621440 | bytes 10485760 | tf_op jit(solution)/shard_map/stack | solution.py:63
  107.4 4.8 %collective-permute-start.9 = (bf16[128,512]{1,0:T(8,128)(2,1)S(1)}, bf16[128,512]{1,0:T(8,128)(2,1)}, u32[]{:S(2)}, u32[]{:S(2)}) collective-permute-start(bf16[128,512]{1,0:T(8,128)(2,1)S(1)} %fusion.38), channel_id=1, source_target_pairs={{0,1},{1,2},{2,3},{3,4},{4,5},{5,6},{6,7},{7,8},{8,9},{9,10},{10,1... | collective-permute-start | bytes 393224 | tf_op jit(solution)/shard_map/ppermute | solution.py:17
  114.2 4.9 %all-to-all-start.1 = ((bf16[16,128,512]{1,2,0:T(8,128)(2,1)}), bf16[16,128,512]{1,2,0:T(8,128)(2,1)}, u32[]{:S(2)}, u32[]{:S(2)}) async-start(bf16[16,128,512]{1,2,0:T(8,128)(2,1)} %broadcast_in_dim.114), calls=%async_computation.1 | async-start | bytes 4194304 | tf_op jit(solution)/shard_map/all_to_all | solution.py:78
  119.1 5.3 %convolution_convert_fusion = bf16[128,5120]{1,0:T(8,128)(2,1)} fusion(bf16[128,512]{1,0:T(8,128)(2,1)S(1)} %add_convert_fusion, bf16[5120,512]{1,0:T(8,128)(2,1)} %bitcast.304), kind=kOutput, calls=%fused_computation.6 | convolution fusion | flops 671744000 | bytes 6684672 | tf_op jit(solution)/shard_map/dot_general | solution.py:227
  128.0 2.4 %copy.130 = bf16[1,128,5120]{2,1,0:T(8,128)(2,1)} copy(bf16[1,128,5120]{1,2,0:T(8,128)(2,1)} %bitcast.306) | data formatting | bytes 2621440
  143.4 4.8 %collective-permute-start.12 = (f32[128,512]{0,1:T(8,128)}, f32[128,512]{0,1:T(8,128)}, u32[]{:S(2)}, u32[]{:S(2)}) collective-permute-start(f32[128,512]{0,1:T(8,128)} %get-tuple-element.43), channel_id=1, source_target_pairs={{0,1},{1,2},{2,3},{3,4},{4,5},{5,6},{6,7},{7,8},{8,9},{9,10},{10,1... | collective-permute-start | bytes 786440 | tf_op jit(solution)/shard_map/ppermute | solution.py:91
  150.3 4.1 %fusion.28 = f32[16,320,32]{1,2,0:T(8,128)} fusion(bf16[16,128,16,32]{1,3,2,0:T(8,128)(2,1)} %bitcast.78, bf16[16,128,320]{1,2,0:T(8,128)(2,1)} %all-to-all-done), kind=kOutput, calls=%fused_computation.41 | convolution fusion | flops 671088640 | bytes 4063232 | tf_op jit(solution)/shard_map/rtk,rtjc->jkc/dot_general | solution.py:212
  154.4 16.4 %all-to-all-start.2 = ((f32[16,320,32]{1,2,0:T(8,128)}), f32[16,320,32]{1,2,0:T(8,128)}, u32[]{:S(2)}, u32[]{:S(2)}) async-start(f32[16,320,32]{1,2,0:T(8,128)} %fusion.28), calls=%async_computation.2 | async-start | bytes 1572864 | tf_op jit(solution)/shard_map/all_to_all | solution.py:78
  178.8 14.9 %all-to-all-done.2 = f32[16,320,32]{1,2,0:T(8,128)} async-done(((f32[16,320,32]{1,2,0:T(8,128)}), f32[16,320,32]{1,2,0:T(8,128)}, u32[]{:S(2)}, u32[]{:S(2)}) %all-to-all-start.2) | async-done | bytes 655392 | tf_op jit(solution)/shard_map/all_to_all | solution.py:78
  (131 shorter events, 61.2 us)
Async XLA Ops:
  1.7 12.2 %collective-permute-start.1 = (bf16[128,512]{0,1:T(8,128)(2,1)S(1)}, bf16[128,512]{0,1:T(8,128)(2,1)S(1)}, u32[]{:S(2)}, u32[]{:S(2)}) collective-permute-start(bf16[128,512]{0,1:T(8,128)(2,1)S(1)} %bitcast.333), channel_id=1, source_target_pairs={{0,1},{1,2},{2,3},{3,4},{4,5},{5,6},{6,7},{7,8},{8,9},{9,10},{10,1... | collective-permute-start | bytes 393224 | tf_op jit(solution)/shard_map/ppermute | solution.py:17
  5.5 8.4 %collective-permute-start.2 = (bf16[128,512]{0,1:T(8,128)(2,1)S(1)}, bf16[128,512]{0,1:T(8,128)(2,1)S(1)}, u32[]{:S(2)}, u32[]{:S(2)}) collective-permute-start(bf16[128,512]{0,1:T(8,128)(2,1)S(1)} %bitcast.334), channel_id=1, source_target_pairs={{1,0},{2,1},{3,2},{4,3},{5,4},{6,5},{7,6},{8,7},{9,8},{10,9},{11,1... | collective-permute-start | bytes 393224 | tf_op jit(solution)/shard_map/ppermute | solution.py:19
  7.5 9.3 %collective-permute-start = (bf16[320,512]{1,0:T(8,128)(2,1)}, bf16[320,512]{1,0:T(8,128)(2,1)S(1)}, u32[]{:S(2)}, u32[]{:S(2)}) collective-permute-start(bf16[320,512]{1,0:T(8,128)(2,1)} %param.11), channel_id=1, source_target_pairs={{0,129},{1,128},{2,131},{3,130},{4,133},{5,132},{6,135},{7,134},{8... | collective-permute-start | bytes 983048 | tf_op jit(solution)/shard_map/ppermute | solution.py:44
  9.1 15.5 %copy-start.7 = (bf16[1,128,2560]{1,2,0:T(8,128)(2,1)}, bf16[1,128,2560]{1,2,0:T(8,128)(2,1)S(1)}, u32[]{:S(2)}) copy-start(bf16[1,128,2560]{1,2,0:T(8,128)(2,1)S(1)} %copy.89) | copy-start | bytes 1966084
  9.1 8.5 %copy-start.13 = (bf16[320,512]{1,0:T(8,128)(2,1)S(1)}, bf16[320,512]{1,0:T(8,128)(2,1)}, u32[]{:S(2)}) copy-start(bf16[320,512]{1,0:T(8,128)(2,1)} %param.11) | copy-start | bytes 983044
  10.8 57.5 %copy-start.4 = (bf16[1,128,2560]{1,2,0:T(8,128)(2,1)}, bf16[1,128,2560]{1,2,0:T(8,128)(2,1)S(1)}, u32[]{:S(2)}) copy-start(bf16[1,128,2560]{1,2,0:T(8,128)(2,1)S(1)} %copy.93) | copy-start | bytes 1966084
  13.9 9.1 %copy-start.10 = (bf16[384,512]{0,1:T(8,128)(2,1)}, bf16[384,512]{0,1:T(8,128)(2,1)S(1)}, u32[]{:S(2)}) copy-start(bf16[384,512]{0,1:T(8,128)(2,1)S(1)} %pad_maximum_fusion.6) | copy-start | bytes 1179652
  18.6 17.9 %collective-permute-start.3 = (bf16[2,320,512]{2,1,0:T(8,128)(2,1)S(1)}, bf16[2,320,512]{2,1,0:T(8,128)(2,1)}, u32[]{:S(2)}, u32[]{:S(2)}) collective-permute-start(bf16[2,320,512]{2,1,0:T(8,128)(2,1)S(1)} %pad_maximum_fusion.4), channel_id=1, source_target_pairs={{0,32},{16,48},{32,64},{48,80},{64,96},{80,112},{96,0},{112,16},{1... | collective-permute-start | bytes 1966088 | tf_op jit(solution)/shard_map/ppermute | solution.py:52
  18.9 19.3 %collective-permute-start.4 = (bf16[2,320,512]{2,1,0:T(8,128)(2,1)S(1)}, bf16[2,320,512]{2,1,0:T(8,128)(2,1)}, u32[]{:S(2)}, u32[]{:S(2)}) collective-permute-start(bf16[2,320,512]{2,1,0:T(8,128)(2,1)S(1)} %pad_maximum_fusion.4), channel_id=1, source_target_pairs={{0,64},{16,80},{32,96},{48,112},{64,0},{80,16},{96,32},{112,48},{1... | collective-permute-start | bytes 1966088 | tf_op jit(solution)/shard_map/ppermute | solution.py:52
  21.5 28.1 %collective-permute-start.5 = (bf16[2,320,512]{2,1,0:T(8,128)(2,1)S(1)}, bf16[2,320,512]{2,1,0:T(8,128)(2,1)}, u32[]{:S(2)}, u32[]{:S(2)}) collective-permute-start(bf16[2,320,512]{2,1,0:T(8,128)(2,1)S(1)} %pad_maximum_fusion.4), channel_id=1, source_target_pairs={{0,96},{16,112},{32,0},{48,16},{64,32},{80,48},{96,64},{112,80},{1... | collective-permute-start | bytes 1966088 | tf_op jit(solution)/shard_map/ppermute | solution.py:52
  52.9 8.4 %copy-start.8 = (bf16[1,128,2560]{1,2,0:T(8,128)(2,1)S(1)}, bf16[1,128,2560]{1,2,0:T(8,128)(2,1)}, u32[]{:S(2)}) copy-start(bf16[1,128,2560]{1,2,0:T(8,128)(2,1)} %copy-done.7) | copy-start | bytes 1966084
  52.9 47.3 %collective-permute-start.8 = (bf16[4,2,320,512]{3,2,1,0:T(8,128)(2,1)}, bf16[4,2,320,512]{3,2,1,0:T(8,128)(2,1)}, u32[]{:S(2)}, u32[]{:S(2)}) collective-permute-start(bf16[4,2,320,512]{3,2,1,0:T(8,128)(2,1)} %pad_maximum_fusion.1), channel_id=1, source_target_pairs={{0,16},{16,0},{32,48},{48,32},{64,80},{80,64},{96,112},{112,96},{1... | collective-permute-start | bytes 7864328 | tf_op jit(solution)/shard_map/ppermute | solution.py:62
  53.0 27.9 %all-to-all-start = ((bf16[16,128,320]{1,2,0:T(8,128)(2,1)}), bf16[16,128,320]{1,2,0:T(8,128)(2,1)}, u32[]{:S(2)}, u32[]{:S(2)}) async-start(bf16[16,128,320]{1,2,0:T(8,128)(2,1)} %bitcast.11), calls=%async_computation | async-start | bytes 2621440 | tf_op jit(solution)/shard_map/all_to_all | solution.py:78
  69.9 20.0 %copy-start.3 = (f32[384,512]{1,0:T(8,128)}, f32[384,512]{1,0:T(8,128)S(1)}, u32[]{:S(2)}) copy-start(f32[384,512]{1,0:T(8,128)S(1)} %pad_maximum_fusion.2) | copy-start | bytes 2359300
  81.8 11.6 %collective-permute-start.6 = (f32[128,512]{1,0:T(8,128)}, f32[128,512]{1,0:T(8,128)S(1)}, u32[]{:S(2)}, u32[]{:S(2)}) collective-permute-start(f32[128,512]{1,0:T(8,128)} %get-tuple-element.44), channel_id=1, source_target_pairs={{1,0},{2,1},{3,2},{4,3},{5,4},{6,5},{7,6},{8,7},{9,8},{10,9},{11,1... | collective-permute-start | bytes 786440 | tf_op jit(solution)/shard_map/ppermute | solution.py:91
  83.7 15.3 %collective-permute-start.7 = (f32[128,512]{1,0:T(8,128)}, f32[128,512]{1,0:T(8,128)}, u32[]{:S(2)}, u32[]{:S(2)}) collective-permute-start(f32[128,512]{1,0:T(8,128)} %get-tuple-element.45), channel_id=1, source_target_pairs={{0,1},{1,2},{2,3},{3,4},{4,5},{5,6},{6,7},{7,8},{8,9},{9,10},{10,1... | collective-permute-start | bytes 786440 | tf_op jit(solution)/shard_map/ppermute | solution.py:91
  105.5 24.9 %collective-permute-start.10 = (bf16[128,512]{1,0:T(8,128)(2,1)S(1)}, bf16[128,512]{1,0:T(8,128)(2,1)}, u32[]{:S(2)}, u32[]{:S(2)}) collective-permute-start(bf16[128,512]{1,0:T(8,128)(2,1)S(1)} %fusion.38), channel_id=1, source_target_pairs={{1,0},{2,1},{3,2},{4,3},{5,4},{6,5},{7,6},{8,7},{9,8},{10,9},{11,1... | collective-permute-start | bytes 393224 | tf_op jit(solution)/shard_map/ppermute | solution.py:19
  107.4 23.0 %collective-permute-start.9 = (bf16[128,512]{1,0:T(8,128)(2,1)S(1)}, bf16[128,512]{1,0:T(8,128)(2,1)}, u32[]{:S(2)}, u32[]{:S(2)}) collective-permute-start(bf16[128,512]{1,0:T(8,128)(2,1)S(1)} %fusion.38), channel_id=1, source_target_pairs={{0,1},{1,2},{2,3},{3,4},{4,5},{5,6},{6,7},{7,8},{8,9},{9,10},{10,1... | collective-permute-start | bytes 393224 | tf_op jit(solution)/shard_map/ppermute | solution.py:17
  114.2 36.1 %all-to-all-start.1 = ((bf16[16,128,512]{1,2,0:T(8,128)(2,1)}), bf16[16,128,512]{1,2,0:T(8,128)(2,1)}, u32[]{:S(2)}, u32[]{:S(2)}) async-start(bf16[16,128,512]{1,2,0:T(8,128)(2,1)} %broadcast_in_dim.114), calls=%async_computation.1 | async-start | bytes 4194304 | tf_op jit(solution)/shard_map/all_to_all | solution.py:78
  133.7 4.4 %copy-start.23 = (f32[5,128,384]{1,2,0:T(8,128)}, f32[5,128,384]{1,2,0:T(8,128)S(1)}, u32[]{:S(2)}) copy-start(f32[5,128,384]{1,2,0:T(8,128)S(1)} %get-tuple-element.61) | copy-start | bytes 2949124
  141.5 35.4 %collective-permute-start.11 = (f32[128,512]{0,1:T(8,128)}, f32[128,512]{0,1:T(8,128)}, u32[]{:S(2)}, u32[]{:S(2)}) collective-permute-start(f32[128,512]{0,1:T(8,128)} %get-tuple-element.42), channel_id=1, source_target_pairs={{1,0},{2,1},{3,2},{4,3},{5,4},{6,5},{7,6},{8,7},{9,8},{10,9},{11,1... | collective-permute-start | bytes 786440 | tf_op jit(solution)/shard_map/ppermute | solution.py:91
  143.4 33.5 %collective-permute-start.12 = (f32[128,512]{0,1:T(8,128)}, f32[128,512]{0,1:T(8,128)}, u32[]{:S(2)}, u32[]{:S(2)}) collective-permute-start(f32[128,512]{0,1:T(8,128)} %get-tuple-element.43), channel_id=1, source_target_pairs={{0,1},{1,2},{2,3},{3,4},{4,5},{5,6},{6,7},{7,8},{8,9},{9,10},{10,1... | collective-permute-start | bytes 786440 | tf_op jit(solution)/shard_map/ppermute | solution.py:91
  150.3 20.5 %copy-start.11 = (bf16[384,512]{0,1:T(8,128)(2,1)S(1)}, bf16[384,512]{0,1:T(8,128)(2,1)}, u32[]{:S(2)}) copy-start(bf16[384,512]{0,1:T(8,128)(2,1)} %copy-done.10) | copy-start | bytes 1179652
  154.4 39.3 %all-to-all-start.2 = ((f32[16,320,32]{1,2,0:T(8,128)}), f32[16,320,32]{1,2,0:T(8,128)}, u32[]{:S(2)}, u32[]{:S(2)}) async-start(f32[16,320,32]{1,2,0:T(8,128)} %fusion.28), calls=%async_computation.2 | async-start | bytes 1572864 | tf_op jit(solution)/shard_map/all_to_all | solution.py:78
  (19 other events, 36.1 us)

commit v13 on v9

--- a/solution.py
+++ b/solution.py
@@ -155,9 +155,9 @@
     lower_rim = grad_block[:tok_count]
     upper_rim = grad_block[tok_count + tok_count :]
     center = grad_block[tok_count : tok_count + tok_count]
-    from_upper = passed_along(lower_rim, "seq", -1)
-    from_lower = passed_along(upper_rim, "seq", 1)
-    return center + from_upper + from_lower
+    from_upper = passed_along(lower_rim.astype(jnp.bfloat16), "seq", -1)
+    from_lower = passed_along(upper_rim.astype(jnp.bfloat16), "seq", 1)
+    return center + from_upper.astype(jnp.float32) + from_lower.astype(jnp.float32)
 
 
 def local(layer_input, query_states, key_states, out_grad, value_weight, segment_ids, pair_split):

time: 194 us -> 181 us (0.933)
  local copies, waits for them, and re-layouts: 24.5 us -> 19.3 us
  waiting for transfers between devices: 67 us -> 62.3 us
  other arithmetic: 15.3 us -> 10.6 us
  starting transfers between devices: 53.6 us -> 55.9 us
    ppermute x4, waiting for transfers between devices: 20.2 us -> 1.13 us  [passed_along(): return lax.ppermute(array, axis, pairs)]
    all_to_all x3, waiting for transfers between devices: 20 us -> 28.6 us  [gathered_copies(): return lax.all_to_all(copies, axis, 0, 0, tiled=True)]
    ppermute x3, waiting for transfers between devices: 19.8 us -> 26.7 us  [spread_weight(): ring.append(lax.ppermute(held, 'dp', pairs))]
    unnamed x77 -> x65, local copies, waits for them, and re-layouts: 16.6 us -> 12.2 us
    another operation x2, other arithmetic: 4.81 us -> 1.93 us  [spread_weight(): jnp.stack(ring)]
    all_to_all x3, starting transfers between devices: 24.3 us -> 26.5 us  [gathered_copies(): return lax.all_to_all(copies, axis, 0, 0, tiled=True)]
  transfers between devices with their start and end apart: 16 -> 16, of which waited for: 9 -> 8; matrix products, arithmetic and copies ran while one was open for 27% -> 27% of each run, Pallas kernels for 0% -> 0%
where the time goes in v13:
time: 181 us; the launch traced here: 180 us
  waiting for transfers between devices  62.3 us (34%)
  starting transfers between devices  55.9 us (31%)
  matrix products  30.2 us (17%)
  local copies, waits for them, and re-layouts  19.3 us (11%)
  other arithmetic  10.6 us (6%)
    all_to_all x3, waiting for transfers between devices, gathered_copies(): return lax.all_to_all(copies, axis, 0, 0, tiled=True)  28.6 us
    ppermute x3, waiting for transfers between devices, spread_weight(): ring.append(lax.ppermute(held, 'dp', pairs))  26.7 us
    all_to_all x3, starting transfers between devices, gathered_copies(): return lax.all_to_all(copies, axis, 0, 0, tiled=True)  26.5 us
    ppermute x4, starting transfers between devices, passed_along(): return lax.ppermute(array, axis, pairs)  13.6 us
    unnamed x65, local copies, waits for them, and re-layouts  12.2 us
    ppermute x2, starting transfers between devices, with_halo(): lax.ppermute(tail, axis, [(i, (i + 1) % count) for i in range(ends)])  8.62 us
    dot_general x4, matrix products, attend_first(): jnp.einsum('gqk,qgd->kd', attention_low, grad_head, preferred_element_typ...  6.74 us
    sub x4, matrix products, attend_first(): weights = jnp.where(visible[None], jnp.exp(masked - highest), 0.0)  5.98 us
  transfers between devices with their start and end apart: 16, of which 8 were waited for; matrix products, arithmetic and copies ran while one was open for 27% of the time, Pallas kernels for 0%

profile of v13, /device:TPU:26, one launch (start us, length us, event | category | flops | bytes accessed | tf_op | source)
XLA Modules:
  0.0 179.5 jit_solution(15750117149139669014)
XLA Ops:
  1.8 3.8 %collective-permute-start.4 = (bf16[128,512]{0,1:T(8,128)(2,1)S(1)}, bf16[128,512]{0,1:T(8,128)(2,1)S(1)}, u32[]{:S(2)}, u32[]{:S(2)}) collective-permute-start(bf16[128,512]{0,1:T(8,128)(2,1)S(1)} %bitcast.324), channel_id=1, source_target_pairs={{0,1},{1,2},{2,3},{3,4},{4,5},{5,6},{6,7},{7,8},{8,9},{9,10},{10,1... | collective-permute-start | bytes 393224 | tf_op jit(solution)/shard_map/ppermute | solution.py:17
  5.6 2.0 %collective-permute-start.5 = (bf16[128,512]{0,1:T(8,128)(2,1)S(1)}, bf16[128,512]{0,1:T(8,128)(2,1)S(1)}, u32[]{:S(2)}, u32[]{:S(2)}) collective-permute-start(bf16[128,512]{0,1:T(8,128)(2,1)S(1)} %bitcast.325), channel_id=1, source_target_pairs={{1,0},{2,1},{3,2},{4,3},{5,4},{6,5},{7,6},{8,7},{9,8},{10,9},{11,1... | collective-permute-start | bytes 393224 | tf_op jit(solution)/shard_map/ppermute | solution.py:19
  7.8 2.5 %copy.90 = bf16[1,128,5120]{1,2,0:T(8,128)(2,1)} copy(bf16[1,128,5120]{2,1,0:T(8,128)(2,1)} %param.7) | data formatting | bytes 2621440 | tf_op args[0]
  11.3 5.7 %collective-permute-done = bf16[320,512]{1,0:T(8,128)(2,1)S(1)} collective-permute-done((bf16[320,512]{1,0:T(8,128)(2,1)}, bf16[320,512]{1,0:T(8,128)(2,1)S(1)}, u32[]{:S(2)}, u32[]{:S(2)}) %collective-permute-start) | collective-permute-done | bytes 327712 | tf_op jit(solution)/shard_map/ppermute | solution.py:44
  17.4 2.6 %collective-permute-start.2 = (bf16[2,320,512]{2,1,0:T(8,128)(2,1)S(1)}, bf16[2,320,512]{2,1,0:T(8,128)(2,1)S(1)}, u32[]{:S(2)}, u32[]{:S(2)}) collective-permute-start(bf16[2,320,512]{2,1,0:T(8,128)(2,1)S(1)} %get-tuple-element.33), channel_id=1, source_target_pairs={{0,64},{16,80},{32,96},{48,112},{64,0},{80,16},{96,32},{112,48},{1... | collective-permute-start | bytes 1966088 | tf_op jit(solution)/shard_map/ppermute | solution.py:51
  21.2 13.6 %collective-permute-done.1 = bf16[2,320,512]{2,1,0:T(8,128)(2,1)S(1)} collective-permute-done((bf16[2,320,512]{2,1,0:T(8,128)(2,1)S(1)}, bf16[2,320,512]{2,1,0:T(8,128)(2,1)S(1)}, u32[]{:S(2)}, u32[]{:S(2)}) %collective-permute-start.1) | collective-permute-done | bytes 655392 | tf_op jit(solution)/shard_map/ppermute | solution.py:51
  36.6 11.3 %collective-permute-done.3 = bf16[2,320,512]{2,1,0:T(8,128)(2,1)S(1)} collective-permute-done((bf16[2,320,512]{2,1,0:T(8,128)(2,1)S(1)}, bf16[2,320,512]{2,1,0:T(8,128)(2,1)S(1)}, u32[]{:S(2)}, u32[]{:S(2)}) %collective-permute-start.3) | collective-permute-done | bytes 655392 | tf_op jit(solution)/shard_map/ppermute | solution.py:51
  49.8 8.3 %all-to-all-start = ((bf16[16,128,320]{1,2,0:T(8,128)(2,1)}), bf16[16,128,320]{1,2,0:T(8,128)(2,1)S(1)}, u32[]{:S(2)}, u32[]{:S(2)}) async-start(bf16[16,128,320]{1,2,0:T(8,128)(2,1)} %bitcast.8), calls=%async_computation | async-start | bytes 2621440 | tf_op jit(solution)/shard_map/all_to_all | solution.py:69
  65.8 2.2 %convolution_bitcast_fusion.5 = f32[384,128]{0,1:T(8,128)} fusion(bf16[128,4,5,128]{0,3,2,1:T(8,128)(2,1)S(1)} %bitcast.318, f32[5,128,384]{1,2,0:T(8,128)} %get-tuple-element.45, f32[5,128]{1,0:T(8,128)S(1)} %get-tuple-element.44), kind=kOutput, calls=%fused_computation.52 | convolution fusion | flops 63406080 | bytes 1347584 | tf_op jit(solution)/shard_map/gqk,qgd->kd/dot_general | solution.py:116
  71.1 6.5 %all-to-all-done = bf16[16,128,320]{1,2,0:T(8,128)(2,1)S(1)} async-done(((bf16[16,128,320]{1,2,0:T(8,128)(2,1)}), bf16[16,128,320]{1,2,0:T(8,128)(2,1)S(1)}, u32[]{:S(2)}, u32[]{:S(2)}) %all-to-all-start) | async-done | bytes 1310752 | tf_op jit(solution)/shard_map/all_to_all | solution.py:69
  77.7 1.9 %collective-permute-start.6 = (bf16[128,512]{0,1:T(8,128)(2,1)S(1)}, bf16[128,512]{0,1:T(8,128)(2,1)S(1)}, u32[]{:S(2)}, u32[]{:S(2)}) collective-permute-start(bf16[128,512]{0,1:T(8,128)(2,1)S(1)} %get-tuple-element.40), channel_id=1, source_target_pairs={{1,0},{2,1},{3,2},{4,3},{5,4},{6,5},{7,6},{8,7},{9,8},{10,9},{11,1... | collective-permute-start | bytes 393224 | tf_op jit(solution)/shard_map/ppermute | solution.py:82
  79.6 4.8 %collective-permute-start.7 = (bf16[128,512]{0,1:T(8,128)(2,1)S(1)}, bf16[128,512]{0,1:T(8,128)(2,1)S(1)}, u32[]{:S(2)}, u32[]{:S(2)}) collective-permute-start(bf16[128,512]{0,1:T(8,128)(2,1)S(1)} %get-tuple-element.41), channel_id=1, source_target_pairs={{0,1},{1,2},{2,3},{3,4},{4,5},{5,6},{6,7},{7,8},{8,9},{9,10},{10,1... | collective-permute-start | bytes 393224 | tf_op jit(solution)/shard_map/ppermute | solution.py:82
  85.7 2.1 %gather_fusion = bf16[16,128,320]{1,2,0:T(8,128)(2,1)S(1)} fusion(bf16[128,16,320]{0,2,1:T(8,128)(2,1)} %bitcast.7, s32[1024]{0:T(1024)S(1)} %pad_clamp_fusion.1), kind=kCustom, calls=%fused_computation | custom fusion | bytes 2621504 | tf_op jit(solution)/shard_map/jit(_take)/gather | solution.py:204
  89.0 3.0 %pad_maximum_fusion = bf16[2,4,2,320,512]{4,3,2,1,0:T(8,128)(2,1)S(1)} fusion(bf16[1,4,2,320,512]{4,3,2,1,0:T(8,128)(2,1)} %bitcast.42, bf16[1,4,2,320,512]{4,3,2,1,0:T(8,128)(2,1)} %bitcast.41), kind=kLoop, calls=%fused_computation.7 | loop fusion | flops 2621440 | bytes 10485760 | tf_op jit(solution)/shard_map/stack | solution.py:54
  96.3 4.8 %collective-permute-start.9 = (bf16[128,512]{1,0:T(8,128)(2,1)S(1)}, bf16[128,512]{1,0:T(8,128)(2,1)}, u32[]{:S(2)}, u32[]{:S(2)}) collective-permute-start(bf16[128,512]{1,0:T(8,128)(2,1)S(1)} %fusion.38), channel_id=1, source_target_pairs={{0,1},{1,2},{2,3},{3,4},{4,5},{5,6},{6,7},{7,8},{8,9},{9,10},{10,1... | collective-permute-start | bytes 393224 | tf_op jit(solution)/shard_map/ppermute | solution.py:17
  102.9 4.9 %all-to-all-start.1 = ((bf16[16,128,512]{1,2,0:T(8,128)(2,1)}), bf16[16,128,512]{1,2,0:T(8,128)(2,1)}, u32[]{:S(2)}, u32[]{:S(2)}) async-start(bf16[16,128,512]{1,2,0:T(8,128)(2,1)} %broadcast_in_dim.114), calls=%async_computation.1 | async-start | bytes 4194304 | tf_op jit(solution)/shard_map/all_to_all | solution.py:69
  107.8 4.4 %convolution_convert_fusion = bf16[128,5120]{1,0:T(8,128)(2,1)S(1)} fusion(bf16[128,512]{0,1:T(8,128)(2,1)S(1)} %add_convert_fusion, bf16[5120,512]{1,0:T(8,128)(2,1)} %bitcast.301), kind=kOutput, calls=%fused_computation.6 | convolution fusion | flops 671744000 | bytes 6684672 | tf_op jit(solution)/shard_map/dot_general | solution.py:213
  124.6 2.0 %collective-permute-start.11 = (bf16[128,512]{0,1:T(8,128)(2,1)}, bf16[128,512]{0,1:T(8,128)(2,1)S(1)}, u32[]{:S(2)}, u32[]{:S(2)}) collective-permute-start(bf16[128,512]{0,1:T(8,128)(2,1)} %get-tuple-element.34), channel_id=1, source_target_pairs={{1,0},{2,1},{3,2},{4,3},{5,4},{6,5},{7,6},{8,7},{9,8},{10,9},{11,1... | collective-permute-start | bytes 393224 | tf_op jit(solution)/shard_map/ppermute | solution.py:82
  126.6 4.8 %collective-permute-start.12 = (bf16[128,512]{0,1:T(8,128)(2,1)}, bf16[128,512]{0,1:T(8,128)(2,1)}, u32[]{:S(2)}, u32[]{:S(2)}) collective-permute-start(bf16[128,512]{0,1:T(8,128)(2,1)} %get-tuple-element.35), channel_id=1, source_target_pairs={{0,1},{1,2},{2,3},{3,4},{4,5},{5,6},{6,7},{7,8},{8,9},{9,10},{10,1... | collective-permute-start | bytes 393224 | tf_op jit(solution)/shard_map/ppermute | solution.py:82
  132.2 6.8 %all-to-all-done.1 = bf16[16,128,512]{1,2,0:T(8,128)(2,1)} async-done(((bf16[16,128,512]{1,2,0:T(8,128)(2,1)}), bf16[16,128,512]{1,2,0:T(8,128)(2,1)}, u32[]{:S(2)}, u32[]{:S(2)}) %all-to-all-start.1) | async-done | bytes 2097184 | tf_op jit(solution)/shard_map/all_to_all | solution.py:69
  139.0 3.7 %fusion.28 = f32[16,320,32]{1,2,0:T(8,128)} fusion(bf16[16,128,16,32]{1,3,2,0:T(8,128)(2,1)} %bitcast.78, bf16[16,128,320]{1,2,0:T(8,128)(2,1)S(1)} %copy-done.2), kind=kOutput, calls=%fused_computation.41 | convolution fusion | flops 671088640 | bytes 4063232 | tf_op jit(solution)/shard_map/rtk,rtjc->jkc/dot_general | solution.py:198
  142.7 13.3 %all-to-all-start.2 = ((f32[16,320,32]{1,2,0:T(8,128)}), f32[16,320,32]{1,2,0:T(8,128)S(1)}, u32[]{:S(2)}, u32[]{:S(2)}) async-start(f32[16,320,32]{1,2,0:T(8,128)} %fusion.28), calls=%async_computation.2 | async-start | bytes 1572864 | tf_op jit(solution)/shard_map/all_to_all | solution.py:69
  156.1 2.3 %fusion.47 = bf16[128,1,5,128]{0,3,2,1:T(8,128)(2,1)S(1)} fusion(f32[5,128,384]{1,2,0:T(8,128)} %copy-done.26, f32[5,128]{1,0:T(8,128)S(1)} %get-tuple-element.54, bf16[384,4,128]{0,2,1:T(8,128)(2,1)S(1)} %bitcast.332, f32[5,128,384]{1,2,0:T(8,128)} %get-tuple-element.47, f32[5,128]{1,0:T(8,128)S(1)} %get-tuple-element.46), kind=kOutput, calls=%fused_computation.66 | convolution fusion | flops 378388480 | bytes 2236416 | tf_op jit(solution)/shard_map/gqk,kd->qgd/dot_general | solution.py:145
  163.6 15.3 %all-to-all-done.2 = f32[16,320,32]{1,2,0:T(8,128)S(1)} async-done(((f32[16,320,32]{1,2,0:T(8,128)}), f32[16,320,32]{1,2,0:T(8,128)S(1)}, u32[]{:S(2)}, u32[]{:S(2)}) %all-to-all-start.2) | async-done | bytes 655392 | tf_op jit(solution)/shard_map/all_to_all | solution.py:69
  (134 shorter events, 45.3 us)
Async XLA Ops:
  0.6 9.6 %copy-start.3 = (bf16[1,128,2560]{2,1,0:T(8,128)(2,1)S(1)}, bf16[1,128,2560]{2,1,0:T(8,128)(2,1)}, u32[]{:S(2)}) copy-start(bf16[1,128,2560]{2,1,0:T(8,128)(2,1)} %param.8) | copy-start | bytes 1966084
  0.6 10.0 %copy-start.4 = (bf16[1,128,2560]{2,1,0:T(8,128)(2,1)S(1)}, bf16[1,128,2560]{2,1,0:T(8,128)(2,1)}, u32[]{:S(2)}) copy-start(bf16[1,128,2560]{2,1,0:T(8,128)(2,1)} %param.10) | copy-start | bytes 1966084
  1.8 18.6 %collective-permute-start.4 = (bf16[128,512]{0,1:T(8,128)(2,1)S(1)}, bf16[128,512]{0,1:T(8,128)(2,1)S(1)}, u32[]{:S(2)}, u32[]{:S(2)}) collective-permute-start(bf16[128,512]{0,1:T(8,128)(2,1)S(1)} %bitcast.324), channel_id=1, source_target_pairs={{0,1},{1,2},{2,3},{3,4},{4,5},{5,6},{6,7},{7,8},{8,9},{9,10},{10,1... | collective-permute-start | bytes 393224 | tf_op jit(solution)/shard_map/ppermute | solution.py:17
  5.6 14.8 %collective-permute-start.5 = (bf16[128,512]{0,1:T(8,128)(2,1)S(1)}, bf16[128,512]{0,1:T(8,128)(2,1)S(1)}, u32[]{:S(2)}, u32[]{:S(2)}) collective-permute-start(bf16[128,512]{0,1:T(8,128)(2,1)S(1)} %bitcast.325), channel_id=1, source_target_pairs={{1,0},{2,1},{3,2},{4,3},{5,4},{6,5},{7,6},{8,7},{9,8},{10,9},{11,1... | collective-permute-start | bytes 393224 | tf_op jit(solution)/shard_map/ppermute | solution.py:19
  7.6 9.3 %collective-permute-start = (bf16[320,512]{1,0:T(8,128)(2,1)}, bf16[320,512]{1,0:T(8,128)(2,1)S(1)}, u32[]{:S(2)}, u32[]{:S(2)}) collective-permute-start(bf16[320,512]{1,0:T(8,128)(2,1)} %param.11), channel_id=1, source_target_pairs={{0,129},{1,128},{2,131},{3,130},{4,133},{5,132},{6,135},{7,134},{8... | collective-permute-start | bytes 983048 | tf_op jit(solution)/shard_map/ppermute | solution.py:44
  7.8 9.2 %copy-start.9 = (bf16[320,512]{1,0:T(8,128)(2,1)S(1)}, bf16[320,512]{1,0:T(8,128)(2,1)}, u32[]{:S(2)}) copy-start(bf16[320,512]{1,0:T(8,128)(2,1)} %param.11) | copy-start | bytes 983044
  10.3 9.7 %copy-start.13 = (s32[1,2048]{1,0:T(1,128)S(1)}, s32[1,2048]{1,0:T(1,128)}, u32[]{:S(2)}) copy-start(s32[1,2048]{1,0:T(1,128)} %param.12) | copy-start | bytes 24580
  10.3 9.8 %copy-start.14 = (s32[1,32]{1,0:T(1,128)S(1)}, s32[1,32]{1,0:T(1,128)}, u32[]{:S(2)}) copy-start(s32[1,32]{1,0:T(1,128)} %param.13) | copy-start | bytes 388
  10.9 58.5 %copy-start.5 = (bf16[1,128,2560]{1,2,0:T(8,128)(2,1)}, bf16[1,128,2560]{1,2,0:T(8,128)(2,1)S(1)}, u32[]{:S(2)}) copy-start(bf16[1,128,2560]{1,2,0:T(8,128)(2,1)S(1)} %copy.94) | copy-start | bytes 1966084
  17.1 17.7 %collective-permute-start.1 = (bf16[2,320,512]{2,1,0:T(8,128)(2,1)S(1)}, bf16[2,320,512]{2,1,0:T(8,128)(2,1)S(1)}, u32[]{:S(2)}, u32[]{:S(2)}) collective-permute-start(bf16[2,320,512]{2,1,0:T(8,128)(2,1)S(1)} %get-tuple-element.33), channel_id=1, source_target_pairs={{0,32},{16,48},{32,64},{48,80},{64,96},{80,112},{96,0},{112,16},{1... | collective-permute-start | bytes 1966088 | tf_op jit(solution)/shard_map/ppermute | solution.py:51
  17.4 19.2 %collective-permute-start.2 = (bf16[2,320,512]{2,1,0:T(8,128)(2,1)S(1)}, bf16[2,320,512]{2,1,0:T(8,128)(2,1)S(1)}, u32[]{:S(2)}, u32[]{:S(2)}) collective-permute-start(bf16[2,320,512]{2,1,0:T(8,128)(2,1)S(1)} %get-tuple-element.33), channel_id=1, source_target_pairs={{0,64},{16,80},{32,96},{48,112},{64,0},{80,16},{96,32},{112,48},{1... | collective-permute-start | bytes 1966088 | tf_op jit(solution)/shard_map/ppermute | solution.py:51
  20.0 28.0 %collective-permute-start.3 = (bf16[2,320,512]{2,1,0:T(8,128)(2,1)S(1)}, bf16[2,320,512]{2,1,0:T(8,128)(2,1)S(1)}, u32[]{:S(2)}, u32[]{:S(2)}) collective-permute-start(bf16[2,320,512]{2,1,0:T(8,128)(2,1)S(1)} %get-tuple-element.33), channel_id=1, source_target_pairs={{0,96},{16,112},{32,0},{48,16},{64,32},{80,48},{96,64},{112,80},{1... | collective-permute-start | bytes 1966088 | tf_op jit(solution)/shard_map/ppermute | solution.py:51
  20.3 40.9 %copy-start.11 = (pred[128,384]{0,1:T(8,128)(4,1)}, pred[128,384]{0,1:T(8,128)(4,1)S(1)}, u32[]{:S(2)}) copy-start(pred[128,384]{0,1:T(8,128)(4,1)S(1)} %or_and_fusion) | copy-start | bytes 147460
  49.8 27.8 %all-to-all-start = ((bf16[16,128,320]{1,2,0:T(8,128)(2,1)}), bf16[16,128,320]{1,2,0:T(8,128)(2,1)S(1)}, u32[]{:S(2)}, u32[]{:S(2)}) async-start(bf16[16,128,320]{1,2,0:T(8,128)(2,1)} %bitcast.8), calls=%async_computation | async-start | bytes 2621440 | tf_op jit(solution)/shard_map/all_to_all | solution.py:69
  58.1 31.0 %collective-permute-start.8 = (bf16[4,2,320,512]{3,2,1,0:T(8,128)(2,1)}, bf16[4,2,320,512]{3,2,1,0:T(8,128)(2,1)}, u32[]{:S(2)}, u32[]{:S(2)}) collective-permute-start(bf16[4,2,320,512]{3,2,1,0:T(8,128)(2,1)} %pad_maximum_fusion.1), channel_id=1, source_target_pairs={{0,16},{16,0},{32,48},{48,32},{64,80},{80,64},{96,112},{112,96},{1... | collective-permute-start | bytes 7864328 | tf_op jit(solution)/shard_map/ppermute | solution.py:53
  77.7 10.2 %collective-permute-start.6 = (bf16[128,512]{0,1:T(8,128)(2,1)S(1)}, bf16[128,512]{0,1:T(8,128)(2,1)S(1)}, u32[]{:S(2)}, u32[]{:S(2)}) collective-permute-start(bf16[128,512]{0,1:T(8,128)(2,1)S(1)} %get-tuple-element.40), channel_id=1, source_target_pairs={{1,0},{2,1},{3,2},{4,3},{5,4},{6,5},{7,6},{8,7},{9,8},{10,9},{11,1... | collective-permute-start | bytes 393224 | tf_op jit(solution)/shard_map/ppermute | solution.py:82
  79.6 9.4 %collective-permute-start.7 = (bf16[128,512]{0,1:T(8,128)(2,1)S(1)}, bf16[128,512]{0,1:T(8,128)(2,1)S(1)}, u32[]{:S(2)}, u32[]{:S(2)}) collective-permute-start(bf16[128,512]{0,1:T(8,128)(2,1)S(1)} %get-tuple-element.41), channel_id=1, source_target_pairs={{0,1},{1,2},{2,3},{3,4},{4,5},{5,6},{6,7},{7,8},{8,9},{9,10},{10,1... | collective-permute-start | bytes 393224 | tf_op jit(solution)/shard_map/ppermute | solution.py:82
  94.3 20.9 %collective-permute-start.10 = (bf16[128,512]{1,0:T(8,128)(2,1)S(1)}, bf16[128,512]{1,0:T(8,128)(2,1)S(1)}, u32[]{:S(2)}, u32[]{:S(2)}) collective-permute-start(bf16[128,512]{1,0:T(8,128)(2,1)S(1)} %fusion.38), channel_id=1, source_target_pairs={{1,0},{2,1},{3,2},{4,3},{5,4},{6,5},{7,6},{8,7},{9,8},{10,9},{11,1... | collective-permute-start | bytes 393224 | tf_op jit(solution)/shard_map/ppermute | solution.py:19
  96.3 19.0 %collective-permute-start.9 = (bf16[128,512]{1,0:T(8,128)(2,1)S(1)}, bf16[128,512]{1,0:T(8,128)(2,1)}, u32[]{:S(2)}, u32[]{:S(2)}) collective-permute-start(bf16[128,512]{1,0:T(8,128)(2,1)S(1)} %fusion.38), channel_id=1, source_target_pairs={{0,1},{1,2},{2,3},{3,4},{4,5},{5,6},{6,7},{7,8},{8,9},{9,10},{10,1... | collective-permute-start | bytes 393224 | tf_op jit(solution)/shard_map/ppermute | solution.py:17
  102.9 36.1 %all-to-all-start.1 = ((bf16[16,128,512]{1,2,0:T(8,128)(2,1)}), bf16[16,128,512]{1,2,0:T(8,128)(2,1)}, u32[]{:S(2)}, u32[]{:S(2)}) async-start(bf16[16,128,512]{1,2,0:T(8,128)(2,1)} %broadcast_in_dim.114), calls=%async_computation.1 | async-start | bytes 4194304 | tf_op jit(solution)/shard_map/all_to_all | solution.py:69
  124.6 14.4 %copy-start.2 = (bf16[16,128,320]{1,2,0:T(8,128)(2,1)S(1)}, bf16[16,128,320]{1,2,0:T(8,128)(2,1)}, u32[]{:S(2)}) copy-start(bf16[16,128,320]{1,2,0:T(8,128)(2,1)} %copy-done.1) | copy-start | bytes 3932164
  124.6 37.3 %collective-permute-start.11 = (bf16[128,512]{0,1:T(8,128)(2,1)}, bf16[128,512]{0,1:T(8,128)(2,1)S(1)}, u32[]{:S(2)}, u32[]{:S(2)}) collective-permute-start(bf16[128,512]{0,1:T(8,128)(2,1)} %get-tuple-element.34), channel_id=1, source_target_pairs={{1,0},{2,1},{3,2},{4,3},{5,4},{6,5},{7,6},{8,7},{9,8},{10,9},{11,1... | collective-permute-start | bytes 393224 | tf_op jit(solution)/shard_map/ppermute | solution.py:82
  126.6 35.2 %collective-permute-start.12 = (bf16[128,512]{0,1:T(8,128)(2,1)}, bf16[128,512]{0,1:T(8,128)(2,1)}, u32[]{:S(2)}, u32[]{:S(2)}) collective-permute-start(bf16[128,512]{0,1:T(8,128)(2,1)} %get-tuple-element.35), channel_id=1, source_target_pairs={{0,1},{1,2},{2,3},{3,4},{4,5},{5,6},{6,7},{7,8},{8,9},{9,10},{10,1... | collective-permute-start | bytes 393224 | tf_op jit(solution)/shard_map/ppermute | solution.py:82
  142.7 36.1 %all-to-all-start.2 = ((f32[16,320,32]{1,2,0:T(8,128)}), f32[16,320,32]{1,2,0:T(8,128)S(1)}, u32[]{:S(2)}, u32[]{:S(2)}) async-start(f32[16,320,32]{1,2,0:T(8,128)} %fusion.28), calls=%async_computation.2 | async-start | bytes 1572864 | tf_op jit(solution)/shard_map/all_to_all | solution.py:69
  (21 other events, 67.6 us)

commit v14 on v13

--- a/solution.py
+++ b/solution.py
@@ -196,9 +196,9 @@
     seq_count = lax.axis_size("seq")
     grad_rows = gathered_copies(grad_copies, "dp").reshape(dp_count, tok_count, seq_count, -1)
     own_pieces = jnp.einsum(
-        "rtk,rtjc->jkc", input_blocks, grad_rows, preferred_element_type=jnp.float32
-    )
-    summed = jnp.sum(gathered_copies(own_pieces, "seq"), axis=0)
+        "rtk,rtjc->jck", input_blocks, grad_rows, preferred_element_type=jnp.float32
+    ).astype(jnp.bfloat16)
+    summed = jnp.sum(gathered_copies(own_pieces, "seq").astype(jnp.float32), axis=0).T
     devices_all = lax.axis_size("dp") * lax.axis_size("seq")
     weight_grad = summed / devices_all
     input_slots = jnp.take(

time: 181 us -> 171 us (0.945)
  waiting for transfers between devices: 62.3 us -> 58.4 us
  starting transfers between devices: 55.9 us -> 53.2 us
  local copies, waits for them, and re-layouts: 19.3 us -> 17.4 us
    all_to_all x3, waiting for transfers between devices: 28.6 us -> 18.6 us  [gathered_copies(): return lax.all_to_all(copies, axis, 0, 0, tiled=True)]
    ppermute x4, waiting for transfers between devices: 1.13 us -> 7.26 us  [passed_along(): return lax.ppermute(array, axis, pairs)]
    all_to_all x3, starting transfers between devices: 26.5 us -> 24 us  [gathered_copies(): return lax.all_to_all(copies, axis, 0, 0, tiled=True)]
    unnamed x65 -> x49, local copies, waits for them, and re-layouts: 12.2 us -> 11.1 us
  transfers between devices with their start and end apart: 16 -> 16, of which waited for: 8 -> 9; matrix products, arithmetic and copies ran while one was open for 27% -> 25% of each run, Pallas kernels for 0% -> 0%
where the time goes in v14:
time: 171 us; the launch traced here: 170 us
  waiting for transfers between devices  58.4 us (34%)
  starting transfers between devices  53.2 us (31%)
  matrix products  29.1 us (17%)
  local copies, waits for them, and re-layouts  17.4 us (10%)
  other arithmetic  10.6 us (6%)
    ppermute x3, waiting for transfers between devices, spread_weight(): ring.append(lax.ppermute(held, 'dp', pairs))  26.8 us
    all_to_all x3, starting transfers between devices, gathered_copies(): return lax.all_to_all(copies, axis, 0, 0, tiled=True)  24 us
    all_to_all x3, waiting for transfers between devices, gathered_copies(): return lax.all_to_all(copies, axis, 0, 0, tiled=True)  18.6 us
    ppermute x4, starting transfers between devices, passed_along(): return lax.ppermute(array, axis, pairs)  13.5 us
    unnamed x49, local copies, waits for them, and re-layouts  11.1 us
    ppermute x2, starting transfers between devices, with_halo(): lax.ppermute(tail, axis, [(i, (i + 1) % count) for i in range(ends)])  8.62 us
    ppermute x4, waiting for transfers between devices, passed_along(): return lax.ppermute(array, axis, pairs)  7.26 us
    dot_general x4, matrix products, attend_first(): jnp.einsum('gqk,qgd->kd', attention_low, grad_head, preferred_element_typ...  6.72 us
  transfers between devices with their start and end apart: 16, of which 9 were waited for; matrix products, arithmetic and copies ran while one was open for 25% of the time, Pallas kernels for 0%

profile of v14, /device:TPU:26, one launch (start us, length us, event | category | flops | bytes accessed | tf_op | source)
XLA Modules:
  0.0 170.0 jit_solution(15400024567487463282)
XLA Ops:
  1.8 3.8 %collective-permute-start.4 = (bf16[128,512]{0,1:T(8,128)(2,1)S(1)}, bf16[128,512]{0,1:T(8,128)(2,1)S(1)}, u32[]{:S(2)}, u32[]{:S(2)}) collective-permute-start(bf16[128,512]{0,1:T(8,128)(2,1)S(1)} %bitcast.328), channel_id=1, source_target_pairs={{0,1},{1,2},{2,3},{3,4},{4,5},{5,6},{6,7},{7,8},{8,9},{9,10},{10,1... | collective-permute-start | bytes 393224 | tf_op jit(solution)/shard_map/ppermute | solution.py:17
  5.6 2.0 %collective-permute-start.5 = (bf16[128,512]{0,1:T(8,128)(2,1)S(1)}, bf16[128,512]{0,1:T(8,128)(2,1)S(1)}, u32[]{:S(2)}, u32[]{:S(2)}) collective-permute-start(bf16[128,512]{0,1:T(8,128)(2,1)S(1)} %bitcast.329), channel_id=1, source_target_pairs={{1,0},{2,1},{3,2},{4,3},{5,4},{6,5},{7,6},{8,7},{9,8},{10,9},{11,1... | collective-permute-start | bytes 393224 | tf_op jit(solution)/shard_map/ppermute | solution.py:19
  7.8 2.5 %copy.90 = bf16[1,128,5120]{1,2,0:T(8,128)(2,1)} copy(bf16[1,128,5120]{2,1,0:T(8,128)(2,1)} %param.7) | data formatting | bytes 2621440 | tf_op args[0]
  11.3 5.7 %collective-permute-done = bf16[320,512]{1,0:T(8,128)(2,1)S(1)} collective-permute-done((bf16[320,512]{1,0:T(8,128)(2,1)}, bf16[320,512]{1,0:T(8,128)(2,1)S(1)}, u32[]{:S(2)}, u32[]{:S(2)}) %collective-permute-start) | collective-permute-done | bytes 327712 | tf_op jit(solution)/shard_map/ppermute | solution.py:44
  17.4 2.6 %collective-permute-start.2 = (bf16[2,320,512]{2,1,0:T(8,128)(2,1)S(1)}, bf16[2,320,512]{2,1,0:T(8,128)(2,1)S(1)}, u32[]{:S(2)}, u32[]{:S(2)}) collective-permute-start(bf16[2,320,512]{2,1,0:T(8,128)(2,1)S(1)} %get-tuple-element.33), channel_id=1, source_target_pairs={{0,64},{16,80},{32,96},{48,112},{64,0},{80,16},{96,32},{112,48},{1... | collective-permute-start | bytes 1966088 | tf_op jit(solution)/shard_map/ppermute | solution.py:51
  21.2 13.6 %collective-permute-done.1 = bf16[2,320,512]{2,1,0:T(8,128)(2,1)S(1)} collective-permute-done((bf16[2,320,512]{2,1,0:T(8,128)(2,1)S(1)}, bf16[2,320,512]{2,1,0:T(8,128)(2,1)S(1)}, u32[]{:S(2)}, u32[]{:S(2)}) %collective-permute-start.1) | collective-permute-done | bytes 655392 | tf_op jit(solution)/shard_map/ppermute | solution.py:51
  36.6 11.3 %collective-permute-done.3 = bf16[2,320,512]{2,1,0:T(8,128)(2,1)S(1)} collective-permute-done((bf16[2,320,512]{2,1,0:T(8,128)(2,1)S(1)}, bf16[2,320,512]{2,1,0:T(8,128)(2,1)S(1)}, u32[]{:S(2)}, u32[]{:S(2)}) %collective-permute-start.3) | collective-permute-done | bytes 655392 | tf_op jit(solution)/shard_map/ppermute | solution.py:51
  49.8 8.3 %all-to-all-start = ((bf16[16,128,320]{1,2,0:T(8,128)(2,1)}), bf16[16,128,320]{1,2,0:T(8,128)(2,1)S(1)}, u32[]{:S(2)}, u32[]{:S(2)}) async-start(bf16[16,128,320]{1,2,0:T(8,128)(2,1)} %bitcast.8), calls=%async_computation | async-start | bytes 2621440 | tf_op jit(solution)/shard_map/all_to_all | solution.py:69
  66.3 2.2 %convolution_bitcast_fusion.5 = f32[384,128]{0,1:T(8,128)} fusion(bf16[128,4,5,128]{0,3,2,1:T(8,128)(2,1)S(1)} %bitcast.322, f32[5,128,384]{1,2,0:T(8,128)} %get-tuple-element.45, f32[5,128]{1,0:T(8,128)S(1)} %get-tuple-element.44), kind=kOutput, calls=%fused_computation.53 | convolution fusion | flops 63406080 | bytes 1347584 | tf_op jit(solution)/shard_map/gqk,qgd->kd/dot_general | solution.py:116
  71.6 6.0 %all-to-all-done = bf16[16,128,320]{1,2,0:T(8,128)(2,1)S(1)} async-done(((bf16[16,128,320]{1,2,0:T(8,128)(2,1)}), bf16[16,128,320]{1,2,0:T(8,128)(2,1)S(1)}, u32[]{:S(2)}, u32[]{:S(2)}) %all-to-all-start) | async-done | bytes 1310752 | tf_op jit(solution)/shard_map/all_to_all | solution.py:69
  77.7 1.9 %collective-permute-start.6 = (bf16[128,512]{0,1:T(8,128)(2,1)S(1)}, bf16[128,512]{0,1:T(8,128)(2,1)S(1)}, u32[]{:S(2)}, u32[]{:S(2)}) collective-permute-start(bf16[128,512]{0,1:T(8,128)(2,1)S(1)} %get-tuple-element.40), channel_id=1, source_target_pairs={{1,0},{2,1},{3,2},{4,3},{5,4},{6,5},{7,6},{8,7},{9,8},{10,9},{11,1... | collective-permute-start | bytes 393224 | tf_op jit(solution)/shard_map/ppermute | solution.py:82
  79.6 4.8 %collective-permute-start.7 = (bf16[128,512]{0,1:T(8,128)(2,1)S(1)}, bf16[128,512]{0,1:T(8,128)(2,1)S(1)}, u32[]{:S(2)}, u32[]{:S(2)}) collective-permute-start(bf16[128,512]{0,1:T(8,128)(2,1)S(1)} %get-tuple-element.41), channel_id=1, source_target_pairs={{0,1},{1,2},{2,3},{3,4},{4,5},{5,6},{6,7},{7,8},{8,9},{9,10},{10,1... | collective-permute-start | bytes 393224 | tf_op jit(solution)/shard_map/ppermute | solution.py:82
  85.7 2.1 %gather_fusion = bf16[16,128,320]{1,2,0:T(8,128)(2,1)S(1)} fusion(bf16[128,16,320]{0,2,1:T(8,128)(2,1)} %bitcast.7, s32[1024]{0:T(1024)S(1)} %pad_clamp_fusion.1), kind=kCustom, calls=%fused_computation | custom fusion | bytes 2621504 | tf_op jit(solution)/shard_map/jit(_take)/gather | solution.py:204
  89.0 3.0 %pad_maximum_fusion = bf16[2,4,2,320,512]{4,3,2,1,0:T(8,128)(2,1)S(1)} fusion(bf16[1,4,2,320,512]{4,3,2,1,0:T(8,128)(2,1)} %bitcast.42, bf16[1,4,2,320,512]{4,3,2,1,0:T(8,128)(2,1)} %bitcast.41), kind=kLoop, calls=%fused_computation.7 | loop fusion | flops 2621440 | bytes 10485760 | tf_op jit(solution)/shard_map/stack | solution.py:54
  94.3 1.9 %collective-permute-start.10 = (bf16[128,512]{1,0:T(8,128)(2,1)S(1)}, bf16[128,512]{1,0:T(8,128)(2,1)S(1)}, u32[]{:S(2)}, u32[]{:S(2)}) collective-permute-start(bf16[128,512]{1,0:T(8,128)(2,1)S(1)} %fusion.41), channel_id=1, source_target_pairs={{1,0},{2,1},{3,2},{4,3},{5,4},{6,5},{7,6},{8,7},{9,8},{10,9},{11,1... | collective-permute-start | bytes 393224 | tf_op jit(solution)/shard_map/ppermute | solution.py:19
  96.2 4.8 %collective-permute-start.9 = (bf16[128,512]{1,0:T(8,128)(2,1)S(1)}, bf16[128,512]{1,0:T(8,128)(2,1)}, u32[]{:S(2)}, u32[]{:S(2)}) collective-permute-start(bf16[128,512]{1,0:T(8,128)(2,1)S(1)} %fusion.41), channel_id=1, source_target_pairs={{0,1},{1,2},{2,3},{3,4},{4,5},{5,6},{6,7},{7,8},{8,9},{9,10},{10,1... | collective-permute-start | bytes 393224 | tf_op jit(solution)/shard_map/ppermute | solution.py:17
  102.9 4.9 %all-to-all-start.1 = ((bf16[16,128,512]{1,2,0:T(8,128)(2,1)}), bf16[16,128,512]{1,2,0:T(8,128)(2,1)}, u32[]{:S(2)}, u32[]{:S(2)}) async-start(bf16[16,128,512]{1,2,0:T(8,128)(2,1)} %broadcast_in_dim.114), calls=%async_computation.1 | async-start | bytes 4194304 | tf_op jit(solution)/shard_map/all_to_all | solution.py:69
  107.8 4.4 %convolution_convert_fusion = bf16[128,5120]{1,0:T(8,128)(2,1)S(1)} fusion(bf16[128,512]{0,1:T(8,128)(2,1)S(1)} %add_convert_fusion, bf16[5120,512]{1,0:T(8,128)(2,1)} %bitcast.305), kind=kOutput, calls=%fused_computation.6 | convolution fusion | flops 671744000 | bytes 6684672 | tf_op jit(solution)/shard_map/dot_general | solution.py:213
  126.3 12.7 %all-to-all-done.1 = bf16[16,128,512]{1,2,0:T(8,128)(2,1)} async-done(((bf16[16,128,512]{1,2,0:T(8,128)(2,1)}), bf16[16,128,512]{1,2,0:T(8,128)(2,1)}, u32[]{:S(2)}, u32[]{:S(2)}) %all-to-all-start.1) | async-done | bytes 2097184 | tf_op jit(solution)/shard_map/all_to_all | solution.py:69
  139.0 3.6 %fusion.31 = bf16[16,32,320]{2,1,0:T(8,128)(2,1)} fusion(bf16[16,128,16,32]{1,3,2,0:T(8,128)(2,1)} %bitcast.78, bf16[16,128,320]{1,2,0:T(8,128)(2,1)S(1)} %copy-done.2), kind=kOutput, calls=%fused_computation.42 | convolution fusion | flops 671252480 | bytes 3735552 | tf_op jit(solution)/shard_map/rtk,rtjc->jck/dot_general | solution.py:198
  142.6 10.8 %all-to-all-start.2 = ((bf16[16,32,320]{2,1,0:T(8,128)(2,1)}), bf16[16,32,320]{2,1,0:T(8,128)(2,1)S(1)}, u32[]{:S(2)}, u32[]{:S(2)}) async-start(bf16[16,32,320]{2,1,0:T(8,128)(2,1)} %fusion.31), calls=%async_computation.2 | async-start | bytes 786432 | tf_op jit(solution)/shard_map/all_to_all | solution.py:69
  153.4 2.0 %collective-permute-start.11 = (bf16[128,512]{0,1:T(8,128)(2,1)S(1)}, bf16[128,512]{0,1:T(8,128)(2,1)S(1)}, u32[]{:S(2)}, u32[]{:S(2)}) collective-permute-start(bf16[128,512]{0,1:T(8,128)(2,1)S(1)} %get-tuple-element.34), channel_id=1, source_target_pairs={{1,0},{2,1},{3,2},{4,3},{5,4},{6,5},{7,6},{8,7},{9,8},{10,9},{11,1... | collective-permute-start | bytes 393224 | tf_op jit(solution)/shard_map/ppermute | solution.py:82
  155.4 4.7 %collective-permute-start.12 = (bf16[128,512]{0,1:T(8,128)(2,1)S(1)}, bf16[128,512]{0,1:T(8,128)(2,1)S(1)}, u32[]{:S(2)}, u32[]{:S(2)}) collective-permute-start(bf16[128,512]{0,1:T(8,128)(2,1)S(1)} %get-tuple-element.35), channel_id=1, source_target_pairs={{0,1},{1,2},{2,3},{3,4},{4,5},{5,6},{6,7},{7,8},{8,9},{9,10},{10,1... | collective-permute-start | bytes 393224 | tf_op jit(solution)/shard_map/ppermute | solution.py:82
  162.3 5.3 %collective-permute-done.11 = bf16[128,512]{0,1:T(8,128)(2,1)S(1)} collective-permute-done((bf16[128,512]{0,1:T(8,128)(2,1)S(1)}, bf16[128,512]{0,1:T(8,128)(2,1)S(1)}, u32[]{:S(2)}, u32[]{:S(2)}) %collective-permute-start.11) | collective-permute-done | bytes 131104 | tf_op jit(solution)/shard_map/ppermute | solution.py:82
  (118 shorter events, 43.7 us)
Async XLA Ops:
  0.6 9.6 %copy-start.3 = (bf16[1,128,2560]{2,1,0:T(8,128)(2,1)S(1)}, bf16[1,128,2560]{2,1,0:T(8,128)(2,1)}, u32[]{:S(2)}) copy-start(bf16[1,128,2560]{2,1,0:T(8,128)(2,1)} %param.8) | copy-start | bytes 1966084
  0.6 10.0 %copy-start.4 = (bf16[1,128,2560]{2,1,0:T(8,128)(2,1)S(1)}, bf16[1,128,2560]{2,1,0:T(8,128)(2,1)}, u32[]{:S(2)}) copy-start(bf16[1,128,2560]{2,1,0:T(8,128)(2,1)} %param.10) | copy-start | bytes 1966084
  1.8 18.6 %collective-permute-start.4 = (bf16[128,512]{0,1:T(8,128)(2,1)S(1)}, bf16[128,512]{0,1:T(8,128)(2,1)S(1)}, u32[]{:S(2)}, u32[]{:S(2)}) collective-permute-start(bf16[128,512]{0,1:T(8,128)(2,1)S(1)} %bitcast.328), channel_id=1, source_target_pairs={{0,1},{1,2},{2,3},{3,4},{4,5},{5,6},{6,7},{7,8},{8,9},{9,10},{10,1... | collective-permute-start | bytes 393224 | tf_op jit(solution)/shard_map/ppermute | solution.py:17
  5.6 14.8 %collective-permute-start.5 = (bf16[128,512]{0,1:T(8,128)(2,1)S(1)}, bf16[128,512]{0,1:T(8,128)(2,1)S(1)}, u32[]{:S(2)}, u32[]{:S(2)}) collective-permute-start(bf16[128,512]{0,1:T(8,128)(2,1)S(1)} %bitcast.329), channel_id=1, source_target_pairs={{1,0},{2,1},{3,2},{4,3},{5,4},{6,5},{7,6},{8,7},{9,8},{10,9},{11,1... | collective-permute-start | bytes 393224 | tf_op jit(solution)/shard_map/ppermute | solution.py:19
  7.6 9.3 %collective-permute-start = (bf16[320,512]{1,0:T(8,128)(2,1)}, bf16[320,512]{1,0:T(8,128)(2,1)S(1)}, u32[]{:S(2)}, u32[]{:S(2)}) collective-permute-start(bf16[320,512]{1,0:T(8,128)(2,1)} %param.11), channel_id=1, source_target_pairs={{0,129},{1,128},{2,131},{3,130},{4,133},{5,132},{6,135},{7,134},{8... | collective-permute-start | bytes 983048 | tf_op jit(solution)/shard_map/ppermute | solution.py:44
  7.8 9.2 %copy-start.9 = (bf16[320,512]{1,0:T(8,128)(2,1)S(1)}, bf16[320,512]{1,0:T(8,128)(2,1)}, u32[]{:S(2)}) copy-start(bf16[320,512]{1,0:T(8,128)(2,1)} %param.11) | copy-start | bytes 983044
  10.3 9.7 %copy-start.13 = (s32[1,2048]{1,0:T(1,128)S(1)}, s32[1,2048]{1,0:T(1,128)}, u32[]{:S(2)}) copy-start(s32[1,2048]{1,0:T(1,128)} %param.12) | copy-start | bytes 24580
  10.3 9.8 %copy-start.14 = (s32[1,32]{1,0:T(1,128)S(1)}, s32[1,32]{1,0:T(1,128)}, u32[]{:S(2)}) copy-start(s32[1,32]{1,0:T(1,128)} %param.13) | copy-start | bytes 388
  10.9 59.1 %copy-start.5 = (bf16[1,128,2560]{1,2,0:T(8,128)(2,1)}, bf16[1,128,2560]{1,2,0:T(8,128)(2,1)S(1)}, u32[]{:S(2)}) copy-start(bf16[1,128,2560]{1,2,0:T(8,128)(2,1)S(1)} %copy.94) | copy-start | bytes 1966084
  17.1 17.7 %collective-permute-start.1 = (bf16[2,320,512]{2,1,0:T(8,128)(2,1)S(1)}, bf16[2,320,512]{2,1,0:T(8,128)(2,1)S(1)}, u32[]{:S(2)}, u32[]{:S(2)}) collective-permute-start(bf16[2,320,512]{2,1,0:T(8,128)(2,1)S(1)} %get-tuple-element.33), channel_id=1, source_target_pairs={{0,32},{16,48},{32,64},{48,80},{64,96},{80,112},{96,0},{112,16},{1... | collective-permute-start | bytes 1966088 | tf_op jit(solution)/shard_map/ppermute | solution.py:51
  17.4 19.2 %collective-permute-start.2 = (bf16[2,320,512]{2,1,0:T(8,128)(2,1)S(1)}, bf16[2,320,512]{2,1,0:T(8,128)(2,1)S(1)}, u32[]{:S(2)}, u32[]{:S(2)}) collective-permute-start(bf16[2,320,512]{2,1,0:T(8,128)(2,1)S(1)} %get-tuple-element.33), channel_id=1, source_target_pairs={{0,64},{16,80},{32,96},{48,112},{64,0},{80,16},{96,32},{112,48},{1... | collective-permute-start | bytes 1966088 | tf_op jit(solution)/shard_map/ppermute | solution.py:51
  20.0 28.0 %collective-permute-start.3 = (bf16[2,320,512]{2,1,0:T(8,128)(2,1)S(1)}, bf16[2,320,512]{2,1,0:T(8,128)(2,1)S(1)}, u32[]{:S(2)}, u32[]{:S(2)}) collective-permute-start(bf16[2,320,512]{2,1,0:T(8,128)(2,1)S(1)} %get-tuple-element.33), channel_id=1, source_target_pairs={{0,96},{16,112},{32,0},{48,16},{64,32},{80,48},{96,64},{112,80},{1... | collective-permute-start | bytes 1966088 | tf_op jit(solution)/shard_map/ppermute | solution.py:51
  20.3 40.9 %copy-start.11 = (pred[128,384]{0,1:T(8,128)(4,1)}, pred[128,384]{0,1:T(8,128)(4,1)S(1)}, u32[]{:S(2)}) copy-start(pred[128,384]{0,1:T(8,128)(4,1)S(1)} %or_and_fusion) | copy-start | bytes 147460
  49.8 27.8 %all-to-all-start = ((bf16[16,128,320]{1,2,0:T(8,128)(2,1)}), bf16[16,128,320]{1,2,0:T(8,128)(2,1)S(1)}, u32[]{:S(2)}, u32[]{:S(2)}) async-start(bf16[16,128,320]{1,2,0:T(8,128)(2,1)} %bitcast.8), calls=%async_computation | async-start | bytes 2621440 | tf_op jit(solution)/shard_map/all_to_all | solution.py:69
  58.0 31.0 %collective-permute-start.8 = (bf16[4,2,320,512]{3,2,1,0:T(8,128)(2,1)}, bf16[4,2,320,512]{3,2,1,0:T(8,128)(2,1)}, u32[]{:S(2)}, u32[]{:S(2)}) collective-permute-start(bf16[4,2,320,512]{3,2,1,0:T(8,128)(2,1)} %pad_maximum_fusion.1), channel_id=1, source_target_pairs={{0,16},{16,0},{32,48},{48,32},{64,80},{80,64},{96,112},{112,96},{1... | collective-permute-start | bytes 7864328 | tf_op jit(solution)/shard_map/ppermute | solution.py:53
  77.7 10.2 %collective-permute-start.6 = (bf16[128,512]{0,1:T(8,128)(2,1)S(1)}, bf16[128,512]{0,1:T(8,128)(2,1)S(1)}, u32[]{:S(2)}, u32[]{:S(2)}) collective-permute-start(bf16[128,512]{0,1:T(8,128)(2,1)S(1)} %get-tuple-element.40), channel_id=1, source_target_pairs={{1,0},{2,1},{3,2},{4,3},{5,4},{6,5},{7,6},{8,7},{9,8},{10,9},{11,1... | collective-permute-start | bytes 393224 | tf_op jit(solution)/shard_map/ppermute | solution.py:82
  79.6 9.4 %collective-permute-start.7 = (bf16[128,512]{0,1:T(8,128)(2,1)S(1)}, bf16[128,512]{0,1:T(8,128)(2,1)S(1)}, u32[]{:S(2)}, u32[]{:S(2)}) collective-permute-start(bf16[128,512]{0,1:T(8,128)(2,1)S(1)} %get-tuple-element.41), channel_id=1, source_target_pairs={{0,1},{1,2},{2,3},{3,4},{4,5},{5,6},{6,7},{7,8},{8,9},{9,10},{10,1... | collective-permute-start | bytes 393224 | tf_op jit(solution)/shard_map/ppermute | solution.py:82
  94.3 20.9 %collective-permute-start.10 = (bf16[128,512]{1,0:T(8,128)(2,1)S(1)}, bf16[128,512]{1,0:T(8,128)(2,1)S(1)}, u32[]{:S(2)}, u32[]{:S(2)}) collective-permute-start(bf16[128,512]{1,0:T(8,128)(2,1)S(1)} %fusion.41), channel_id=1, source_target_pairs={{1,0},{2,1},{3,2},{4,3},{5,4},{6,5},{7,6},{8,7},{9,8},{10,9},{11,1... | collective-permute-start | bytes 393224 | tf_op jit(solution)/shard_map/ppermute | solution.py:19
  96.2 19.0 %collective-permute-start.9 = (bf16[128,512]{1,0:T(8,128)(2,1)S(1)}, bf16[128,512]{1,0:T(8,128)(2,1)}, u32[]{:S(2)}, u32[]{:S(2)}) collective-permute-start(bf16[128,512]{1,0:T(8,128)(2,1)S(1)} %fusion.41), channel_id=1, source_target_pairs={{0,1},{1,2},{2,3},{3,4},{4,5},{5,6},{6,7},{7,8},{8,9},{9,10},{10,1... | collective-permute-start | bytes 393224 | tf_op jit(solution)/shard_map/ppermute | solution.py:17
  102.9 36.1 %all-to-all-start.1 = ((bf16[16,128,512]{1,2,0:T(8,128)(2,1)}), bf16[16,128,512]{1,2,0:T(8,128)(2,1)}, u32[]{:S(2)}, u32[]{:S(2)}) async-start(bf16[16,128,512]{1,2,0:T(8,128)(2,1)} %broadcast_in_dim.114), calls=%async_computation.1 | async-start | bytes 4194304 | tf_op jit(solution)/shard_map/all_to_all | solution.py:69
  124.9 14.1 %copy-start.2 = (bf16[16,128,320]{1,2,0:T(8,128)(2,1)S(1)}, bf16[16,128,320]{1,2,0:T(8,128)(2,1)}, u32[]{:S(2)}) copy-start(bf16[16,128,320]{1,2,0:T(8,128)(2,1)} %copy-done.1) | copy-start | bytes 3932164
  142.6 26.7 %all-to-all-start.2 = ((bf16[16,32,320]{2,1,0:T(8,128)(2,1)}), bf16[16,32,320]{2,1,0:T(8,128)(2,1)S(1)}, u32[]{:S(2)}, u32[]{:S(2)}) async-start(bf16[16,32,320]{2,1,0:T(8,128)(2,1)} %fusion.31), calls=%async_computation.2 | async-start | bytes 786432 | tf_op jit(solution)/shard_map/all_to_all | solution.py:69
  153.4 14.3 %collective-permute-start.11 = (bf16[128,512]{0,1:T(8,128)(2,1)S(1)}, bf16[128,512]{0,1:T(8,128)(2,1)S(1)}, u32[]{:S(2)}, u32[]{:S(2)}) collective-permute-start(bf16[128,512]{0,1:T(8,128)(2,1)S(1)} %get-tuple-element.34), channel_id=1, source_target_pairs={{1,0},{2,1},{3,2},{4,3},{5,4},{6,5},{7,6},{8,7},{9,8},{10,9},{11,1... | collective-permute-start | bytes 393224 | tf_op jit(solution)/shard_map/ppermute | solution.py:82
  155.4 13.0 %collective-permute-start.12 = (bf16[128,512]{0,1:T(8,128)(2,1)S(1)}, bf16[128,512]{0,1:T(8,128)(2,1)S(1)}, u32[]{:S(2)}, u32[]{:S(2)}) collective-permute-start(bf16[128,512]{0,1:T(8,128)(2,1)S(1)} %get-tuple-element.35), channel_id=1, source_target_pairs={{0,1},{1,2},{2,3},{3,4},{4,5},{5,6},{6,7},{7,8},{8,9},{9,10},{10,1... | collective-permute-start | bytes 393224 | tf_op jit(solution)/shard_map/ppermute | solution.py:82
  (13 other events, 32.0 us)

commit v15 on v14

--- a/solution.py
+++ b/solution.py
@@ -198,7 +198,10 @@
     own_pieces = jnp.einsum(
         "rtk,rtjc->jck", input_blocks, grad_rows, preferred_element_type=jnp.float32
     ).astype(jnp.bfloat16)
-    summed = jnp.sum(gathered_copies(own_pieces, "seq").astype(jnp.float32), axis=0).T
+    piece_shape = own_pieces.shape[1:]
+    dense_pieces = own_pieces.reshape(own_pieces.shape[0], -1, 128)
+    summed = jnp.sum(gathered_copies(dense_pieces, "seq").astype(jnp.float32), axis=0)
+    summed = summed.reshape(piece_shape).T
     devices_all = lax.axis_size("dp") * lax.axis_size("seq")
     weight_grad = summed / devices_all
     input_slots = jnp.take(

time: 171 us -> 171 us (level)
  local copies, waits for them, and re-layouts: 17.4 us -> 19.3 us
where the time goes in v15:
time: 171 us; the launch traced here: 170 us
  waiting for transfers between devices  57.5 us (34%)
  starting transfers between devices  53.2 us (31%)
  matrix products  28.3 us (17%)
  local copies, waits for them, and re-layouts  19.3 us (11%)
  other arithmetic  9.93 us (6%)
    ppermute x3, waiting for transfers between devices, spread_weight(): ring.append(lax.ppermute(held, 'dp', pairs))  26.8 us
    all_to_all x3, starting transfers between devices, gathered_copies(): return lax.all_to_all(copies, axis, 0, 0, tiled=True)  24 us
    all_to_all x3, waiting for transfers between devices, gathered_copies(): return lax.all_to_all(copies, axis, 0, 0, tiled=True)  18.7 us
    ppermute x4, starting transfers between devices, passed_along(): return lax.ppermute(array, axis, pairs)  13.5 us
    unnamed x49, local copies, waits for them, and re-layouts  11.2 us
    ppermute x2, starting transfers between devices, with_halo(): lax.ppermute(tail, axis, [(i, (i + 1) % count) for i in range(ends)])  8.62 us
    dot_general x4, matrix products, attend_first(): jnp.einsum('gqk,qgd->kd', attention_low, grad_head, preferred_element_typ...  6.72 us
    ppermute x4, waiting for transfers between devices, passed_along(): return lax.ppermute(array, axis, pairs)  6.32 us
  transfers between devices with their start and end apart: 16, of which 9 were waited for; matrix products, arithmetic and copies ran while one was open for 25% of the time, Pallas kernels for 0%

profile of v15, /device:TPU:26, one launch (start us, length us, event | category | flops | bytes accessed | tf_op | source)
XLA Modules:
  0.0 169.5 jit_solution(10984946301370022959)
XLA Ops:
  1.8 3.8 %collective-permute-start.4 = (bf16[128,512]{0,1:T(8,128)(2,1)S(1)}, bf16[128,512]{0,1:T(8,128)(2,1)S(1)}, u32[]{:S(2)}, u32[]{:S(2)}) collective-permute-start(bf16[128,512]{0,1:T(8,128)(2,1)S(1)} %bitcast.327), channel_id=1, source_target_pairs={{0,1},{1,2},{2,3},{3,4},{4,5},{5,6},{6,7},{7,8},{8,9},{9,10},{10,1... | collective-permute-start | bytes 393224 | tf_op jit(solution)/shard_map/ppermute | solution.py:17
  5.6 2.0 %collective-permute-start.5 = (bf16[128,512]{0,1:T(8,128)(2,1)S(1)}, bf16[128,512]{0,1:T(8,128)(2,1)S(1)}, u32[]{:S(2)}, u32[]{:S(2)}) collective-permute-start(bf16[128,512]{0,1:T(8,128)(2,1)S(1)} %bitcast.328), channel_id=1, source_target_pairs={{1,0},{2,1},{3,2},{4,3},{5,4},{6,5},{7,6},{8,7},{9,8},{10,9},{11,1... | collective-permute-start | bytes 393224 | tf_op jit(solution)/shard_map/ppermute | solution.py:19
  7.8 2.5 %copy.90 = bf16[1,128,5120]{1,2,0:T(8,128)(2,1)} copy(bf16[1,128,5120]{2,1,0:T(8,128)(2,1)} %param.7) | data formatting | bytes 2621440 | tf_op args[0]
  11.3 5.7 %collective-permute-done = bf16[320,512]{1,0:T(8,128)(2,1)S(1)} collective-permute-done((bf16[320,512]{1,0:T(8,128)(2,1)}, bf16[320,512]{1,0:T(8,128)(2,1)S(1)}, u32[]{:S(2)}, u32[]{:S(2)}) %collective-permute-start) | collective-permute-done | bytes 327712 | tf_op jit(solution)/shard_map/ppermute | solution.py:44
  17.4 2.6 %collective-permute-start.2 = (bf16[2,320,512]{2,1,0:T(8,128)(2,1)S(1)}, bf16[2,320,512]{2,1,0:T(8,128)(2,1)S(1)}, u32[]{:S(2)}, u32[]{:S(2)}) collective-permute-start(bf16[2,320,512]{2,1,0:T(8,128)(2,1)S(1)} %get-tuple-element.33), channel_id=1, source_target_pairs={{0,64},{16,80},{32,96},{48,112},{64,0},{80,16},{96,32},{112,48},{1... | collective-permute-start | bytes 1966088 | tf_op jit(solution)/shard_map/ppermute | solution.py:51
  21.2 13.6 %collective-permute-done.1 = bf16[2,320,512]{2,1,0:T(8,128)(2,1)S(1)} collective-permute-done((bf16[2,320,512]{2,1,0:T(8,128)(2,1)S(1)}, bf16[2,320,512]{2,1,0:T(8,128)(2,1)S(1)}, u32[]{:S(2)}, u32[]{:S(2)}) %collective-permute-start.1) | collective-permute-done | bytes 655392 | tf_op jit(solution)/shard_map/ppermute | solution.py:51
  36.6 11.3 %collective-permute-done.3 = bf16[2,320,512]{2,1,0:T(8,128)(2,1)S(1)} collective-permute-done((bf16[2,320,512]{2,1,0:T(8,128)(2,1)S(1)}, bf16[2,320,512]{2,1,0:T(8,128)(2,1)S(1)}, u32[]{:S(2)}, u32[]{:S(2)}) %collective-permute-start.3) | collective-permute-done | bytes 655392 | tf_op jit(solution)/shard_map/ppermute | solution.py:51
  49.8 8.3 %all-to-all-start = ((bf16[16,128,320]{1,2,0:T(8,128)(2,1)}), bf16[16,128,320]{1,2,0:T(8,128)(2,1)S(1)}, u32[]{:S(2)}, u32[]{:S(2)}) async-start(bf16[16,128,320]{1,2,0:T(8,128)(2,1)} %bitcast.8), calls=%async_computation | async-start | bytes 2621440 | tf_op jit(solution)/shard_map/all_to_all | solution.py:69
  66.3 2.2 %convolution_bitcast_fusion.5 = f32[384,128]{0,1:T(8,128)} fusion(bf16[128,4,5,128]{0,3,2,1:T(8,128)(2,1)S(1)} %bitcast.321, f32[5,128,384]{1,2,0:T(8,128)} %get-tuple-element.45, f32[5,128]{1,0:T(8,128)S(1)} %get-tuple-element.44), kind=kOutput, calls=%fused_computation.53 | convolution fusion | flops 63406080 | bytes 1347584 | tf_op jit(solution)/shard_map/gqk,qgd->kd/dot_general | solution.py:116
  71.6 6.0 %all-to-all-done = bf16[16,128,320]{1,2,0:T(8,128)(2,1)S(1)} async-done(((bf16[16,128,320]{1,2,0:T(8,128)(2,1)}), bf16[16,128,320]{1,2,0:T(8,128)(2,1)S(1)}, u32[]{:S(2)}, u32[]{:S(2)}) %all-to-all-start) | async-done | bytes 1310752 | tf_op jit(solution)/shard_map/all_to_all | solution.py:69
  77.7 1.9 %collective-permute-start.6 = (bf16[128,512]{0,1:T(8,128)(2,1)S(1)}, bf16[128,512]{0,1:T(8,128)(2,1)S(1)}, u32[]{:S(2)}, u32[]{:S(2)}) collective-permute-start(bf16[128,512]{0,1:T(8,128)(2,1)S(1)} %get-tuple-element.40), channel_id=1, source_target_pairs={{1,0},{2,1},{3,2},{4,3},{5,4},{6,5},{7,6},{8,7},{9,8},{10,9},{11,1... | collective-permute-start | bytes 393224 | tf_op jit(solution)/shard_map/ppermute | solution.py:82
  79.6 4.8 %collective-permute-start.7 = (bf16[128,512]{0,1:T(8,128)(2,1)S(1)}, bf16[128,512]{0,1:T(8,128)(2,1)S(1)}, u32[]{:S(2)}, u32[]{:S(2)}) collective-permute-start(bf16[128,512]{0,1:T(8,128)(2,1)S(1)} %get-tuple-element.41), channel_id=1, source_target_pairs={{0,1},{1,2},{2,3},{3,4},{4,5},{5,6},{6,7},{7,8},{8,9},{9,10},{10,1... | collective-permute-start | bytes 393224 | tf_op jit(solution)/shard_map/ppermute | solution.py:82
  85.7 2.1 %gather_fusion = bf16[16,128,320]{1,2,0:T(8,128)(2,1)S(1)} fusion(bf16[128,16,320]{0,2,1:T(8,128)(2,1)} %bitcast.7, s32[1024]{0:T(1024)S(1)} %pad_clamp_fusion.1), kind=kCustom, calls=%fused_computation | custom fusion | bytes 2621504 | tf_op jit(solution)/shard_map/jit(_take)/gather | solution.py:207
  89.0 3.0 %pad_maximum_fusion = bf16[2,4,2,320,512]{4,3,2,1,0:T(8,128)(2,1)S(1)} fusion(bf16[1,4,2,320,512]{4,3,2,1,0:T(8,128)(2,1)} %bitcast.42, bf16[1,4,2,320,512]{4,3,2,1,0:T(8,128)(2,1)} %bitcast.41), kind=kLoop, calls=%fused_computation.7 | loop fusion | flops 2621440 | bytes 10485760 | tf_op jit(solution)/shard_map/stack | solution.py:54
  94.3 1.9 %collective-permute-start.10 = (bf16[128,512]{1,0:T(8,128)(2,1)S(1)}, bf16[128,512]{1,0:T(8,128)(2,1)S(1)}, u32[]{:S(2)}, u32[]{:S(2)}) collective-permute-start(bf16[128,512]{1,0:T(8,128)(2,1)S(1)} %fusion.41), channel_id=1, source_target_pairs={{1,0},{2,1},{3,2},{4,3},{5,4},{6,5},{7,6},{8,7},{9,8},{10,9},{11,1... | collective-permute-start | bytes 393224 | tf_op jit(solution)/shard_map/ppermute | solution.py:19
  96.2 4.8 %collective-permute-start.9 = (bf16[128,512]{1,0:T(8,128)(2,1)S(1)}, bf16[128,512]{1,0:T(8,128)(2,1)}, u32[]{:S(2)}, u32[]{:S(2)}) collective-permute-start(bf16[128,512]{1,0:T(8,128)(2,1)S(1)} %fusion.41), channel_id=1, source_target_pairs={{0,1},{1,2},{2,3},{3,4},{4,5},{5,6},{6,7},{7,8},{8,9},{9,10},{10,1... | collective-permute-start | bytes 393224 | tf_op jit(solution)/shard_map/ppermute | solution.py:17
  102.9 4.9 %all-to-all-start.1 = ((bf16[16,128,512]{1,2,0:T(8,128)(2,1)}), bf16[16,128,512]{1,2,0:T(8,128)(2,1)}, u32[]{:S(2)}, u32[]{:S(2)}) async-start(bf16[16,128,512]{1,2,0:T(8,128)(2,1)} %broadcast_in_dim.114), calls=%async_computation.1 | async-start | bytes 4194304 | tf_op jit(solution)/shard_map/all_to_all | solution.py:69
  107.8 4.3 %convolution_convert_fusion = bf16[128,5120]{1,0:T(8,128)(2,1)S(1)} fusion(bf16[128,512]{0,1:T(8,128)(2,1)S(1)} %add_convert_fusion, bf16[5120,512]{1,0:T(8,128)(2,1)} %bitcast.304), kind=kOutput, calls=%fused_computation.6 | convolution fusion | flops 671744000 | bytes 6684672 | tf_op jit(solution)/shard_map/dot_general | solution.py:216
  126.2 12.8 %all-to-all-done.1 = bf16[16,128,512]{1,2,0:T(8,128)(2,1)} async-done(((bf16[16,128,512]{1,2,0:T(8,128)(2,1)}), bf16[16,128,512]{1,2,0:T(8,128)(2,1)}, u32[]{:S(2)}, u32[]{:S(2)}) %all-to-all-start.1) | async-done | bytes 2097184 | tf_op jit(solution)/shard_map/all_to_all | solution.py:69
  139.0 2.9 %fusion.31 = bf16[16,32,320]{2,1,0:T(8,128)(2,1)S(1)} fusion(bf16[16,128,16,32]{1,3,2,0:T(8,128)(2,1)} %bitcast.78, bf16[16,128,320]{1,2,0:T(8,128)(2,1)S(1)} %copy-done.2), kind=kOutput, calls=%fused_computation.42 | convolution fusion | flops 671252480 | bytes 3735552 | tf_op jit(solution)/shard_map/rtk,rtjc->jck/dot_general | solution.py:198
  143.0 10.8 %all-to-all-start.2 = ((bf16[16,80,128]{2,1,0:T(8,128)(2,1)}), bf16[16,80,128]{2,1,0:T(8,128)(2,1)S(1)}, u32[]{:S(2)}, u32[]{:S(2)}) async-start(bf16[16,80,128]{2,1,0:T(8,128)(2,1)} %reshape.288), calls=%async_computation.2 | async-start | bytes 655360 | tf_op jit(solution)/shard_map/all_to_all | solution.py:69
  153.9 2.0 %collective-permute-start.11 = (bf16[128,512]{0,1:T(8,128)(2,1)S(1)}, bf16[128,512]{0,1:T(8,128)(2,1)S(1)}, u32[]{:S(2)}, u32[]{:S(2)}) collective-permute-start(bf16[128,512]{0,1:T(8,128)(2,1)S(1)} %get-tuple-element.34), channel_id=1, source_target_pairs={{1,0},{2,1},{3,2},{4,3},{5,4},{6,5},{7,6},{8,7},{9,8},{10,9},{11,1... | collective-permute-start | bytes 393224 | tf_op jit(solution)/shard_map/ppermute | solution.py:82
  155.9 4.7 %collective-permute-start.12 = (bf16[128,512]{0,1:T(8,128)(2,1)S(1)}, bf16[128,512]{0,1:T(8,128)(2,1)S(1)}, u32[]{:S(2)}, u32[]{:S(2)}) collective-permute-start(bf16[128,512]{0,1:T(8,128)(2,1)S(1)} %get-tuple-element.35), channel_id=1, source_target_pairs={{0,1},{1,2},{2,3},{3,4},{4,5},{5,6},{6,7},{7,8},{8,9},{9,10},{10,1... | collective-permute-start | bytes 393224 | tf_op jit(solution)/shard_map/ppermute | solution.py:82
  162.8 3.9 %collective-permute-done.11 = bf16[128,512]{0,1:T(8,128)(2,1)S(1)} collective-permute-done((bf16[128,512]{0,1:T(8,128)(2,1)S(1)}, bf16[128,512]{0,1:T(8,128)(2,1)S(1)}, u32[]{:S(2)}, u32[]{:S(2)}) %collective-permute-start.11) | collective-permute-done | bytes 131104 | tf_op jit(solution)/shard_map/ppermute | solution.py:82
  (120 shorter events, 45.4 us)
Async XLA Ops:
  0.6 9.6 %copy-start.3 = (bf16[1,128,2560]{2,1,0:T(8,128)(2,1)S(1)}, bf16[1,128,2560]{2,1,0:T(8,128)(2,1)}, u32[]{:S(2)}) copy-start(bf16[1,128,2560]{2,1,0:T(8,128)(2,1)} %param.8) | copy-start | bytes 1966084
  0.6 10.0 %copy-start.4 = (bf16[1,128,2560]{2,1,0:T(8,128)(2,1)S(1)}, bf16[1,128,2560]{2,1,0:T(8,128)(2,1)}, u32[]{:S(2)}) copy-start(bf16[1,128,2560]{2,1,0:T(8,128)(2,1)} %param.10) | copy-start | bytes 1966084
  1.8 18.6 %collective-permute-start.4 = (bf16[128,512]{0,1:T(8,128)(2,1)S(1)}, bf16[128,512]{0,1:T(8,128)(2,1)S(1)}, u32[]{:S(2)}, u32[]{:S(2)}) collective-permute-start(bf16[128,512]{0,1:T(8,128)(2,1)S(1)} %bitcast.327), channel_id=1, source_target_pairs={{0,1},{1,2},{2,3},{3,4},{4,5},{5,6},{6,7},{7,8},{8,9},{9,10},{10,1... | collective-permute-start | bytes 393224 | tf_op jit(solution)/shard_map/ppermute | solution.py:17
  5.6 14.8 %collective-permute-start.5 = (bf16[128,512]{0,1:T(8,128)(2,1)S(1)}, bf16[128,512]{0,1:T(8,128)(2,1)S(1)}, u32[]{:S(2)}, u32[]{:S(2)}) collective-permute-start(bf16[128,512]{0,1:T(8,128)(2,1)S(1)} %bitcast.328), channel_id=1, source_target_pairs={{1,0},{2,1},{3,2},{4,3},{5,4},{6,5},{7,6},{8,7},{9,8},{10,9},{11,1... | collective-permute-start | bytes 393224 | tf_op jit(solution)/shard_map/ppermute | solution.py:19
  7.6 9.3 %collective-permute-start = (bf16[320,512]{1,0:T(8,128)(2,1)}, bf16[320,512]{1,0:T(8,128)(2,1)S(1)}, u32[]{:S(2)}, u32[]{:S(2)}) collective-permute-start(bf16[320,512]{1,0:T(8,128)(2,1)} %param.11), channel_id=1, source_target_pairs={{0,129},{1,128},{2,131},{3,130},{4,133},{5,132},{6,135},{7,134},{8... | collective-permute-start | bytes 983048 | tf_op jit(solution)/shard_map/ppermute | solution.py:44
  7.8 9.2 %copy-start.9 = (bf16[320,512]{1,0:T(8,128)(2,1)S(1)}, bf16[320,512]{1,0:T(8,128)(2,1)}, u32[]{:S(2)}) copy-start(bf16[320,512]{1,0:T(8,128)(2,1)} %param.11) | copy-start | bytes 983044
  10.3 9.7 %copy-start.13 = (s32[1,2048]{1,0:T(1,128)S(1)}, s32[1,2048]{1,0:T(1,128)}, u32[]{:S(2)}) copy-start(s32[1,2048]{1,0:T(1,128)} %param.12) | copy-start | bytes 24580
  10.3 9.8 %copy-start.14 = (s32[1,32]{1,0:T(1,128)S(1)}, s32[1,32]{1,0:T(1,128)}, u32[]{:S(2)}) copy-start(s32[1,32]{1,0:T(1,128)} %param.13) | copy-start | bytes 388
  10.9 59.1 %copy-start.5 = (bf16[1,128,2560]{1,2,0:T(8,128)(2,1)}, bf16[1,128,2560]{1,2,0:T(8,128)(2,1)S(1)}, u32[]{:S(2)}) copy-start(bf16[1,128,2560]{1,2,0:T(8,128)(2,1)S(1)} %copy.94) | copy-start | bytes 1966084
  17.1 17.7 %collective-permute-start.1 = (bf16[2,320,512]{2,1,0:T(8,128)(2,1)S(1)}, bf16[2,320,512]{2,1,0:T(8,128)(2,1)S(1)}, u32[]{:S(2)}, u32[]{:S(2)}) collective-permute-start(bf16[2,320,512]{2,1,0:T(8,128)(2,1)S(1)} %get-tuple-element.33), channel_id=1, source_target_pairs={{0,32},{16,48},{32,64},{48,80},{64,96},{80,112},{96,0},{112,16},{1... | collective-permute-start | bytes 1966088 | tf_op jit(solution)/shard_map/ppermute | solution.py:51
  17.4 19.2 %collective-permute-start.2 = (bf16[2,320,512]{2,1,0:T(8,128)(2,1)S(1)}, bf16[2,320,512]{2,1,0:T(8,128)(2,1)S(1)}, u32[]{:S(2)}, u32[]{:S(2)}) collective-permute-start(bf16[2,320,512]{2,1,0:T(8,128)(2,1)S(1)} %get-tuple-element.33), channel_id=1, source_target_pairs={{0,64},{16,80},{32,96},{48,112},{64,0},{80,16},{96,32},{112,48},{1... | collective-permute-start | bytes 1966088 | tf_op jit(solution)/shard_map/ppermute | solution.py:51
  20.0 28.0 %collective-permute-start.3 = (bf16[2,320,512]{2,1,0:T(8,128)(2,1)S(1)}, bf16[2,320,512]{2,1,0:T(8,128)(2,1)S(1)}, u32[]{:S(2)}, u32[]{:S(2)}) collective-permute-start(bf16[2,320,512]{2,1,0:T(8,128)(2,1)S(1)} %get-tuple-element.33), channel_id=1, source_target_pairs={{0,96},{16,112},{32,0},{48,16},{64,32},{80,48},{96,64},{112,80},{1... | collective-permute-start | bytes 1966088 | tf_op jit(solution)/shard_map/ppermute | solution.py:51
  20.3 40.9 %copy-start.11 = (pred[128,384]{0,1:T(8,128)(4,1)}, pred[128,384]{0,1:T(8,128)(4,1)S(1)}, u32[]{:S(2)}) copy-start(pred[128,384]{0,1:T(8,128)(4,1)S(1)} %or_and_fusion) | copy-start | bytes 147460
  49.8 27.8 %all-to-all-start = ((bf16[16,128,320]{1,2,0:T(8,128)(2,1)}), bf16[16,128,320]{1,2,0:T(8,128)(2,1)S(1)}, u32[]{:S(2)}, u32[]{:S(2)}) async-start(bf16[16,128,320]{1,2,0:T(8,128)(2,1)} %bitcast.8), calls=%async_computation | async-start | bytes 2621440 | tf_op jit(solution)/shard_map/all_to_all | solution.py:69
  58.0 31.0 %collective-permute-start.8 = (bf16[4,2,320,512]{3,2,1,0:T(8,128)(2,1)}, bf16[4,2,320,512]{3,2,1,0:T(8,128)(2,1)}, u32[]{:S(2)}, u32[]{:S(2)}) collective-permute-start(bf16[4,2,320,512]{3,2,1,0:T(8,128)(2,1)} %pad_maximum_fusion.1), channel_id=1, source_target_pairs={{0,16},{16,0},{32,48},{48,32},{64,80},{80,64},{96,112},{112,96},{1... | collective-permute-start | bytes 7864328 | tf_op jit(solution)/shard_map/ppermute | solution.py:53
  77.7 10.2 %collective-permute-start.6 = (bf16[128,512]{0,1:T(8,128)(2,1)S(1)}, bf16[128,512]{0,1:T(8,128)(2,1)S(1)}, u32[]{:S(2)}, u32[]{:S(2)}) collective-permute-start(bf16[128,512]{0,1:T(8,128)(2,1)S(1)} %get-tuple-element.40), channel_id=1, source_target_pairs={{1,0},{2,1},{3,2},{4,3},{5,4},{6,5},{7,6},{8,7},{9,8},{10,9},{11,1... | collective-permute-start | bytes 393224 | tf_op jit(solution)/shard_map/ppermute | solution.py:82
  79.6 9.4 %collective-permute-start.7 = (bf16[128,512]{0,1:T(8,128)(2,1)S(1)}, bf16[128,512]{0,1:T(8,128)(2,1)S(1)}, u32[]{:S(2)}, u32[]{:S(2)}) collective-permute-start(bf16[128,512]{0,1:T(8,128)(2,1)S(1)} %get-tuple-element.41), channel_id=1, source_target_pairs={{0,1},{1,2},{2,3},{3,4},{4,5},{5,6},{6,7},{7,8},{8,9},{9,10},{10,1... | collective-permute-start | bytes 393224 | tf_op jit(solution)/shard_map/ppermute | solution.py:82
  94.3 20.8 %collective-permute-start.10 = (bf16[128,512]{1,0:T(8,128)(2,1)S(1)}, bf16[128,512]{1,0:T(8,128)(2,1)S(1)}, u32[]{:S(2)}, u32[]{:S(2)}) collective-permute-start(bf16[128,512]{1,0:T(8,128)(2,1)S(1)} %fusion.41), channel_id=1, source_target_pairs={{1,0},{2,1},{3,2},{4,3},{5,4},{6,5},{7,6},{8,7},{9,8},{10,9},{11,1... | collective-permute-start | bytes 393224 | tf_op jit(solution)/shard_map/ppermute | solution.py:19
  96.2 18.9 %collective-permute-start.9 = (bf16[128,512]{1,0:T(8,128)(2,1)S(1)}, bf16[128,512]{1,0:T(8,128)(2,1)}, u32[]{:S(2)}, u32[]{:S(2)}) collective-permute-start(bf16[128,512]{1,0:T(8,128)(2,1)S(1)} %fusion.41), channel_id=1, source_target_pairs={{0,1},{1,2},{2,3},{3,4},{4,5},{5,6},{6,7},{7,8},{8,9},{9,10},{10,1... | collective-permute-start | bytes 393224 | tf_op jit(solution)/shard_map/ppermute | solution.py:17
  102.9 36.1 %all-to-all-start.1 = ((bf16[16,128,512]{1,2,0:T(8,128)(2,1)}), bf16[16,128,512]{1,2,0:T(8,128)(2,1)}, u32[]{:S(2)}, u32[]{:S(2)}) async-start(bf16[16,128,512]{1,2,0:T(8,128)(2,1)} %broadcast_in_dim.114), calls=%async_computation.1 | async-start | bytes 4194304 | tf_op jit(solution)/shard_map/all_to_all | solution.py:69
  124.8 14.1 %copy-start.2 = (bf16[16,128,320]{1,2,0:T(8,128)(2,1)S(1)}, bf16[16,128,320]{1,2,0:T(8,128)(2,1)}, u32[]{:S(2)}) copy-start(bf16[16,128,320]{1,2,0:T(8,128)(2,1)} %copy-done.1) | copy-start | bytes 3932164
  143.0 25.8 %all-to-all-start.2 = ((bf16[16,80,128]{2,1,0:T(8,128)(2,1)}), bf16[16,80,128]{2,1,0:T(8,128)(2,1)S(1)}, u32[]{:S(2)}, u32[]{:S(2)}) async-start(bf16[16,80,128]{2,1,0:T(8,128)(2,1)} %reshape.288), calls=%async_computation.2 | async-start | bytes 655360 | tf_op jit(solution)/shard_map/all_to_all | solution.py:69
  153.9 12.8 %collective-permute-start.11 = (bf16[128,512]{0,1:T(8,128)(2,1)S(1)}, bf16[128,512]{0,1:T(8,128)(2,1)S(1)}, u32[]{:S(2)}, u32[]{:S(2)}) collective-permute-start(bf16[128,512]{0,1:T(8,128)(2,1)S(1)} %get-tuple-element.34), channel_id=1, source_target_pairs={{1,0},{2,1},{3,2},{4,3},{5,4},{6,5},{7,6},{8,7},{9,8},{10,9},{11,1... | collective-permute-start | bytes 393224 | tf_op jit(solution)/shard_map/ppermute | solution.py:82
  155.9 12.1 %collective-permute-start.12 = (bf16[128,512]{0,1:T(8,128)(2,1)S(1)}, bf16[128,512]{0,1:T(8,128)(2,1)S(1)}, u32[]{:S(2)}, u32[]{:S(2)}) collective-permute-start(bf16[128,512]{0,1:T(8,128)(2,1)S(1)} %get-tuple-element.35), channel_id=1, source_target_pairs={{0,1},{1,2},{2,3},{3,4},{4,5},{5,6},{6,7},{7,8},{8,9},{9,10},{10,1... | collective-permute-start | bytes 393224 | tf_op jit(solution)/shard_map/ppermute | solution.py:82
  (13 other events, 32.0 us)

commit v16 on v14

--- a/solution.py
+++ b/solution.py
@@ -42,6 +42,7 @@
         for s in range(seq_count)
     ]
     held = jnp.stack([weight, lax.ppermute(weight, ("dp", "seq"), partner_pairs)])
+    held, riders = lax.optimization_barrier((held, riders))
     ring = [held]
     for shift in range(1, y_count):
         pairs = []
@@ -49,7 +50,7 @@
             upper, y_here, core = d // half, (d // cores) % y_count, d % cores
             pairs.append((d, upper * half + ((y_here + shift) % y_count) * cores + core))
         ring.append(lax.ppermute(held, "dp", pairs))
-    mine, ready, riders = lax.optimization_barrier((jnp.stack(ring), ready, riders))
+    mine, ready = lax.optimization_barrier((jnp.stack(ring), ready))
     sibling = lax.ppermute(mine, "dp", [(d, d ^ 1) for d in range(dp_count)])
     stacked = jnp.stack([mine, sibling]).reshape(dp_count, rows, width)
     me = lax.axis_index("dp")

time: 171 us -> 178 us (1.041)
  waiting for transfers between devices: 58.4 us -> 61.6 us
    ppermute x4, waiting for transfers between devices: 7.26 us -> 10.6 us  [passed_along(): return lax.ppermute(array, axis, pairs)]
    dot_general x1, matrix products: 4.35 us -> 1.83 us  [local(): lax.dot_general(value_grad, weight_full, (((1,), (1,)), ((), ())), prefer...]
    ppermute x1, waiting for transfers between devices: 5.72 us -> 3.5 us  [spread_weight(): lax.ppermute(weight, ('dp', 'seq'), partner_pairs)]
    unnamed x49 -> x55, local copies, waits for them, and re-layouts: 11.1 us -> 11.1 us
  transfers between devices with their start and end apart: 16 -> 16, of which waited for: 9 -> 6; matrix products, arithmetic and copies ran while one was open for 25% -> 27% of each run, Pallas kernels for 0% -> 0%
where the time goes in v16:
time: 178 us; the launch traced here: 176 us
  waiting for transfers between devices  61.6 us (35%)
  starting transfers between devices  54.1 us (30%)
  matrix products  28.7 us (16%)
  local copies, waits for them, and re-layouts  18.2 us (10%)
  other arithmetic  12.2 us (7%)
    ppermute x3, waiting for transfers between devices, spread_weight(): ring.append(lax.ppermute(held, 'dp', pairs))  28.4 us
    all_to_all x3, starting transfers between devices, gathered_copies(): return lax.all_to_all(copies, axis, 0, 0, tiled=True)  23.2 us
    all_to_all x3, waiting for transfers between devices, gathered_copies(): return lax.all_to_all(copies, axis, 0, 0, tiled=True)  19.1 us
    ppermute x4, starting transfers between devices, passed_along(): return lax.ppermute(array, axis, pairs)  12.7 us
    unnamed x55, local copies, waits for them, and re-layouts  11.1 us
    ppermute x4, waiting for transfers between devices, passed_along(): return lax.ppermute(array, axis, pairs)  10.6 us
    ppermute x2, starting transfers between devices, with_halo(): lax.ppermute(tail, axis, [(i, (i + 1) % count) for i in range(ends)])  9.3 us
    sub x4, matrix products, attend_first(): weights = jnp.where(visible[None], jnp.exp(masked - highest), 0.0)  7.03 us
  transfers between devices with their start and end apart: 16, of which 6 were waited for; matrix products, arithmetic and copies ran while one was open for 27% of the time, Pallas kernels for 0%

profile of v16, /device:TPU:26, one launch (start us, length us, event | category | flops | bytes accessed | tf_op | source)
XLA Modules:
  0.0 176.0 jit_solution(111832199193509974)
XLA Ops:
  1.8 2.4 %collective-permute-start.5 = (bf16[128,512]{0,1:T(8,128)(2,1)S(1)}, bf16[128,512]{0,1:T(8,128)(2,1)S(1)}, u32[]{:S(2)}, u32[]{:S(2)}) collective-permute-start(bf16[128,512]{0,1:T(8,128)(2,1)S(1)} %bitcast.328), channel_id=1, source_target_pairs={{1,0},{2,1},{3,2},{4,3},{5,4},{6,5},{7,6},{8,7},{9,8},{10,9},{11,1... | collective-permute-start | bytes 393224 | tf_op jit(solution)/shard_map/ppermute | solution.py:19
  4.3 4.3 %collective-permute-start.4 = (bf16[128,512]{0,1:T(8,128)(2,1)S(1)}, bf16[128,512]{0,1:T(8,128)(2,1)S(1)}, u32[]{:S(2)}, u32[]{:S(2)}) collective-permute-start(bf16[128,512]{0,1:T(8,128)(2,1)S(1)} %bitcast.329), channel_id=1, source_target_pairs={{0,1},{1,2},{2,3},{3,4},{4,5},{5,6},{6,7},{7,8},{8,9},{9,10},{10,1... | collective-permute-start | bytes 393224 | tf_op jit(solution)/shard_map/ppermute | solution.py:17
  9.3 2.2 %copy.92 = bf16[1,128,2560]{1,2,0:T(8,128)(2,1)} copy(bf16[1,128,2560]{2,1,0:T(8,128)(2,1)} %param.8) | data formatting | bytes 1310720 | tf_op args[1]
  14.3 3.5 %collective-permute-done = bf16[320,512]{1,0:T(8,128)(2,1)S(1)} collective-permute-done((bf16[320,512]{1,0:T(8,128)(2,1)}, bf16[320,512]{1,0:T(8,128)(2,1)S(1)}, u32[]{:S(2)}, u32[]{:S(2)}) %collective-permute-start) | collective-permute-done | bytes 327712 | tf_op jit(solution)/shard_map/ppermute | solution.py:44
  19.6 2.2 %collective-permute-start.1 = (bf16[2,320,512]{2,1,0:T(8,128)(2,1)S(1)}, bf16[2,320,512]{2,1,0:T(8,128)(2,1)}, u32[]{:S(2)}, u32[]{:S(2)}) collective-permute-start(bf16[2,320,512]{2,1,0:T(8,128)(2,1)S(1)} %pad_maximum_fusion.4), channel_id=1, source_target_pairs={{0,32},{16,48},{32,64},{48,80},{64,96},{80,112},{96,0},{112,16},{1... | collective-permute-start | bytes 1966088 | tf_op jit(solution)/shard_map/ppermute | solution.py:52
  23.6 7.3 %all-to-all-start = ((bf16[16,128,320]{1,2,0:T(8,128)(2,1)}), bf16[16,128,320]{1,2,0:T(8,128)(2,1)S(1)}, u32[]{:S(2)}, u32[]{:S(2)}) async-start(bf16[16,128,320]{1,2,0:T(8,128)(2,1)} %bitcast.3), calls=%async_computation | async-start | bytes 2621440 | tf_op jit(solution)/shard_map/all_to_all | solution.py:70
  30.9 25.5 %collective-permute-done.3 = bf16[2,320,512]{2,1,0:T(8,128)(2,1)S(1)} collective-permute-done((bf16[2,320,512]{2,1,0:T(8,128)(2,1)S(1)}, bf16[2,320,512]{2,1,0:T(8,128)(2,1)S(1)}, u32[]{:S(2)}, u32[]{:S(2)}) %collective-permute-start.3) | collective-permute-done | bytes 655392 | tf_op jit(solution)/shard_map/ppermute | solution.py:52
  56.3 3.0 %collective-permute-done.2 = bf16[2,320,512]{2,1,0:T(8,128)(2,1)S(1)} collective-permute-done((bf16[2,320,512]{2,1,0:T(8,128)(2,1)S(1)}, bf16[2,320,512]{2,1,0:T(8,128)(2,1)S(1)}, u32[]{:S(2)}, u32[]{:S(2)}) %collective-permute-start.2) | collective-permute-done | bytes 655392 | tf_op jit(solution)/shard_map/ppermute | solution.py:52
  59.3 2.9 %pad_maximum_fusion.1 = bf16[4,2,320,512]{3,2,1,0:T(8,128)(2,1)} fusion(bf16[1,2,320,512]{3,2,1,0:T(8,128)(2,1)S(1)} %bitcast.310, bf16[1,2,320,512]{3,2,1,0:T(8,128)(2,1)S(1)} %bitcast.311, bf16[1,2,320,512]{3,2,1,0:T(8,128)(2,1)} %bitcast.5, bf16[1,2,320,512]{3,2,1,0:T(8,128)(2,1)S(1)} %bitcast.307), kind=kLoop, calls=%fused_computation.8 | loop fusion | flops 3932160 | bytes 5242880 | tf_op jit(solution)/shard_map/stack | solution.py:53
  62.2 2.5 %fusion.82 = (f32[5,128]{1,0:T(8,128)S(1)}, f32[5,128,384]{1,2,0:T(8,128)}) fusion(pred[128,384]{0,1:T(8,128)(4,1)S(1)} %copy-done.11, bf16[128,4,5,128]{0,3,2,1:T(8,128)(2,1)} %bitcast.312, bf16[384,4,128]{0,2,1:T(8,128)(2,1)} %bitcast.331), kind=kOutput, calls=%fused_computation.159 | convolution fusion | flops 64143744 | bytes 1346048 | tf_op jit(solution)/shard_map/sub | solution.py:112
  70.9 2.2 %convolution_bitcast_fusion.6 = f32[384,128]{0,1:T(8,128)} fusion(bf16[128,4,5,128]{0,3,2,1:T(8,128)(2,1)S(1)} %bitcast.322, f32[5,128,384]{1,2,0:T(8,128)} %get-tuple-element.47, f32[5,128]{1,0:T(8,128)S(1)} %get-tuple-element.46), kind=kOutput, calls=%fused_computation.54 | convolution fusion | flops 63406080 | bytes 1347584 | tf_op jit(solution)/shard_map/gqk,qgd->kd/dot_general | solution.py:117
  77.2 4.9 %collective-permute-start.7 = (bf16[128,512]{0,1:T(8,128)(2,1)}, bf16[128,512]{0,1:T(8,128)(2,1)S(1)}, u32[]{:S(2)}, u32[]{:S(2)}) collective-permute-start(bf16[128,512]{0,1:T(8,128)(2,1)} %get-tuple-element.41), channel_id=1, source_target_pairs={{0,1},{1,2},{2,3},{3,4},{4,5},{5,6},{6,7},{7,8},{8,9},{9,10},{10,1... | collective-permute-start | bytes 393224 | tf_op jit(solution)/shard_map/ppermute | solution.py:83
  82.1 1.9 %collective-permute-start.6 = (bf16[128,512]{0,1:T(8,128)(2,1)}, bf16[128,512]{0,1:T(8,128)(2,1)}, u32[]{:S(2)}, u32[]{:S(2)}) collective-permute-start(bf16[128,512]{0,1:T(8,128)(2,1)} %get-tuple-element.40), channel_id=1, source_target_pairs={{1,0},{2,1},{3,2},{4,3},{5,4},{6,5},{7,6},{8,7},{9,8},{10,9},{11,1... | collective-permute-start | bytes 393224 | tf_op jit(solution)/shard_map/ppermute | solution.py:83
  85.3 2.1 %gather_fusion = bf16[16,128,320]{1,2,0:T(8,128)(2,1)S(1)} fusion(bf16[128,16,320]{0,2,1:T(8,128)(2,1)} %bitcast.2, s32[1024]{0:T(1024)S(1)} %pad_clamp_fusion.1), kind=kCustom, calls=%fused_computation | custom fusion | bytes 2621504 | tf_op jit(solution)/shard_map/jit(_take)/gather | solution.py:205
  87.5 3.3 %collective-permute-done.6 = bf16[128,512]{0,1:T(8,128)(2,1)} collective-permute-done((bf16[128,512]{0,1:T(8,128)(2,1)}, bf16[128,512]{0,1:T(8,128)(2,1)}, u32[]{:S(2)}, u32[]{:S(2)}) %collective-permute-start.6) | collective-permute-done | bytes 131104 | tf_op jit(solution)/shard_map/ppermute | solution.py:83
  91.7 3.0 %pad_maximum_fusion = bf16[2,4,2,320,512]{4,3,2,1,0:T(8,128)(2,1)S(1)} fusion(bf16[1,4,2,320,512]{4,3,2,1,0:T(8,128)(2,1)} %bitcast.42, bf16[1,4,2,320,512]{4,3,2,1,0:T(8,128)(2,1)} %bitcast.41), kind=kLoop, calls=%fused_computation.7 | loop fusion | flops 2621440 | bytes 10485760 | tf_op jit(solution)/shard_map/stack | solution.py:55
  98.2 5.0 %collective-permute-start.9 = (bf16[128,512]{1,0:T(8,128)(2,1)}, bf16[128,512]{1,0:T(8,128)(2,1)S(1)}, u32[]{:S(2)}, u32[]{:S(2)}) collective-permute-start(bf16[128,512]{1,0:T(8,128)(2,1)} %fusion.41), channel_id=1, source_target_pairs={{0,1},{1,2},{2,3},{3,4},{4,5},{5,6},{6,7},{7,8},{8,9},{9,10},{10,1... | collective-permute-start | bytes 393224 | tf_op jit(solution)/shard_map/ppermute | solution.py:17
  109.8 5.3 %all-to-all-start.1 = ((bf16[16,128,512]{1,2,0:T(8,128)(2,1)}), bf16[16,128,512]{1,2,0:T(8,128)(2,1)S(1)}, u32[]{:S(2)}, u32[]{:S(2)}) async-start(bf16[16,128,512]{1,2,0:T(8,128)(2,1)} %broadcast_in_dim.114), calls=%async_computation.1 | async-start | bytes 4194304 | tf_op jit(solution)/shard_map/all_to_all | solution.py:70
  127.1 19.1 %all-to-all-done.1 = bf16[16,128,512]{1,2,0:T(8,128)(2,1)S(1)} async-done(((bf16[16,128,512]{1,2,0:T(8,128)(2,1)}), bf16[16,128,512]{1,2,0:T(8,128)(2,1)S(1)}, u32[]{:S(2)}, u32[]{:S(2)}) %all-to-all-start.1) | async-done | bytes 2097184 | tf_op jit(solution)/shard_map/all_to_all | solution.py:70
  146.2 3.3 %fusion.31 = bf16[16,32,320]{2,1,0:T(8,128)(2,1)} fusion(bf16[16,128,16,32]{1,3,2,0:T(8,128)(2,1)S(1)} %bitcast.309, bf16[16,128,320]{1,2,0:T(8,128)(2,1)} %copy-done.1), kind=kOutput, calls=%fused_computation.42 | convolution fusion | flops 671252480 | bytes 3735552 | tf_op jit(solution)/shard_map/rtk,rtjc->jck/dot_general | solution.py:199
  149.5 10.6 %all-to-all-start.2 = ((bf16[16,32,320]{2,1,0:T(8,128)(2,1)}), bf16[16,32,320]{2,1,0:T(8,128)(2,1)S(1)}, u32[]{:S(2)}, u32[]{:S(2)}) async-start(bf16[16,32,320]{2,1,0:T(8,128)(2,1)} %fusion.31), calls=%async_computation.2 | async-start | bytes 786432 | tf_op jit(solution)/shard_map/all_to_all | solution.py:70
  161.3 3.4 %collective-permute-start.12 = (bf16[128,512]{0,1:T(8,128)(2,1)S(1)}, bf16[128,512]{0,1:T(8,128)(2,1)S(1)}, u32[]{:S(2)}, u32[]{:S(2)}) collective-permute-start(bf16[128,512]{0,1:T(8,128)(2,1)S(1)} %get-tuple-element.35), channel_id=1, source_target_pairs={{0,1},{1,2},{2,3},{3,4},{4,5},{5,6},{6,7},{7,8},{8,9},{9,10},{10,1... | collective-permute-start | bytes 393224 | tf_op jit(solution)/shard_map/ppermute | solution.py:83
  164.6 2.5 %collective-permute-start.11 = (bf16[128,512]{0,1:T(8,128)(2,1)S(1)}, bf16[128,512]{0,1:T(8,128)(2,1)S(1)}, u32[]{:S(2)}, u32[]{:S(2)}) collective-permute-start(bf16[128,512]{0,1:T(8,128)(2,1)S(1)} %get-tuple-element.34), channel_id=1, source_target_pairs={{1,0},{2,1},{3,2},{4,3},{5,4},{6,5},{7,6},{8,7},{9,8},{10,9},{11,1... | collective-permute-start | bytes 393224 | tf_op jit(solution)/shard_map/ppermute | solution.py:83
  167.2 7.3 %collective-permute-done.12 = bf16[128,512]{0,1:T(8,128)(2,1)S(1)} collective-permute-done((bf16[128,512]{0,1:T(8,128)(2,1)S(1)}, bf16[128,512]{0,1:T(8,128)(2,1)S(1)}, u32[]{:S(2)}, u32[]{:S(2)}) %collective-permute-start.12) | collective-permute-done | bytes 131104 | tf_op jit(solution)/shard_map/ppermute | solution.py:83
  (124 shorter events, 45.3 us)
Async XLA Ops:
  0.6 10.8 %copy-start = (bf16[1,128,5120]{2,1,0:T(8,128)(2,1)S(1)}, bf16[1,128,5120]{2,1,0:T(8,128)(2,1)}, u32[]{:S(2)}) copy-start(bf16[1,128,5120]{2,1,0:T(8,128)(2,1)} %param.7) | copy-start | bytes 3932164
  0.6 12.2 %copy-start.2 = (bf16[1,128,2560]{2,1,0:T(8,128)(2,1)S(1)}, bf16[1,128,2560]{2,1,0:T(8,128)(2,1)}, u32[]{:S(2)}) copy-start(bf16[1,128,2560]{2,1,0:T(8,128)(2,1)} %param.10) | copy-start | bytes 1966084
  1.8 20.9 %collective-permute-start.5 = (bf16[128,512]{0,1:T(8,128)(2,1)S(1)}, bf16[128,512]{0,1:T(8,128)(2,1)S(1)}, u32[]{:S(2)}, u32[]{:S(2)}) collective-permute-start(bf16[128,512]{0,1:T(8,128)(2,1)S(1)} %bitcast.328), channel_id=1, source_target_pairs={{1,0},{2,1},{3,2},{4,3},{5,4},{6,5},{7,6},{8,7},{9,8},{10,9},{11,1... | collective-permute-start | bytes 393224 | tf_op jit(solution)/shard_map/ppermute | solution.py:19
  4.3 18.5 %collective-permute-start.4 = (bf16[128,512]{0,1:T(8,128)(2,1)S(1)}, bf16[128,512]{0,1:T(8,128)(2,1)S(1)}, u32[]{:S(2)}, u32[]{:S(2)}) collective-permute-start(bf16[128,512]{0,1:T(8,128)(2,1)S(1)} %bitcast.329), channel_id=1, source_target_pairs={{0,1},{1,2},{2,3},{3,4},{4,5},{5,6},{6,7},{7,8},{8,9},{9,10},{10,1... | collective-permute-start | bytes 393224 | tf_op jit(solution)/shard_map/ppermute | solution.py:17
  8.6 9.2 %collective-permute-start = (bf16[320,512]{1,0:T(8,128)(2,1)}, bf16[320,512]{1,0:T(8,128)(2,1)S(1)}, u32[]{:S(2)}, u32[]{:S(2)}) collective-permute-start(bf16[320,512]{1,0:T(8,128)(2,1)} %param.11), channel_id=1, source_target_pairs={{0,129},{1,128},{2,131},{3,130},{4,133},{5,132},{6,135},{7,134},{8... | collective-permute-start | bytes 983048 | tf_op jit(solution)/shard_map/ppermute | solution.py:44
  11.4 6.3 %copy-start.9 = (bf16[320,512]{1,0:T(8,128)(2,1)S(1)}, bf16[320,512]{1,0:T(8,128)(2,1)}, u32[]{:S(2)}) copy-start(bf16[320,512]{1,0:T(8,128)(2,1)} %param.11) | copy-start | bytes 983044
  11.4 10.4 %copy-start.12 = (s32[1,2048]{1,0:T(1,128)S(1)}, s32[1,2048]{1,0:T(1,128)}, u32[]{:S(2)}) copy-start(s32[1,2048]{1,0:T(1,128)} %param.12) | copy-start | bytes 24580
  11.4 10.4 %copy-start.13 = (s32[1,32]{1,0:T(1,128)S(1)}, s32[1,32]{1,0:T(1,128)}, u32[]{:S(2)}) copy-start(s32[1,32]{1,0:T(1,128)} %param.13) | copy-start | bytes 388
  17.8 38.5 %collective-permute-start.3 = (bf16[2,320,512]{2,1,0:T(8,128)(2,1)S(1)}, bf16[2,320,512]{2,1,0:T(8,128)(2,1)S(1)}, u32[]{:S(2)}, u32[]{:S(2)}) collective-permute-start(bf16[2,320,512]{2,1,0:T(8,128)(2,1)S(1)} %pad_maximum_fusion.4), channel_id=1, source_target_pairs={{0,96},{16,112},{32,0},{48,16},{64,32},{80,48},{96,64},{112,80},{1... | collective-permute-start | bytes 1966088 | tf_op jit(solution)/shard_map/ppermute | solution.py:52
  18.7 40.6 %collective-permute-start.2 = (bf16[2,320,512]{2,1,0:T(8,128)(2,1)S(1)}, bf16[2,320,512]{2,1,0:T(8,128)(2,1)S(1)}, u32[]{:S(2)}, u32[]{:S(2)}) collective-permute-start(bf16[2,320,512]{2,1,0:T(8,128)(2,1)S(1)} %pad_maximum_fusion.4), channel_id=1, source_target_pairs={{0,64},{16,80},{32,96},{48,112},{64,0},{80,16},{96,32},{112,48},{1... | collective-permute-start | bytes 1966088 | tf_op jit(solution)/shard_map/ppermute | solution.py:52
  19.6 39.7 %collective-permute-start.1 = (bf16[2,320,512]{2,1,0:T(8,128)(2,1)S(1)}, bf16[2,320,512]{2,1,0:T(8,128)(2,1)}, u32[]{:S(2)}, u32[]{:S(2)}) collective-permute-start(bf16[2,320,512]{2,1,0:T(8,128)(2,1)S(1)} %pad_maximum_fusion.4), channel_id=1, source_target_pairs={{0,32},{16,48},{32,64},{48,80},{64,96},{80,112},{96,0},{112,16},{1... | collective-permute-start | bytes 1966088 | tf_op jit(solution)/shard_map/ppermute | solution.py:52
  23.6 52.7 %all-to-all-start = ((bf16[16,128,320]{1,2,0:T(8,128)(2,1)}), bf16[16,128,320]{1,2,0:T(8,128)(2,1)S(1)}, u32[]{:S(2)}, u32[]{:S(2)}) async-start(bf16[16,128,320]{1,2,0:T(8,128)(2,1)} %bitcast.3), calls=%async_computation | async-start | bytes 2621440 | tf_op jit(solution)/shard_map/all_to_all | solution.py:70
  62.2 29.5 %collective-permute-start.8 = (bf16[4,2,320,512]{3,2,1,0:T(8,128)(2,1)}, bf16[4,2,320,512]{3,2,1,0:T(8,128)(2,1)}, u32[]{:S(2)}, u32[]{:S(2)}) collective-permute-start(bf16[4,2,320,512]{3,2,1,0:T(8,128)(2,1)} %pad_maximum_fusion.1), channel_id=1, source_target_pairs={{0,16},{16,0},{32,48},{48,32},{64,80},{80,64},{96,112},{112,96},{1... | collective-permute-start | bytes 7864328 | tf_op jit(solution)/shard_map/ppermute | solution.py:54
  64.8 3.2 %copy-start.18 = (f32[5,128]{1,0:T(8,128)}, f32[5,128]{1,0:T(8,128)S(1)}, u32[]{:S(2)}) copy-start(f32[5,128]{1,0:T(8,128)S(1)} %get-tuple-element.42) | copy-start | bytes 7684
  70.9 3.7 %copy-start.22 = (f32[5,128]{1,0:T(8,128)}, f32[5,128]{1,0:T(8,128)S(1)}, u32[]{:S(2)}) copy-start(f32[5,128]{1,0:T(8,128)S(1)} %get-tuple-element.46) | copy-start | bytes 7684
  76.3 9.1 %copy-start.1 = (bf16[16,128,320]{1,2,0:T(8,128)(2,1)}, bf16[16,128,320]{1,2,0:T(8,128)(2,1)S(1)}, u32[]{:S(2)}) copy-start(bf16[16,128,320]{1,2,0:T(8,128)(2,1)S(1)} %all-to-all-done) | copy-start | bytes 3932164
  77.2 10.3 %collective-permute-start.7 = (bf16[128,512]{0,1:T(8,128)(2,1)}, bf16[128,512]{0,1:T(8,128)(2,1)S(1)}, u32[]{:S(2)}, u32[]{:S(2)}) collective-permute-start(bf16[128,512]{0,1:T(8,128)(2,1)} %get-tuple-element.41), channel_id=1, source_target_pairs={{0,1},{1,2},{2,3},{3,4},{4,5},{5,6},{6,7},{7,8},{8,9},{9,10},{10,1... | collective-permute-start | bytes 393224 | tf_op jit(solution)/shard_map/ppermute | solution.py:83
  82.1 8.7 %collective-permute-start.6 = (bf16[128,512]{0,1:T(8,128)(2,1)}, bf16[128,512]{0,1:T(8,128)(2,1)}, u32[]{:S(2)}, u32[]{:S(2)}) collective-permute-start(bf16[128,512]{0,1:T(8,128)(2,1)} %get-tuple-element.40), channel_id=1, source_target_pairs={{1,0},{2,1},{3,2},{4,3},{5,4},{6,5},{7,6},{8,7},{9,8},{10,9},{11,1... | collective-permute-start | bytes 393224 | tf_op jit(solution)/shard_map/ppermute | solution.py:83
  96.3 18.9 %collective-permute-start.10 = (bf16[128,512]{1,0:T(8,128)(2,1)}, bf16[128,512]{1,0:T(8,128)(2,1)S(1)}, u32[]{:S(2)}, u32[]{:S(2)}) collective-permute-start(bf16[128,512]{1,0:T(8,128)(2,1)} %fusion.41), channel_id=1, source_target_pairs={{1,0},{2,1},{3,2},{4,3},{5,4},{6,5},{7,6},{8,7},{9,8},{10,9},{11,1... | collective-permute-start | bytes 393224 | tf_op jit(solution)/shard_map/ppermute | solution.py:19
  98.2 17.0 %collective-permute-start.9 = (bf16[128,512]{1,0:T(8,128)(2,1)}, bf16[128,512]{1,0:T(8,128)(2,1)S(1)}, u32[]{:S(2)}, u32[]{:S(2)}) collective-permute-start(bf16[128,512]{1,0:T(8,128)(2,1)} %fusion.41), channel_id=1, source_target_pairs={{0,1},{1,2},{2,3},{3,4},{4,5},{5,6},{6,7},{7,8},{8,9},{9,10},{10,1... | collective-permute-start | bytes 393224 | tf_op jit(solution)/shard_map/ppermute | solution.py:17
  109.8 36.4 %all-to-all-start.1 = ((bf16[16,128,512]{1,2,0:T(8,128)(2,1)}), bf16[16,128,512]{1,2,0:T(8,128)(2,1)S(1)}, u32[]{:S(2)}, u32[]{:S(2)}) async-start(bf16[16,128,512]{1,2,0:T(8,128)(2,1)} %broadcast_in_dim.114), calls=%async_computation.1 | async-start | bytes 4194304 | tf_op jit(solution)/shard_map/all_to_all | solution.py:70
  149.5 25.8 %all-to-all-start.2 = ((bf16[16,32,320]{2,1,0:T(8,128)(2,1)}), bf16[16,32,320]{2,1,0:T(8,128)(2,1)S(1)}, u32[]{:S(2)}, u32[]{:S(2)}) async-start(bf16[16,32,320]{2,1,0:T(8,128)(2,1)} %fusion.31), calls=%async_computation.2 | async-start | bytes 786432 | tf_op jit(solution)/shard_map/all_to_all | solution.py:70
  161.3 13.3 %collective-permute-start.12 = (bf16[128,512]{0,1:T(8,128)(2,1)S(1)}, bf16[128,512]{0,1:T(8,128)(2,1)S(1)}, u32[]{:S(2)}, u32[]{:S(2)}) collective-permute-start(bf16[128,512]{0,1:T(8,128)(2,1)S(1)} %get-tuple-element.35), channel_id=1, source_target_pairs={{0,1},{1,2},{2,3},{3,4},{4,5},{5,6},{6,7},{7,8},{8,9},{9,10},{10,1... | collective-permute-start | bytes 393224 | tf_op jit(solution)/shard_map/ppermute | solution.py:83
  164.6 9.9 %collective-permute-start.11 = (bf16[128,512]{0,1:T(8,128)(2,1)S(1)}, bf16[128,512]{0,1:T(8,128)(2,1)S(1)}, u32[]{:S(2)}, u32[]{:S(2)}) collective-permute-start(bf16[128,512]{0,1:T(8,128)(2,1)S(1)} %get-tuple-element.34), channel_id=1, source_target_pairs={{1,0},{2,1},{3,2},{4,3},{5,4},{6,5},{7,6},{8,7},{9,8},{10,9},{11,1... | collective-permute-start | bytes 393224 | tf_op jit(solution)/shard_map/ppermute | solution.py:83
  (16 other events, 27.2 us)

commit v17 on v14

--- a/solution.py
+++ b/solution.py
@@ -189,9 +189,24 @@
     )
     attentions, value_part = attend_first(query_states[0], key_block, out_grad[0], visible)
     value_part, input_blocks = lax.optimization_barrier((value_part, input_blocks))
-    value_grad = rim_sum(value_part, tok_count).astype(jnp.bfloat16)
-    value_grad, weight_slots = lax.optimization_barrier((value_grad, weight_slots))
     weight_full = weight_slots.reshape(-1, kv_width)
+    input_slots = jnp.take(
+        layer_rows.reshape(tok_count, dp_count, -1), slot_owner, axis=1, mode="clip"
+    ).reshape(tok_count, -1)
+    value_rows = jnp.dot(input_slots, weight_full, preferred_element_type=jnp.float32)
+    value_low = value_rows.astype(jnp.bfloat16)
+    rim_low = value_part[:tok_count].astype(jnp.bfloat16)
+    rim_high = value_part[tok_count + tok_count :].astype(jnp.bfloat16)
+    from_below = passed_along(jnp.concatenate([value_low[-tok_count:], rim_high], axis=1), "seq", 1)
+    from_above = passed_along(jnp.concatenate([value_low[:tok_count], rim_low], axis=1), "seq", -1)
+    value_block = jnp.concatenate(
+        [from_below[:, :kv_width], value_low, from_above[:, :kv_width]], axis=0
+    )
+    value_grad = (
+        value_part[tok_count : tok_count + tok_count]
+        + from_above[:, kv_width:].astype(jnp.float32)
+        + from_below[:, kv_width:].astype(jnp.float32)
+    ).astype(jnp.bfloat16)
     grad_copies = jnp.broadcast_to(value_grad[None], (dp_count,) + value_grad.shape)
     seq_count = lax.axis_size("seq")
     grad_rows = gathered_copies(grad_copies, "dp").reshape(dp_count, tok_count, seq_count, -1)
@@ -201,11 +216,6 @@
     summed = jnp.sum(gathered_copies(own_pieces, "seq").astype(jnp.float32), axis=0).T
     devices_all = lax.axis_size("dp") * lax.axis_size("seq")
     weight_grad = summed / devices_all
-    input_slots = jnp.take(
-        layer_rows.reshape(tok_count, dp_count, -1), slot_owner, axis=1, mode="clip"
-    ).reshape(tok_count, -1)
-    value_rows = jnp.dot(input_slots, weight_full, preferred_element_type=jnp.float32)
-    value_block = with_halo(value_rows.astype(jnp.bfloat16), (("seq", 0),), tok_count)
     query_grad, key_part = attend_second(
         query_states[0], key_block, value_block, out_grad[0], attentions
     )

time: 171 us -> 182 us (1.064)
  matrix products: 29.1 us -> 43.1 us
  waiting for transfers between devices: 58.4 us -> 52.7 us
  local copies, waits for them, and re-layouts: 17.4 us -> 20.8 us
  starting transfers between devices: 53.2 us -> 50.2 us
    ppermute x3, waiting for transfers between devices: 26.8 us -> 17.3 us  [spread_weight(): ring.append(lax.ppermute(held, 'dp', pairs))]
    dot_general x4, matrix products: 1.12 us -> 8.04 us  [attend_second(): jnp.einsum('qgd,kd->gqk', grad_head, value_head, preferred_element_type=j...]
    ppermute x2 -> x1, starting transfers between devices: 8.62 us -> 4.3 us  [with_halo(): lax.ppermute(tail, axis, [(i, (i + 1) % count) for i in range(ends)])]
    sub x4, matrix products: 5.98 us -> 9.48 us  [attend_first(): weights = jnp.where(visible[None], jnp.exp(masked - highest), 0.0)]
    ppermute x1, waiting for transfers between devices: 5.72 us -> 7.83 us  [spread_weight(): lax.ppermute(weight, ('dp', 'seq'), partner_pairs)]
    ppermute x2 -> x1, starting transfers between devices: 3.96 us -> 2.44 us  [with_halo(): lax.ppermute(head, axis, [((i + 1) % count, i) for i in range(ends)])]
    unnamed x49 -> x103, local copies, waits for them, and re-layouts: 11.1 us -> 12.1 us
  transfers between devices with their start and end apart: 16 -> 14, of which waited for: 9 -> 8; matrix products, arithmetic and copies ran while one was open for 25% -> 30% of each run, Pallas kernels for 0% -> 0%
where the time goes in v17:
time: 182 us; the launch traced here: 180 us
  waiting for transfers between devices  52.7 us (29%)
  starting transfers between devices  50.2 us (28%)
  matrix products  43.1 us (24%)
  local copies, waits for them, and re-layouts  20.8 us (11%)
  other arithmetic  12.2 us (7%)
    all_to_all x3, starting transfers between devices, gathered_copies(): return lax.all_to_all(copies, axis, 0, 0, tiled=True)  25.3 us
    all_to_all x3, waiting for transfers between devices, gathered_copies(): return lax.all_to_all(copies, axis, 0, 0, tiled=True)  18.8 us
    ppermute x3, waiting for transfers between devices, spread_weight(): ring.append(lax.ppermute(held, 'dp', pairs))  17.3 us
    ppermute x4, starting transfers between devices, passed_along(): return lax.ppermute(array, axis, pairs)  12.9 us
    unnamed x103, local copies, waits for them, and re-layouts  12.1 us
    sub x4, matrix products, attend_first(): weights = jnp.where(visible[None], jnp.exp(masked - highest), 0.0)  9.48 us
    ppermute x4, waiting for transfers between devices, passed_along(): return lax.ppermute(array, axis, pairs)  8.7 us
    dot_general x4, matrix products, attend_first(): jnp.einsum('gqk,qgd->kd', attention_low, grad_head, preferred_element_typ...  8.09 us
  transfers between devices with their start and end apart: 14, of which 8 were waited for; matrix products, arithmetic and copies ran while one was open for 30% of the time, Pallas kernels for 0%

profile of v17, /device:TPU:26, one launch (start us, length us, event | category | flops | bytes accessed | tf_op | source)
XLA Modules:
  0.0 180.3 jit_solution(15959448226568481485)
XLA Ops:
  1.8 2.4 %collective-permute-start.5 = (bf16[128,512]{0,1:T(8,128)(2,1)S(1)}, bf16[128,512]{0,1:T(8,128)(2,1)S(1)}, u32[]{:S(2)}, u32[]{:S(2)}) collective-permute-start(bf16[128,512]{0,1:T(8,128)(2,1)S(1)} %bitcast.320), channel_id=1, source_target_pairs={{1,0},{2,1},{3,2},{4,3},{5,4},{6,5},{7,6},{8,7},{9,8},{10,9},{11,1... | collective-permute-start | bytes 393224 | tf_op jit(solution)/shard_map/ppermute | solution.py:19
  4.3 4.3 %collective-permute-start.4 = (bf16[128,512]{0,1:T(8,128)(2,1)S(1)}, bf16[128,512]{0,1:T(8,128)(2,1)}, u32[]{:S(2)}, u32[]{:S(2)}) collective-permute-start(bf16[128,512]{0,1:T(8,128)(2,1)S(1)} %bitcast.321), channel_id=1, source_target_pairs={{0,1},{1,2},{2,3},{3,4},{4,5},{5,6},{6,7},{7,8},{8,9},{9,10},{10,1... | collective-permute-start | bytes 393224 | tf_op jit(solution)/shard_map/ppermute | solution.py:17
  9.9 7.8 %collective-permute-done = bf16[320,512]{1,0:T(8,128)(2,1)S(1)} collective-permute-done((bf16[320,512]{1,0:T(8,128)(2,1)}, bf16[320,512]{1,0:T(8,128)(2,1)S(1)}, u32[]{:S(2)}, u32[]{:S(2)}) %collective-permute-start) | collective-permute-done | bytes 327712 | tf_op jit(solution)/shard_map/ppermute | solution.py:44
  28.5 3.2 %gather_fusion = bf16[16,128,320]{1,2,0:T(8,128)(2,1)} fusion(bf16[128,16,320]{0,2,1:T(8,128)(2,1)} %bitcast.7, s32[1024]{0:T(1024)} %pad_clamp_fusion.1), kind=kCustom, calls=%fused_computation | custom fusion | bytes 2621504 | tf_op jit(solution)/shard_map/jit(_take)/gather | solution.py:193
  33.6 16.6 %collective-permute-done.3 = bf16[2,320,512]{2,1,0:T(8,128)(2,1)} collective-permute-done((bf16[2,320,512]{2,1,0:T(8,128)(2,1)}, bf16[2,320,512]{2,1,0:T(8,128)(2,1)}, u32[]{:S(2)}, u32[]{:S(2)}) %collective-permute-start.3) | collective-permute-done | bytes 655392 | tf_op jit(solution)/shard_map/ppermute | solution.py:51
  53.0 7.4 %all-to-all-start = ((bf16[16,128,320]{1,2,0:T(8,128)(2,1)}), bf16[16,128,320]{1,2,0:T(8,128)(2,1)}, u32[]{:S(2)}, u32[]{:S(2)}) async-start(bf16[16,128,320]{1,2,0:T(8,128)(2,1)} %bitcast.8), calls=%async_computation | async-start | bytes 2621440 | tf_op jit(solution)/shard_map/all_to_all | solution.py:69
  60.4 2.4 %fusion.75 = (f32[5,128]{1,0:T(8,128)S(1)}, f32[5,128,384]{1,2,0:T(8,128)}) fusion(pred[128,384]{0,1:T(8,128)(4,1)S(1)} %or_and_fusion, bf16[128,4,5,128]{0,3,2,1:T(8,128)(2,1)S(1)} %bitcast.305, bf16[384,4,128]{0,2,1:T(8,128)(2,1)} %bitcast.323), kind=kOutput, calls=%fused_computation.159 | convolution fusion | flops 64143744 | bytes 1346048 | tf_op jit(solution)/shard_map/sub | solution.py:111
  64.9 2.4 %fusion.76 = (f32[5,128]{1,0:T(8,128)S(1)}, f32[5,128,384]{1,2,0:T(8,128)}) fusion(pred[128,384]{0,1:T(8,128)(4,1)S(1)} %or_and_fusion, bf16[128,4,5,128]{0,3,2,1:T(8,128)(2,1)S(1)} %bitcast.306, bf16[384,4,128]{0,2,1:T(8,128)(2,1)} %bitcast.324), kind=kOutput, calls=%fused_computation.160 | convolution fusion | flops 64143744 | bytes 1346048 | tf_op jit(solution)/shard_map/sub | solution.py:111
  69.5 2.4 %fusion.77 = (f32[5,128]{1,0:T(8,128)S(1)}, f32[5,128,384]{1,2,0:T(8,128)}) fusion(pred[128,384]{0,1:T(8,128)(4,1)S(1)} %or_and_fusion, bf16[128,4,5,128]{0,3,2,1:T(8,128)(2,1)S(1)} %bitcast.307, bf16[384,4,128]{0,2,1:T(8,128)(2,1)} %bitcast.325), kind=kOutput, calls=%fused_computation.161 | convolution fusion | flops 64143744 | bytes 1346048 | tf_op jit(solution)/shard_map/sub | solution.py:111
  74.1 2.4 %fusion.78 = (f32[5,128]{1,0:T(8,128)S(1)}, f32[5,128,384]{1,2,0:T(8,128)}) fusion(pred[128,384]{0,1:T(8,128)(4,1)S(1)} %or_and_fusion, bf16[128,4,5,128]{0,3,2,1:T(8,128)(2,1)S(1)} %bitcast.308, bf16[384,4,128]{0,2,1:T(8,128)(2,1)} %bitcast.326), kind=kOutput, calls=%fused_computation.162 | convolution fusion | flops 64143744 | bytes 1346048 | tf_op jit(solution)/shard_map/sub | solution.py:111
  80.1 2.3 %pad_maximum_fusion = bf16[2,4,2,320,512]{4,3,2,1,0:T(8,128)(2,1)S(1)} fusion(bf16[1,4,2,320,512]{4,3,2,1,0:T(8,128)(2,1)} %bitcast.22, bf16[1,4,2,320,512]{4,3,2,1,0:T(8,128)(2,1)S(1)} %bitcast.298), kind=kLoop, calls=%fused_computation.7 | loop fusion | flops 2621440 | bytes 10485760 | tf_op jit(solution)/shard_map/stack | solution.py:54
  84.8 3.1 %collective-permute-start.8 = (bf16[128,1024]{1,0:T(8,128)(2,1)S(1)}, bf16[128,1024]{1,0:T(8,128)(2,1)S(1)}, u32[]{:S(2)}, u32[]{:S(2)}) collective-permute-start(bf16[128,1024]{1,0:T(8,128)(2,1)S(1)} %get-tuple-element.39), channel_id=1, source_target_pairs={{1,0},{2,1},{3,2},{4,3},{5,4},{6,5},{7,6},{8,7},{9,8},{10,9},{11,1... | collective-permute-start | bytes 786440 | tf_op jit(solution)/shard_map/ppermute | solution.py:82
  88.0 3.9 %collective-permute-start.7 = (bf16[128,1024]{1,0:T(8,128)(2,1)S(1)}, bf16[128,1024]{1,0:T(8,128)(2,1)S(1)}, u32[]{:S(2)}, u32[]{:S(2)}) collective-permute-start(bf16[128,1024]{1,0:T(8,128)(2,1)S(1)} %get-tuple-element.38), channel_id=1, source_target_pairs={{0,1},{1,2},{2,3},{3,4},{4,5},{5,6},{6,7},{7,8},{8,9},{9,10},{10,1... | collective-permute-start | bytes 786440 | tf_op jit(solution)/shard_map/ppermute | solution.py:82
  93.2 3.2 %collective-permute-done.8 = bf16[128,1024]{1,0:T(8,128)(2,1)S(1)} collective-permute-done((bf16[128,1024]{1,0:T(8,128)(2,1)S(1)}, bf16[128,1024]{1,0:T(8,128)(2,1)S(1)}, u32[]{:S(2)}, u32[]{:S(2)}) %collective-permute-start.8) | collective-permute-done | bytes 262176 | tf_op jit(solution)/shard_map/ppermute | solution.py:82
  96.4 5.5 %collective-permute-done.7 = bf16[128,1024]{1,0:T(8,128)(2,1)S(1)} collective-permute-done((bf16[128,1024]{1,0:T(8,128)(2,1)S(1)}, bf16[128,1024]{1,0:T(8,128)(2,1)S(1)}, u32[]{:S(2)}, u32[]{:S(2)}) %collective-permute-start.7) | collective-permute-done | bytes 262176 | tf_op jit(solution)/shard_map/ppermute | solution.py:82
  102.6 3.1 %multiply_reduce_fusion = (f32[5,128]{1,0:T(8,128)}, f32[5,128,384]{1,2,0:T(8,128)}) fusion(f32[5,128,384]{1,2,0:T(8,128)} %get-tuple-element.41, f32[5,128]{1,0:T(8,128)S(1)} %get-tuple-element.40, bf16[128,4,5,128]{0,3,2,1:T(8,128)(2,1)S(1)} %bitcast.316, bf16[384,1,128]{2,1,0:T(2,128)(2,1)S(1)} %get-tuple-element.35), kind=kOutput, calls=%fused_computation.67 | convolution fusion | flops 63651200 | bytes 2333184 | tf_op jit(solution)/shard_map/qgd,kd->gqk/dot_general | solution.py:137
  112.6 5.3 %all-to-all-start.1 = ((bf16[16,128,512]{1,2,0:T(8,128)(2,1)}), bf16[16,128,512]{1,2,0:T(8,128)(2,1)S(1)}, u32[]{:S(2)}, u32[]{:S(2)}) async-start(bf16[16,128,512]{1,2,0:T(8,128)(2,1)} %broadcast_in_dim.114), calls=%async_computation.1 | async-start | bytes 4194304 | tf_op jit(solution)/shard_map/all_to_all | solution.py:69
  124.5 2.4 %fusion.36 = f32[384,128]{0,1:T(8,128)S(1)} fusion(f32[5,128,384]{1,2,0:T(8,128)} %get-tuple-element.49, f32[5,128]{1,0:T(8,128)} %get-tuple-element.48, bf16[128,4,5,128]{0,3,2,1:T(8,128)(2,1)} %bitcast.304, f32[5,128,384]{1,2,0:T(8,128)} %get-tuple-element.41, f32[5,128]{1,0:T(8,128)S(1)} %get-tuple-element.40), kind=kOutput, calls=%fused_computation.54 | convolution fusion | flops 378273792 | bytes 2333184 | tf_op jit(solution)/shard_map/gqk,qgd->kd/dot_general | solution.py:148
  131.7 3.6 %collective-permute-start.10 = (bf16[128,512]{0,1:T(8,128)(2,1)}, bf16[128,512]{0,1:T(8,128)(2,1)S(1)}, u32[]{:S(2)}, u32[]{:S(2)}) collective-permute-start(bf16[128,512]{0,1:T(8,128)(2,1)} %get-tuple-element.31), channel_id=1, source_target_pairs={{0,1},{1,2},{2,3},{3,4},{4,5},{5,6},{6,7},{7,8},{8,9},{9,10},{10,1... | collective-permute-start | bytes 393224 | tf_op jit(solution)/shard_map/ppermute | solution.py:82
  137.5 11.4 %all-to-all-done.1 = bf16[16,128,512]{1,2,0:T(8,128)(2,1)S(1)} async-done(((bf16[16,128,512]{1,2,0:T(8,128)(2,1)}), bf16[16,128,512]{1,2,0:T(8,128)(2,1)S(1)}, u32[]{:S(2)}, u32[]{:S(2)}) %all-to-all-start.1) | async-done | bytes 2097184 | tf_op jit(solution)/shard_map/all_to_all | solution.py:69
  149.0 3.3 %fusion.29 = bf16[16,32,320]{2,1,0:T(8,128)(2,1)} fusion(bf16[16,128,16,32]{1,3,2,0:T(8,128)(2,1)S(1)} %bitcast.303, bf16[16,128,320]{1,2,0:T(8,128)(2,1)} %all-to-all-done), kind=kOutput, calls=%fused_computation.40 | convolution fusion | flops 671252480 | bytes 3735552 | tf_op jit(solution)/shard_map/rtk,rtjc->jck/dot_general | solution.py:213
  152.3 12.6 %all-to-all-start.2 = ((bf16[16,32,320]{2,1,0:T(8,128)(2,1)}), bf16[16,32,320]{2,1,0:T(8,128)(2,1)S(1)}, u32[]{:S(2)}, u32[]{:S(2)}) async-start(bf16[16,32,320]{2,1,0:T(8,128)(2,1)} %fusion.29), calls=%async_computation.2 | async-start | bytes 786432 | tf_op jit(solution)/shard_map/all_to_all | solution.py:69
  164.9 4.3 %convolution_convert_fusion = bf16[128,5120]{1,0:T(8,128)(2,1)S(1)} fusion(bf16[128,512]{1,0:T(8,128)(2,1)S(1)} %add_convert_fusion, bf16[5120,512]{1,0:T(8,128)(2,1)} %bitcast.297), kind=kOutput, calls=%fused_computation.6 | convolution fusion | flops 671744000 | bytes 6684672 | tf_op jit(solution)/shard_map/dot_general | solution.py:223
  174.1 5.4 %all-to-all-done.2 = bf16[16,32,320]{2,1,0:T(8,128)(2,1)S(1)} async-done(((bf16[16,32,320]{2,1,0:T(8,128)(2,1)}), bf16[16,32,320]{2,1,0:T(8,128)(2,1)S(1)}, u32[]{:S(2)}, u32[]{:S(2)}) %all-to-all-start.2) | async-done | bytes 327712 | tf_op jit(solution)/shard_map/all_to_all | solution.py:69
  (172 shorter events, 57.9 us)
Async XLA Ops:
  0.6 23.7 %copy-start.18 = (s32[1,2048]{1,0:T(1,128)S(1)}, s32[1,2048]{1,0:T(1,128)}, u32[]{:S(2)}) copy-start(s32[1,2048]{1,0:T(1,128)} %param.12) | copy-start | bytes 24580
  0.6 24.3 %copy-start.9 = (bf16[1,128,2560]{2,1,0:T(8,128)(2,1)S(1)}, bf16[1,128,2560]{2,1,0:T(8,128)(2,1)}, u32[]{:S(2)}) copy-start(bf16[1,128,2560]{2,1,0:T(8,128)(2,1)} %param.8) | copy-start | bytes 1966084
  0.7 25.4 %copy-start.2 = (bf16[1,128,5120]{2,1,0:T(8,128)(2,1)S(1)}, bf16[1,128,5120]{2,1,0:T(8,128)(2,1)}, u32[]{:S(2)}) copy-start(bf16[1,128,5120]{2,1,0:T(8,128)(2,1)} %param.7) | copy-start | bytes 3932164
  1.8 30.0 %collective-permute-start.5 = (bf16[128,512]{0,1:T(8,128)(2,1)S(1)}, bf16[128,512]{0,1:T(8,128)(2,1)S(1)}, u32[]{:S(2)}, u32[]{:S(2)}) collective-permute-start(bf16[128,512]{0,1:T(8,128)(2,1)S(1)} %bitcast.320), channel_id=1, source_target_pairs={{1,0},{2,1},{3,2},{4,3},{5,4},{6,5},{7,6},{8,7},{9,8},{10,9},{11,1... | collective-permute-start | bytes 393224 | tf_op jit(solution)/shard_map/ppermute | solution.py:19
  4.3 27.6 %collective-permute-start.4 = (bf16[128,512]{0,1:T(8,128)(2,1)S(1)}, bf16[128,512]{0,1:T(8,128)(2,1)}, u32[]{:S(2)}, u32[]{:S(2)}) collective-permute-start(bf16[128,512]{0,1:T(8,128)(2,1)S(1)} %bitcast.321), channel_id=1, source_target_pairs={{0,1},{1,2},{2,3},{3,4},{4,5},{5,6},{6,7},{7,8},{8,9},{9,10},{10,1... | collective-permute-start | bytes 393224 | tf_op jit(solution)/shard_map/ppermute | solution.py:17
  8.6 9.2 %collective-permute-start = (bf16[320,512]{1,0:T(8,128)(2,1)}, bf16[320,512]{1,0:T(8,128)(2,1)S(1)}, u32[]{:S(2)}, u32[]{:S(2)}) collective-permute-start(bf16[320,512]{1,0:T(8,128)(2,1)} %param.11), channel_id=1, source_target_pairs={{0,129},{1,128},{2,131},{3,130},{4,133},{5,132},{6,135},{7,134},{8... | collective-permute-start | bytes 983048 | tf_op jit(solution)/shard_map/ppermute | solution.py:44
  19.7 7.8 %copy-start.10 = (bf16[1,128,2560]{2,1,0:T(8,128)(2,1)S(1)}, bf16[1,128,2560]{2,1,0:T(8,128)(2,1)}, u32[]{:S(2)}) copy-start(bf16[1,128,2560]{2,1,0:T(8,128)(2,1)} %param.10) | copy-start | bytes 1966084
  19.7 30.6 %collective-permute-start.3 = (bf16[2,320,512]{2,1,0:T(8,128)(2,1)}, bf16[2,320,512]{2,1,0:T(8,128)(2,1)}, u32[]{:S(2)}, u32[]{:S(2)}) collective-permute-start(bf16[2,320,512]{2,1,0:T(8,128)(2,1)} %get-tuple-element.29), channel_id=1, source_target_pairs={{0,96},{16,112},{32,0},{48,16},{64,32},{80,48},{96,64},{112,80},{1... | collective-permute-start | bytes 1966088 | tf_op jit(solution)/shard_map/ppermute | solution.py:51
  20.4 29.8 %collective-permute-start.2 = (bf16[2,320,512]{2,1,0:T(8,128)(2,1)}, bf16[2,320,512]{2,1,0:T(8,128)(2,1)}, u32[]{:S(2)}, u32[]{:S(2)}) collective-permute-start(bf16[2,320,512]{2,1,0:T(8,128)(2,1)} %get-tuple-element.29), channel_id=1, source_target_pairs={{0,64},{16,80},{32,96},{48,112},{64,0},{80,16},{96,32},{112,48},{1... | collective-permute-start | bytes 1966088 | tf_op jit(solution)/shard_map/ppermute | solution.py:51
  21.4 29.5 %collective-permute-start.1 = (bf16[2,320,512]{2,1,0:T(8,128)(2,1)}, bf16[2,320,512]{2,1,0:T(8,128)(2,1)}, u32[]{:S(2)}, u32[]{:S(2)}) collective-permute-start(bf16[2,320,512]{2,1,0:T(8,128)(2,1)} %get-tuple-element.29), channel_id=1, source_target_pairs={{0,32},{16,48},{32,64},{48,80},{64,96},{80,112},{96,0},{112,16},{1... | collective-permute-start | bytes 1966088 | tf_op jit(solution)/shard_map/ppermute | solution.py:51
  52.7 7.7 %copy-start.11 = (bf16[1,128,2560]{1,2,0:T(8,128)(2,1)S(1)}, bf16[1,128,2560]{1,2,0:T(8,128)(2,1)}, u32[]{:S(2)}) copy-start(bf16[1,128,2560]{1,2,0:T(8,128)(2,1)} %copy.100) | copy-start | bytes 1966084
  52.7 27.4 %collective-permute-start.6 = (bf16[4,2,320,512]{3,2,1,0:T(8,128)(2,1)S(1)}, bf16[4,2,320,512]{3,2,1,0:T(8,128)(2,1)}, u32[]{:S(2)}, u32[]{:S(2)}) collective-permute-start(bf16[4,2,320,512]{3,2,1,0:T(8,128)(2,1)S(1)} %pad_maximum_fusion.1), channel_id=1, source_target_pairs={{0,16},{16,0},{32,48},{48,32},{64,80},{80,64},{96,112},{112,96},{1... | collective-permute-start | bytes 7864328 | tf_op jit(solution)/shard_map/ppermute | solution.py:53
  53.0 27.1 %all-to-all-start = ((bf16[16,128,320]{1,2,0:T(8,128)(2,1)}), bf16[16,128,320]{1,2,0:T(8,128)(2,1)}, u32[]{:S(2)}, u32[]{:S(2)}) async-start(bf16[16,128,320]{1,2,0:T(8,128)(2,1)} %bitcast.8), calls=%async_computation | async-start | bytes 2621440 | tf_op jit(solution)/shard_map/all_to_all | solution.py:69
  71.9 35.7 %copy-start.38 = (f32[5,128]{1,0:T(8,128)}, f32[5,128]{1,0:T(8,128)S(1)}, u32[]{:S(2)}) copy-start(f32[5,128]{1,0:T(8,128)S(1)} %get-tuple-element.44) | copy-start | bytes 7684
  82.5 9.5 %copy-start.20 = (s32[16]{0:T(128)S(1)}, s32[16]{0:T(128)}, u32[]{:S(2)}) copy-start(s32[16]{0:T(128)} %copy-done.19) | copy-start | bytes 196
  84.8 17.8 %copy-start.13 = (bf16[1,128,2560]{1,2,0:T(8,128)(2,1)S(1)}, bf16[1,128,2560]{1,2,0:T(8,128)(2,1)}, u32[]{:S(2)}) copy-start(bf16[1,128,2560]{1,2,0:T(8,128)(2,1)} %copy.102) | copy-start | bytes 1966084
  84.8 11.5 %collective-permute-start.8 = (bf16[128,1024]{1,0:T(8,128)(2,1)S(1)}, bf16[128,1024]{1,0:T(8,128)(2,1)S(1)}, u32[]{:S(2)}, u32[]{:S(2)}) collective-permute-start(bf16[128,1024]{1,0:T(8,128)(2,1)S(1)} %get-tuple-element.39), channel_id=1, source_target_pairs={{1,0},{2,1},{3,2},{4,3},{5,4},{6,5},{7,6},{8,7},{9,8},{10,9},{11,1... | collective-permute-start | bytes 786440 | tf_op jit(solution)/shard_map/ppermute | solution.py:82
  88.0 13.9 %collective-permute-start.7 = (bf16[128,1024]{1,0:T(8,128)(2,1)S(1)}, bf16[128,1024]{1,0:T(8,128)(2,1)S(1)}, u32[]{:S(2)}, u32[]{:S(2)}) collective-permute-start(bf16[128,1024]{1,0:T(8,128)(2,1)S(1)} %get-tuple-element.38), channel_id=1, source_target_pairs={{0,1},{1,2},{2,3},{3,4},{4,5},{5,6},{6,7},{7,8},{8,9},{9,10},{10,1... | collective-permute-start | bytes 786440 | tf_op jit(solution)/shard_map/ppermute | solution.py:82
  110.7 11.8 %copy-start.41 = (f32[5,128]{1,0:T(8,128)}, f32[5,128]{1,0:T(8,128)S(1)}, u32[]{:S(2)}) copy-start(f32[5,128]{1,0:T(8,128)S(1)} %get-tuple-element.54) | copy-start | bytes 7684
  112.6 5.3 %copy-start.47 = (f32[5,128]{1,0:T(8,128)S(1)}, f32[5,128]{1,0:T(8,128)}, u32[]{:S(2)}) copy-start(f32[5,128]{1,0:T(8,128)} %get-tuple-element.48) | copy-start | bytes 7684
  112.6 36.4 %all-to-all-start.1 = ((bf16[16,128,512]{1,2,0:T(8,128)(2,1)}), bf16[16,128,512]{1,2,0:T(8,128)(2,1)S(1)}, u32[]{:S(2)}, u32[]{:S(2)}) async-start(bf16[16,128,512]{1,2,0:T(8,128)(2,1)} %broadcast_in_dim.114), calls=%async_computation.1 | async-start | bytes 4194304 | tf_op jit(solution)/shard_map/all_to_all | solution.py:69
  131.7 40.7 %collective-permute-start.10 = (bf16[128,512]{0,1:T(8,128)(2,1)}, bf16[128,512]{0,1:T(8,128)(2,1)S(1)}, u32[]{:S(2)}, u32[]{:S(2)}) collective-permute-start(bf16[128,512]{0,1:T(8,128)(2,1)} %get-tuple-element.31), channel_id=1, source_target_pairs={{0,1},{1,2},{2,3},{3,4},{4,5},{5,6},{6,7},{7,8},{8,9},{9,10},{10,1... | collective-permute-start | bytes 393224 | tf_op jit(solution)/shard_map/ppermute | solution.py:82
  135.3 37.1 %collective-permute-start.9 = (bf16[128,512]{0,1:T(8,128)(2,1)}, bf16[128,512]{0,1:T(8,128)(2,1)}, u32[]{:S(2)}, u32[]{:S(2)}) collective-permute-start(bf16[128,512]{0,1:T(8,128)(2,1)} %get-tuple-element.30), channel_id=1, source_target_pairs={{1,0},{2,1},{3,2},{4,3},{5,4},{6,5},{7,6},{8,7},{9,8},{10,9},{11,1... | collective-permute-start | bytes 393224 | tf_op jit(solution)/shard_map/ppermute | solution.py:82
  152.3 27.3 %all-to-all-start.2 = ((bf16[16,32,320]{2,1,0:T(8,128)(2,1)}), bf16[16,32,320]{2,1,0:T(8,128)(2,1)S(1)}, u32[]{:S(2)}, u32[]{:S(2)}) async-start(bf16[16,32,320]{2,1,0:T(8,128)(2,1)} %fusion.29), calls=%async_computation.2 | async-start | bytes 786432 | tf_op jit(solution)/shard_map/all_to_all | solution.py:69
  (38 other events, 78.6 us)

commit v18 on v14

--- a/solution.py
+++ b/solution.py
@@ -42,13 +42,17 @@
         for s in range(seq_count)
     ]
     held = jnp.stack([weight, lax.ppermute(weight, ("dp", "seq"), partner_pairs)])
-    ring = [held]
-    for shift in range(1, y_count):
+    def shifted(array, shift):
         pairs = []
         for d in range(dp_count):
             upper, y_here, core = d // half, (d // cores) % y_count, d % cores
             pairs.append((d, upper * half + ((y_here + shift) % y_count) * cores + core))
-        ring.append(lax.ppermute(held, "dp", pairs))
+        return lax.ppermute(array, "dp", pairs)
+
+    from_before = shifted(held, 1)
+    from_after = shifted(held, y_count - 1)
+    two_away = jnp.stack([shifted(from_before[0], 1), shifted(from_after[1], y_count - 1)])
+    ring = [held, from_before, two_away, from_after]
     mine, ready, riders = lax.optimization_barrier((jnp.stack(ring), ready, riders))
     sibling = lax.ppermute(mine, "dp", [(d, d ^ 1) for d in range(dp_count)])
     stacked = jnp.stack([mine, sibling]).reshape(dp_count, rows, width)

time: 171 us -> 165 us (0.965)
  waiting for transfers between devices: 58.4 us -> 51 us
    ppermute x3 -> x4, waiting for transfers between devices: 26.8 us -> 18.7 us  [shifted(): return lax.ppermute(array, 'dp', pairs)]
    ppermute x3 -> x4, starting transfers between devices: 2.89 us -> 4.3 us  [shifted(): return lax.ppermute(array, 'dp', pairs)]
    unnamed x49 -> x59, local copies, waits for them, and re-layouts: 11.1 us -> 10.6 us
  transfers between devices with their start and end apart: 16 -> 17, of which waited for: 9 -> 9; matrix products, arithmetic and copies ran while one was open for 25% -> 26% of each run, Pallas kernels for 0% -> 0%
where the time goes in v18:
time: 165 us; the launch traced here: 164 us
  starting transfers between devices  54.4 us (33%)
  waiting for transfers between devices  51 us (31%)
  matrix products  29.1 us (18%)
  local copies, waits for them, and re-layouts  16.9 us (10%)
  other arithmetic  11.5 us (7%)
    all_to_all x3, starting transfers between devices, gathered_copies(): return lax.all_to_all(copies, axis, 0, 0, tiled=True)  24.7 us
    all_to_all x3, waiting for transfers between devices, gathered_copies(): return lax.all_to_all(copies, axis, 0, 0, tiled=True)  19.2 us
    ppermute x4, waiting for transfers between devices, shifted(): return lax.ppermute(array, 'dp', pairs)  18.7 us
    ppermute x4, starting transfers between devices, passed_along(): return lax.ppermute(array, axis, pairs)  13.5 us
    unnamed x59, local copies, waits for them, and re-layouts  10.6 us
    ppermute x2, starting transfers between devices, with_halo(): lax.ppermute(tail, axis, [(i, (i + 1) % count) for i in range(ends)])  7.45 us
    ppermute x4, waiting for transfers between devices, passed_along(): return lax.ppermute(array, axis, pairs)  7.23 us
    dot_general x4, matrix products, attend_first(): jnp.einsum('gqk,qgd->kd', attention_low, grad_head, preferred_element_typ...  6.74 us
  transfers between devices with their start and end apart: 17, of which 9 were waited for; matrix products, arithmetic and copies ran while one was open for 26% of the time, Pallas kernels for 0%

profile of v18, /device:TPU:26, one launch (start us, length us, event | category | flops | bytes accessed | tf_op | source)
XLA Modules:
  0.0 164.1 jit_solution(11444414226212533454)
XLA Ops:
  1.8 3.8 %collective-permute-start.5 = (bf16[128,512]{0,1:T(8,128)(2,1)S(1)}, bf16[128,512]{0,1:T(8,128)(2,1)S(1)}, u32[]{:S(2)}, u32[]{:S(2)}) collective-permute-start(bf16[128,512]{0,1:T(8,128)(2,1)S(1)} %bitcast.334), channel_id=1, source_target_pairs={{0,1},{1,2},{2,3},{3,4},{4,5},{5,6},{6,7},{7,8},{8,9},{9,10},{10,1... | collective-permute-start | bytes 393224 | tf_op jit(solution)/shard_map/ppermute | solution.py:17
  5.6 2.0 %collective-permute-start.6 = (bf16[128,512]{0,1:T(8,128)(2,1)S(1)}, bf16[128,512]{0,1:T(8,128)(2,1)}, u32[]{:S(2)}, u32[]{:S(2)}) collective-permute-start(bf16[128,512]{0,1:T(8,128)(2,1)S(1)} %bitcast.335), channel_id=1, source_target_pairs={{1,0},{2,1},{3,2},{4,3},{5,4},{6,5},{7,6},{8,7},{9,8},{10,9},{11,1... | collective-permute-start | bytes 393224 | tf_op jit(solution)/shard_map/ppermute | solution.py:19
  7.8 2.5 %copy.90 = bf16[1,128,5120]{1,2,0:T(8,128)(2,1)} copy(bf16[1,128,5120]{2,1,0:T(8,128)(2,1)} %param.7) | data formatting | bytes 2621440 | tf_op args[0]
  11.1 5.9 %collective-permute-done = bf16[320,512]{1,0:T(8,128)(2,1)S(1)} collective-permute-done((bf16[320,512]{1,0:T(8,128)(2,1)}, bf16[320,512]{1,0:T(8,128)(2,1)S(1)}, u32[]{:S(2)}, u32[]{:S(2)}) %collective-permute-start) | collective-permute-done | bytes 327712 | tf_op jit(solution)/shard_map/ppermute | solution.py:44
  20.2 12.1 %collective-permute-done.1 = bf16[2,320,512]{2,1,0:T(8,128)(2,1)S(1)} collective-permute-done((bf16[2,320,512]{2,1,0:T(8,128)(2,1)S(1)}, bf16[2,320,512]{2,1,0:T(8,128)(2,1)S(1)}, u32[]{:S(2)}, u32[]{:S(2)}) %collective-permute-start.1) | collective-permute-done | bytes 655392 | tf_op jit(solution)/shard_map/ppermute | solution.py:50
  35.7 3.9 %collective-permute-done.2 = bf16[320,512]{1,0:T(8,128)(2,1)S(1)} collective-permute-done((bf16[320,512]{1,0:T(8,128)(2,1)S(1)}, bf16[320,512]{1,0:T(8,128)(2,1)S(1)}, u32[]{:S(2)}, u32[]{:S(2)}) %collective-permute-start.2) | collective-permute-done | bytes 327712 | tf_op jit(solution)/shard_map/ppermute | solution.py:50
  39.6 2.7 %collective-permute-done.4 = bf16[320,512]{1,0:T(8,128)(2,1)S(1)} collective-permute-done((bf16[320,512]{1,0:T(8,128)(2,1)S(1)}, bf16[320,512]{1,0:T(8,128)(2,1)S(1)}, u32[]{:S(2)}, u32[]{:S(2)}) %collective-permute-start.4) | collective-permute-done | bytes 327712 | tf_op jit(solution)/shard_map/ppermute | solution.py:50
  44.2 7.8 %all-to-all-start = ((bf16[16,128,320]{1,2,0:T(8,128)(2,1)}), bf16[16,128,320]{1,2,0:T(8,128)(2,1)S(1)}, u32[]{:S(2)}, u32[]{:S(2)}) async-start(bf16[16,128,320]{1,2,0:T(8,128)(2,1)} %bitcast.12), calls=%async_computation | async-start | bytes 2621440 | tf_op jit(solution)/shard_map/all_to_all | solution.py:73
  59.7 2.2 %convolution_bitcast_fusion.5 = f32[384,128]{0,1:T(8,128)} fusion(bf16[128,4,5,128]{0,3,2,1:T(8,128)(2,1)S(1)} %bitcast.328, f32[5,128,384]{1,2,0:T(8,128)} %get-tuple-element.45, f32[5,128]{1,0:T(8,128)S(1)} %get-tuple-element.44), kind=kOutput, calls=%fused_computation.53 | convolution fusion | flops 63406080 | bytes 1347584 | tf_op jit(solution)/shard_map/gqk,qgd->kd/dot_general | solution.py:120
  65.0 6.5 %all-to-all-done = bf16[16,128,320]{1,2,0:T(8,128)(2,1)S(1)} async-done(((bf16[16,128,320]{1,2,0:T(8,128)(2,1)}), bf16[16,128,320]{1,2,0:T(8,128)(2,1)S(1)}, u32[]{:S(2)}, u32[]{:S(2)}) %all-to-all-start) | async-done | bytes 1310752 | tf_op jit(solution)/shard_map/all_to_all | solution.py:73
  71.6 1.9 %collective-permute-start.7 = (bf16[128,512]{0,1:T(8,128)(2,1)S(1)}, bf16[128,512]{0,1:T(8,128)(2,1)S(1)}, u32[]{:S(2)}, u32[]{:S(2)}) collective-permute-start(bf16[128,512]{0,1:T(8,128)(2,1)S(1)} %get-tuple-element.40), channel_id=1, source_target_pairs={{1,0},{2,1},{3,2},{4,3},{5,4},{6,5},{7,6},{8,7},{9,8},{10,9},{11,1... | collective-permute-start | bytes 393224 | tf_op jit(solution)/shard_map/ppermute | solution.py:86
  73.5 4.8 %collective-permute-start.8 = (bf16[128,512]{0,1:T(8,128)(2,1)S(1)}, bf16[128,512]{0,1:T(8,128)(2,1)S(1)}, u32[]{:S(2)}, u32[]{:S(2)}) collective-permute-start(bf16[128,512]{0,1:T(8,128)(2,1)S(1)} %get-tuple-element.41), channel_id=1, source_target_pairs={{0,1},{1,2},{2,3},{3,4},{4,5},{5,6},{6,7},{7,8},{8,9},{9,10},{10,1... | collective-permute-start | bytes 393224 | tf_op jit(solution)/shard_map/ppermute | solution.py:86
  79.6 2.1 %gather_fusion = bf16[16,128,320]{1,2,0:T(8,128)(2,1)S(1)} fusion(bf16[128,16,320]{0,2,1:T(8,128)(2,1)} %bitcast.11, s32[1024]{0:T(1024)S(1)} %pad_clamp_fusion.1), kind=kCustom, calls=%fused_computation | custom fusion | bytes 2621504 | tf_op jit(solution)/shard_map/jit(_take)/gather | solution.py:208
  82.9 3.0 %pad_maximum_fusion = bf16[2,4,2,320,512]{4,3,2,1,0:T(8,128)(2,1)S(1)} fusion(bf16[1,4,2,320,512]{4,3,2,1,0:T(8,128)(2,1)} %bitcast.46, bf16[1,4,2,320,512]{4,3,2,1,0:T(8,128)(2,1)} %bitcast.45), kind=kLoop, calls=%fused_computation.7 | loop fusion | flops 2621440 | bytes 10485760 | tf_op jit(solution)/shard_map/stack | solution.py:58
  88.3 3.6 %collective-permute-start.10 = (bf16[128,512]{1,0:T(8,128)(2,1)S(1)}, bf16[128,512]{1,0:T(8,128)(2,1)S(1)}, u32[]{:S(2)}, u32[]{:S(2)}) collective-permute-start(bf16[128,512]{1,0:T(8,128)(2,1)S(1)} %fusion.41), channel_id=1, source_target_pairs={{0,1},{1,2},{2,3},{3,4},{4,5},{5,6},{6,7},{7,8},{8,9},{9,10},{10,1... | collective-permute-start | bytes 393224 | tf_op jit(solution)/shard_map/ppermute | solution.py:17
  91.9 2.2 %collective-permute-start.11 = (bf16[128,512]{1,0:T(8,128)(2,1)S(1)}, bf16[128,512]{1,0:T(8,128)(2,1)}, u32[]{:S(2)}, u32[]{:S(2)}) collective-permute-start(bf16[128,512]{1,0:T(8,128)(2,1)S(1)} %fusion.41), channel_id=1, source_target_pairs={{1,0},{2,1},{3,2},{4,3},{5,4},{6,5},{7,6},{8,7},{9,8},{10,9},{11,1... | collective-permute-start | bytes 393224 | tf_op jit(solution)/shard_map/ppermute | solution.py:19
  95.9 4.9 %all-to-all-start.1 = ((bf16[16,128,512]{1,2,0:T(8,128)(2,1)}), bf16[16,128,512]{1,2,0:T(8,128)(2,1)}, u32[]{:S(2)}, u32[]{:S(2)}) async-start(bf16[16,128,512]{1,2,0:T(8,128)(2,1)} %broadcast_in_dim.114), calls=%async_computation.1 | async-start | bytes 4194304 | tf_op jit(solution)/shard_map/all_to_all | solution.py:73
  100.8 4.3 %convolution_convert_fusion = bf16[128,5120]{1,0:T(8,128)(2,1)S(1)} fusion(bf16[128,512]{0,1:T(8,128)(2,1)S(1)} %add_convert_fusion, bf16[5120,512]{1,0:T(8,128)(2,1)} %bitcast.312), kind=kOutput, calls=%fused_computation.6 | convolution fusion | flops 671744000 | bytes 6684672 | tf_op jit(solution)/shard_map/dot_general | solution.py:217
  119.3 12.7 %all-to-all-done.1 = bf16[16,128,512]{1,2,0:T(8,128)(2,1)} async-done(((bf16[16,128,512]{1,2,0:T(8,128)(2,1)}), bf16[16,128,512]{1,2,0:T(8,128)(2,1)}, u32[]{:S(2)}, u32[]{:S(2)}) %all-to-all-start.1) | async-done | bytes 2097184 | tf_op jit(solution)/shard_map/all_to_all | solution.py:73
  132.0 3.6 %fusion.31 = bf16[16,32,320]{2,1,0:T(8,128)(2,1)} fusion(bf16[16,128,16,32]{1,3,2,0:T(8,128)(2,1)} %bitcast.82, bf16[16,128,320]{1,2,0:T(8,128)(2,1)S(1)} %copy-done.2), kind=kOutput, calls=%fused_computation.42 | convolution fusion | flops 671252480 | bytes 3735552 | tf_op jit(solution)/shard_map/rtk,rtjc->jck/dot_general | solution.py:202
  135.6 12.0 %all-to-all-start.2 = ((bf16[16,32,320]{2,1,0:T(8,128)(2,1)}), bf16[16,32,320]{2,1,0:T(8,128)(2,1)S(1)}, u32[]{:S(2)}, u32[]{:S(2)}) async-start(bf16[16,32,320]{2,1,0:T(8,128)(2,1)} %fusion.31), calls=%async_computation.2 | async-start | bytes 786432 | tf_op jit(solution)/shard_map/all_to_all | solution.py:73
  147.6 2.0 %collective-permute-start.12 = (bf16[128,512]{0,1:T(8,128)(2,1)S(1)}, bf16[128,512]{0,1:T(8,128)(2,1)S(1)}, u32[]{:S(2)}, u32[]{:S(2)}) collective-permute-start(bf16[128,512]{0,1:T(8,128)(2,1)S(1)} %get-tuple-element.34), channel_id=1, source_target_pairs={{1,0},{2,1},{3,2},{4,3},{5,4},{6,5},{7,6},{8,7},{9,8},{10,9},{11,1... | collective-permute-start | bytes 393224 | tf_op jit(solution)/shard_map/ppermute | solution.py:86
  149.6 4.7 %collective-permute-start.13 = (bf16[128,512]{0,1:T(8,128)(2,1)S(1)}, bf16[128,512]{0,1:T(8,128)(2,1)S(1)}, u32[]{:S(2)}, u32[]{:S(2)}) collective-permute-start(bf16[128,512]{0,1:T(8,128)(2,1)S(1)} %get-tuple-element.35), channel_id=1, source_target_pairs={{0,1},{1,2},{2,3},{3,4},{4,5},{5,6},{6,7},{7,8},{8,9},{9,10},{10,1... | collective-permute-start | bytes 393224 | tf_op jit(solution)/shard_map/ppermute | solution.py:86
  156.5 5.3 %collective-permute-done.12 = bf16[128,512]{0,1:T(8,128)(2,1)S(1)} collective-permute-done((bf16[128,512]{0,1:T(8,128)(2,1)S(1)}, bf16[128,512]{0,1:T(8,128)(2,1)S(1)}, u32[]{:S(2)}, u32[]{:S(2)}) %collective-permute-start.12) | collective-permute-done | bytes 131104 | tf_op jit(solution)/shard_map/ppermute | solution.py:86
  (133 shorter events, 46.2 us)
Async XLA Ops:
  0.6 9.6 %copy-start.3 = (bf16[1,128,2560]{2,1,0:T(8,128)(2,1)S(1)}, bf16[1,128,2560]{2,1,0:T(8,128)(2,1)}, u32[]{:S(2)}) copy-start(bf16[1,128,2560]{2,1,0:T(8,128)(2,1)} %param.8) | copy-start | bytes 1966084
  0.6 9.9 %copy-start.4 = (bf16[1,128,2560]{2,1,0:T(8,128)(2,1)S(1)}, bf16[1,128,2560]{2,1,0:T(8,128)(2,1)}, u32[]{:S(2)}) copy-start(bf16[1,128,2560]{2,1,0:T(8,128)(2,1)} %param.10) | copy-start | bytes 1966084
  1.8 32.9 %collective-permute-start.5 = (bf16[128,512]{0,1:T(8,128)(2,1)S(1)}, bf16[128,512]{0,1:T(8,128)(2,1)S(1)}, u32[]{:S(2)}, u32[]{:S(2)}) collective-permute-start(bf16[128,512]{0,1:T(8,128)(2,1)S(1)} %bitcast.334), channel_id=1, source_target_pairs={{0,1},{1,2},{2,3},{3,4},{4,5},{5,6},{6,7},{7,8},{8,9},{9,10},{10,1... | collective-permute-start | bytes 393224 | tf_op jit(solution)/shard_map/ppermute | solution.py:17
  5.6 29.1 %collective-permute-start.6 = (bf16[128,512]{0,1:T(8,128)(2,1)S(1)}, bf16[128,512]{0,1:T(8,128)(2,1)}, u32[]{:S(2)}, u32[]{:S(2)}) collective-permute-start(bf16[128,512]{0,1:T(8,128)(2,1)S(1)} %bitcast.335), channel_id=1, source_target_pairs={{1,0},{2,1},{3,2},{4,3},{5,4},{6,5},{7,6},{8,7},{9,8},{10,9},{11,1... | collective-permute-start | bytes 393224 | tf_op jit(solution)/shard_map/ppermute | solution.py:19
  7.6 9.3 %collective-permute-start = (bf16[320,512]{1,0:T(8,128)(2,1)}, bf16[320,512]{1,0:T(8,128)(2,1)S(1)}, u32[]{:S(2)}, u32[]{:S(2)}) collective-permute-start(bf16[320,512]{1,0:T(8,128)(2,1)} %param.11), channel_id=1, source_target_pairs={{0,129},{1,128},{2,131},{3,130},{4,133},{5,132},{6,135},{7,134},{8... | collective-permute-start | bytes 983048 | tf_op jit(solution)/shard_map/ppermute | solution.py:44
  7.8 9.2 %copy-start.9 = (bf16[320,512]{1,0:T(8,128)(2,1)S(1)}, bf16[320,512]{1,0:T(8,128)(2,1)}, u32[]{:S(2)}) copy-start(bf16[320,512]{1,0:T(8,128)(2,1)} %param.11) | copy-start | bytes 983044
  10.9 52.5 %copy-start.5 = (bf16[1,128,2560]{1,2,0:T(8,128)(2,1)}, bf16[1,128,2560]{1,2,0:T(8,128)(2,1)S(1)}, u32[]{:S(2)}) copy-start(bf16[1,128,2560]{1,2,0:T(8,128)(2,1)S(1)} %copy.94) | copy-start | bytes 1966084
  17.1 15.2 %collective-permute-start.1 = (bf16[2,320,512]{2,1,0:T(8,128)(2,1)S(1)}, bf16[2,320,512]{2,1,0:T(8,128)(2,1)S(1)}, u32[]{:S(2)}, u32[]{:S(2)}) collective-permute-start(bf16[2,320,512]{2,1,0:T(8,128)(2,1)S(1)} %get-tuple-element.33), channel_id=1, source_target_pairs={{0,32},{16,48},{32,64},{48,80},{64,96},{80,112},{96,0},{112,16},{1... | collective-permute-start | bytes 1966088 | tf_op jit(solution)/shard_map/ppermute | solution.py:50
  17.5 16.4 %collective-permute-start.3 = (bf16[2,320,512]{2,1,0:T(8,128)(2,1)S(1)}, bf16[2,320,512]{2,1,0:T(8,128)(2,1)S(1)}, u32[]{:S(2)}, u32[]{:S(2)}) collective-permute-start(bf16[2,320,512]{2,1,0:T(8,128)(2,1)S(1)} %get-tuple-element.33), channel_id=1, source_target_pairs={{0,96},{16,112},{32,0},{48,16},{64,32},{80,48},{96,64},{112,80},{1... | collective-permute-start | bytes 1966088 | tf_op jit(solution)/shard_map/ppermute | solution.py:50
  32.3 7.3 %collective-permute-start.2 = (bf16[320,512]{1,0:T(8,128)(2,1)S(1)}, bf16[320,512]{1,0:T(8,128)(2,1)S(1)}, u32[]{:S(2)}, u32[]{:S(2)}) collective-permute-start(bf16[320,512]{1,0:T(8,128)(2,1)S(1)} %slice_bitcast_fusion.1), channel_id=1, source_target_pairs={{0,32},{16,48},{32,64},{48,80},{64,96},{80,112},{96,0},{112,16},{1... | collective-permute-start | bytes 983048 | tf_op jit(solution)/shard_map/ppermute | solution.py:50
  33.9 8.4 %collective-permute-start.4 = (bf16[320,512]{1,0:T(8,128)(2,1)S(1)}, bf16[320,512]{1,0:T(8,128)(2,1)S(1)}, u32[]{:S(2)}, u32[]{:S(2)}) collective-permute-start(bf16[320,512]{1,0:T(8,128)(2,1)S(1)} %slice_bitcast_fusion), channel_id=1, source_target_pairs={{0,96},{16,112},{32,0},{48,16},{64,32},{80,48},{96,64},{112,80},{1... | collective-permute-start | bytes 983048 | tf_op jit(solution)/shard_map/ppermute | solution.py:50
  34.7 20.5 %copy-start.11 = (pred[128,384]{0,1:T(8,128)(4,1)}, pred[128,384]{0,1:T(8,128)(4,1)S(1)}, u32[]{:S(2)}) copy-start(pred[128,384]{0,1:T(8,128)(4,1)S(1)} %or_and_fusion) | copy-start | bytes 147460
  35.7 26.2 %copy-start.7 = (bf16[384,512]{0,1:T(8,128)(2,1)}, bf16[384,512]{0,1:T(8,128)(2,1)S(1)}, u32[]{:S(2)}) copy-start(bf16[384,512]{0,1:T(8,128)(2,1)S(1)} %pad_maximum_fusion.6) | copy-start | bytes 1179652
  44.2 27.3 %all-to-all-start = ((bf16[16,128,320]{1,2,0:T(8,128)(2,1)}), bf16[16,128,320]{1,2,0:T(8,128)(2,1)S(1)}, u32[]{:S(2)}, u32[]{:S(2)}) async-start(bf16[16,128,320]{1,2,0:T(8,128)(2,1)} %bitcast.12), calls=%async_computation | async-start | bytes 2621440 | tf_op jit(solution)/shard_map/all_to_all | solution.py:73
  52.0 31.0 %collective-permute-start.9 = (bf16[4,2,320,512]{3,2,1,0:T(8,128)(2,1)}, bf16[4,2,320,512]{3,2,1,0:T(8,128)(2,1)}, u32[]{:S(2)}, u32[]{:S(2)}) collective-permute-start(bf16[4,2,320,512]{3,2,1,0:T(8,128)(2,1)} %pad_maximum_fusion.1), channel_id=1, source_target_pairs={{0,16},{16,0},{32,48},{48,32},{64,80},{80,64},{96,112},{112,96},{1... | collective-permute-start | bytes 7864328 | tf_op jit(solution)/shard_map/ppermute | solution.py:57
  71.6 10.2 %collective-permute-start.7 = (bf16[128,512]{0,1:T(8,128)(2,1)S(1)}, bf16[128,512]{0,1:T(8,128)(2,1)S(1)}, u32[]{:S(2)}, u32[]{:S(2)}) collective-permute-start(bf16[128,512]{0,1:T(8,128)(2,1)S(1)} %get-tuple-element.40), channel_id=1, source_target_pairs={{1,0},{2,1},{3,2},{4,3},{5,4},{6,5},{7,6},{8,7},{9,8},{10,9},{11,1... | collective-permute-start | bytes 393224 | tf_op jit(solution)/shard_map/ppermute | solution.py:86
  73.5 9.4 %collective-permute-start.8 = (bf16[128,512]{0,1:T(8,128)(2,1)S(1)}, bf16[128,512]{0,1:T(8,128)(2,1)S(1)}, u32[]{:S(2)}, u32[]{:S(2)}) collective-permute-start(bf16[128,512]{0,1:T(8,128)(2,1)S(1)} %get-tuple-element.41), channel_id=1, source_target_pairs={{0,1},{1,2},{2,3},{3,4},{4,5},{5,6},{6,7},{7,8},{8,9},{9,10},{10,1... | collective-permute-start | bytes 393224 | tf_op jit(solution)/shard_map/ppermute | solution.py:86
  88.3 19.9 %collective-permute-start.10 = (bf16[128,512]{1,0:T(8,128)(2,1)S(1)}, bf16[128,512]{1,0:T(8,128)(2,1)S(1)}, u32[]{:S(2)}, u32[]{:S(2)}) collective-permute-start(bf16[128,512]{1,0:T(8,128)(2,1)S(1)} %fusion.41), channel_id=1, source_target_pairs={{0,1},{1,2},{2,3},{3,4},{4,5},{5,6},{6,7},{7,8},{8,9},{9,10},{10,1... | collective-permute-start | bytes 393224 | tf_op jit(solution)/shard_map/ppermute | solution.py:17
  91.9 16.3 %collective-permute-start.11 = (bf16[128,512]{1,0:T(8,128)(2,1)S(1)}, bf16[128,512]{1,0:T(8,128)(2,1)}, u32[]{:S(2)}, u32[]{:S(2)}) collective-permute-start(bf16[128,512]{1,0:T(8,128)(2,1)S(1)} %fusion.41), channel_id=1, source_target_pairs={{1,0},{2,1},{3,2},{4,3},{5,4},{6,5},{7,6},{8,7},{9,8},{10,9},{11,1... | collective-permute-start | bytes 393224 | tf_op jit(solution)/shard_map/ppermute | solution.py:19
  95.9 36.1 %all-to-all-start.1 = ((bf16[16,128,512]{1,2,0:T(8,128)(2,1)}), bf16[16,128,512]{1,2,0:T(8,128)(2,1)}, u32[]{:S(2)}, u32[]{:S(2)}) async-start(bf16[16,128,512]{1,2,0:T(8,128)(2,1)} %broadcast_in_dim.114), calls=%async_computation.1 | async-start | bytes 4194304 | tf_op jit(solution)/shard_map/all_to_all | solution.py:73
  117.9 14.1 %copy-start.2 = (bf16[16,128,320]{1,2,0:T(8,128)(2,1)S(1)}, bf16[16,128,320]{1,2,0:T(8,128)(2,1)}, u32[]{:S(2)}) copy-start(bf16[16,128,320]{1,2,0:T(8,128)(2,1)} %copy-done.1) | copy-start | bytes 3932164
  135.6 27.8 %all-to-all-start.2 = ((bf16[16,32,320]{2,1,0:T(8,128)(2,1)}), bf16[16,32,320]{2,1,0:T(8,128)(2,1)S(1)}, u32[]{:S(2)}, u32[]{:S(2)}) async-start(bf16[16,32,320]{2,1,0:T(8,128)(2,1)} %fusion.31), calls=%async_computation.2 | async-start | bytes 786432 | tf_op jit(solution)/shard_map/all_to_all | solution.py:73
  147.6 14.3 %collective-permute-start.12 = (bf16[128,512]{0,1:T(8,128)(2,1)S(1)}, bf16[128,512]{0,1:T(8,128)(2,1)S(1)}, u32[]{:S(2)}, u32[]{:S(2)}) collective-permute-start(bf16[128,512]{0,1:T(8,128)(2,1)S(1)} %get-tuple-element.34), channel_id=1, source_target_pairs={{1,0},{2,1},{3,2},{4,3},{5,4},{6,5},{7,6},{8,7},{9,8},{10,9},{11,1... | collective-permute-start | bytes 393224 | tf_op jit(solution)/shard_map/ppermute | solution.py:86
  149.6 13.0 %collective-permute-start.13 = (bf16[128,512]{0,1:T(8,128)(2,1)S(1)}, bf16[128,512]{0,1:T(8,128)(2,1)S(1)}, u32[]{:S(2)}, u32[]{:S(2)}) collective-permute-start(bf16[128,512]{0,1:T(8,128)(2,1)S(1)} %get-tuple-element.35), channel_id=1, source_target_pairs={{0,1},{1,2},{2,3},{3,4},{4,5},{5,6},{6,7},{7,8},{8,9},{9,10},{10,1... | collective-permute-start | bytes 393224 | tf_op jit(solution)/shard_map/ppermute | solution.py:86
  (19 other events, 46.1 us)

commit v19 on v18

--- a/solution.py
+++ b/solution.py
@@ -49,9 +49,11 @@
             pairs.append((d, upper * half + ((y_here + shift) % y_count) * cores + core))
         return lax.ppermute(array, "dp", pairs)
 
-    from_before = shifted(held, 1)
-    from_after = shifted(held, y_count - 1)
-    two_away = jnp.stack([shifted(from_before[0], 1), shifted(from_after[1], y_count - 1)])
+    before_own = shifted(held[0], 1)
+    after_partner = shifted(held[1], y_count - 1)
+    two_away = jnp.stack([shifted(before_own, 1), shifted(after_partner, y_count - 1)])
+    from_before = jnp.stack([before_own, shifted(held[1], 1)])
+    from_after = jnp.stack([shifted(held[0], y_count - 1), after_partner])
     ring = [held, from_before, two_away, from_after]
     mine, ready, riders = lax.optimization_barrier((jnp.stack(ring), ready, riders))
     sibling = lax.ppermute(mine, "dp", [(d, d ^ 1) for d in range(dp_count)])

time: 165 us -> 158 us (0.958)
  waiting for transfers between devices: 51 us -> 36.9 us
  starting transfers between devices: 54.4 us -> 57.6 us
  other arithmetic: 11.5 us -> 13.5 us
    ppermute x4 -> x6, waiting for transfers between devices: 18.7 us -> 9.22 us  [shifted(): return lax.ppermute(array, 'dp', pairs)]
    ppermute x1, waiting for transfers between devices: 5.9 us -> 0.01 us  [spread_weight(): lax.ppermute(weight, ('dp', 'seq'), partner_pairs)]
    all_to_all x3, starting transfers between devices: 24.7 us -> 20.1 us  [gathered_copies(): return lax.all_to_all(copies, axis, 0, 0, tiled=True)]
    ppermute x4 -> x6, starting transfers between devices: 4.3 us -> 8.56 us  [shifted(): return lax.ppermute(array, 'dp', pairs)]
    another operation x3 -> x5, other arithmetic: 1.98 us -> 5.2 us  [spread_weight(): jnp.stack(ring)]
    ppermute x4, waiting for transfers between devices: 7.23 us -> 9.73 us  [passed_along(): return lax.ppermute(array, axis, pairs)]
    unnamed x59 -> x41, local copies, waits for them, and re-layouts: 10.6 us -> 10.4 us
  transfers between devices with their start and end apart: 17 -> 19, of which waited for: 9 -> 8; matrix products, arithmetic and copies ran while one was open for 26% -> 31% of each run, Pallas kernels for 0% -> 0%
where the time goes in v19:
time: 158 us; the launch traced here: 157 us
  starting transfers between devices  57.6 us (36%)
  waiting for transfers between devices  36.9 us (23%)
  matrix products  30.3 us (19%)
  local copies, waits for them, and re-layouts  17.4 us (11%)
  other arithmetic  13.5 us (9%)
    all_to_all x3, starting transfers between devices, gathered_copies(): return lax.all_to_all(copies, axis, 0, 0, tiled=True)  20.1 us
    all_to_all x3, waiting for transfers between devices, gathered_copies(): return lax.all_to_all(copies, axis, 0, 0, tiled=True)  18 us
    ppermute x4, starting transfers between devices, passed_along(): return lax.ppermute(array, axis, pairs)  13.6 us
    unnamed x41, local copies, waits for them, and re-layouts  10.4 us
    ppermute x4, waiting for transfers between devices, passed_along(): return lax.ppermute(array, axis, pairs)  9.73 us
    ppermute x6, waiting for transfers between devices, shifted(): return lax.ppermute(array, 'dp', pairs)  9.22 us
    ppermute x6, starting transfers between devices, shifted(): return lax.ppermute(array, 'dp', pairs)  8.56 us
    ppermute x2, starting transfers between devices, with_halo(): lax.ppermute(tail, axis, [(i, (i + 1) % count) for i in range(ends)])  8.27 us
  transfers between devices with their start and end apart: 19, of which 8 were waited for; matrix products, arithmetic and copies ran while one was open for 31% of the time, Pallas kernels for 0%

profile of v19, /device:TPU:26, one launch (start us, length us, event | category | flops | bytes accessed | tf_op | source)
XLA Modules:
  0.0 157.0 jit_solution(13008255022316375093)
XLA Ops:
  3.5 5.2 %collective-permute-start.7 = (bf16[128,512]{0,1:T(8,128)(2,1)S(1)}, bf16[128,512]{0,1:T(8,128)(2,1)S(1)}, u32[]{:S(2)}, u32[]{:S(2)}) collective-permute-start(bf16[128,512]{0,1:T(8,128)(2,1)S(1)} %bitcast.334), channel_id=1, source_target_pairs={{0,1},{1,2},{2,3},{3,4},{4,5},{5,6},{6,7},{7,8},{8,9},{9,10},{10,1... | collective-permute-start | bytes 393224 | tf_op jit(solution)/shard_map/ppermute | solution.py:17
  16.6 2.4 %copy.90 = bf16[1,128,5120]{1,2,0:T(8,128)(2,1)} copy(bf16[1,128,5120]{2,1,0:T(8,128)(2,1)} %param.7) | data formatting | bytes 2621440 | tf_op args[0]
  20.5 2.7 %collective-permute-start.3 = (bf16[320,512]{1,0:T(8,128)(2,1)}, bf16[320,512]{1,0:T(8,128)(2,1)S(1)}, u32[]{:S(2)}, u32[]{:S(2)}) collective-permute-start(bf16[320,512]{1,0:T(8,128)(2,1)} %collective-permute-done.1), channel_id=1, source_target_pairs={{0,32},{16,48},{32,64},{48,80},{64,96},{80,112},{96,0},{112,16},{1... | collective-permute-start | bytes 983048 | tf_op jit(solution)/shard_map/ppermute | solution.py:50
  28.3 3.6 %collective-permute-done.6 = bf16[320,512]{1,0:T(8,128)(2,1)S(1)} collective-permute-done((bf16[320,512]{1,0:T(8,128)(2,1)}, bf16[320,512]{1,0:T(8,128)(2,1)S(1)}, u32[]{:S(2)}, u32[]{:S(2)}) %collective-permute-start.6) | collective-permute-done | bytes 327712 | tf_op jit(solution)/shard_map/ppermute | solution.py:50
  32.9 4.4 %collective-permute-done.5 = bf16[320,512]{1,0:T(8,128)(2,1)S(1)} collective-permute-done((bf16[320,512]{1,0:T(8,128)(2,1)}, bf16[320,512]{1,0:T(8,128)(2,1)S(1)}, u32[]{:S(2)}, u32[]{:S(2)}) %collective-permute-start.5) | collective-permute-done | bytes 327712 | tf_op jit(solution)/shard_map/ppermute | solution.py:50
  39.3 4.5 %all-to-all-start = ((bf16[16,128,320]{1,2,0:T(8,128)(2,1)}), bf16[16,128,320]{1,2,0:T(8,128)(2,1)S(1)}, u32[]{:S(2)}, u32[]{:S(2)}) async-start(bf16[16,128,320]{1,2,0:T(8,128)(2,1)} %bitcast.14), calls=%async_computation | async-start | bytes 2621440 | tf_op jit(solution)/shard_map/all_to_all | solution.py:75
  48.5 2.2 %convolution_bitcast_fusion.6 = f32[384,128]{0,1:T(8,128)} fusion(bf16[128,4,5,128]{0,3,2,1:T(8,128)(2,1)S(1)} %bitcast.327, f32[5,128,384]{1,2,0:T(8,128)} %get-tuple-element.45, f32[5,128]{1,0:T(8,128)S(1)} %get-tuple-element.44), kind=kOutput, calls=%fused_computation.54 | convolution fusion | flops 63406080 | bytes 1347584 | tf_op jit(solution)/shard_map/gqk,qgd->kd/dot_general | solution.py:122
  52.1 2.2 %convolution_bitcast_fusion.5 = f32[384,128]{0,1:T(8,128)} fusion(bf16[128,4,5,128]{0,3,2,1:T(8,128)(2,1)S(1)} %bitcast.328, f32[5,128,384]{1,2,0:T(8,128)} %get-tuple-element.43, f32[5,128]{1,0:T(8,128)S(1)} %get-tuple-element.42), kind=kOutput, calls=%fused_computation.53 | convolution fusion | flops 63406080 | bytes 1347584 | tf_op jit(solution)/shard_map/gqk,qgd->kd/dot_general | solution.py:122
  57.5 5.9 %all-to-all-done = bf16[16,128,320]{1,2,0:T(8,128)(2,1)S(1)} async-done(((bf16[16,128,320]{1,2,0:T(8,128)(2,1)}), bf16[16,128,320]{1,2,0:T(8,128)(2,1)S(1)}, u32[]{:S(2)}, u32[]{:S(2)}) %all-to-all-start) | async-done | bytes 1310752 | tf_op jit(solution)/shard_map/all_to_all | solution.py:75
  63.4 4.8 %collective-permute-start.10 = (bf16[128,512]{0,1:T(8,128)(2,1)S(1)}, bf16[128,512]{0,1:T(8,128)(2,1)S(1)}, u32[]{:S(2)}, u32[]{:S(2)}) collective-permute-start(bf16[128,512]{0,1:T(8,128)(2,1)S(1)} %get-tuple-element.39), channel_id=1, source_target_pairs={{0,1},{1,2},{2,3},{3,4},{4,5},{5,6},{6,7},{7,8},{8,9},{9,10},{10,1... | collective-permute-start | bytes 393224 | tf_op jit(solution)/shard_map/ppermute | solution.py:88
  68.2 2.1 %collective-permute-start.9 = (bf16[128,512]{0,1:T(8,128)(2,1)S(1)}, bf16[128,512]{0,1:T(8,128)(2,1)S(1)}, u32[]{:S(2)}, u32[]{:S(2)}) collective-permute-start(bf16[128,512]{0,1:T(8,128)(2,1)S(1)} %get-tuple-element.38), channel_id=1, source_target_pairs={{1,0},{2,1},{3,2},{4,3},{5,4},{6,5},{7,6},{8,7},{9,8},{10,9},{11,1... | collective-permute-start | bytes 393224 | tf_op jit(solution)/shard_map/ppermute | solution.py:88
  71.6 2.1 %gather_fusion = bf16[16,128,320]{1,2,0:T(8,128)(2,1)S(1)} fusion(bf16[128,16,320]{0,2,1:T(8,128)(2,1)} %bitcast.13, s32[1024]{0:T(1024)S(1)} %pad_clamp_fusion.1), kind=kCustom, calls=%fused_computation | custom fusion | bytes 2621504 | tf_op jit(solution)/shard_map/jit(_take)/gather | solution.py:210
  73.7 2.7 %collective-permute-done.9 = bf16[128,512]{0,1:T(8,128)(2,1)S(1)} collective-permute-done((bf16[128,512]{0,1:T(8,128)(2,1)S(1)}, bf16[128,512]{0,1:T(8,128)(2,1)S(1)}, u32[]{:S(2)}, u32[]{:S(2)}) %collective-permute-start.9) | collective-permute-done | bytes 131104 | tf_op jit(solution)/shard_map/ppermute | solution.py:88
  76.5 3.0 %pad_maximum_fusion = bf16[2,4,2,320,512]{4,3,2,1,0:T(8,128)(2,1)S(1)} fusion(bf16[1,4,2,320,512]{4,3,2,1,0:T(8,128)(2,1)} %bitcast.48, bf16[1,4,2,320,512]{4,3,2,1,0:T(8,128)(2,1)} %bitcast.47), kind=kLoop, calls=%fused_computation.7 | loop fusion | flops 2621440 | bytes 10485760 | tf_op jit(solution)/shard_map/stack | solution.py:60
  81.8 3.1 %collective-permute-start.12 = (bf16[128,512]{1,0:T(8,128)(2,1)S(1)}, bf16[128,512]{1,0:T(8,128)(2,1)}, u32[]{:S(2)}, u32[]{:S(2)}) collective-permute-start(bf16[128,512]{1,0:T(8,128)(2,1)S(1)} %fusion.41), channel_id=1, source_target_pairs={{0,1},{1,2},{2,3},{3,4},{4,5},{5,6},{6,7},{7,8},{8,9},{9,10},{10,1... | collective-permute-start | bytes 393224 | tf_op jit(solution)/shard_map/ppermute | solution.py:17
  84.9 3.4 %collective-permute-start.13 = (bf16[128,512]{1,0:T(8,128)(2,1)S(1)}, bf16[128,512]{1,0:T(8,128)(2,1)}, u32[]{:S(2)}, u32[]{:S(2)}) collective-permute-start(bf16[128,512]{1,0:T(8,128)(2,1)S(1)} %fusion.41), channel_id=1, source_target_pairs={{1,0},{2,1},{3,2},{4,3},{5,4},{6,5},{7,6},{8,7},{9,8},{10,9},{11,1... | collective-permute-start | bytes 393224 | tf_op jit(solution)/shard_map/ppermute | solution.py:19
  90.1 5.2 %all-to-all-start.1 = ((bf16[16,128,512]{1,2,0:T(8,128)(2,1)}), bf16[16,128,512]{1,2,0:T(8,128)(2,1)}, u32[]{:S(2)}, u32[]{:S(2)}) async-start(bf16[16,128,512]{1,2,0:T(8,128)(2,1)} %broadcast_in_dim.114), calls=%async_computation.1 | async-start | bytes 4194304 | tf_op jit(solution)/shard_map/all_to_all | solution.py:75
  95.3 4.3 %convolution_convert_fusion = bf16[128,5120]{1,0:T(8,128)(2,1)S(1)} fusion(bf16[128,512]{0,1:T(8,128)(2,1)S(1)} %add_convert_fusion, bf16[5120,512]{1,0:T(8,128)(2,1)} %bitcast.314), kind=kOutput, calls=%fused_computation.6 | convolution fusion | flops 671744000 | bytes 6684672 | tf_op jit(solution)/shard_map/dot_general | solution.py:219
  114.3 12.1 %all-to-all-done.1 = bf16[16,128,512]{1,2,0:T(8,128)(2,1)} async-done(((bf16[16,128,512]{1,2,0:T(8,128)(2,1)}), bf16[16,128,512]{1,2,0:T(8,128)(2,1)}, u32[]{:S(2)}, u32[]{:S(2)}) %all-to-all-start.1) | async-done | bytes 2097184 | tf_op jit(solution)/shard_map/all_to_all | solution.py:75
  126.4 3.6 %fusion.31 = bf16[16,32,320]{2,1,0:T(8,128)(2,1)} fusion(bf16[16,128,16,32]{1,3,2,0:T(8,128)(2,1)} %bitcast.84, bf16[16,128,320]{1,2,0:T(8,128)(2,1)S(1)} %copy-done.2), kind=kOutput, calls=%fused_computation.42 | convolution fusion | flops 671252480 | bytes 3735552 | tf_op jit(solution)/shard_map/rtk,rtjc->jck/dot_general | solution.py:204
  130.0 10.4 %all-to-all-start.2 = ((bf16[16,32,320]{2,1,0:T(8,128)(2,1)}), bf16[16,32,320]{2,1,0:T(8,128)(2,1)S(1)}, u32[]{:S(2)}, u32[]{:S(2)}) async-start(bf16[16,32,320]{2,1,0:T(8,128)(2,1)} %fusion.31), calls=%async_computation.2 | async-start | bytes 786432 | tf_op jit(solution)/shard_map/all_to_all | solution.py:75
  140.4 2.0 %collective-permute-start.14 = (bf16[128,512]{0,1:T(8,128)(2,1)S(1)}, bf16[128,512]{0,1:T(8,128)(2,1)S(1)}, u32[]{:S(2)}, u32[]{:S(2)}) collective-permute-start(bf16[128,512]{0,1:T(8,128)(2,1)S(1)} %get-tuple-element.32), channel_id=1, source_target_pairs={{1,0},{2,1},{3,2},{4,3},{5,4},{6,5},{7,6},{8,7},{9,8},{10,9},{11,1... | collective-permute-start | bytes 393224 | tf_op jit(solution)/shard_map/ppermute | solution.py:88
  142.5 4.7 %collective-permute-start.15 = (bf16[128,512]{0,1:T(8,128)(2,1)S(1)}, bf16[128,512]{0,1:T(8,128)(2,1)S(1)}, u32[]{:S(2)}, u32[]{:S(2)}) collective-permute-start(bf16[128,512]{0,1:T(8,128)(2,1)S(1)} %get-tuple-element.33), channel_id=1, source_target_pairs={{0,1},{1,2},{2,3},{3,4},{4,5},{5,6},{6,7},{7,8},{8,9},{9,10},{10,1... | collective-permute-start | bytes 393224 | tf_op jit(solution)/shard_map/ppermute | solution.py:88
  148.4 6.3 %collective-permute-done.14 = bf16[128,512]{0,1:T(8,128)(2,1)S(1)} collective-permute-done((bf16[128,512]{0,1:T(8,128)(2,1)S(1)}, bf16[128,512]{0,1:T(8,128)(2,1)S(1)}, u32[]{:S(2)}, u32[]{:S(2)}) %collective-permute-start.14) | collective-permute-done | bytes 131104 | tf_op jit(solution)/shard_map/ppermute | solution.py:88
  (119 shorter events, 52.9 us)
Async XLA Ops:
  0.6 18.3 %copy-start.3 = (bf16[1,128,2560]{2,1,0:T(8,128)(2,1)S(1)}, bf16[1,128,2560]{2,1,0:T(8,128)(2,1)}, u32[]{:S(2)}) copy-start(bf16[1,128,2560]{2,1,0:T(8,128)(2,1)} %param.8) | copy-start | bytes 1966084
  0.6 12.5 %collective-permute-start = (bf16[320,512]{1,0:T(8,128)(2,1)}, bf16[320,512]{1,0:T(8,128)(2,1)}, u32[]{:S(2)}, u32[]{:S(2)}) collective-permute-start(bf16[320,512]{1,0:T(8,128)(2,1)} %param.11), channel_id=1, source_target_pairs={{0,129},{1,128},{2,131},{3,130},{4,133},{5,132},{6,135},{7,134},{8... | collective-permute-start | bytes 983048 | tf_op jit(solution)/shard_map/ppermute | solution.py:44
  2.2 18.3 %collective-permute-start.1 = (bf16[320,512]{1,0:T(8,128)(2,1)}, bf16[320,512]{1,0:T(8,128)(2,1)}, u32[]{:S(2)}, u32[]{:S(2)}) collective-permute-start(bf16[320,512]{1,0:T(8,128)(2,1)} %param.11), channel_id=1, source_target_pairs={{0,32},{16,48},{32,64},{48,80},{64,96},{80,112},{96,0},{112,16},{1... | collective-permute-start | bytes 983048 | tf_op jit(solution)/shard_map/ppermute | solution.py:50
  3.5 15.8 %copy-start.4 = (bf16[1,128,2560]{2,1,0:T(8,128)(2,1)S(1)}, bf16[1,128,2560]{2,1,0:T(8,128)(2,1)}, u32[]{:S(2)}) copy-start(bf16[1,128,2560]{2,1,0:T(8,128)(2,1)} %param.10) | copy-start | bytes 1966084
  3.5 16.3 %collective-permute-start.7 = (bf16[128,512]{0,1:T(8,128)(2,1)S(1)}, bf16[128,512]{0,1:T(8,128)(2,1)S(1)}, u32[]{:S(2)}, u32[]{:S(2)}) collective-permute-start(bf16[128,512]{0,1:T(8,128)(2,1)S(1)} %bitcast.334), channel_id=1, source_target_pairs={{0,1},{1,2},{2,3},{3,4},{4,5},{5,6},{6,7},{7,8},{8,9},{9,10},{10,1... | collective-permute-start | bytes 393224 | tf_op jit(solution)/shard_map/ppermute | solution.py:17
  8.7 11.7 %collective-permute-start.8 = (bf16[128,512]{0,1:T(8,128)(2,1)S(1)}, bf16[128,512]{0,1:T(8,128)(2,1)S(1)}, u32[]{:S(2)}, u32[]{:S(2)}) collective-permute-start(bf16[128,512]{0,1:T(8,128)(2,1)S(1)} %bitcast.335), channel_id=1, source_target_pairs={{1,0},{2,1},{3,2},{4,3},{5,4},{6,5},{7,6},{8,7},{9,8},{10,9},{11,1... | collective-permute-start | bytes 393224 | tf_op jit(solution)/shard_map/ppermute | solution.py:19
  13.2 11.2 %collective-permute-start.4 = (bf16[320,512]{1,0:T(8,128)(2,1)}, bf16[320,512]{1,0:T(8,128)(2,1)}, u32[]{:S(2)}, u32[]{:S(2)}) collective-permute-start(bf16[320,512]{1,0:T(8,128)(2,1)} %collective-permute-done), channel_id=1, source_target_pairs={{0,96},{16,112},{32,0},{48,16},{64,32},{80,48},{96,64},{112,80},{1... | collective-permute-start | bytes 983048 | tf_op jit(solution)/shard_map/ppermute | solution.py:50
  15.1 12.1 %collective-permute-start.2 = (bf16[320,512]{1,0:T(8,128)(2,1)}, bf16[320,512]{1,0:T(8,128)(2,1)}, u32[]{:S(2)}, u32[]{:S(2)}) collective-permute-start(bf16[320,512]{1,0:T(8,128)(2,1)} %collective-permute-done), channel_id=1, source_target_pairs={{0,32},{16,48},{32,64},{48,80},{64,96},{80,112},{96,0},{112,16},{1... | collective-permute-start | bytes 983048 | tf_op jit(solution)/shard_map/ppermute | solution.py:50
  19.6 36.2 %copy-start.5 = (bf16[1,128,2560]{1,2,0:T(8,128)(2,1)}, bf16[1,128,2560]{1,2,0:T(8,128)(2,1)S(1)}, u32[]{:S(2)}) copy-start(bf16[1,128,2560]{1,2,0:T(8,128)(2,1)S(1)} %copy.94) | copy-start | bytes 1966084
  19.7 12.1 %collective-permute-start.6 = (bf16[320,512]{1,0:T(8,128)(2,1)}, bf16[320,512]{1,0:T(8,128)(2,1)S(1)}, u32[]{:S(2)}, u32[]{:S(2)}) collective-permute-start(bf16[320,512]{1,0:T(8,128)(2,1)} %param.11), channel_id=1, source_target_pairs={{0,96},{16,112},{32,0},{48,16},{64,32},{80,48},{96,64},{112,80},{1... | collective-permute-start | bytes 983048 | tf_op jit(solution)/shard_map/ppermute | solution.py:50
  20.5 33.9 %copy-start.7 = (bf16[384,512]{0,1:T(8,128)(2,1)}, bf16[384,512]{0,1:T(8,128)(2,1)S(1)}, u32[]{:S(2)}) copy-start(bf16[384,512]{0,1:T(8,128)(2,1)S(1)} %pad_maximum_fusion.5) | copy-start | bytes 1179652
  20.5 12.4 %collective-permute-start.3 = (bf16[320,512]{1,0:T(8,128)(2,1)}, bf16[320,512]{1,0:T(8,128)(2,1)S(1)}, u32[]{:S(2)}, u32[]{:S(2)}) collective-permute-start(bf16[320,512]{1,0:T(8,128)(2,1)} %collective-permute-done.1), channel_id=1, source_target_pairs={{0,32},{16,48},{32,64},{48,80},{64,96},{80,112},{96,0},{112,16},{1... | collective-permute-start | bytes 983048 | tf_op jit(solution)/shard_map/ppermute | solution.py:50
  24.4 13.0 %collective-permute-start.5 = (bf16[320,512]{1,0:T(8,128)(2,1)}, bf16[320,512]{1,0:T(8,128)(2,1)S(1)}, u32[]{:S(2)}, u32[]{:S(2)}) collective-permute-start(bf16[320,512]{1,0:T(8,128)(2,1)} %collective-permute-done.4), channel_id=1, source_target_pairs={{0,96},{16,112},{32,0},{48,16},{64,32},{80,48},{96,64},{112,80},{1... | collective-permute-start | bytes 983048 | tf_op jit(solution)/shard_map/ppermute | solution.py:50
  39.3 24.1 %all-to-all-start = ((bf16[16,128,320]{1,2,0:T(8,128)(2,1)}), bf16[16,128,320]{1,2,0:T(8,128)(2,1)S(1)}, u32[]{:S(2)}, u32[]{:S(2)}) async-start(bf16[16,128,320]{1,2,0:T(8,128)(2,1)} %bitcast.14), calls=%async_computation | async-start | bytes 2621440 | tf_op jit(solution)/shard_map/all_to_all | solution.py:75
  43.8 32.6 %collective-permute-start.11 = (bf16[4,2,320,512]{3,2,1,0:T(8,128)(2,1)}, bf16[4,2,320,512]{3,2,1,0:T(8,128)(2,1)}, u32[]{:S(2)}, u32[]{:S(2)}) collective-permute-start(bf16[4,2,320,512]{3,2,1,0:T(8,128)(2,1)} %pad_maximum_fusion.1), channel_id=1, source_target_pairs={{0,16},{16,0},{32,48},{48,32},{64,80},{80,64},{96,112},{112,96},{1... | collective-permute-start | bytes 7864328 | tf_op jit(solution)/shard_map/ppermute | solution.py:59
  63.4 10.3 %collective-permute-start.10 = (bf16[128,512]{0,1:T(8,128)(2,1)S(1)}, bf16[128,512]{0,1:T(8,128)(2,1)S(1)}, u32[]{:S(2)}, u32[]{:S(2)}) collective-permute-start(bf16[128,512]{0,1:T(8,128)(2,1)S(1)} %get-tuple-element.39), channel_id=1, source_target_pairs={{0,1},{1,2},{2,3},{3,4},{4,5},{5,6},{6,7},{7,8},{8,9},{9,10},{10,1... | collective-permute-start | bytes 393224 | tf_op jit(solution)/shard_map/ppermute | solution.py:88
  68.2 8.2 %collective-permute-start.9 = (bf16[128,512]{0,1:T(8,128)(2,1)S(1)}, bf16[128,512]{0,1:T(8,128)(2,1)S(1)}, u32[]{:S(2)}, u32[]{:S(2)}) collective-permute-start(bf16[128,512]{0,1:T(8,128)(2,1)S(1)} %get-tuple-element.38), channel_id=1, source_target_pairs={{1,0},{2,1},{3,2},{4,3},{5,4},{6,5},{7,6},{8,7},{9,8},{10,9},{11,1... | collective-permute-start | bytes 393224 | tf_op jit(solution)/shard_map/ppermute | solution.py:88
  81.8 20.8 %collective-permute-start.12 = (bf16[128,512]{1,0:T(8,128)(2,1)S(1)}, bf16[128,512]{1,0:T(8,128)(2,1)}, u32[]{:S(2)}, u32[]{:S(2)}) collective-permute-start(bf16[128,512]{1,0:T(8,128)(2,1)S(1)} %fusion.41), channel_id=1, source_target_pairs={{0,1},{1,2},{2,3},{3,4},{4,5},{5,6},{6,7},{7,8},{8,9},{9,10},{10,1... | collective-permute-start | bytes 393224 | tf_op jit(solution)/shard_map/ppermute | solution.py:17
  84.9 17.8 %collective-permute-start.13 = (bf16[128,512]{1,0:T(8,128)(2,1)S(1)}, bf16[128,512]{1,0:T(8,128)(2,1)}, u32[]{:S(2)}, u32[]{:S(2)}) collective-permute-start(bf16[128,512]{1,0:T(8,128)(2,1)S(1)} %fusion.41), channel_id=1, source_target_pairs={{1,0},{2,1},{3,2},{4,3},{5,4},{6,5},{7,6},{8,7},{9,8},{10,9},{11,1... | collective-permute-start | bytes 393224 | tf_op jit(solution)/shard_map/ppermute | solution.py:19
  90.1 36.4 %all-to-all-start.1 = ((bf16[16,128,512]{1,2,0:T(8,128)(2,1)}), bf16[16,128,512]{1,2,0:T(8,128)(2,1)}, u32[]{:S(2)}, u32[]{:S(2)}) async-start(bf16[16,128,512]{1,2,0:T(8,128)(2,1)} %broadcast_in_dim.114), calls=%async_computation.1 | async-start | bytes 4194304 | tf_op jit(solution)/shard_map/all_to_all | solution.py:75
  113.6 12.8 %copy-start.2 = (bf16[16,128,320]{1,2,0:T(8,128)(2,1)S(1)}, bf16[16,128,320]{1,2,0:T(8,128)(2,1)}, u32[]{:S(2)}) copy-start(bf16[16,128,320]{1,2,0:T(8,128)(2,1)} %copy-done.1) | copy-start | bytes 3932164
  130.0 26.3 %all-to-all-start.2 = ((bf16[16,32,320]{2,1,0:T(8,128)(2,1)}), bf16[16,32,320]{2,1,0:T(8,128)(2,1)S(1)}, u32[]{:S(2)}, u32[]{:S(2)}) async-start(bf16[16,32,320]{2,1,0:T(8,128)(2,1)} %fusion.31), calls=%async_computation.2 | async-start | bytes 786432 | tf_op jit(solution)/shard_map/all_to_all | solution.py:75
  140.4 14.3 %collective-permute-start.14 = (bf16[128,512]{0,1:T(8,128)(2,1)S(1)}, bf16[128,512]{0,1:T(8,128)(2,1)S(1)}, u32[]{:S(2)}, u32[]{:S(2)}) collective-permute-start(bf16[128,512]{0,1:T(8,128)(2,1)S(1)} %get-tuple-element.32), channel_id=1, source_target_pairs={{1,0},{2,1},{3,2},{4,3},{5,4},{6,5},{7,6},{8,7},{9,8},{10,9},{11,1... | collective-permute-start | bytes 393224 | tf_op jit(solution)/shard_map/ppermute | solution.py:88
  142.5 13.0 %collective-permute-start.15 = (bf16[128,512]{0,1:T(8,128)(2,1)S(1)}, bf16[128,512]{0,1:T(8,128)(2,1)S(1)}, u32[]{:S(2)}, u32[]{:S(2)}) collective-permute-start(bf16[128,512]{0,1:T(8,128)(2,1)S(1)} %get-tuple-element.33), channel_id=1, source_target_pairs={{0,1},{1,2},{2,3},{3,4},{4,5},{5,6},{6,7},{7,8},{8,9},{9,10},{10,1... | collective-permute-start | bytes 393224 | tf_op jit(solution)/shard_map/ppermute | solution.py:88
  (12 other events, 26.7 us)

commit v20 on v19

--- a/solution.py
+++ b/solution.py
@@ -55,8 +55,11 @@
     from_before = jnp.stack([before_own, shifted(held[1], 1)])
     from_after = jnp.stack([shifted(held[0], y_count - 1), after_partner])
     ring = [held, from_before, two_away, from_after]
+    swap_pairs = [(d, d ^ 1) for d in range(dp_count)]
+    near = lax.ppermute(jnp.stack([held, from_before, from_after]), "dp", swap_pairs)
     mine, ready, riders = lax.optimization_barrier((jnp.stack(ring), ready, riders))
-    sibling = lax.ppermute(mine, "dp", [(d, d ^ 1) for d in range(dp_count)])
+    far = lax.ppermute(mine[2], "dp", swap_pairs)
+    sibling = jnp.stack([near[0], near[1], far, near[2]])
     stacked = jnp.stack([mine, sibling]).reshape(dp_count, rows, width)
     me = lax.axis_index("dp")
     upper, y_here, core = me // half, (me // cores) % y_count, me % cores

time: 158 us -> 166 us (1.051)
  local copies, waits for them, and re-layouts: 17.4 us -> 25.7 us
  matrix products: 30.3 us -> 33.5 us
  waiting for transfers between devices: 36.9 us -> 35.1 us
    sub x4, matrix products: 5.98 us -> 9.56 us  [attend_first(): weights = jnp.where(visible[None], jnp.exp(masked - highest), 0.0)]
    unnamed x41 -> x59, local copies, waits for them, and re-layouts: 10.4 us -> 13.6 us
    another operation x5, other arithmetic: 5.2 us -> 2.52 us  [spread_weight(): jnp.stack(ring)]
    slice x0 -> x2, local copies, waits for them, and re-layouts: none -> 2.53 us  [spread_weight(): sibling = jnp.stack([near[0], near[1], far, near[2]])]
  transfers between devices with their start and end apart: 19 -> 20, of which waited for: 8 -> 7; matrix products, arithmetic and copies ran while one was open for 31% -> 35% of each run, Pallas kernels for 0% -> 0%
where the time goes in v20:
time: 166 us; the launch traced here: 164 us
  starting transfers between devices  56.8 us (34%)
  waiting for transfers between devices  35.1 us (21%)
  matrix products  33.5 us (20%)
  local copies, waits for them, and re-layouts  25.7 us (15%)
  other arithmetic  12 us (7%)
    all_to_all x3, starting transfers between devices, gathered_copies(): return lax.all_to_all(copies, axis, 0, 0, tiled=True)  21.3 us
    all_to_all x3, waiting for transfers between devices, gathered_copies(): return lax.all_to_all(copies, axis, 0, 0, tiled=True)  17.8 us
    unnamed x59, local copies, waits for them, and re-layouts  13.6 us
    ppermute x4, starting transfers between devices, passed_along(): return lax.ppermute(array, axis, pairs)  13.6 us
    sub x4, matrix products, attend_first(): weights = jnp.where(visible[None], jnp.exp(masked - highest), 0.0)  9.56 us
    ppermute x4, waiting for transfers between devices, passed_along(): return lax.ppermute(array, axis, pairs)  8.78 us
    ppermute x6, waiting for transfers between devices, shifted(): return lax.ppermute(array, 'dp', pairs)  8.48 us
    ppermute x2, starting transfers between devices, with_halo(): lax.ppermute(tail, axis, [(i, (i + 1) % count) for i in range(ends)])  8.48 us
  transfers between devices with their start and end apart: 20, of which 7 were waited for; matrix products, arithmetic and copies ran while one was open for 35% of the time, Pallas kernels for 0%

profile of v20, /device:TPU:26, one launch (start us, length us, event | category | flops | bytes accessed | tf_op | source)
XLA Modules:
  0.0 164.2 jit_solution(14148789770668123499)
XLA Ops:
  3.5 5.2 %collective-permute-start.7 = (bf16[128,512]{0,1:T(8,128)(2,1)S(1)}, bf16[128,512]{0,1:T(8,128)(2,1)S(1)}, u32[]{:S(2)}, u32[]{:S(2)}) collective-permute-start(bf16[128,512]{0,1:T(8,128)(2,1)S(1)} %bitcast.339), channel_id=1, source_target_pairs={{0,1},{1,2},{2,3},{3,4},{4,5},{5,6},{6,7},{7,8},{8,9},{9,10},{10,1... | collective-permute-start | bytes 393224 | tf_op jit(solution)/shard_map/ppermute | solution.py:17
  16.6 2.5 %copy.90 = bf16[1,128,5120]{1,2,0:T(8,128)(2,1)} copy(bf16[1,128,5120]{2,1,0:T(8,128)(2,1)} %param.7) | data formatting | bytes 2621440 | tf_op args[0]
  22.0 2.6 %collective-permute-start.3 = (bf16[320,512]{1,0:T(8,128)(2,1)S(1)}, bf16[320,512]{1,0:T(8,128)(2,1)S(1)}, u32[]{:S(2)}, u32[]{:S(2)}) collective-permute-start(bf16[320,512]{1,0:T(8,128)(2,1)S(1)} %collective-permute-done.1), channel_id=1, source_target_pairs={{0,32},{16,48},{32,64},{48,80},{64,96},{80,112},{96,0},{112,16},{1... | collective-permute-start | bytes 983048 | tf_op jit(solution)/shard_map/ppermute | solution.py:50
  26.2 6.3 %collective-permute-done.6 = bf16[320,512]{1,0:T(8,128)(2,1)S(1)} collective-permute-done((bf16[320,512]{1,0:T(8,128)(2,1)S(1)}, bf16[320,512]{1,0:T(8,128)(2,1)S(1)}, u32[]{:S(2)}, u32[]{:S(2)}) %collective-permute-start.6) | collective-permute-done | bytes 327712 | tf_op jit(solution)/shard_map/ppermute | solution.py:50
  35.0 2.1 %collective-permute-done.5 = bf16[320,512]{1,0:T(8,128)(2,1)S(1)} collective-permute-done((bf16[320,512]{1,0:T(8,128)(2,1)}, bf16[320,512]{1,0:T(8,128)(2,1)S(1)}, u32[]{:S(2)}, u32[]{:S(2)}) %collective-permute-start.5) | collective-permute-done | bytes 327712 | tf_op jit(solution)/shard_map/ppermute | solution.py:50
  37.6 2.4 %fusion.85 = (f32[5,128]{1,0:T(8,128)S(1)}, f32[5,128,384]{1,2,0:T(8,128)}) fusion(pred[128,384]{0,1:T(8,128)(4,1)S(1)} %or_and_fusion, bf16[128,4,5,128]{0,3,2,1:T(8,128)(2,1)S(1)} %bitcast.323, bf16[384,4,128]{0,2,1:T(8,128)(2,1)} %bitcast.342), kind=kOutput, calls=%fused_computation.168 | convolution fusion | flops 64143744 | bytes 1346048 | tf_op jit(solution)/shard_map/sub | solution.py:120
  39.9 2.4 %fusion.84 = (f32[5,128]{1,0:T(8,128)S(1)}, f32[5,128,384]{1,2,0:T(8,128)}) fusion(pred[128,384]{0,1:T(8,128)(4,1)S(1)} %or_and_fusion, bf16[128,4,5,128]{0,3,2,1:T(8,128)(2,1)S(1)} %bitcast.324, bf16[384,4,128]{0,2,1:T(8,128)(2,1)} %bitcast.343), kind=kOutput, calls=%fused_computation.167 | convolution fusion | flops 64143744 | bytes 1346048 | tf_op jit(solution)/shard_map/sub | solution.py:120
  42.3 4.5 %all-to-all-start = ((bf16[16,128,320]{1,2,0:T(8,128)(2,1)}), bf16[16,128,320]{1,2,0:T(8,128)(2,1)}, u32[]{:S(2)}, u32[]{:S(2)}) async-start(bf16[16,128,320]{1,2,0:T(8,128)(2,1)} %bitcast.14), calls=%async_computation | async-start | bytes 2621440 | tf_op jit(solution)/shard_map/all_to_all | solution.py:78
  47.9 2.3 %convolution_bitcast_fusion.7 = f32[384,128]{0,1:T(8,128)} fusion(bf16[128,4,5,128]{0,3,2,1:T(8,128)(2,1)} %bitcast.331, f32[5,128,384]{1,2,0:T(8,128)} %get-tuple-element.47, f32[5,128]{1,0:T(8,128)S(1)} %get-tuple-element.46), kind=kOutput, calls=%fused_computation.57 | convolution fusion | flops 63406080 | bytes 1346048 | tf_op jit(solution)/shard_map/gqk,qgd->kd/dot_general | solution.py:125
  52.1 2.4 %fusion.83 = (f32[5,128]{1,0:T(8,128)S(1)}, f32[5,128,384]{1,2,0:T(8,128)}) fusion(pred[128,384]{0,1:T(8,128)(4,1)S(1)} %or_and_fusion, bf16[128,4,5,128]{0,3,2,1:T(8,128)(2,1)S(1)} %bitcast.325, bf16[384,4,128]{0,2,1:T(8,128)(2,1)} %bitcast.344), kind=kOutput, calls=%fused_computation.166 | convolution fusion | flops 64143744 | bytes 1346048 | tf_op jit(solution)/shard_map/sub | solution.py:120
  55.1 2.2 %convolution_bitcast_fusion.5 = f32[384,128]{0,1:T(8,128)} fusion(bf16[128,4,5,128]{0,3,2,1:T(8,128)(2,1)} %bitcast.333, f32[5,128,384]{1,2,0:T(8,128)} %get-tuple-element.43, f32[5,128]{1,0:T(8,128)S(1)} %get-tuple-element.42), kind=kOutput, calls=%fused_computation.55 | convolution fusion | flops 63406080 | bytes 1346048 | tf_op jit(solution)/shard_map/gqk,qgd->kd/dot_general | solution.py:125
  57.3 2.4 %fusion.82 = (f32[5,128]{1,0:T(8,128)S(1)}, f32[5,128,384]{1,2,0:T(8,128)}) fusion(pred[128,384]{0,1:T(8,128)(4,1)S(1)} %or_and_fusion, bf16[128,4,5,128]{0,3,2,1:T(8,128)(2,1)S(1)} %bitcast.326, bf16[384,4,128]{0,2,1:T(8,128)(2,1)} %bitcast.345), kind=kOutput, calls=%fused_computation.165 | convolution fusion | flops 64143744 | bytes 1346048 | tf_op jit(solution)/shard_map/sub | solution.py:120
  61.9 4.6 %all-to-all-done = bf16[16,128,320]{1,2,0:T(8,128)(2,1)} async-done(((bf16[16,128,320]{1,2,0:T(8,128)(2,1)}), bf16[16,128,320]{1,2,0:T(8,128)(2,1)}, u32[]{:S(2)}, u32[]{:S(2)}) %all-to-all-start) | async-done | bytes 1310752 | tf_op jit(solution)/shard_map/all_to_all | solution.py:78
  67.2 4.7 %collective-permute-start.10 = (bf16[128,512]{0,1:T(8,128)(2,1)}, bf16[128,512]{0,1:T(8,128)(2,1)}, u32[]{:S(2)}, u32[]{:S(2)}) collective-permute-start(bf16[128,512]{0,1:T(8,128)(2,1)} %get-tuple-element.39), channel_id=1, source_target_pairs={{0,1},{1,2},{2,3},{3,4},{4,5},{5,6},{6,7},{7,8},{8,9},{9,10},{10,1... | collective-permute-start | bytes 393224 | tf_op jit(solution)/shard_map/ppermute | solution.py:91
  75.4 3.1 %gather_fusion = bf16[16,128,320]{1,2,0:T(8,128)(2,1)} fusion(bf16[128,16,320]{0,2,1:T(8,128)(2,1)} %bitcast.13, s32[1024]{0:T(1024)S(1)} %pad_clamp_fusion.1), kind=kCustom, calls=%fused_computation | custom fusion | bytes 2621504 | tf_op jit(solution)/shard_map/jit(_take)/gather | solution.py:213
  88.1 3.3 %collective-permute-start.13 = (bf16[128,512]{1,0:T(8,128)(2,1)S(1)}, bf16[128,512]{1,0:T(8,128)(2,1)S(1)}, u32[]{:S(2)}, u32[]{:S(2)}) collective-permute-start(bf16[128,512]{1,0:T(8,128)(2,1)S(1)} %fusion.41), channel_id=1, source_target_pairs={{0,1},{1,2},{2,3},{3,4},{4,5},{5,6},{6,7},{7,8},{8,9},{9,10},{10,1... | collective-permute-start | bytes 393224 | tf_op jit(solution)/shard_map/ppermute | solution.py:17
  91.3 2.6 %collective-permute-start.14 = (bf16[128,512]{1,0:T(8,128)(2,1)S(1)}, bf16[128,512]{1,0:T(8,128)(2,1)S(1)}, u32[]{:S(2)}, u32[]{:S(2)}) collective-permute-start(bf16[128,512]{1,0:T(8,128)(2,1)S(1)} %fusion.41), channel_id=1, source_target_pairs={{1,0},{2,1},{3,2},{4,3},{5,4},{6,5},{7,6},{8,7},{9,8},{10,9},{11,1... | collective-permute-start | bytes 393224 | tf_op jit(solution)/shard_map/ppermute | solution.py:19
  95.7 5.2 %all-to-all-start.1 = ((bf16[16,128,512]{1,2,0:T(8,128)(2,1)}), bf16[16,128,512]{1,2,0:T(8,128)(2,1)}, u32[]{:S(2)}, u32[]{:S(2)}) async-start(bf16[16,128,512]{1,2,0:T(8,128)(2,1)} %broadcast_in_dim.114), calls=%async_computation.1 | async-start | bytes 4194304 | tf_op jit(solution)/shard_map/all_to_all | solution.py:78
  100.9 4.3 %convolution_convert_fusion = bf16[128,5120]{1,0:T(8,128)(2,1)S(1)} fusion(bf16[128,512]{0,1:T(8,128)(2,1)S(1)} %add_convert_fusion, bf16[5120,512]{1,0:T(8,128)(2,1)} %bitcast.318), kind=kOutput, calls=%fused_computation.6 | convolution fusion | flops 671744000 | bytes 6684672 | tf_op jit(solution)/shard_map/dot_general | solution.py:222
  118.9 13.2 %all-to-all-done.1 = bf16[16,128,512]{1,2,0:T(8,128)(2,1)} async-done(((bf16[16,128,512]{1,2,0:T(8,128)(2,1)}), bf16[16,128,512]{1,2,0:T(8,128)(2,1)}, u32[]{:S(2)}, u32[]{:S(2)}) %all-to-all-start.1) | async-done | bytes 2097184 | tf_op jit(solution)/shard_map/all_to_all | solution.py:78
  132.1 4.0 %fusion.31 = bf16[16,32,320]{2,1,0:T(8,128)(2,1)} fusion(bf16[16,128,16,32]{1,3,2,0:T(8,128)(2,1)} %bitcast.86, bf16[16,128,320]{1,2,0:T(8,128)(2,1)} %all-to-all-done), kind=kOutput, calls=%fused_computation.44 | convolution fusion | flops 671252480 | bytes 3735552 | tf_op jit(solution)/shard_map/rtk,rtjc->jck/dot_general | solution.py:207
  136.1 11.6 %all-to-all-start.2 = ((bf16[16,32,320]{2,1,0:T(8,128)(2,1)}), bf16[16,32,320]{2,1,0:T(8,128)(2,1)S(1)}, u32[]{:S(2)}, u32[]{:S(2)}) async-start(bf16[16,32,320]{2,1,0:T(8,128)(2,1)} %fusion.31), calls=%async_computation.2 | async-start | bytes 786432 | tf_op jit(solution)/shard_map/all_to_all | solution.py:78
  149.7 4.7 %collective-permute-start.16 = (bf16[128,512]{0,1:T(8,128)(2,1)S(1)}, bf16[128,512]{0,1:T(8,128)(2,1)S(1)}, u32[]{:S(2)}, u32[]{:S(2)}) collective-permute-start(bf16[128,512]{0,1:T(8,128)(2,1)S(1)} %get-tuple-element.33), channel_id=1, source_target_pairs={{0,1},{1,2},{2,3},{3,4},{4,5},{5,6},{6,7},{7,8},{8,9},{9,10},{10,1... | collective-permute-start | bytes 393224 | tf_op jit(solution)/shard_map/ppermute | solution.py:91
  155.7 6.3 %collective-permute-done.15 = bf16[128,512]{0,1:T(8,128)(2,1)S(1)} collective-permute-done((bf16[128,512]{0,1:T(8,128)(2,1)S(1)}, bf16[128,512]{0,1:T(8,128)(2,1)S(1)}, u32[]{:S(2)}, u32[]{:S(2)}) %collective-permute-start.15) | collective-permute-done | bytes 131104 | tf_op jit(solution)/shard_map/ppermute | solution.py:91
  (144 shorter events, 58.1 us)
Async XLA Ops:
  0.6 18.4 %copy-start.2 = (bf16[1,128,2560]{2,1,0:T(8,128)(2,1)S(1)}, bf16[1,128,2560]{2,1,0:T(8,128)(2,1)}, u32[]{:S(2)}) copy-start(bf16[1,128,2560]{2,1,0:T(8,128)(2,1)} %param.8) | copy-start | bytes 1966084
  0.6 12.5 %collective-permute-start = (bf16[320,512]{1,0:T(8,128)(2,1)}, bf16[320,512]{1,0:T(8,128)(2,1)S(1)}, u32[]{:S(2)}, u32[]{:S(2)}) collective-permute-start(bf16[320,512]{1,0:T(8,128)(2,1)} %param.11), channel_id=1, source_target_pairs={{0,129},{1,128},{2,131},{3,130},{4,133},{5,132},{6,135},{7,134},{8... | collective-permute-start | bytes 983048 | tf_op jit(solution)/shard_map/ppermute | solution.py:44
  2.2 19.8 %collective-permute-start.1 = (bf16[320,512]{1,0:T(8,128)(2,1)}, bf16[320,512]{1,0:T(8,128)(2,1)S(1)}, u32[]{:S(2)}, u32[]{:S(2)}) collective-permute-start(bf16[320,512]{1,0:T(8,128)(2,1)} %param.11), channel_id=1, source_target_pairs={{0,32},{16,48},{32,64},{48,80},{64,96},{80,112},{96,0},{112,16},{1... | collective-permute-start | bytes 983048 | tf_op jit(solution)/shard_map/ppermute | solution.py:50
  3.5 15.9 %copy-start.3 = (bf16[1,128,2560]{2,1,0:T(8,128)(2,1)S(1)}, bf16[1,128,2560]{2,1,0:T(8,128)(2,1)}, u32[]{:S(2)}) copy-start(bf16[1,128,2560]{2,1,0:T(8,128)(2,1)} %param.10) | copy-start | bytes 1966084
  3.5 17.1 %collective-permute-start.7 = (bf16[128,512]{0,1:T(8,128)(2,1)S(1)}, bf16[128,512]{0,1:T(8,128)(2,1)S(1)}, u32[]{:S(2)}, u32[]{:S(2)}) collective-permute-start(bf16[128,512]{0,1:T(8,128)(2,1)S(1)} %bitcast.339), channel_id=1, source_target_pairs={{0,1},{1,2},{2,3},{3,4},{4,5},{5,6},{6,7},{7,8},{8,9},{9,10},{10,1... | collective-permute-start | bytes 393224 | tf_op jit(solution)/shard_map/ppermute | solution.py:17
  8.7 12.5 %collective-permute-start.8 = (bf16[128,512]{0,1:T(8,128)(2,1)S(1)}, bf16[128,512]{0,1:T(8,128)(2,1)S(1)}, u32[]{:S(2)}, u32[]{:S(2)}) collective-permute-start(bf16[128,512]{0,1:T(8,128)(2,1)S(1)} %bitcast.340), channel_id=1, source_target_pairs={{1,0},{2,1},{3,2},{4,3},{5,4},{6,5},{7,6},{8,7},{9,8},{10,9},{11,1... | collective-permute-start | bytes 393224 | tf_op jit(solution)/shard_map/ppermute | solution.py:19
  13.2 11.6 %collective-permute-start.4 = (bf16[320,512]{1,0:T(8,128)(2,1)S(1)}, bf16[320,512]{1,0:T(8,128)(2,1)}, u32[]{:S(2)}, u32[]{:S(2)}) collective-permute-start(bf16[320,512]{1,0:T(8,128)(2,1)S(1)} %collective-permute-done), channel_id=1, source_target_pairs={{0,96},{16,112},{32,0},{48,16},{64,32},{80,48},{96,64},{112,80},{1... | collective-permute-start | bytes 983048 | tf_op jit(solution)/shard_map/ppermute | solution.py:50
  15.1 10.1 %collective-permute-start.2 = (bf16[320,512]{1,0:T(8,128)(2,1)S(1)}, bf16[320,512]{1,0:T(8,128)(2,1)}, u32[]{:S(2)}, u32[]{:S(2)}) collective-permute-start(bf16[320,512]{1,0:T(8,128)(2,1)S(1)} %collective-permute-done), channel_id=1, source_target_pairs={{0,32},{16,48},{32,64},{48,80},{64,96},{80,112},{96,0},{112,16},{1... | collective-permute-start | bytes 983048 | tf_op jit(solution)/shard_map/ppermute | solution.py:50
  19.4 37.9 %copy-start.4 = (bf16[1,128,2560]{1,2,0:T(8,128)(2,1)}, bf16[1,128,2560]{1,2,0:T(8,128)(2,1)S(1)}, u32[]{:S(2)}) copy-start(bf16[1,128,2560]{1,2,0:T(8,128)(2,1)S(1)} %copy.92) | copy-start | bytes 1966084
  20.5 11.9 %collective-permute-start.6 = (bf16[320,512]{1,0:T(8,128)(2,1)S(1)}, bf16[320,512]{1,0:T(8,128)(2,1)S(1)}, u32[]{:S(2)}, u32[]{:S(2)}) collective-permute-start(bf16[320,512]{1,0:T(8,128)(2,1)S(1)} %copy-done.8), channel_id=1, source_target_pairs={{0,96},{16,112},{32,0},{48,16},{64,32},{80,48},{96,64},{112,80},{1... | collective-permute-start | bytes 983048 | tf_op jit(solution)/shard_map/ppermute | solution.py:50
  22.0 13.0 %collective-permute-start.3 = (bf16[320,512]{1,0:T(8,128)(2,1)S(1)}, bf16[320,512]{1,0:T(8,128)(2,1)S(1)}, u32[]{:S(2)}, u32[]{:S(2)}) collective-permute-start(bf16[320,512]{1,0:T(8,128)(2,1)S(1)} %collective-permute-done.1), channel_id=1, source_target_pairs={{0,32},{16,48},{32,64},{48,80},{64,96},{80,112},{96,0},{112,16},{1... | collective-permute-start | bytes 983048 | tf_op jit(solution)/shard_map/ppermute | solution.py:50
  24.8 12.4 %collective-permute-start.5 = (bf16[320,512]{1,0:T(8,128)(2,1)}, bf16[320,512]{1,0:T(8,128)(2,1)S(1)}, u32[]{:S(2)}, u32[]{:S(2)}) collective-permute-start(bf16[320,512]{1,0:T(8,128)(2,1)} %collective-permute-done.4), channel_id=1, source_target_pairs={{0,96},{16,112},{32,0},{48,16},{64,32},{80,48},{96,64},{112,80},{1... | collective-permute-start | bytes 983048 | tf_op jit(solution)/shard_map/ppermute | solution.py:50
  35.0 46.3 %collective-permute-start.11 = (bf16[3,2,320,512]{3,2,1,0:T(8,128)(2,1)}, bf16[3,2,320,512]{3,2,1,0:T(8,128)(2,1)}, u32[]{:S(2)}, u32[]{:S(2)}) collective-permute-start(bf16[3,2,320,512]{3,2,1,0:T(8,128)(2,1)} %pad_maximum_fusion.2), channel_id=1, source_target_pairs={{0,16},{16,0},{32,48},{48,32},{64,80},{80,64},{96,112},{112,96},{1... | collective-permute-start | bytes 5898248 | tf_op jit(solution)/shard_map/ppermute | solution.py:59
  39.9 8.0 %copy-start.20 = (f32[5,128]{1,0:T(8,128)}, f32[5,128]{1,0:T(8,128)S(1)}, u32[]{:S(2)}) copy-start(f32[5,128]{1,0:T(8,128)S(1)} %get-tuple-element.46) | copy-start | bytes 7684
  42.3 24.2 %all-to-all-start = ((bf16[16,128,320]{1,2,0:T(8,128)(2,1)}), bf16[16,128,320]{1,2,0:T(8,128)(2,1)}, u32[]{:S(2)}, u32[]{:S(2)}) async-start(bf16[16,128,320]{1,2,0:T(8,128)(2,1)} %bitcast.14), calls=%async_computation | async-start | bytes 2621440 | tf_op jit(solution)/shard_map/all_to_all | solution.py:78
  47.7 36.1 %collective-permute-start.12 = (bf16[2,320,512]{2,1,0:T(8,128)(2,1)}, bf16[2,320,512]{2,1,0:T(8,128)(2,1)}, u32[]{:S(2)}, u32[]{:S(2)}) collective-permute-start(bf16[2,320,512]{2,1,0:T(8,128)(2,1)} %slice_bitcast_fusion), channel_id=1, source_target_pairs={{0,16},{16,0},{32,48},{48,32},{64,80},{80,64},{96,112},{112,96},{1... | collective-permute-start | bytes 1966088 | tf_op jit(solution)/shard_map/ppermute | solution.py:61
  67.2 11.3 %collective-permute-start.10 = (bf16[128,512]{0,1:T(8,128)(2,1)}, bf16[128,512]{0,1:T(8,128)(2,1)}, u32[]{:S(2)}, u32[]{:S(2)}) collective-permute-start(bf16[128,512]{0,1:T(8,128)(2,1)} %get-tuple-element.39), channel_id=1, source_target_pairs={{0,1},{1,2},{2,3},{3,4},{4,5},{5,6},{6,7},{7,8},{8,9},{9,10},{10,1... | collective-permute-start | bytes 393224 | tf_op jit(solution)/shard_map/ppermute | solution.py:91
  72.0 8.3 %collective-permute-start.9 = (bf16[128,512]{0,1:T(8,128)(2,1)S(1)}, bf16[128,512]{0,1:T(8,128)(2,1)}, u32[]{:S(2)}, u32[]{:S(2)}) collective-permute-start(bf16[128,512]{0,1:T(8,128)(2,1)S(1)} %get-tuple-element.38), channel_id=1, source_target_pairs={{1,0},{2,1},{3,2},{4,3},{5,4},{6,5},{7,6},{8,7},{9,8},{10,9},{11,1... | collective-permute-start | bytes 393224 | tf_op jit(solution)/shard_map/ppermute | solution.py:91
  88.1 20.2 %collective-permute-start.13 = (bf16[128,512]{1,0:T(8,128)(2,1)S(1)}, bf16[128,512]{1,0:T(8,128)(2,1)S(1)}, u32[]{:S(2)}, u32[]{:S(2)}) collective-permute-start(bf16[128,512]{1,0:T(8,128)(2,1)S(1)} %fusion.41), channel_id=1, source_target_pairs={{0,1},{1,2},{2,3},{3,4},{4,5},{5,6},{6,7},{7,8},{8,9},{9,10},{10,1... | collective-permute-start | bytes 393224 | tf_op jit(solution)/shard_map/ppermute | solution.py:17
  91.3 16.9 %collective-permute-start.14 = (bf16[128,512]{1,0:T(8,128)(2,1)S(1)}, bf16[128,512]{1,0:T(8,128)(2,1)S(1)}, u32[]{:S(2)}, u32[]{:S(2)}) collective-permute-start(bf16[128,512]{1,0:T(8,128)(2,1)S(1)} %fusion.41), channel_id=1, source_target_pairs={{1,0},{2,1},{3,2},{4,3},{5,4},{6,5},{7,6},{8,7},{9,8},{10,9},{11,1... | collective-permute-start | bytes 393224 | tf_op jit(solution)/shard_map/ppermute | solution.py:19
  95.7 36.4 %all-to-all-start.1 = ((bf16[16,128,512]{1,2,0:T(8,128)(2,1)}), bf16[16,128,512]{1,2,0:T(8,128)(2,1)}, u32[]{:S(2)}, u32[]{:S(2)}) async-start(bf16[16,128,512]{1,2,0:T(8,128)(2,1)} %broadcast_in_dim.114), calls=%async_computation.1 | async-start | bytes 4194304 | tf_op jit(solution)/shard_map/all_to_all | solution.py:78
  136.1 27.5 %all-to-all-start.2 = ((bf16[16,32,320]{2,1,0:T(8,128)(2,1)}), bf16[16,32,320]{2,1,0:T(8,128)(2,1)S(1)}, u32[]{:S(2)}, u32[]{:S(2)}) async-start(bf16[16,32,320]{2,1,0:T(8,128)(2,1)} %fusion.31), calls=%async_computation.2 | async-start | bytes 786432 | tf_op jit(solution)/shard_map/all_to_all | solution.py:78
  147.7 14.3 %collective-permute-start.15 = (bf16[128,512]{0,1:T(8,128)(2,1)S(1)}, bf16[128,512]{0,1:T(8,128)(2,1)S(1)}, u32[]{:S(2)}, u32[]{:S(2)}) collective-permute-start(bf16[128,512]{0,1:T(8,128)(2,1)S(1)} %get-tuple-element.32), channel_id=1, source_target_pairs={{1,0},{2,1},{3,2},{4,3},{5,4},{6,5},{7,6},{8,7},{9,8},{10,9},{11,1... | collective-permute-start | bytes 393224 | tf_op jit(solution)/shard_map/ppermute | solution.py:91
  149.7 13.0 %collective-permute-start.16 = (bf16[128,512]{0,1:T(8,128)(2,1)S(1)}, bf16[128,512]{0,1:T(8,128)(2,1)S(1)}, u32[]{:S(2)}, u32[]{:S(2)}) collective-permute-start(bf16[128,512]{0,1:T(8,128)(2,1)S(1)} %get-tuple-element.33), channel_id=1, source_target_pairs={{0,1},{1,2},{2,3},{3,4},{4,5},{5,6},{6,7},{7,8},{8,9},{9,10},{10,1... | collective-permute-start | bytes 393224 | tf_op jit(solution)/shard_map/ppermute | solution.py:91
  (22 other events, 40.4 us)
